TPU v7x, 32 devices: a whole 2x2x4 slice. The times are simulated.
32 devices in a mesh: dp: 8 (over z, x), fsdp: 4 (over y, core).
Axes of the slice: x: 2, y: 2, z: 4, core: 2. Of those that a mesh axis runs over, the one named last changes fastest.
Arguments:
- hidden_in: float32 [32, 496, 768], P(('dp', 'fsdp')), may hold values from -6 to 6
- cotangent: float32 [32, 496, 768], P(('dp', 'fsdp')), may hold values from -6 to 6
- lengths: int32 [32], P(('dp', 'fsdp')), may hold values from 397 to 496, as said below
- qkv_weight: float32 [2, 768, 2304], P(None, ('dp', 'fsdp')), may hold values from -0.21875 to 0.21875
- out_weight: float32 [2, 768, 768], P(None, ('dp', 'fsdp')), may hold values from -6 to 6
- up_weight: float32 [2, 768, 3072], P(None, ('dp', 'fsdp')), may hold values from -0.21875 to 0.21875
- down_weight: float32 [2, 3072, 768], P(None, None, ('dp', 'fsdp')), may hold values from -0.109375 to 0.109375
- norm_gains: float32 [2, 2, 768], P(None, None, ('dp', 'fsdp')), may hold values from 0.5 to 1.5
- biases: float32 [2, 6, 768], P(None, None, ('dp', 'fsdp')), may hold values from -1.2 to 1.2
- up_bias: float32 [2, 3072], P(None, ('dp', 'fsdp')), may hold values from -1.2 to 1.2
Outputs:
- output: float32 [32, 496, 768], P(('dp', 'fsdp'))
- input_grad: float32 [32, 496, 768], P(('dp', 'fsdp'))
- qkv_grad: float32 [2, 768, 2304], P(None, ('dp', 'fsdp'))
- out_grad: float32 [2, 768, 768], P(None, ('dp', 'fsdp'))
- up_grad: float32 [2, 768, 3072], P(None, ('dp', 'fsdp'))
- down_grad: float32 [2, 3072, 768], P(None, None, ('dp', 'fsdp'))
- gains_grad: float32 [2, 2, 768], P(None, None, ('dp', 'fsdp'))
- biases_grad: float32 [2, 6, 768], P(None, None, ('dp', 'fsdp'))
- up_bias_grad: float32 [2, 3072], P(None, ('dp', 'fsdp'))
Inputs may be any that keep to these rules, and one draw needn't show every extreme that they name: `lengths`: valid patches of each clip; some clip has exactly 496.
All inputs are finite; a program needn't handle non-finite values.
Results may differ from a plain program's by a relative error of at most 0.013.
Values may be sent and summed in bfloat16 or wider, within the bound.
No kernel may reach another device: no remote copies, remote signals or barrier semaphores. Data moves between devices by JAX's collectives and lax.ppermute only.
A program may use at most 320 MiB of HBM per device.

v0:
```python
import jax
import jax.numpy as jnp
from jax import lax
from jax.sharding import PartitionSpec as P

HEADS = 12
HEAD_WIDTH = 64


norm_eps = 1e-06
section_kinds = ("rows", "rows", "rows", "cols", "cols", "flat", "cols")


def layer_norm(values, gain, shift):
    center = values - jnp.mean(values, axis=-1, keepdims=True)
    spread = jnp.mean(center * center, axis=-1, keepdims=True)
    return center * lax.rsqrt(spread + norm_eps) * gain + shift


def gelu_exact(values):
    return jax.nn.gelu(values, approximate=False)


def pack_owned(pieces):
    return jnp.concatenate([piece.reshape(1, -1) for piece in pieces], axis=1)


def unpack_whole(gathered, shapes):
    count = gathered.shape[0]
    result = []
    offset = 0
    for shape, kind in zip(shapes, section_kinds):
        length = 1
        for extent in shape:
            length = length * extent
        section = gathered[:, offset : offset + length]
        offset = offset + length
        if kind == "rows":
            result.append(section.reshape((count * shape[0],) + tuple(shape[1:])))
        elif kind == "cols":
            result.append(
                section.reshape(count, shape[0], shape[1])
                .transpose(1, 0, 2)
                .reshape(shape[0], count * shape[1])
            )
        else:
            result.append(section.reshape(count * shape[0]))
    return tuple(result)


def pack_blocks(grads, count):
    pieces = []
    for grad, kind in zip(grads, section_kinds):
        if kind == "cols":
            pieces.append(
                grad.reshape(grad.shape[0], count, -1).transpose(1, 0, 2).reshape(count, -1)
            )
        else:
            pieces.append(grad.reshape(count, -1))
    return jnp.concatenate(pieces, axis=1)


def unpack_owned(owned_row, shapes):
    result = []
    offset = 0
    for shape in shapes:
        length = 1
        for extent in shape:
            length = length * extent
        result.append(owned_row[0, offset : offset + length].reshape(shape))
        offset = offset + length
    return tuple(result)


def collect(w_qkv, w_out, w_up, w_down, gains, up_shift, shifts):
    pieces = (w_qkv, w_out, w_up, w_down, gains, up_shift, shifts)
    shapes = [piece.shape for piece in pieces]
    owned_row = pack_owned(pieces)
    gathered = lax.all_gather(owned_row, ("dp", "fsdp"), axis=0, tiled=True)
    return unpack_whole(gathered, shapes)


def spread_grads(grads, shapes):
    count = lax.axis_size("dp") * lax.axis_size("fsdp")
    blocks = pack_blocks(grads, count)
    owned_row = lax.psum_scatter(blocks, ("dp", "fsdp"), scatter_dimension=0, tiled=True)
    return unpack_owned(owned_row, shapes)


def split_heads(qkv_rows, clips, slots):
    parts = qkv_rows.reshape(clips, slots, 3, HEADS, HEAD_WIDTH)
    return (parts[:, :, 0], parts[:, :, 1], parts[:, :, 2])


def masked_scores(query_matrix, key_matrix, valid):
    attention_scores = jnp.einsum(
        "clhd,cmhd->chlm", query_matrix, key_matrix, preferred_element_type=jnp.float32
    ) * HEAD_WIDTH ** (-0.5)
    return jnp.where(valid[:, None, None, :], attention_scores, -1e30)


def forward_layer(residual, matrices, valid, clips, slots):
    w_qkv, w_out, w_up, w_down, gains_low, up_low, shifts_low = matrices
    gains = gains_low.astype(jnp.float32)
    shifts = shifts_low.astype(jnp.float32)
    normed = layer_norm(residual, gains[0], shifts[4]).astype(jnp.bfloat16)
    qkv_bias = jnp.concatenate([shifts[0], jnp.zeros_like(shifts[0]), shifts[1]])
    qkv_rows = (jnp.dot(normed, w_qkv, preferred_element_type=jnp.float32) + qkv_bias).astype(
        jnp.bfloat16
    )
    query_matrix, key_matrix, value_matrix = split_heads(qkv_rows, clips, slots)
    masked = masked_scores(query_matrix, key_matrix, valid)
    peak = jnp.max(masked, axis=-1, keepdims=True)
    expo = jnp.exp(masked - peak)
    total = jnp.sum(expo, axis=-1, keepdims=True)
    attention_probabilities = (expo / total).astype(jnp.bfloat16)
    log_total = peak + jnp.log(total)
    mixed = jnp.einsum(
        "chlm,cmhd->clhd", attention_probabilities, value_matrix, preferred_element_type=jnp.float32
    )
    mixed = mixed.reshape(clips * slots, residual.shape[1]).astype(jnp.bfloat16)
    middle = residual + (jnp.dot(mixed, w_out, preferred_element_type=jnp.float32) + shifts[2])
    normed_two = layer_norm(middle, gains[1], shifts[5]).astype(jnp.bfloat16)
    hidden_pre = jnp.dot(normed_two, w_up, preferred_element_type=jnp.float32) + up_low.astype(
        jnp.float32
    )
    hidden = gelu_exact(hidden_pre).astype(jnp.bfloat16)
    result = middle + (jnp.dot(hidden, w_down, preferred_element_type=jnp.float32) + shifts[3])
    return (
        result,
        (residual, normed, qkv_rows, log_total, mixed, middle, normed_two, hidden_pre, hidden),
    )


def backward_layer(grad_result, matrices, record, valid, clips, slots):
    w_qkv, w_out, w_up, w_down, gains_low, up_low, shifts_low = matrices
    gains = gains_low.astype(jnp.float32)
    shifts = shifts_low.astype(jnp.float32)
    residual, normed, qkv_rows, log_total, mixed, middle, normed_two, hidden_pre, hidden = record
    width = residual.shape[1]
    down_low = grad_result.astype(jnp.bfloat16)
    grad_down = jnp.einsum("tf,td->fd", hidden, down_low, preferred_element_type=jnp.float32)
    grad_down_bias = jnp.sum(down_low, axis=0, dtype=jnp.float32)
    grad_hidden = jnp.einsum("td,fd->tf", down_low, w_down, preferred_element_type=jnp.float32)
    unused, gelu_pull = jax.vjp(gelu_exact, hidden_pre)
    grad_pre = gelu_pull(grad_hidden)[0].astype(jnp.bfloat16)
    grad_up = jnp.einsum("td,tf->df", normed_two, grad_pre, preferred_element_type=jnp.float32)
    grad_up_bias = jnp.sum(grad_pre, axis=0, dtype=jnp.float32)
    grad_normed_two = jnp.einsum("tf,df->td", grad_pre, w_up, preferred_element_type=jnp.float32)
    unused_two, norm_pull_two = jax.vjp(layer_norm, middle, gains[1], shifts[5])
    grad_mid_part, grad_gain_two, grad_shift_two = norm_pull_two(grad_normed_two)
    grad_middle = grad_result + grad_mid_part
    branch_low = grad_middle.astype(jnp.bfloat16)
    grad_out_weight = jnp.einsum("te,td->ed", mixed, branch_low, preferred_element_type=jnp.float32)
    grad_out_bias = jnp.sum(branch_low, axis=0, dtype=jnp.float32)
    grad_mixed = jnp.einsum(
        "td,ed->te", branch_low, w_out, preferred_element_type=jnp.float32
    ).astype(jnp.bfloat16)
    query_matrix, key_matrix, value_matrix = split_heads(qkv_rows, clips, slots)
    masked = masked_scores(query_matrix, key_matrix, valid)
    attention_probabilities = jnp.exp(masked - log_total)
    grad_heads = grad_mixed.reshape(clips, slots, HEADS, HEAD_WIDTH)
    grad_probs = jnp.einsum(
        "clhd,cmhd->chlm", grad_heads, value_matrix, preferred_element_type=jnp.float32
    )
    grad_values = jnp.einsum(
        "chlm,clhd->cmhd",
        attention_probabilities.astype(jnp.bfloat16),
        grad_heads,
        preferred_element_type=jnp.float32,
    )
    row_terms = jnp.sum(attention_probabilities * grad_probs, axis=-1, keepdims=True)
    grad_scores = (attention_probabilities * (grad_probs - row_terms)).astype(jnp.bfloat16)
    grad_queries = jnp.einsum(
        "chlm,cmhd->clhd", grad_scores, key_matrix, preferred_element_type=jnp.float32
    ) * HEAD_WIDTH ** (-0.5)
    grad_keys = jnp.einsum(
        "chlm,clhd->cmhd", grad_scores, query_matrix, preferred_element_type=jnp.float32
    ) * HEAD_WIDTH ** (-0.5)
    grad_qkv_rows = (
        jnp.stack([grad_queries, grad_keys, grad_values], axis=2)
        .reshape(clips * slots, 3 * width)
        .astype(jnp.bfloat16)
    )
    grad_qkv = jnp.einsum("td,te->de", normed, grad_qkv_rows, preferred_element_type=jnp.float32)
    grad_query_bias = jnp.sum(grad_qkv_rows[:, :width], axis=0, dtype=jnp.float32)
    grad_value_bias = jnp.sum(grad_qkv_rows[:, 2 * width :], axis=0, dtype=jnp.float32)
    grad_normed = jnp.einsum("te,de->td", grad_qkv_rows, w_qkv, preferred_element_type=jnp.float32)
    unused_one, norm_pull_one = jax.vjp(layer_norm, residual, gains[0], shifts[4])
    grad_res_part, grad_gain_one, grad_shift_one = norm_pull_one(grad_normed)
    grad_input = grad_middle + grad_res_part
    grad_gains = jnp.stack([grad_gain_one, grad_gain_two])
    grad_shifts = jnp.stack(
        [
            grad_query_bias,
            grad_value_bias,
            grad_out_bias,
            grad_down_bias,
            grad_shift_one,
            grad_shift_two,
        ]
    )
    return (
        grad_input,
        (grad_qkv, grad_out_weight, grad_up, grad_down, grad_gains, grad_up_bias, grad_shifts),
    )


def local(
    hidden_in,
    cotangent,
    lengths,
    qkv_weight,
    out_weight,
    up_weight,
    down_weight,
    norm_gains,
    biases,
    up_bias,
):
    clips, slots, width = hidden_in.shape
    layers = qkv_weight.shape[0]
    valid = lax.broadcasted_iota(jnp.int32, (clips, slots), 1) < lengths[:, None]
    owned_shapes = [
        qkv_weight.shape[1:],
        out_weight.shape[1:],
        up_weight.shape[1:],
        down_weight.shape[1:],
        norm_gains.shape[1:],
        up_bias.shape[1:],
        biases.shape[1:],
    ]

    def fetch(layer_index):
        return collect(
            qkv_weight[layer_index].astype(jnp.bfloat16),
            out_weight[layer_index].astype(jnp.bfloat16),
            up_weight[layer_index].astype(jnp.bfloat16),
            down_weight[layer_index].astype(jnp.bfloat16),
            norm_gains[layer_index].astype(jnp.bfloat16),
            up_bias[layer_index].astype(jnp.bfloat16),
            biases[layer_index].astype(jnp.bfloat16),
        )

    residual = hidden_in.reshape(clips * slots, width)
    kept_matrices = []
    records = []
    for layer_index in range(layers):
        matrices = fetch(layer_index)
        residual, record = forward_layer(residual, matrices, valid, clips, slots)
        kept_matrices.append(matrices)
        records.append(record)
    result = residual.reshape(clips, slots, width)
    grad_rows = cotangent.reshape(clips * slots, width)
    owned_grads = [None] * layers
    for layer_index in reversed(range(layers)):
        matrices = fetch(layer_index)
        grad_rows, terms = backward_layer(
            grad_rows, matrices, records[layer_index], valid, clips, slots
        )
        owned_grads[layer_index] = spread_grads(terms, owned_shapes)

    def stacked(member):
        return jnp.stack([owned_grads[layer_index][member] for layer_index in range(layers)])

    return (
        result,
        grad_rows.reshape(clips, slots, width),
        stacked(0),
        stacked(1),
        stacked(2),
        stacked(3),
        stacked(4),
        stacked(6),
        stacked(5),
    )


def solution(mesh):
    return jax.shard_map(
        local,
        mesh=mesh,
        in_specs=(
            P(("dp", "fsdp"), None, None),
            P(("dp", "fsdp"), None, None),
            P(("dp", "fsdp")),
            P(None, ("dp", "fsdp"), None),
            P(None, ("dp", "fsdp"), None),
            P(None, ("dp", "fsdp"), None),
            P(None, None, ("dp", "fsdp")),
            P(None, None, ("dp", "fsdp")),
            P(None, None, ("dp", "fsdp")),
            P(None, ("dp", "fsdp")),
        ),
        out_specs=(
            P(("dp", "fsdp"), None, None),
            P(("dp", "fsdp"), None, None),
            P(None, ("dp", "fsdp"), None),
            P(None, ("dp", "fsdp"), None),
            P(None, ("dp", "fsdp"), None),
            P(None, None, ("dp", "fsdp")),
            P(None, None, ("dp", "fsdp")),
            P(None, None, ("dp", "fsdp")),
            P(None, ("dp", "fsdp")),
        ),
        check_vma=False,
    )
```

profile of v0, /device:TPU:0, one launch (start us, length us, event | category | flops | bytes accessed | tf_op | source)
XLA Modules:
  0.0 1921.5 jit_solution(10509792829952141196)
XLA Ops:
  25.8 2.8 convert_element_type.422
  45.8 148.9 %all-gather.5.cloned.1.call-done = bf16[32,1,221472]{2,1,0:T(2,128)(2,1)} async-done(((bf16[1,1,221472]{2,1,0:T(2,128)(2,1)}), bf16[32,1,221472]{2,1,0:T(2,128)(2,1)}) %all-gather.5.cloned.1.call-update) | async-done | bytes 14174224 | tf_op jit(solution)/shard_map/all_gather | solution.py:79
  194.7 15.4 copy.165
  216.2 8.1 fusion.78
  224.2 142.1 %all-gather.7.cloned.1.call-done = bf16[32,1,221472]{2,1,0:T(2,128)(2,1)} async-done(((bf16[1,1,221472]{2,1,0:T(2,128)(2,1)}), bf16[32,1,221472]{2,1,0:T(2,128)(2,1)}) %all-gather.7.cloned.1.call-update) | async-done | bytes 14174224 | tf_op jit(solution)/shard_map/all_gather | solution.py:79
  366.3 15.0 copy.164
  387.9 8.0 fusion.77
  401.5 3.1 reshape.862
  411.3 6.0 fusion.31
  417.3 3.0 copy.100
  420.3 3.0 fusion.86
  428.6 3.1 fusion.41
  435.9 6.2 reshape.868
  446.6 55.6 %reshape.869 = bf16[32,3072,24]{2,1,0:T(8,128)(2,1)} reshape(bf16[32,73728]{1,0:T(8,128)(2,1)} %get-tuple-element.73) | data formatting | bytes 9437184 | tf_op jit(solution)/shard_map/reshape | solution.py:42
  502.1 20.0 %copy.105 = bf16[3072,32,24]{0,2,1:T(8,128)(2,1)} copy(bf16[3072,32,24]{2,0,1:T(8,128)(2,1)} %bitcast.250) | data formatting | bytes 9437184 | tf_op jit(solution)/shard_map/transpose | solution.py:43
  522.1 3.2 reshape.871
  527.8 20.6 %multiply_convert_fusion.3 = (bf16[496,3072]{1,0:T(8,128)(2,1)S(1)}, f32[496,3072]{1,0:T(8,128)}, f32[496,3072]{1,0:T(8,128)}) fusion(f32[3072]{0:T(1024)} %reshape.900, bf16[768,3072]{1,0:T(8,128)(2,1)} %reshape.868, f32[496,768]{1,0:T(8,128)} %copy-done.27, f32[768]{0:T(1024)} %add.213, f32[768]{0:T(1024)} %mul.380, f32[496]{0:T(512)} %fusion.53, ...), kind=kOutput, calls=%fused_computation.51 | convolution fusion | flops 2442891264 | bytes 21501824 | tf_op jit(solution)/shard_map/dot_general | solution.py:124
  548.4 2.7 fusion.88
  552.2 3.6 fusion.32
  555.8 3.0 copy.114
  558.8 3.0 fusion.89
  566.2 3.1 fusion.40
  572.8 6.2 reshape.877
  582.1 55.6 %reshape.878 = bf16[32,3072,24]{2,1,0:T(8,128)(2,1)} reshape(bf16[32,73728]{1,0:T(8,128)(2,1)} %get-tuple-element.71) | data formatting | bytes 9437184 | tf_op jit(solution)/shard_map/reshape | solution.py:42
  637.7 19.9 %copy.119 = bf16[3072,32,24]{0,2,1:T(8,128)(2,1)} copy(bf16[3072,32,24]{2,0,1:T(8,128)(2,1)} %bitcast.251) | data formatting | bytes 9437184 | tf_op jit(solution)/shard_map/transpose | solution.py:43
  657.5 18.4 multiply_convert_fusion.2
  676.0 5.3 convert_reduce_fusion
  681.3 6.9 multiply_reduce_fusion.2
  692.1 7.5 fusion.34
  699.5 6.3 multiply_reduce_fusion.1
  705.9 3.8 multiply_convert_fusion.1
  709.7 3.2 multiply_bitcast_fusion.2
  721.3 8.0 convert_reduce_fusion.1
  729.4 3.4 multiply_reduce_fusion.4
  736.7 7.5 fusion.37
  744.1 6.3 multiply_reduce_fusion
  750.5 3.7 multiply_convert_fusion
  754.2 3.2 multiply_bitcast_fusion
  759.6 5.3 fusion.67
  767.1 5.5 fusion.68
  775.1 4.0 multiply_reduce_fusion.5
  779.1 5.3 fusion.62
  786.7 5.9 fusion.65
  792.6 5.1 fusion.91
  798.0 6.6 reshape.893
  804.6 6.4 constant_dynamic-update-slice_fusion.27
  812.8 8.1 reshape.895
  821.0 6.9 convolution_bitcast_fusion
  827.8 25.7 %copy.136 = f32[32,3072,24]{2,1,0:T(8,128)} copy(f32[32,3072,24]{1,0,2:T(8,128)} %convolution_bitcast_fusion) | data formatting | bytes 18874368 | tf_op jit(solution)/shard_map/transpose | solution.py:56
  853.6 70.8 %reshape.896 = f32[32,73728]{1,0:T(8,128)} reshape(f32[32,3072,24]{2,1,0:T(8,128)} %copy.136) | data formatting | bytes 18874368 | tf_op jit(solution)/shard_map/reshape | solution.py:56
  925.6 6.6 reshape.885
  932.2 6.3 constant_dynamic-update-slice_fusion.17
  938.4 2.8 reshape.886
  941.3 8.1 reshape.887
  949.4 25.7 %copy.129 = f32[3072,32,24]{2,0,1:T(8,128)} copy(f32[3072,32,24]{0,2,1:T(8,128)} %bitcast.278) | data formatting | bytes 18874368 | tf_op jit(solution)/shard_map/reshape | solution.py:56
  975.1 71.1 %reshape.889 = f32[32,73728]{1,0:T(8,128)} reshape(f32[32,3072,24]{2,1,0:T(8,128)} %bitcast.249) | data formatting | bytes 18874368 | tf_op jit(solution)/shard_map/reshape | solution.py:56
  1049.0 8.5 constant_dynamic-update-slice_fusion.25
  1057.5 4.1 constant_dynamic-update-slice_fusion.24
  1067.6 8.4 constant_dynamic-update-slice_fusion.15
  1076.0 4.2 constant_dynamic-update-slice_fusion.14
  1089.7 6.2 add_bitcast_fusion.1
  1095.9 795.2 %all-reduce.5.cloned.1.call-done = (f32[32,221472]{1,0:T(8,128)}, f32[32,221472]{1,0:T(8,128)}) async-done(((f32[32,221472]{1,0:T(8,128)}, f32[32,221472]{1,0:T(8,128)}), (f32[32,221472]{1,0:T(8,128)}, f32[32,221472]{1,0:T(8,128)})) %all-reduce.5.cloned.1.call-update) | async-done | bytes 56696848
  1891.1 3.2 dynamic-slice_reduce_fusion.4
  1897.7 7.2 dynamic-slice_reduce_fusion
  (513 shorter events, 147.0 us)
Async XLA Ops:
  7.2 7.8 copy-start.111
  7.2 7.9 copy-start.112
  7.2 7.9 copy-start.95
  7.2 187.5 %all-gather.5.cloned.1.call-start = ((), (), s32[]{:S(2)}) async-start(), calls=%async_computation | async-start | bytes 29246976 | tf_op jit(solution)/shard_map/all_gather | solution.py:79
  13.9 26.1 %copy-start.22 = (f32[1,496,768]{2,1,0:T(8,128)S(1)}, f32[1,496,768]{2,1,0:T(8,128)}, u32[]{:S(2)}) copy-start(f32[1,496,768]{2,1,0:T(8,128)} %param.11) | copy-start | bytes 4571140
  21.9 344.5 %all-gather.7.cloned.1.call-start = ((), (), s32[]{:S(2)}) async-start(), calls=%async_computation.1 | async-start | bytes 29246976 | tf_op jit(solution)/shard_map/all_gather | solution.py:79
  21.9 21.4 %copy-start.15 = (f32[1,496,768]{2,1,0:T(8,128)S(1)}, f32[1,496,768]{2,1,0:T(8,128)}, u32[]{:S(2)}) copy-start(f32[1,496,768]{2,1,0:T(8,128)} %param.10) | copy-start | bytes 4571140
  39.2 1851.9 %all-reduce.5.cloned.1.call-start = ((), (), s32[]{:S(2)}) async-start(), calls=%async_computation.2 | async-start | bytes 113442816
  381.4 6.4 copy-start.3
  411.3 9.0 copy-start.108
  435.9 7.0 copy-start.62
  435.9 7.7 copy-start.16
  435.9 7.7 copy-start.44
  435.9 7.7 copy-start.47
  435.9 7.7 copy-start.105
  502.1 20.0 %copy-start.11 = (bf16[32,55296]{1,0:T(8,128)(2,1)S(1)}, bf16[32,55296]{1,0:T(8,128)(2,1)}, u32[]{:S(2)}) copy-start(bf16[32,55296]{1,0:T(8,128)(2,1)} %slice.370) | copy-start | bytes 10616836
  526.2 25.3 %copy-start.100 = (f32[768]{0:T(1024)}, f32[768]{0:T(1024)S(1)}, u32[]{:S(2)}) copy-start(f32[768]{0:T(1024)S(1)} %add.223) | copy-start | bytes 9220
  527.7 23.7 %copy-start.82 = (f32[768]{0:T(1024)}, f32[768]{0:T(1024)S(1)}, u32[]{:S(2)}) copy-start(f32[768]{0:T(1024)S(1)} %mul.389) | copy-start | bytes 9220
  527.7 20.6 %copy-start.28 = (f32[496,768]{1,0:T(8,128)S(1)}, f32[496,768]{1,0:T(8,128)}, u32[]{:S(2)}) copy-start(f32[496,768]{1,0:T(8,128)} %copy-done.27) | copy-start | bytes 4571140
  527.7 20.6 %copy-start.36 = (bf16[3072,32,24]{0,2,1:T(8,128)(2,1)S(1)}, bf16[3072,32,24]{0,2,1:T(8,128)(2,1)}, u32[]{:S(2)}) copy-start(bf16[3072,32,24]{0,2,1:T(8,128)(2,1)} %copy.105) | copy-start | bytes 14155780
  527.8 20.6 %copy-start.106 = (f32[768]{0:T(1024)S(1)}, f32[768]{0:T(1024)}, u32[]{:S(2)}) copy-start(f32[768]{0:T(1024)} %add.218) | copy-start | bytes 9220
  552.2 6.6 copy-start.109
  572.8 6.5 copy-start.32
  572.8 6.5 copy-start.107
  581.8 106.4 %copy-start.24 = (f32[496,768]{1,0:T(8,128)}, f32[496,768]{1,0:T(8,128)S(1)}, u32[]{:S(2)}) copy-start(f32[496,768]{1,0:T(8,128)S(1)} %get-tuple-element.116) | copy-start | bytes 4571140
  657.5 18.4 copy-start.23
  657.5 18.4 copy-start.35
  681.3 6.9 copy-start.115
  692.0 13.8 slice-start.3
  692.1 13.8 slice-start.4
  714.5 6.6 slice-start.12
  714.6 6.6 slice-start.16
  719.0 10.3 slice-start.14
  721.2 8.1 copy-start.51
  721.2 8.1 copy-start.29
  721.2 8.1 slice-start.15
  721.2 8.1 copy-start.67
  721.2 8.1 copy-start.80
  721.2 8.1 copy-start.92
  736.6 13.8 slice-start
  736.6 13.8 slice-start.1
  759.6 7.5 copy-start.25
  759.6 7.5 copy-start.116
  779.0 7.6 copy-start.30
  779.1 7.6 copy-start.98
  779.1 7.6 copy-start.118
  812.8 8.1 copy-start.50
  853.5 70.9 %copy-start.103 = (f32[768]{0:T(1024)S(1)}, f32[768]{0:T(1024)}, u32[]{:S(2)}) copy-start(f32[768]{0:T(1024)} %get-tuple-element.37) | copy-start | bytes 9220
  853.5 71.2 %copy-start.86 = (f32[3072]{0:T(1024)S(1)}, f32[3072]{0:T(1024)}, u32[]{:S(2)}) copy-start(f32[3072]{0:T(1024)} %get-tuple-element.126) | copy-start | bytes 36868
  853.5 71.5 %copy-start.85 = (f32[768]{0:T(1024)S(1)}, f32[768]{0:T(1024)}, u32[]{:S(2)}) copy-start(f32[768]{0:T(1024)} %get-tuple-element.57) | copy-start | bytes 9220
  853.5 71.6 %copy-start.84 = (f32[768]{0:T(1024)S(1)}, f32[768]{0:T(1024)}, u32[]{:S(2)}) copy-start(f32[768]{0:T(1024)} %get-tuple-element.75) | copy-start | bytes 9220
  853.5 71.7 %copy-start.99 = (f32[768]{0:T(1024)S(1)}, f32[768]{0:T(1024)}, u32[]{:S(2)}) copy-start(f32[768]{0:T(1024)} %get-tuple-element.45) | copy-start | bytes 9220
  975.1 71.1 %copy-start.104 = (f32[768]{0:T(1024)S(1)}, f32[768]{0:T(1024)}, u32[]{:S(2)}) copy-start(f32[768]{0:T(1024)} %get-tuple-element.33) | copy-start | bytes 9220
  975.1 71.4 %copy-start.88 = (f32[3072]{0:T(1024)S(1)}, f32[3072]{0:T(1024)}, u32[]{:S(2)}) copy-start(f32[3072]{0:T(1024)} %get-tuple-element.55) | copy-start | bytes 36868
  975.1 71.7 %copy-start.76 = (f32[768]{0:T(1024)S(1)}, f32[768]{0:T(1024)}, u32[]{:S(2)}) copy-start(f32[768]{0:T(1024)} %get-tuple-element.53) | copy-start | bytes 9220
  975.1 71.8 %copy-start.81 = (f32[768]{0:T(1024)S(1)}, f32[768]{0:T(1024)}, u32[]{:S(2)}) copy-start(f32[768]{0:T(1024)} %get-tuple-element.51) | copy-start | bytes 9220
  975.1 72.0 %copy-start.102 = (f32[768]{0:T(1024)S(1)}, f32[768]{0:T(1024)}, u32[]{:S(2)}) copy-start(f32[768]{0:T(1024)} %get-tuple-element.43) | copy-start | bytes 9220
  1047.4 10.0 slice-start.6
  1049.0 8.5 slice-start.7
  1049.0 8.5 slice-start.8
  1057.5 8.5 copy-start.19
  1066.0 10.0 slice-start.9
  1067.6 8.4 slice-start.10
  1067.6 8.4 slice-start.11
  (77 other events, 230.2 us)
Sparse Core Ops, SparseCore 0:
  22.0 172.6 all-gather.4
  198.2 168.1 all-gather.6
  1084.7 806.3 all-reduce.4
where the time goes:
time: 1930 us; the launch traced here: 1920 us
  waiting for transfers between devices  1090 us (56%)
  local copies, waits for them, and re-layouts  599 us (31%)
  matrix products  179 us (9%)
  other arithmetic  40.2 us (2%)
    unnamed x4, waiting for transfers between devices  795 us
    all_gather x2, waiting for transfers between devices, collect(): gathered = lax.all_gather(owned_row, ('dp', 'fsdp'), axis=0, tiled=True)  291 us
    reshape x7, local copies, waits for them, and re-layouts, pack_blocks(): grad.reshape(grad.shape[0], count, -1).transpose(1, 0, 2).reshape(count, -1)  168 us
    unnamed x322, local copies, waits for them, and re-layouts  114 us
    reshape x2, local copies, waits for them, and re-layouts, unpack_whole(): section.reshape(count, shape[0], shape[1]).transpose(1, 0, 2)  111 us
    transpose x2, local copies, waits for them, and re-layouts, unpack_whole(): result.append(section.reshape(count, shape[0], shape[1]).transpose(1, 0,...  39.8 us
    dot_general x2, matrix products, forward_layer(): jnp.dot(normed_two, w_up, preferred_element_type=jnp.float32)  39 us
  transfers between devices with their start and end apart: 3, of which 3 were waited for; matrix products, arithmetic and copies ran while one was open for 3% of the time, Pallas kernels for 0%

commit v1 on v0

--- a/solution.py
+++ b/solution.py
@@ -1,14 +1,183 @@
 import jax
 import jax.numpy as jnp
 from jax import lax
+from jax.experimental import pallas as pl
+from jax.experimental.pallas import tpu as pltpu
 from jax.sharding import PartitionSpec as P
 
 HEADS = 12
 HEAD_WIDTH = 64
+AXES = ("dp", "fsdp")
+LANES = 128
 
 
 norm_eps = 1e-06
-section_kinds = ("rows", "rows", "rows", "cols", "cols", "flat", "cols")
+
+
+def linear(z, x, y, c):
+    return ((z * 2 + x) * 2 + y) * 2 + c
+
+
+def pairs_of(step):
+    result = []
+    for z in range(4):
+        for x in range(2):
+            for y in range(2):
+                for c in range(2):
+                    result.append((linear(z, x, y, c), linear(*step(z, x, y, c))))
+    return result
+
+
+TO_CORE = pairs_of(lambda z, x, y, c: (z, x, y, 1 - c))
+TO_RING = pairs_of(lambda z, x, y, c: ((z + 1) % 4, x, y, c))
+TO_XY = pairs_of(lambda z, x, y, c: (z, x, 1 - y, c) if c else (z, 1 - x, y, c))
+TO_YX = pairs_of(lambda z, x, y, c: (z, 1 - x, y, c) if c else (z, x, 1 - y, c))
+
+
+def send(value, pairs):
+    return lax.ppermute(value, AXES, pairs)
+
+
+def place():
+    dp = lax.axis_index("dp")
+    fsdp = lax.axis_index("fsdp")
+    return dp // 2, dp % 2, fsdp // 2, fsdp % 2
+
+
+def blocked():
+    return lax.axis_size("dp") == 8 and lax.axis_size("fsdp") == 4
+
+
+def assemble(own, other, widths, rows):
+    z, x, y, c = place()
+    spots = jnp.stack([z, x, y, c]).astype(jnp.int32)
+    halves = [width // 2 for width in widths]
+    count = 32 * len(widths)
+
+    def body(spot, own_ref, other_ref, *rest):
+        outs, sems = rest[:-1], rest[-1]
+        z, x, y, c = spot[0], spot[1], spot[2], spot[3]
+        copies = []
+        for side, ref in enumerate((own_ref, other_ref)):
+            owner = c if side == 0 else 1 - c
+            for block in range(16):
+                bz, bx, by = block // 4, (block // 2) % 2, block % 2
+                zr = lax.rem(z - bz + 4, 4)
+                xr = lax.rem(x + bx, 2)
+                yr = lax.rem(y + by, 2)
+                first = jnp.where(owner == 0, yr, xr)
+                second = jnp.where(owner == 0, xr, yr)
+                start = pl.multiple_of(((first * 2 + second) * 4 + zr) * rows, 8)
+                column = 0
+                for half, out in zip(halves, outs):
+                    target = pl.multiple_of(owner * half, LANES)
+                    copies.append(
+                        pltpu.make_async_copy(
+                            ref.at[pl.ds(start, rows), pl.ds(column, half)],
+                            out.at[pl.ds(block * rows, rows), pl.ds(target, half)],
+                            sems.at[len(copies)],
+                        )
+                    )
+                    column = column + half
+        for copy in copies:
+            copy.start()
+        for copy in copies:
+            copy.wait()
+
+    return pl.pallas_call(
+        body,
+        out_shape=[jax.ShapeDtypeStruct((16 * rows, width), own.dtype) for width in widths],
+        in_specs=[
+            pl.BlockSpec(memory_space=pltpu.SMEM),
+            pl.BlockSpec(memory_space=pl.ANY),
+            pl.BlockSpec(memory_space=pl.ANY),
+        ],
+        out_specs=[pl.BlockSpec(memory_space=pl.ANY) for width in widths],
+        scratch_shapes=[pltpu.SemaphoreType.DMA((count,))],
+        cost_estimate=pl.CostEstimate(
+            flops=0, bytes_accessed=4 * own.size * own.dtype.itemsize, transcendentals=0
+        ),
+    )(spots, own, other)
+
+
+def gather_rows(pieces):
+    if not blocked():
+        return [lax.all_gather(piece, AXES, axis=0, tiled=True) for piece in pieces]
+    z, x, y, c = place()
+    widths = [piece.shape[1] for piece in pieces]
+    low = jnp.concatenate([piece[:, : piece.shape[1] // 2] for piece in pieces], axis=1)
+    high = jnp.concatenate([piece[:, piece.shape[1] // 2 :] for piece in pieces], axis=1)
+    mine = jnp.where(c == 0, low, high)
+    got = send(jnp.where(c == 0, high, low), TO_CORE)
+    block = jnp.where(
+        c == 0, jnp.concatenate([mine, got], axis=0), jnp.concatenate([got, mine], axis=0)
+    )
+    ring = [block]
+    for step in range(3):
+        ring.append(send(ring[-1], TO_RING))
+    stack = jnp.concatenate(ring, axis=0)
+    stack = jnp.concatenate([stack, send(stack, TO_XY)], axis=0)
+    stack = jnp.concatenate([stack, send(stack, TO_YX)], axis=0)
+    other = send(stack, TO_CORE)
+    return assemble(stack, other, widths, block.shape[0])
+
+
+def add_up(kept, got):
+    return (kept.astype(jnp.float32) + got.astype(jnp.float32)).astype(jnp.bfloat16)
+
+
+def scatter_rows(grads):
+    if not blocked():
+        return [
+            lax.psum_scatter(
+                grad.astype(jnp.bfloat16), AXES, scatter_dimension=0, tiled=True
+            ).astype(jnp.float32)
+            for grad in grads
+        ]
+    z, x, y, c = place()
+    halves = [grad.shape[1] // 2 for grad in grads]
+    low = jnp.concatenate([g[:, :half] for g, half in zip(grads, halves)], axis=1)
+    high = jnp.concatenate([g[:, half:] for g, half in zip(grads, halves)], axis=1)
+    low = low.astype(jnp.bfloat16)
+    high = high.astype(jnp.bfloat16)
+    width = low.shape[1]
+    got = send(jnp.where(c == 0, high, low), TO_CORE)
+    part = add_up(jnp.where(c == 0, low, high), got)
+    rows = part.shape[0] // 16
+    part = part.reshape(4, 2, 2, rows, width)
+
+    def pick(block_x, block_y):
+        along_y = lax.dynamic_index_in_dim(part, block_y, axis=2, keepdims=False)
+        along_x = lax.dynamic_index_in_dim(part, block_x, axis=1, keepdims=False)
+        return jnp.where(c == 0, along_y, along_x)
+
+    got = send(pick(1 - x, 1 - y), TO_YX)
+    part = add_up(pick(x, y), got)
+    spot = jnp.where(c == 0, x, y)
+    got = send(lax.dynamic_index_in_dim(part, 1 - spot, axis=1, keepdims=False), TO_XY)
+    part = add_up(lax.dynamic_index_in_dim(part, spot, axis=1, keepdims=False), got)
+
+    def block_at(step):
+        return lax.dynamic_index_in_dim(part, (z + 3 - step) % 4, axis=0, keepdims=False)
+
+    moving = block_at(0)
+    for step in range(3):
+        moving = add_up(block_at(step + 1), send(moving, TO_RING))
+    half_rows = rows // 2
+    kept = jnp.where(c == 0, moving[:half_rows], moving[half_rows:])
+    got = send(jnp.where(c == 0, moving[half_rows:], moving[:half_rows]), TO_CORE)
+    result = []
+    start = 0
+    for half in halves:
+        a = kept[:, start : start + half]
+        b = got[:, start : start + half]
+        result.append(
+            jnp.where(
+                c == 0, jnp.concatenate([a, b], axis=1), jnp.concatenate([b, a], axis=1)
+            ).astype(jnp.float32)
+        )
+        start = start + half
+    return result
 
 
 def layer_norm(values, gain, shift):
@@ -21,70 +190,16 @@
     return jax.nn.gelu(values, approximate=False)
 
 
-def pack_owned(pieces):
-    return jnp.concatenate([piece.reshape(1, -1) for piece in pieces], axis=1)
-
-
-def unpack_whole(gathered, shapes):
-    count = gathered.shape[0]
-    result = []
-    offset = 0
-    for shape, kind in zip(shapes, section_kinds):
-        length = 1
-        for extent in shape:
-            length = length * extent
-        section = gathered[:, offset : offset + length]
-        offset = offset + length
-        if kind == "rows":
-            result.append(section.reshape((count * shape[0],) + tuple(shape[1:])))
-        elif kind == "cols":
-            result.append(
-                section.reshape(count, shape[0], shape[1])
-                .transpose(1, 0, 2)
-                .reshape(shape[0], count * shape[1])
-            )
-        else:
-            result.append(section.reshape(count * shape[0]))
-    return tuple(result)
-
-
-def pack_blocks(grads, count):
-    pieces = []
-    for grad, kind in zip(grads, section_kinds):
-        if kind == "cols":
-            pieces.append(
-                grad.reshape(grad.shape[0], count, -1).transpose(1, 0, 2).reshape(count, -1)
-            )
-        else:
-            pieces.append(grad.reshape(count, -1))
-    return jnp.concatenate(pieces, axis=1)
-
-
-def unpack_owned(owned_row, shapes):
-    result = []
-    offset = 0
-    for shape in shapes:
-        length = 1
-        for extent in shape:
-            length = length * extent
-        result.append(owned_row[0, offset : offset + length].reshape(shape))
-        offset = offset + length
-    return tuple(result)
-
-
-def collect(w_qkv, w_out, w_up, w_down, gains, up_shift, shifts):
-    pieces = (w_qkv, w_out, w_up, w_down, gains, up_shift, shifts)
-    shapes = [piece.shape for piece in pieces]
-    owned_row = pack_owned(pieces)
-    gathered = lax.all_gather(owned_row, ("dp", "fsdp"), axis=0, tiled=True)
-    return unpack_whole(gathered, shapes)
-
-
-def spread_grads(grads, shapes):
-    count = lax.axis_size("dp") * lax.axis_size("fsdp")
-    blocks = pack_blocks(grads, count)
-    owned_row = lax.psum_scatter(blocks, ("dp", "fsdp"), scatter_dimension=0, tiled=True)
-    return unpack_owned(owned_row, shapes)
+def pack_small(gains, shifts, up_bias):
+    rows = gains.shape[1]
+    packed = jnp.concatenate([gains.T, shifts.T, up_bias.reshape(rows, -1)], axis=1)
+    packed = jnp.pad(packed, ((0, 0), (0, LANES - packed.shape[1])))
+    return jnp.concatenate([packed, packed], axis=1)
+
+
+def unpack_small(packed):
+    rows = packed.shape[0]
+    return packed[:, :2].T, packed[:, 2:8].T, packed[:, 8:12].reshape(4 * rows)
 
 
 def split_heads(qkv_rows, clips, slots):
@@ -100,7 +215,7 @@
 
 
 def forward_layer(residual, matrices, valid, clips, slots):
-    w_qkv, w_out, w_up, w_down, gains_low, up_low, shifts_low = matrices
+    w_qkv, w_out, w_up, w_down_t, gains_low, up_low, shifts_low = matrices
     gains = gains_low.astype(jnp.float32)
     shifts = shifts_low.astype(jnp.float32)
     normed = layer_norm(residual, gains[0], shifts[4]).astype(jnp.bfloat16)
@@ -125,7 +240,7 @@
         jnp.float32
     )
     hidden = gelu_exact(hidden_pre).astype(jnp.bfloat16)
-    result = middle + (jnp.dot(hidden, w_down, preferred_element_type=jnp.float32) + shifts[3])
+    result = middle + (jnp.einsum("tf,df->td", hidden, w_down_t, preferred_element_type=jnp.float32) + shifts[3])
     return (
         result,
         (residual, normed, qkv_rows, log_total, mixed, middle, normed_two, hidden_pre, hidden),
@@ -133,15 +248,15 @@
 
 
 def backward_layer(grad_result, matrices, record, valid, clips, slots):
-    w_qkv, w_out, w_up, w_down, gains_low, up_low, shifts_low = matrices
+    w_qkv, w_out, w_up, w_down_t, gains_low, up_low, shifts_low = matrices
     gains = gains_low.astype(jnp.float32)
     shifts = shifts_low.astype(jnp.float32)
     residual, normed, qkv_rows, log_total, mixed, middle, normed_two, hidden_pre, hidden = record
     width = residual.shape[1]
     down_low = grad_result.astype(jnp.bfloat16)
-    grad_down = jnp.einsum("tf,td->fd", hidden, down_low, preferred_element_type=jnp.float32)
+    grad_down = jnp.einsum("td,tf->df", down_low, hidden, preferred_element_type=jnp.float32)
     grad_down_bias = jnp.sum(down_low, axis=0, dtype=jnp.float32)
-    grad_hidden = jnp.einsum("td,fd->tf", down_low, w_down, preferred_element_type=jnp.float32)
+    grad_hidden = jnp.dot(down_low, w_down_t, preferred_element_type=jnp.float32)
     unused, gelu_pull = jax.vjp(gelu_exact, hidden_pre)
     grad_pre = gelu_pull(grad_hidden)[0].astype(jnp.bfloat16)
     grad_up = jnp.einsum("td,tf->df", normed_two, grad_pre, preferred_element_type=jnp.float32)
@@ -221,47 +336,41 @@
     clips, slots, width = hidden_in.shape
     layers = qkv_weight.shape[0]
     valid = lax.broadcasted_iota(jnp.int32, (clips, slots), 1) < lengths[:, None]
-    owned_shapes = [
-        qkv_weight.shape[1:],
-        out_weight.shape[1:],
-        up_weight.shape[1:],
-        down_weight.shape[1:],
-        norm_gains.shape[1:],
-        up_bias.shape[1:],
-        biases.shape[1:],
+    low = jnp.bfloat16
+    small = [
+        pack_small(norm_gains[i], biases[i], up_bias[i]).astype(low) for i in range(layers)
     ]
-
-    def fetch(layer_index):
-        return collect(
-            qkv_weight[layer_index].astype(jnp.bfloat16),
-            out_weight[layer_index].astype(jnp.bfloat16),
-            up_weight[layer_index].astype(jnp.bfloat16),
-            down_weight[layer_index].astype(jnp.bfloat16),
-            norm_gains[layer_index].astype(jnp.bfloat16),
-            up_bias[layer_index].astype(jnp.bfloat16),
-            biases[layer_index].astype(jnp.bfloat16),
-        )
+    down_t = jnp.swapaxes(down_weight, 1, 2).astype(low)
+    matrices = []
+    for i in range(layers):
+        qkv, packed = gather_rows([qkv_weight[i].astype(low), small[i]])
+        out, up = gather_rows([out_weight[i].astype(low), up_weight[i].astype(low)])
+        (down,) = gather_rows([down_t[i]])
+        gains, shifts, up_shift = unpack_small(packed)
+        matrices.append((qkv, out, up, down, gains, up_shift, shifts))
 
     residual = hidden_in.reshape(clips * slots, width)
-    kept_matrices = []
     records = []
-    for layer_index in range(layers):
-        matrices = fetch(layer_index)
-        residual, record = forward_layer(residual, matrices, valid, clips, slots)
-        kept_matrices.append(matrices)
+    for i in range(layers):
+        residual, record = forward_layer(residual, matrices[i], valid, clips, slots)
         records.append(record)
     result = residual.reshape(clips, slots, width)
     grad_rows = cotangent.reshape(clips * slots, width)
-    owned_grads = [None] * layers
-    for layer_index in reversed(range(layers)):
-        matrices = fetch(layer_index)
+    owned = [None] * layers
+    for i in reversed(range(layers)):
         grad_rows, terms = backward_layer(
-            grad_rows, matrices, records[layer_index], valid, clips, slots
+            grad_rows, matrices[i], records[i], valid, clips, slots
         )
-        owned_grads[layer_index] = spread_grads(terms, owned_shapes)
+        grad_qkv, grad_out, grad_up, grad_down, grad_gains, grad_up_bias, grad_shifts = terms
+        (own_down,) = scatter_rows([grad_down])
+        own_out, own_up = scatter_rows([grad_out, grad_up])
+        grad_small = pack_small(grad_gains, grad_shifts, grad_up_bias)
+        own_qkv, own_small = scatter_rows([grad_qkv, grad_small])
+        gains, shifts, up_shift = unpack_small(own_small)
+        owned[i] = (own_qkv, own_out, own_up, own_down.T, gains, shifts, up_shift)
 
     def stacked(member):
-        return jnp.stack([owned_grads[layer_index][member] for layer_index in range(layers)])
+        return jnp.stack([owned[i][member] for i in range(layers)])
 
     return (
         result,
@@ -271,8 +380,8 @@
         stacked(2),
         stacked(3),
         stacked(4),
+        stacked(5),
         stacked(6),
-        stacked(5),
     )
 
 

time: 1930 us -> 1540 us (0.80)
  Pallas kernels: 0 us -> 895 us
  waiting for transfers between devices: 1090 us -> 208 us
  local copies, waits for them, and re-layouts: 599 us -> 115 us
  starting transfers between devices: 0.29 us -> 58.9 us
  other arithmetic: 40.2 us -> 86.9 us
    pallas_call x0 -> x6, Pallas kernels: none -> 895 us  [assemble(): pl.pallas_call(body, out_shape=[jax.ShapeDtypeStruct((16 * rows, width),...]
    unnamed x4 -> x0, waiting for transfers between devices: 795 us -> none
    reshape x23 -> x10, local copies, waits for them, and re-layouts: 335 us -> 9.1 us  [the longest x8 5.51 us: layer_norm(): return center * lax.rsqrt(spread + norm_eps) * gain + shift]
    all_gather x2 -> x0, waiting for transfers between devices: 291 us -> none  [collect(): gathered = lax.all_gather(owned_row, ('dp', 'fsdp'), axis=0, tiled=True)]
    ppermute x0 -> x84, waiting for transfers between devices: none -> 208 us  [send(): return lax.ppermute(value, AXES, pairs)]
    unnamed x322 -> x276, local copies, waits for them, and re-layouts: 114 us -> 35.2 us
    transpose x7 -> x4, local copies, waits for them, and re-layouts: 65.9 us -> 1.46 us  [unpack_small(): packed[:, :2]]
    ppermute x0 -> x84, starting transfers between devices: none -> 58.9 us  [send(): return lax.ppermute(value, AXES, pairs)]
  transfers between devices with their start and end apart: 3 -> 84, of which waited for: 3 -> 39; matrix products, arithmetic and copies ran while one was open for 3% -> 13% of each run, Pallas kernels for 0% -> 46%
where the time goes in v1:
time: 1540 us
  Pallas kernels  895 us (58%)
  waiting for transfers between devices  208 us (14%)
  matrix products  169 us (11%)
  local copies, waits for them, and re-layouts  115 us (7%)
  other arithmetic  86.9 us (6%)
  starting transfers between devices  58.9 us (4%)
    pallas_call x6, Pallas kernels, assemble(): pl.pallas_call(body, out_shape=[jax.ShapeDtypeStruct((16 * rows, width),...  895 us
    ppermute x84, waiting for transfers between devices, send(): return lax.ppermute(value, AXES, pairs)  208 us
    ppermute x84, starting transfers between devices, send(): return lax.ppermute(value, AXES, pairs)  58.9 us
    dot_general x2, matrix products, forward_layer(): jnp.dot(normed_two, w_up, preferred_element_type=jnp.float32)  38.8 us
    unnamed x276, local copies, waits for them, and re-layouts  35.2 us
  transfers between devices with their start and end apart: 84, of which 39 were waited for; matrix products, arithmetic and copies ran while one was open for 13% of the time, Pallas kernels for 46%

profile of v1, /device:TPU:0, one launch (start us, length us, event | category | flops | bytes accessed | tf_op | source)
XLA Modules:
  0.0 1537.0 jit_solution(1266478334941600363)
XLA Ops:
  9.7 3.0 collective-permute-start.1
  32.8 2.9 collective-permute-done.29
  41.0 3.1 collective-permute-done.16
  48.1 9.7 collective-permute-done.3
  69.7 2.9 collective-permute-done.10
  80.5 15.6 %collective-permute-done.39 = bf16[192,1536]{1,0:T(8,128)(2,1)S(1)} collective-permute-done((bf16[192,1536]{1,0:T(8,128)(2,1)S(1)}, bf16[192,1536]{1,0:T(8,128)(2,1)S(1)}, u32[]{:S(2)}, u32[]{:S(2)}) %collective-permute-start.39) | collective-permute-done | bytes 589856 | tf_op jit(solution)/shard_map/ppermute | solution.py:38
  100.7 11.1 collective-permute-done.11
  116.6 11.0 collective-permute-done.32
  134.5 12.9 collective-permute-done.19
  153.2 10.0 collective-permute-done.12
  168.0 11.0 collective-permute-done.33
  183.5 121.5 %shard_map.169 = (bf16[768,2304]{1,0:T(8,128)(2,1)}, bf16[768,256]{1,0:T(8,128)(2,1)}) custom-call(s32[4]{0:T(128)} %pad_add_fusion.spot, bf16[768,1280]{1,0:T(8,128)(2,1)} %constant_dynamic-update-slice_fusion.5.own_ref, bf16[768,1280]{1,0:T(8,128)(2,1)} %collective-permute-done.6.other_ref), custom_call_target="tpu_custom_call" | custom-call | bytes 7864320 | tf_op jit(solution)/shard_map/pallas_call | solution.py:87
  308.8 121.5 %shard_map.172 = (bf16[768,2304]{1,0:T(8,128)(2,1)}, bf16[768,256]{1,0:T(8,128)(2,1)}) custom-call(s32[4]{0:T(128)} %pad_add_fusion.spot, bf16[768,1280]{1,0:T(8,128)(2,1)} %constant_dynamic-update-slice_fusion.38.own_ref, bf16[768,1280]{1,0:T(8,128)(2,1)} %collective-permute-done.27.other_ref), custom_call_target="tpu_custom_call" | custom-call | bytes 7864320 | tf_op jit(solution)/shard_map/pallas_call | solution.py:87
  438.2 5.4 fusion.32
  443.7 3.1 copy.186
  446.8 3.0 fusion.138
  456.6 145.0 %shard_map.171 = bf16[768,3072]{1,0:T(8,128)(2,1)} custom-call(s32[4]{0:T(128)} %pad_add_fusion.spot, bf16[768,1536]{1,0:T(8,128)(2,1)} %constant_dynamic-update-slice_fusion.27.own_ref, bf16[768,1536]{1,0:T(8,128)(2,1)} %collective-permute-done.20.other_ref), custom_call_target="tpu_custom_call" | custom-call | bytes 9437184 | tf_op jit(solution)/shard_map/pallas_call | solution.py:87
  601.6 145.0 %shard_map.174 = bf16[768,3072]{1,0:T(8,128)(2,1)} custom-call(s32[4]{0:T(128)} %pad_add_fusion.spot, bf16[768,1536]{1,0:T(8,128)(2,1)} %constant_dynamic-update-slice_fusion.60.own_ref, bf16[768,1536]{1,0:T(8,128)(2,1)} %collective-permute-done.41.other_ref), custom_call_target="tpu_custom_call" | custom-call | bytes 9437184 | tf_op jit(solution)/shard_map/pallas_call | solution.py:87
  746.7 181.2 %shard_map.170 = (bf16[768,768]{1,0:T(8,128)(2,1)}, bf16[768,3072]{1,0:T(8,128)(2,1)}) custom-call(s32[4]{0:T(128)} %pad_add_fusion.spot, bf16[768,1920]{1,0:T(8,128)(2,1)} %constant_dynamic-update-slice_fusion.16.own_ref, bf16[768,1920]{1,0:T(8,128)(2,1)} %collective-permute-done.13.other_ref), custom_call_target="tpu_custom_call" | custom-call | bytes 11796480 | tf_op jit(solution)/shard_map/pallas_call | solution.py:87
  930.6 19.4 %multiply_convert_fusion.3 = (bf16[496,3072]{1,0:T(8,128)(2,1)S(1)}, f32[496,3072]{1,0:T(8,128)}, f32[496,3072]{1,0:T(8,128)}) fusion(f32[3072]{0:T(1024)S(1)} %reshape.915, bf16[768,3072]{1,0:T(8,128)(2,1)} %get-tuple-element.20, f32[496,768]{1,0:T(8,128)S(1)} %get-tuple-element.247, f32[768]{0:T(1024)S(1)} %get-tuple-element.68, ...), kind=kOutput, calls=%fused_computation.49 | convolution fusion | flops 2442891264 | bytes 21501824 | tf_op jit(solution)/shard_map/dot_general | solution.py:239
  953.9 3.5 fusion.33
  957.4 3.0 copy.190
  960.4 3.0 fusion.141
  970.3 181.2 %shard_map.173 = (bf16[768,768]{1,0:T(8,128)(2,1)}, bf16[768,3072]{1,0:T(8,128)(2,1)}) custom-call(s32[4]{0:T(128)} %pad_add_fusion.spot, bf16[768,1920]{1,0:T(8,128)(2,1)} %constant_dynamic-update-slice_fusion.49.own_ref, bf16[768,1920]{1,0:T(8,128)(2,1)} %collective-permute-done.34.other_ref), custom_call_target="tpu_custom_call" | custom-call | bytes 11796480 | tf_op jit(solution)/shard_map/pallas_call | solution.py:87
  1154.1 19.4 %multiply_convert_fusion.2 = (bf16[496,3072]{1,0:T(8,128)(2,1)}, f32[496,3072]{1,0:T(8,128)S(1)}, f32[496,3072]{1,0:T(8,128)}) fusion(f32[3072]{0:T(1024)S(1)} %reshape.916, bf16[768,3072]{1,0:T(8,128)(2,1)} %get-tuple-element.24, f32[496,768]{1,0:T(8,128)S(1)} %get-tuple-element.254, f32[768]{0:T(1024)S(1)} %get-tuple-element.60, ...), kind=kOutput, calls=%fused_computation.36 | convolution fusion | flops 2442891264 | bytes 21501824 | tf_op jit(solution)/shard_map/dot_general | solution.py:239
  1173.6 7.5 convert_reduce_fusion
  1184.0 4.8 convolution_convert_fusion.2
  1193.6 7.5 fusion.48
  1201.1 6.3 multiply_reduce_fusion.1
  1207.5 3.9 multiply_convert_fusion.1
  1211.4 3.2 fusion.52
  1217.6 3.0 multiply_reduce_fusion.3
  1220.9 4.1 convolution_convert_fusion.4
  1227.4 7.6 convert_reduce_fusion.1
  1235.0 3.4 multiply_reduce_fusion.4
  1238.4 4.9 convolution_convert_fusion.3
  1248.7 4.3 convolution_convert_fusion.1
  1253.4 7.5 fusion.34
  1260.9 6.3 multiply_reduce_fusion
  1267.2 3.7 multiply_convert_fusion
  1271.0 3.2 multiply_bitcast_fusion
  1277.2 4.1 multiply_reduce_fusion.5
  1282.2 4.3 convolution_convert_fusion.5
  1294.1 4.8 fusion.31
  1325.1 3.9 broadcast_select_fusion.4
  1329.4 4.2 broadcast_select_fusion.3
  1348.9 5.6 add_bitcast_fusion.1
  1388.7 5.8 collective-permute-done.51
  1396.2 12.5 collective-permute-done.44
  1410.8 9.0 collective-permute-done.71
  1423.7 6.6 collective-permute-done.53
  1430.3 6.6 collective-permute-done.46
  1437.0 6.6 collective-permute-done.54
  1444.5 6.0 collective-permute-done.47
  1470.5 7.1 collective-permute-done.80
  1480.3 4.7 collective-permute-done.81
  1485.2 3.5 collective-permute-done.74
  1498.0 4.5 collective-permute-done.65
  1502.7 7.6 collective-permute-done.58
  1512.1 6.2 collective-permute-done.59
  1518.5 3.4 collective-permute-done.67
  1522.0 4.3 collective-permute-done.60
  1526.3 4.2 collective-permute-done.68
  1530.7 2.9 collective-permute-done.61
  (703 shorter events, 274.5 us)
Async XLA Ops:
  6.7 13.5 collective-permute-start.28
  7.2 11.4 collective-permute-start.7
  9.7 13.6 collective-permute-start.1
  12.8 12.7 collective-permute-start.22
  15.7 11.4 collective-permute-start.15
  18.7 9.4 collective-permute-start.36
  20.2 11.6 collective-permute-start.8
  23.3 12.4 collective-permute-start.29
  25.5 12.8 collective-permute-start.2
  27.1 13.9 collective-permute-start.23
  28.0 16.1 %collective-permute-start.16 = (bf16[48,1536]{1,0:T(8,128)(2,1)S(1)}, bf16[48,1536]{1,0:T(8,128)(2,1)S(1)}, u32[]{:S(2)}, u32[]{:S(2)}) collective-permute-start(bf16[48,1536]{1,0:T(8,128)(2,1)S(1)} %collective-permute-done.15), channel_id=1, source_target_pairs={{0,8},{1,9},{2,10},{3,11},{4,12},{5,13},{6,14},{7,15},{8,16},{9,17... | collective-permute-start | bytes 442376 | tf_op jit(solution)/shard_map/ppermute | solution.py:38
  31.8 15.5 %collective-permute-start.37 = (bf16[48,1536]{1,0:T(8,128)(2,1)S(1)}, bf16[48,1536]{1,0:T(8,128)(2,1)S(1)}, u32[]{:S(2)}, u32[]{:S(2)}) collective-permute-start(bf16[48,1536]{1,0:T(8,128)(2,1)S(1)} %collective-permute-done.36), channel_id=1, source_target_pairs={{0,8},{1,9},{2,10},{3,11},{4,12},{5,13},{6,14},{7,15},{8,16},{9,17... | collective-permute-start | bytes 442376 | tf_op jit(solution)/shard_map/ppermute | solution.py:38
  35.7 27.2 %collective-permute-start.9 = (bf16[48,1920]{1,0:T(8,128)(2,1)S(1)}, bf16[48,1920]{1,0:T(8,128)(2,1)S(1)}, u32[]{:S(2)}, u32[]{:S(2)}) collective-permute-start(bf16[48,1920]{1,0:T(8,128)(2,1)S(1)} %collective-permute-done.8), channel_id=1, source_target_pairs={{0,8},{1,9},{2,10},{3,11},{4,12},{5,13},{6,14},{7,15},{8,16},{9,17... | collective-permute-start | bytes 552968 | tf_op jit(solution)/shard_map/ppermute | solution.py:38
  38.4 25.6 %collective-permute-start.30 = (bf16[48,1920]{1,0:T(8,128)(2,1)S(1)}, bf16[48,1920]{1,0:T(8,128)(2,1)S(1)}, u32[]{:S(2)}, u32[]{:S(2)}) collective-permute-start(bf16[48,1920]{1,0:T(8,128)(2,1)S(1)} %collective-permute-done.29), channel_id=1, source_target_pairs={{0,8},{1,9},{2,10},{3,11},{4,12},{5,13},{6,14},{7,15},{8,16},{9,17... | collective-permute-start | bytes 552968 | tf_op jit(solution)/shard_map/ppermute | solution.py:38
  41.0 16.9 %collective-permute-start.3 = (bf16[48,1280]{1,0:T(8,128)(2,1)S(1)}, bf16[48,1280]{1,0:T(8,128)(2,1)S(1)}, u32[]{:S(2)}, u32[]{:S(2)}) collective-permute-start(bf16[48,1280]{1,0:T(8,128)(2,1)S(1)} %collective-permute-done.2), channel_id=1, source_target_pairs={{0,8},{1,9},{2,10},{3,11},{4,12},{5,13},{6,14},{7,15},{8,16},{9,17... | collective-permute-start | bytes 368648 | tf_op jit(solution)/shard_map/ppermute | solution.py:38
  44.1 16.3 %collective-permute-start.24 = (bf16[48,1280]{1,0:T(8,128)(2,1)S(1)}, bf16[48,1280]{1,0:T(8,128)(2,1)S(1)}, u32[]{:S(2)}, u32[]{:S(2)}) collective-permute-start(bf16[48,1280]{1,0:T(8,128)(2,1)S(1)} %collective-permute-done.23), channel_id=1, source_target_pairs={{0,8},{1,9},{2,10},{3,11},{4,12},{5,13},{6,14},{7,15},{8,16},{9,17... | collective-permute-start | bytes 368648 | tf_op jit(solution)/shard_map/ppermute | solution.py:38
  47.3 17.5 %collective-permute-start.17 = (bf16[48,1536]{1,0:T(8,128)(2,1)S(1)}, bf16[48,1536]{1,0:T(8,128)(2,1)S(1)}, u32[]{:S(2)}, u32[]{:S(2)}) collective-permute-start(bf16[48,1536]{1,0:T(8,128)(2,1)S(1)} %collective-permute-done.16), channel_id=1, source_target_pairs={{0,8},{1,9},{2,10},{3,11},{4,12},{5,13},{6,14},{7,15},{8,16},{9,17... | collective-permute-start | bytes 442376 | tf_op jit(solution)/shard_map/ppermute | solution.py:38
  57.8 8.8 collective-permute-start.38
  60.5 17.0 %collective-permute-start.4 = (bf16[192,1280]{1,0:T(8,128)(2,1)S(1)}, bf16[192,1280]{1,0:T(8,128)(2,1)S(1)}, u32[]{:S(2)}, u32[]{:S(2)}) collective-permute-start(bf16[192,1280]{1,0:T(8,128)(2,1)S(1)} %pad_maximum_fusion.13), channel_id=1, source_target_pairs={{0,4},{1,3},{2,6},{3,1},{4,0},{5,7},{6,2},{7,5},{8,12},{9,11},{10,... | collective-permute-start | bytes 1474568 | tf_op jit(solution)/shard_map/ppermute | solution.py:38
  62.9 16.2 %collective-permute-start.25 = (bf16[192,1280]{1,0:T(8,128)(2,1)S(1)}, bf16[192,1280]{1,0:T(8,128)(2,1)S(1)}, u32[]{:S(2)}, u32[]{:S(2)}) collective-permute-start(bf16[192,1280]{1,0:T(8,128)(2,1)S(1)} %pad_maximum_fusion.14), channel_id=1, source_target_pairs={{0,4},{1,3},{2,6},{3,1},{4,0},{5,7},{6,2},{7,5},{8,12},{9,11},{10,... | collective-permute-start | bytes 1474568 | tf_op jit(solution)/shard_map/ppermute | solution.py:38
  64.0 8.7 collective-permute-start.10
  64.8 9.9 collective-permute-start.31
  66.6 33.0 %collective-permute-start.18 = (bf16[192,1536]{1,0:T(8,128)(2,1)S(1)}, bf16[192,1536]{1,0:T(8,128)(2,1)S(1)}, u32[]{:S(2)}, u32[]{:S(2)}) collective-permute-start(bf16[192,1536]{1,0:T(8,128)(2,1)S(1)} %pad_maximum_fusion.11), channel_id=1, source_target_pairs={{0,4},{1,3},{2,6},{3,1},{4,0},{5,7},{6,2},{7,5},{8,12},{9,11},{10,... | collective-permute-start | bytes 1769480 | tf_op jit(solution)/shard_map/ppermute | solution.py:38
  72.7 23.4 %collective-permute-start.39 = (bf16[192,1536]{1,0:T(8,128)(2,1)S(1)}, bf16[192,1536]{1,0:T(8,128)(2,1)S(1)}, u32[]{:S(2)}, u32[]{:S(2)}) collective-permute-start(bf16[192,1536]{1,0:T(8,128)(2,1)S(1)} %pad_maximum_fusion.12), channel_id=1, source_target_pairs={{0,4},{1,3},{2,6},{3,1},{4,0},{5,7},{6,2},{7,5},{8,12},{9,11},{10,... | collective-permute-start | bytes 1769480 | tf_op jit(solution)/shard_map/ppermute | solution.py:38
  74.6 37.2 %collective-permute-start.11 = (bf16[192,1920]{1,0:T(8,128)(2,1)S(1)}, bf16[192,1920]{1,0:T(8,128)(2,1)S(1)}, u32[]{:S(2)}, u32[]{:S(2)}) collective-permute-start(bf16[192,1920]{1,0:T(8,128)(2,1)S(1)} %pad_maximum_fusion.9), channel_id=1, source_target_pairs={{0,4},{1,3},{2,6},{3,1},{4,0},{5,7},{6,2},{7,5},{8,12},{9,11},{10,... | collective-permute-start | bytes 2211848 | tf_op jit(solution)/shard_map/ppermute | solution.py:38
  77.5 50.2 %collective-permute-start.32 = (bf16[192,1920]{1,0:T(8,128)(2,1)S(1)}, bf16[192,1920]{1,0:T(8,128)(2,1)S(1)}, u32[]{:S(2)}, u32[]{:S(2)}) collective-permute-start(bf16[192,1920]{1,0:T(8,128)(2,1)S(1)} %pad_maximum_fusion.10), channel_id=1, source_target_pairs={{0,4},{1,3},{2,6},{3,1},{4,0},{5,7},{6,2},{7,5},{8,12},{9,11},{10,... | collective-permute-start | bytes 2211848 | tf_op jit(solution)/shard_map/ppermute | solution.py:38
  79.1 36.5 %collective-permute-start.5 = (bf16[384,1280]{1,0:T(8,128)(2,1)S(1)}, bf16[384,1280]{1,0:T(8,128)(2,1)S(1)}, u32[]{:S(2)}, u32[]{:S(2)}) collective-permute-start(bf16[384,1280]{1,0:T(8,128)(2,1)S(1)} %get-tuple-element.156), channel_id=1, source_target_pairs={{0,2},{1,5},{2,0},{3,7},{4,6},{5,1},{6,4},{7,3},{8,10},{9,13},{10,... | collective-permute-start | bytes 2949128 | tf_op jit(solution)/shard_map/ppermute | solution.py:38
  96.0 32.9 %collective-permute-start.26 = (bf16[384,1280]{1,0:T(8,128)(2,1)S(1)}, bf16[384,1280]{1,0:T(8,128)(2,1)}, u32[]{:S(2)}, u32[]{:S(2)}) collective-permute-start(bf16[384,1280]{1,0:T(8,128)(2,1)S(1)} %get-tuple-element.154), channel_id=1, source_target_pairs={{0,2},{1,5},{2,0},{3,7},{4,6},{5,1},{6,4},{7,3},{8,10},{9,13},{10,... | collective-permute-start | bytes 2949128 | tf_op jit(solution)/shard_map/ppermute | solution.py:38
  99.6 52.4 %collective-permute-start.40 = (bf16[384,1536]{1,0:T(8,128)(2,1)}, bf16[384,1536]{1,0:T(8,128)(2,1)S(1)}, u32[]{:S(2)}, u32[]{:S(2)}) collective-permute-start(bf16[384,1536]{1,0:T(8,128)(2,1)} %get-tuple-element.150), channel_id=1, source_target_pairs={{0,2},{1,5},{2,0},{3,7},{4,6},{5,1},{6,4},{7,3},{8,10},{9,13},{10,... | collective-permute-start | bytes 3538952 | tf_op jit(solution)/shard_map/ppermute | solution.py:38
  111.8 35.6 %collective-permute-start.19 = (bf16[384,1536]{1,0:T(8,128)(2,1)}, bf16[384,1536]{1,0:T(8,128)(2,1)}, u32[]{:S(2)}, u32[]{:S(2)}) collective-permute-start(bf16[384,1536]{1,0:T(8,128)(2,1)} %get-tuple-element.152), channel_id=1, source_target_pairs={{0,2},{1,5},{2,0},{3,7},{4,6},{5,1},{6,4},{7,3},{8,10},{9,13},{10,... | collective-permute-start | bytes 3538952 | tf_op jit(solution)/shard_map/ppermute | solution.py:38
  115.6 47.6 %collective-permute-start.12 = (bf16[384,1920]{1,0:T(8,128)(2,1)}, bf16[384,1920]{1,0:T(8,128)(2,1)}, u32[]{:S(2)}, u32[]{:S(2)}) collective-permute-start(bf16[384,1920]{1,0:T(8,128)(2,1)} %get-tuple-element.148), channel_id=1, source_target_pairs={{0,2},{1,5},{2,0},{3,7},{4,6},{5,1},{6,4},{7,3},{8,10},{9,13},{10,... | collective-permute-start | bytes 4423688 | tf_op jit(solution)/shard_map/ppermute | solution.py:38
  127.6 55.9 %collective-permute-start.6 = (bf16[768,1280]{1,0:T(8,128)(2,1)}, bf16[768,1280]{1,0:T(8,128)(2,1)}, u32[]{:S(2)}, u32[]{:S(2)}) collective-permute-start(bf16[768,1280]{1,0:T(8,128)(2,1)} %constant_dynamic-update-slice_fusion.5.own_ref), channel_id=1, source_target_pairs={{0,1},{1,0},{2,3},{3,2},{4,5},{5,4},{6,7},{7,6},{8,9},{9,8},{10,11... | collective-permute-start | bytes 5898248 | tf_op jit(solution)/shard_map/ppermute | solution.py:38
  128.9 50.1 %collective-permute-start.33 = (bf16[384,1920]{1,0:T(8,128)(2,1)}, bf16[384,1920]{1,0:T(8,128)(2,1)}, u32[]{:S(2)}, u32[]{:S(2)}) collective-permute-start(bf16[384,1920]{1,0:T(8,128)(2,1)} %get-tuple-element.146), channel_id=1, source_target_pairs={{0,2},{1,5},{2,0},{3,7},{4,6},{5,1},{6,4},{7,3},{8,10},{9,13},{10,... | collective-permute-start | bytes 4423688 | tf_op jit(solution)/shard_map/ppermute | solution.py:38
  147.4 161.4 %collective-permute-start.27 = (bf16[768,1280]{1,0:T(8,128)(2,1)}, bf16[768,1280]{1,0:T(8,128)(2,1)}, u32[]{:S(2)}, u32[]{:S(2)}) collective-permute-start(bf16[768,1280]{1,0:T(8,128)(2,1)} %constant_dynamic-update-slice_fusion.38.own_ref), channel_id=1, source_target_pairs={{0,1},{1,0},{2,3},{3,2},{4,5},{5,4},{6,7},{7,6},{8,9},{9,8},{10,11... | collective-permute-start | bytes 5898248 | tf_op jit(solution)/shard_map/ppermute | solution.py:38
  152.0 304.6 %collective-permute-start.20 = (bf16[768,1536]{1,0:T(8,128)(2,1)}, bf16[768,1536]{1,0:T(8,128)(2,1)}, u32[]{:S(2)}, u32[]{:S(2)}) collective-permute-start(bf16[768,1536]{1,0:T(8,128)(2,1)} %constant_dynamic-update-slice_fusion.27.own_ref), channel_id=1, source_target_pairs={{0,1},{1,0},{2,3},{3,2},{4,5},{5,4},{6,7},{7,6},{8,9},{9,8},{10,11... | collective-permute-start | bytes 7077896 | tf_op jit(solution)/shard_map/ppermute | solution.py:38
  163.2 438.4 %collective-permute-start.41 = (bf16[768,1536]{1,0:T(8,128)(2,1)}, bf16[768,1536]{1,0:T(8,128)(2,1)}, u32[]{:S(2)}, u32[]{:S(2)}) collective-permute-start(bf16[768,1536]{1,0:T(8,128)(2,1)} %constant_dynamic-update-slice_fusion.60.own_ref), channel_id=1, source_target_pairs={{0,1},{1,0},{2,3},{3,2},{4,5},{5,4},{6,7},{7,6},{8,9},{9,8},{10,11... | collective-permute-start | bytes 7077896 | tf_op jit(solution)/shard_map/ppermute | solution.py:38
  179.0 567.7 %collective-permute-start.13 = (bf16[768,1920]{1,0:T(8,128)(2,1)}, bf16[768,1920]{1,0:T(8,128)(2,1)}, u32[]{:S(2)}, u32[]{:S(2)}) collective-permute-start(bf16[768,1920]{1,0:T(8,128)(2,1)} %constant_dynamic-update-slice_fusion.16.own_ref), channel_id=1, source_target_pairs={{0,1},{1,0},{2,3},{3,2},{4,5},{5,4},{6,7},{7,6},{8,9},{9,8},{10,11... | collective-permute-start | bytes 8847368 | tf_op jit(solution)/shard_map/ppermute | solution.py:38
  183.5 786.7 %collective-permute-start.34 = (bf16[768,1920]{1,0:T(8,128)(2,1)}, bf16[768,1920]{1,0:T(8,128)(2,1)}, u32[]{:S(2)}, u32[]{:S(2)}) collective-permute-start(bf16[768,1920]{1,0:T(8,128)(2,1)} %constant_dynamic-update-slice_fusion.49.own_ref), channel_id=1, source_target_pairs={{0,1},{1,0},{2,3},{3,2},{4,5},{5,4},{6,7},{7,6},{8,9},{9,8},{10,11... | collective-permute-start | bytes 8847368 | tf_op jit(solution)/shard_map/ppermute | solution.py:38
  1302.1 60.2 %collective-permute-start.77 = (bf16[768,1536]{1,0:T(8,128)(2,1)}, bf16[768,1536]{1,0:T(8,128)(2,1)}, u32[]{:S(2)}, u32[]{:S(2)}) collective-permute-start(bf16[768,1536]{1,0:T(8,128)(2,1)} %broadcast_select_fusion.2), channel_id=1, source_target_pairs={{0,1},{1,0},{2,3},{3,2},{4,5},{5,4},{6,7},{7,6},{8,9},{9,8},{10,11... | collective-permute-start | bytes 7077896 | tf_op jit(solution)/shard_map/ppermute | solution.py:38
  1305.0 66.8 %collective-permute-start.63 = (bf16[768,1920]{1,0:T(8,128)(2,1)}, bf16[768,1920]{1,0:T(8,128)(2,1)}, u32[]{:S(2)}, u32[]{:S(2)}) collective-permute-start(bf16[768,1920]{1,0:T(8,128)(2,1)} %broadcast_select_fusion), channel_id=1, source_target_pairs={{0,1},{1,0},{2,3},{3,2},{4,5},{5,4},{6,7},{7,6},{8,9},{9,8},{10,11... | collective-permute-start | bytes 8847368 | tf_op jit(solution)/shard_map/ppermute | solution.py:38
  1329.0 26.5 %collective-permute-start.49 = (bf16[768,1280]{1,0:T(8,128)(2,1)}, bf16[768,1280]{1,0:T(8,128)(2,1)}, u32[]{:S(2)}, u32[]{:S(2)}) collective-permute-start(bf16[768,1280]{1,0:T(8,128)(2,1)} %broadcast_select_fusion.4), channel_id=1, source_target_pairs={{0,1},{1,0},{2,3},{3,2},{4,5},{5,4},{6,7},{7,6},{8,9},{9,8},{10,11... | collective-permute-start | bytes 5898248 | tf_op jit(solution)/shard_map/ppermute | solution.py:38
  1333.6 33.2 %collective-permute-start.70 = (bf16[768,1536]{1,0:T(8,128)(2,1)}, bf16[768,1536]{1,0:T(8,128)(2,1)}, u32[]{:S(2)}, u32[]{:S(2)}) collective-permute-start(bf16[768,1536]{1,0:T(8,128)(2,1)} %broadcast_select_fusion.3), channel_id=1, source_target_pairs={{0,1},{1,0},{2,3},{3,2},{4,5},{5,4},{6,7},{7,6},{8,9},{9,8},{10,11... | collective-permute-start | bytes 7077896 | tf_op jit(solution)/shard_map/ppermute | solution.py:38
  1346.6 12.7 collective-permute-start.42
  1355.5 24.8 %collective-permute-start.56 = (bf16[768,1920]{1,0:T(8,128)(2,1)S(1)}, bf16[768,1920]{1,0:T(8,128)(2,1)S(1)}, u32[]{:S(2)}, u32[]{:S(2)}) collective-permute-start(bf16[768,1920]{1,0:T(8,128)(2,1)S(1)} %broadcast_select_fusion.1), channel_id=1, source_target_pairs={{0,1},{1,0},{2,3},{3,2},{4,5},{5,4},{6,7},{7,6},{8,9},{9,8},{10,11... | collective-permute-start | bytes 8847368 | tf_op jit(solution)/shard_map/ppermute | solution.py:38
  1359.3 18.6 %collective-permute-start.50 = (bf16[4,2,48,1280]{3,2,0,1:T(8,128)(2,1)S(1)}, bf16[4,2,48,1280]{3,2,0,1:T(8,128)(2,1)}, u32[]{:S(2)}, u32[]{:S(2)}) collective-permute-start(bf16[4,2,48,1280]{3,2,0,1:T(8,128)(2,1)S(1)} %fusion.59), channel_id=1, source_target_pairs={{0,2},{1,5},{2,0},{3,7},{4,6},{5,1},{6,4},{7,3},{8,10},{9,13},{10,... | collective-permute-start | bytes 2949128 | tf_op jit(solution)/shard_map/ppermute | solution.py:38
  1362.3 24.8 %collective-permute-start.43 = (bf16[4,2,48,1280]{3,2,0,1:T(8,128)(2,1)S(1)}, bf16[4,2,48,1280]{3,2,0,1:T(8,128)(2,1)S(1)}, u32[]{:S(2)}, u32[]{:S(2)}) collective-permute-start(bf16[4,2,48,1280]{3,2,0,1:T(8,128)(2,1)S(1)} %fusion.61), channel_id=1, source_target_pairs={{0,2},{1,5},{2,0},{3,7},{4,6},{5,1},{6,4},{7,3},{8,10},{9,13},{10,... | collective-permute-start | bytes 2949128 | tf_op jit(solution)/shard_map/ppermute | solution.py:38
  1366.8 42.1 %collective-permute-start.78 = (bf16[4,2,48,1536]{3,2,0,1:T(8,128)(2,1)S(1)}, bf16[4,2,48,1536]{3,2,0,1:T(8,128)(2,1)S(1)}, u32[]{:S(2)}, u32[]{:S(2)}) collective-permute-start(bf16[4,2,48,1536]{3,2,0,1:T(8,128)(2,1)S(1)} %fusion.53), channel_id=1, source_target_pairs={{0,2},{1,5},{2,0},{3,7},{4,6},{5,1},{6,4},{7,3},{8,10},{9,13},{10,... | collective-permute-start | bytes 3538952 | tf_op jit(solution)/shard_map/ppermute | solution.py:38
  1371.7 48.1 %collective-permute-start.71 = (bf16[4,2,48,1536]{3,2,0,1:T(8,128)(2,1)S(1)}, bf16[4,2,48,1536]{3,2,0,1:T(8,128)(2,1)S(1)}, u32[]{:S(2)}, u32[]{:S(2)}) collective-permute-start(bf16[4,2,48,1536]{3,2,0,1:T(8,128)(2,1)S(1)} %fusion.55), channel_id=1, source_target_pairs={{0,2},{1,5},{2,0},{3,7},{4,6},{5,1},{6,4},{7,3},{8,10},{9,13},{10,... | collective-permute-start | bytes 3538952 | tf_op jit(solution)/shard_map/ppermute | solution.py:38
  1377.9 110.9 %collective-permute-start.64 = (bf16[4,2,48,1920]{3,2,0,1:T(8,128)(2,1)}, bf16[4,2,48,1920]{3,2,0,1:T(8,128)(2,1)}, u32[]{:S(2)}, u32[]{:S(2)}) collective-permute-start(bf16[4,2,48,1920]{3,2,0,1:T(8,128)(2,1)} %fusion.37), channel_id=1, source_target_pairs={{0,2},{1,5},{2,0},{3,7},{4,6},{5,1},{6,4},{7,3},{8,10},{9,13},{10,... | collective-permute-start | bytes 4423688 | tf_op jit(solution)/shard_map/ppermute | solution.py:38
  1380.3 14.2 collective-permute-start.51
  1387.1 105.6 %collective-permute-start.57 = (bf16[4,2,48,1920]{3,2,0,1:T(8,128)(2,1)}, bf16[4,2,48,1920]{3,2,0,1:T(8,128)(2,1)}, u32[]{:S(2)}, u32[]{:S(2)}) collective-permute-start(bf16[4,2,48,1920]{3,2,0,1:T(8,128)(2,1)} %fusion.39), channel_id=1, source_target_pairs={{0,2},{1,5},{2,0},{3,7},{4,6},{5,1},{6,4},{7,3},{8,10},{9,13},{10,... | collective-permute-start | bytes 4423688 | tf_op jit(solution)/shard_map/ppermute | solution.py:38
  1394.5 14.2 collective-permute-start.44
  1408.7 14.5 collective-permute-start.52
  1408.9 14.7 collective-permute-start.45
  1419.8 47.9 %collective-permute-start.79 = (bf16[4,48,1536]{2,1,0:T(8,128)(2,1)S(1)}, bf16[4,48,1536]{2,1,0:T(8,128)(2,1)}, u32[]{:S(2)}, u32[]{:S(2)}) collective-permute-start(bf16[4,48,1536]{2,1,0:T(8,128)(2,1)S(1)} %dynamic-slice_bitcast_fusion.2), channel_id=1, source_target_pairs={{0,4},{1,3},{2,6},{3,1},{4,0},{5,7},{6,2},{7,5},{8,12},{9,11},{10,... | collective-permute-start | bytes 1769480 | tf_op jit(solution)/shard_map/ppermute | solution.py:38
  1423.2 46.0 %collective-permute-start.72 = (bf16[4,48,1536]{2,1,0:T(8,128)(2,1)}, bf16[4,48,1536]{2,1,0:T(8,128)(2,1)}, u32[]{:S(2)}, u32[]{:S(2)}) collective-permute-start(bf16[4,48,1536]{2,1,0:T(8,128)(2,1)} %dynamic-slice_bitcast_fusion.3), channel_id=1, source_target_pairs={{0,4},{1,3},{2,6},{3,1},{4,0},{5,7},{6,2},{7,5},{8,12},{9,11},{10,... | collective-permute-start | bytes 1769480 | tf_op jit(solution)/shard_map/ppermute | solution.py:38
  1469.1 8.5 collective-permute-start.80
  1470.4 9.8 collective-permute-start.73
  1480.3 8.3 collective-permute-start.74
  1485.1 10.0 collective-permute-start.82
  1490.9 11.5 collective-permute-start.65
  1494.8 15.6 %collective-permute-start.58 = (bf16[4,48,1920]{2,1,0:T(8,128)(2,1)S(1)}, bf16[4,48,1920]{2,1,0:T(8,128)(2,1)S(1)}, u32[]{:S(2)}, u32[]{:S(2)}) collective-permute-start(bf16[4,48,1920]{2,1,0:T(8,128)(2,1)S(1)} %dynamic-slice_bitcast_fusion.1), channel_id=1, source_target_pairs={{0,4},{1,3},{2,6},{3,1},{4,0},{5,7},{6,2},{7,5},{8,12},{9,11},{10,... | collective-permute-start | bytes 2211848 | tf_op jit(solution)/shard_map/ppermute | solution.py:38
  1510.7 11.2 collective-permute-start.67
  1521.9 8.6 collective-permute-start.68
  (145 other events, 3449.1 us)

commit v2 on v1

v2 whole, which is shorter than its diff:
```python
import jax
import jax.numpy as jnp
from jax import lax
from jax.experimental import pallas as pl
from jax.experimental.pallas import tpu as pltpu
from jax.sharding import PartitionSpec as P

HEADS = 12
HEAD_WIDTH = 64
LANES = 128
PAIRS = HEADS * HEAD_WIDTH // LANES
LOW = jnp.bfloat16
WIDE = jnp.float32
norm_eps = 1e-06
AXES = ("dp", "fsdp")
VMEM_LIMIT = 60 * 1024 * 1024


def cost(flops, moved, hard=0):
    return pl.CostEstimate(flops=int(flops), bytes_accessed=int(moved), transcendentals=int(hard))


def params():
    return pltpu.CompilerParams(vmem_limit_bytes=VMEM_LIMIT)


def vmem_specs(count):
    return [pl.BlockSpec(memory_space=pltpu.VMEM)] * count


def any_specs(count):
    return [pl.BlockSpec(memory_space=pl.ANY)] * count


def dot(a, b):
    return jnp.dot(a, b, preferred_element_type=WIDE)


def dot_nt(a, b):
    return lax.dot_general(a, b, (((1,), (1,)), ((), ())), preferred_element_type=WIDE)


def dot_tn(a, b):
    return lax.dot_general(a, b, (((0,), (0,)), ((), ())), preferred_element_type=WIDE)


def piece_copies(spot, own_ref, other_ref, target, sems, column, half):
    z, x, y, c = spot[0], spot[1], spot[2], spot[3]
    rows = own_ref.shape[0] // 16
    copies = []
    for side, ref in enumerate((own_ref, other_ref)):
        owner = c if side == 0 else 1 - c
        to = pl.multiple_of(owner * half, LANES)
        for block in range(16):
            bz, bx, by = block // 4, (block // 2) % 2, block % 2
            zr = lax.rem(z - bz + 4, 4)
            xr = lax.rem(x + bx, 2)
            yr = lax.rem(y + by, 2)
            first = jnp.where(owner == 0, yr, xr)
            second = jnp.where(owner == 0, xr, yr)
            start = pl.multiple_of(((first * 2 + second) * 4 + zr) * rows, 8)
            copies.append(
                pltpu.make_async_copy(
                    ref.at[pl.ds(start, rows), pl.ds(column, half)],
                    target.at[pl.ds(block * rows, rows), pl.ds(to, half)],
                    sems.at[len(copies)],
                )
            )
    return copies


def norm_rows(v):
    center = v - jnp.mean(v, axis=-1, keepdims=True)
    r = lax.rsqrt(jnp.mean(center * center, axis=-1, keepdims=True) + norm_eps)
    return center * r, r


def norm_back(v, gain, d):
    xh, r = norm_rows(v)
    dg = d * gain
    m1 = jnp.mean(dg, axis=-1, keepdims=True)
    m2 = jnp.mean(dg * xh, axis=-1, keepdims=True)
    return (
        r * (dg - m1 - xh * m2),
        jnp.sum(d * xh, axis=0, keepdims=True),
        jnp.sum(d, axis=0, keepdims=True),
    )


GAIN1, GAIN2, BQ, BV, BO, BD, SH1, SH2 = range(8)


def qkv_forward(spot, own, other, column, h, table):
    rows, width = h.shape
    wide = 3 * width
    tile = 256

    def body(spot_ref, own_ref, other_ref, h_ref, t_ref, qkv_ref, a_ref, w_ref, sems):
        copies = piece_copies(spot_ref, own_ref, other_ref, w_ref, sems, column, wide // 2)
        for copy in copies:
            copy.start()
        xh, r = norm_rows(h_ref[...])
        a_ref[...] = (xh * t_ref[GAIN1 : GAIN1 + 1, :] + t_ref[SH1 : SH1 + 1, :]).astype(LOW)
        for copy in copies:
            copy.wait()
        a = a_ref[...]
        for n in range(wide // tile):
            s = n * tile
            out = dot(a, w_ref[:, s : s + tile])
            if s < width:
                out = out + t_ref[BQ : BQ + 1, s : s + tile]
            elif s >= 2 * width:
                out = out + t_ref[BV : BV + 1, s - 2 * width : s - 2 * width + tile]
            qkv_ref[:, s : s + tile] = out.astype(LOW)

    return pl.pallas_call(
        body,
        out_shape=[
            jax.ShapeDtypeStruct((rows, wide), LOW),
            jax.ShapeDtypeStruct((rows, width), LOW),
        ],
        in_specs=[pl.BlockSpec(memory_space=pltpu.SMEM)] + any_specs(2) + vmem_specs(2),
        out_specs=vmem_specs(2),
        scratch_shapes=[pltpu.VMEM((width, wide), LOW), pltpu.SemaphoreType.DMA((32,))],
        compiler_params=params(),
        cost_estimate=cost(2 * rows * width * wide, 2 * width * wide + 9 * rows * width),
        name="qkv_forward",
    )(spot, own, other, h, table)


def attention_forward(lengths, qkv):
    rows, wide = qkv.shape
    width = wide // 3

    def body(len_ref, q_ref, k_ref, v_ref, o_ref, lse_ref):
        pair = pl.program_id(0)
        lane = lax.broadcasted_iota(jnp.int32, (1, LANES), 1)
        key = lax.broadcasted_iota(jnp.int32, (1, rows), 1)
        shut = jnp.where(key < len_ref[0], 0.0, -1e30)
        q = q_ref[...] * jnp.asarray(HEAD_WIDTH**-0.5, LOW)
        k = k_ref[...]
        v = v_ref[...]
        outs = []
        stats = jnp.where(pair == 0, jnp.zeros((rows, LANES), WIDE), lse_ref[...])
        for side in range(2):
            inside = (lane >= HEAD_WIDTH) == (side == 1)
            qs = jnp.where(inside, q, jnp.zeros_like(q))
            s = dot_nt(qs, k) + shut
            peak = jnp.max(s, axis=1, keepdims=True)
            e = jnp.exp(s - peak)
            total = jnp.sum(e, axis=1, keepdims=True)
            p = (e * (1.0 / total)).astype(LOW)
            outs.append(dot(p, v))
            stats = jnp.where(lane == pair * 2 + side, peak + jnp.log(total), stats)
        lse_ref[...] = stats
        o_ref[...] = jnp.where(lane < HEAD_WIDTH, outs[0], outs[1]).astype(LOW)

    return pl.pallas_call(
        body,
        out_shape=[
            jax.ShapeDtypeStruct((rows, width), LOW),
            jax.ShapeDtypeStruct((rows, LANES), WIDE),
        ],
        grid_spec=pltpu.PrefetchScalarGridSpec(
            num_scalar_prefetch=1,
            grid=(PAIRS,),
            in_specs=[
                pl.BlockSpec((rows, LANES), lambda p, n: (0, p)),
                pl.BlockSpec((rows, LANES), lambda p, n: (0, p + PAIRS)),
                pl.BlockSpec((rows, LANES), lambda p, n: (0, p + 2 * PAIRS)),
            ],
            out_specs=[
                pl.BlockSpec((rows, LANES), lambda p, n: (0, p)),
                pl.BlockSpec((rows, LANES), lambda p, n: (0, 0)),
            ],
        ),
        compiler_params=params(),
        cost_estimate=cost(16 * rows * rows * width, 8 * rows * width, HEADS * rows * rows),
        name="attention_forward",
    )(lengths, qkv, qkv, qkv)


def out_forward(spot, own, other, column, h, mixed, table):
    rows, width = h.shape

    def body(spot_ref, own_ref, other_ref, h_ref, m_ref, t_ref, h2_ref, a_ref, w_ref, sems):
        copies = piece_copies(spot_ref, own_ref, other_ref, w_ref, sems, column, width // 2)
        for copy in copies:
            copy.start()
        for copy in copies:
            copy.wait()
        h2 = h_ref[...] + (dot(m_ref[...], w_ref[...]) + t_ref[BO : BO + 1, :])
        h2_ref[...] = h2
        xh, r = norm_rows(h2)
        a_ref[...] = (xh * t_ref[GAIN2 : GAIN2 + 1, :] + t_ref[SH2 : SH2 + 1, :]).astype(LOW)

    return pl.pallas_call(
        body,
        out_shape=[
            jax.ShapeDtypeStruct((rows, width), WIDE),
            jax.ShapeDtypeStruct((rows, width), LOW),
        ],
        in_specs=[pl.BlockSpec(memory_space=pltpu.SMEM)] + any_specs(2) + vmem_specs(3),
        out_specs=vmem_specs(2),
        scratch_shapes=[pltpu.VMEM((width, width), LOW), pltpu.SemaphoreType.DMA((32,))],
        compiler_params=params(),
        cost_estimate=cost(2 * rows * width * width, 2 * width * width + 12 * rows * width),
        name="out_forward",
    )(spot, own, other, h, mixed, table)


def gelu_parts(u):
    cdf = 0.5 * (1.0 + lax.erf(u * (0.5**0.5)))
    pdf = jnp.exp(-0.5 * u * u) * (0.3989422804014327)
    return cdf, pdf


def mlp_forward(spot, up, down, h2, a2, up_bias, table):
    rows, width = h2.shape
    hidden = up_bias.shape[1]
    tile = 512
    (up_own, up_other, up_col), (down_own, down_other, down_col) = up, down

    def body(
        spot_ref, uo_ref, up_ref, do_ref, dp_ref, h_ref, a_ref, b_ref, t_ref,
        z_ref, g_ref, o_ref, wu_ref, wd_ref, sems_u, sems_d,
    ):
        ups = piece_copies(spot_ref, uo_ref, up_ref, wu_ref, sems_u, up_col, hidden // 2)
        downs = piece_copies(spot_ref, do_ref, dp_ref, wd_ref, sems_d, down_col, hidden // 2)
        for copy in ups + downs:
            copy.start()
        o_ref[...] = h_ref[...] + t_ref[BD : BD + 1, :]
        for copy in ups + downs:
            copy.wait()

        def step(n, carry):
            at = pl.ds(pl.multiple_of(n * tile, tile), tile)
            u = dot(a_ref[...], wu_ref[:, at]) + b_ref[:, at]
            cdf, pdf = gelu_parts(u)
            z = (u * cdf).astype(LOW)
            z_ref[:, at] = z
            g_ref[:, at] = (cdf + u * pdf).astype(LOW)
            o_ref[...] += dot_nt(z, wd_ref[:, at])
            return carry

        lax.fori_loop(0, hidden // tile, step, 0)

    return pl.pallas_call(
        body,
        out_shape=[
            jax.ShapeDtypeStruct((rows, hidden), LOW),
            jax.ShapeDtypeStruct((rows, hidden), LOW),
            jax.ShapeDtypeStruct((rows, width), WIDE),
        ],
        in_specs=[pl.BlockSpec(memory_space=pltpu.SMEM)] + any_specs(4) + vmem_specs(4),
        out_specs=vmem_specs(3),
        scratch_shapes=[
            pltpu.VMEM((width, hidden), LOW),
            pltpu.VMEM((width, hidden), LOW),
            pltpu.SemaphoreType.DMA((32,)),
            pltpu.SemaphoreType.DMA((32,)),
        ],
        compiler_params=params(),
        cost_estimate=cost(
            4 * rows * width * hidden, 4 * width * hidden + 4 * rows * hidden, 2 * rows * hidden
        ),
        name="mlp_forward",
    )(spot, up_own, up_other, down_own, down_other, h2, a2, up_bias, table)


def block_starts(spot, owner, rows):
    z, x, y = spot[0], spot[1], spot[2]
    result = []
    for block in range(16):
        bz, bx, by = block // 4, (block // 2) % 2, block % 2
        zr = lax.rem(z - bz + 4, 4)
        xr = lax.rem(x + bx, 2)
        yr = lax.rem(y + by, 2)
        first = jnp.where(owner == 0, yr, xr)
        second = jnp.where(owner == 0, xr, yr)
        result.append(pl.multiple_of(((first * 2 + second) * 4 + zr) * rows, 16))
    return result


def put_blocks(value, out_ref, starts, column, width):
    rows = value.shape[0] // 16
    low = value.astype(LOW)
    for block, start in enumerate(starts):
        out_ref[pl.ds(start, rows), pl.ds(column, width)] = low[block * rows : (block + 1) * rows]


def column_sum(value):
    return jnp.sum(value.astype(WIDE), axis=0, keepdims=True)


def down_backward(spot, down, e, z, slope):
    rows, width = e.shape
    hidden = z.shape[1]
    half = hidden // 2
    tile = 512
    own, other, column = down

    def body(
        spot_ref, own_ref, other_ref, e_ref, z_ref, s_ref,
        du_ref, mine_ref, rest_ref, bd_ref, bu_ref, w_ref, em_ref, emt_ref, sems,
    ):
        copies = piece_copies(spot_ref, own_ref, other_ref, w_ref, sems, column, half)
        for copy in copies:
            copy.start()
        em = e_ref[...].astype(LOW)
        em_ref[...] = em
        bd_ref[...] = column_sum(em)
        emt_ref[...] = em.T
        for copy in copies:
            copy.wait()
        c = spot_ref[3]
        for owner, out_ref in ((c, mine_ref), (1 - c, rest_ref)):
            starts = block_starts(spot_ref, owner, width // 16)

            def step(n, carry):
                at = pl.ds(pl.multiple_of(owner * half + n * tile, LANES), tile)
                dz = dot(em_ref[...], w_ref[:, at])
                du = (dz * s_ref[:, at].astype(WIDE)).astype(LOW)
                du_ref[:, at] = du
                bu_ref[:, at] = column_sum(du)
                grad = dot(emt_ref[...], z_ref[:, at])
                put_blocks(grad, out_ref, starts, pl.multiple_of(n * tile, LANES), tile)
                return carry

            lax.fori_loop(0, half // tile, step, 0)

    return pl.pallas_call(
        body,
        out_shape=[
            jax.ShapeDtypeStruct((rows, hidden), LOW),
            jax.ShapeDtypeStruct((width, half), LOW),
            jax.ShapeDtypeStruct((width, half), LOW),
            jax.ShapeDtypeStruct((1, width), WIDE),
            jax.ShapeDtypeStruct((1, hidden), WIDE),
        ],
        in_specs=[pl.BlockSpec(memory_space=pltpu.SMEM)] + any_specs(2) + vmem_specs(3),
        out_specs=vmem_specs(5),
        scratch_shapes=[
            pltpu.VMEM((width, hidden), LOW),
            pltpu.VMEM((rows, width), LOW),
            pltpu.VMEM((width, rows), LOW),
            pltpu.SemaphoreType.DMA((32,)),
        ],
        compiler_params=params(),
        cost_estimate=cost(4 * rows * width * hidden, 4 * width * hidden + 6 * rows * hidden),
        name="down_backward",
    )(spot, own, other, e, z, slope)


def up_backward(spot, up, out, e, h2, a2, mixed, du, table):
    rows, width = e.shape
    hidden = du.shape[1]
    half = hidden // 2
    tile = 512
    (up_own, up_other, up_col), (out_own, out_other, out_col) = up, out

    def body(
        spot_ref, uo_ref, up_ref, oo_ref, op_ref, e_ref, h_ref, a_ref, m_ref, du_ref, t_ref,
        e2_ref, da_ref, mine_ref, rest_ref, omine_ref, orest_ref, sums_ref,
        wu_ref, wo_ref, at_ref, mt_ref, ey_ref, acc_ref, sems_u, sems_o,
    ):
        ups = piece_copies(spot_ref, uo_ref, up_ref, wu_ref, sems_u, up_col, half)
        outs = piece_copies(spot_ref, oo_ref, op_ref, wo_ref, sems_o, out_col, width // 2)
        for copy in ups + outs:
            copy.start()
        at_ref[...] = a_ref[...].T
        mt_ref[...] = m_ref[...].T
        acc_ref[...] = jnp.zeros_like(acc_ref)
        for copy in ups:
            copy.wait()
        c = spot_ref[3]
        for owner, out_ref in ((c, mine_ref), (1 - c, rest_ref)):
            starts = block_starts(spot_ref, owner, width // 16)

            def step(n, carry):
                at = pl.ds(pl.multiple_of(owner * half + n * tile, LANES), tile)
                d = du_ref[:, at]
                put_blocks(
                    dot(at_ref[...], d), out_ref, starts, pl.multiple_of(n * tile, LANES), tile
                )
                acc_ref[...] += dot_nt(d, wu_ref[:, at])
                return carry

            lax.fori_loop(0, half // tile, step, 0)
        dv, gain, shift = norm_back(h_ref[...], t_ref[GAIN2 : GAIN2 + 1, :], acc_ref[...])
        e2 = e_ref[...] + dv
        e2_ref[...] = e2
        ey = e2.astype(LOW)
        ey_ref[...] = ey
        sums_ref[0:1, :] = gain
        sums_ref[1:2, :] = shift
        sums_ref[2:3, :] = column_sum(ey)
        for copy in outs:
            copy.wait()
        da_ref[...] = dot_nt(ey, wo_ref[...]).astype(LOW)
        for owner, out_ref in ((c, omine_ref), (1 - c, orest_ref)):
            starts = block_starts(spot_ref, owner, width // 16)
            at = pl.ds(pl.multiple_of(owner * (width // 2), LANES), width // 2)
            put_blocks(dot(mt_ref[...], ey_ref[:, at]), out_ref, starts, 0, width // 2)

    return pl.pallas_call(
        body,
        out_shape=[
            jax.ShapeDtypeStruct((rows, width), WIDE),
            jax.ShapeDtypeStruct((rows, width), LOW),
            jax.ShapeDtypeStruct((width, half), LOW),
            jax.ShapeDtypeStruct((width, half), LOW),
            jax.ShapeDtypeStruct((width, width // 2), LOW),
            jax.ShapeDtypeStruct((width, width // 2), LOW),
            jax.ShapeDtypeStruct((8, width), WIDE),
        ],
        in_specs=[pl.BlockSpec(memory_space=pltpu.SMEM)] + any_specs(4) + vmem_specs(6),
        out_specs=vmem_specs(7),
        scratch_shapes=[
            pltpu.VMEM((width, hidden), LOW),
            pltpu.VMEM((width, width), LOW),
            pltpu.VMEM((width, rows), LOW),
            pltpu.VMEM((width, rows), LOW),
            pltpu.VMEM((rows, width), LOW),
            pltpu.VMEM((rows, width), WIDE),
            pltpu.SemaphoreType.DMA((32,)),
            pltpu.SemaphoreType.DMA((32,)),
        ],
        compiler_params=params(),
        cost_estimate=cost(
            4 * rows * width * (hidden + width), 4 * width * (hidden + width) + 2 * rows * hidden
        ),
        name="up_backward",
    )(spot, up_own, up_other, out_own, out_other, e, h2, a2, mixed, du, table)


def attention_backward(lengths, qkv, da, mixed, lse):
    rows, wide = qkv.shape
    width = wide // 3

    def body(len_ref, q_ref, k_ref, v_ref, d_ref, m_ref, lse_ref, out_ref, row_ref):
        pair = pl.program_id(0)

        @pl.when(pair == 0)
        def start():
            row_ref[...] = lse_ref[...].T

        lane = lax.broadcasted_iota(jnp.int32, (1, LANES), 1)
        sub = lax.broadcasted_iota(jnp.int32, (LANES, 1), 0)
        key = lax.broadcasted_iota(jnp.int32, (rows, 1), 0)
        shut = jnp.where(key < len_ref[0], 0.0, -1e30)
        scale = jnp.asarray(HEAD_WIDTH**-0.5, LOW)
        q = q_ref[...] * scale
        k = k_ref[...]
        v = v_ref[...]
        d = d_ref[...]
        kt = k.T * scale
        prod = (d.astype(WIDE) * m_ref[...].astype(WIDE)).T
        dks, dvs = [], []
        dqt = jnp.zeros((LANES, rows), WIDE)
        for side in range(2):
            inside = (lane >= HEAD_WIDTH) == (side == 1)
            down = (sub >= HEAD_WIDTH) == (side == 1)
            ks = jnp.where(inside, k, jnp.zeros_like(k))
            vs = jnp.where(inside, v, jnp.zeros_like(v))
            kts = jnp.where(down, kt, jnp.zeros_like(kt))
            first = side * HEAD_WIDTH
            delta = jnp.sum(prod[first : first + HEAD_WIDTH], axis=0, keepdims=True)
            log_total = row_ref[pl.ds(pair * 2 + side, 1), :]
            p = jnp.exp((dot_nt(ks, q) + shut) - log_total)
            dp = dot_nt(vs, d)
            dvs.append(dot(p.astype(LOW), d))
            ds = (p * (dp - delta)).astype(LOW)
            dks.append(dot(ds, q))
            dqt = dqt + dot(kts, ds)
        dq = dqt.T
        dk = jnp.where(lane < HEAD_WIDTH, dks[0], dks[1])
        dv = jnp.where(lane < HEAD_WIDTH, dvs[0], dvs[1])
        for n, value in enumerate((dq, dk, dv)):
            at = pl.ds(pl.multiple_of(n * width + pair * LANES, LANES), LANES)
            out_ref[:, at] = value.astype(LOW)

    return pl.pallas_call(
        body,
        out_shape=jax.ShapeDtypeStruct((rows, wide), LOW),
        grid_spec=pltpu.PrefetchScalarGridSpec(
            num_scalar_prefetch=1,
            grid=(PAIRS,),
            in_specs=[
                pl.BlockSpec((rows, LANES), lambda p, n: (0, p)),
                pl.BlockSpec((rows, LANES), lambda p, n: (0, p + PAIRS)),
                pl.BlockSpec((rows, LANES), lambda p, n: (0, p + 2 * PAIRS)),
                pl.BlockSpec((rows, LANES), lambda p, n: (0, p)),
                pl.BlockSpec((rows, LANES), lambda p, n: (0, p)),
                pl.BlockSpec((rows, LANES), lambda p, n: (0, 0)),
            ],
            out_specs=pl.BlockSpec((rows, wide), lambda p, n: (0, 0)),
            scratch_shapes=[pltpu.VMEM((LANES, rows), WIDE)],
        ),
        compiler_params=params(),
        cost_estimate=cost(40 * rows * rows * width, 16 * rows * width, HEADS * rows * rows),
        name="attention_backward",
    )(lengths, qkv, qkv, qkv, da, mixed, lse)


def qkv_backward(spot, own, other, column, dqkv, e2, h, a1, table):
    rows, wide = dqkv.shape
    width = wide // 3
    half = wide // 2
    tile = 384

    def body(
        spot_ref, own_ref, other_ref, d_ref, e_ref, h_ref, a_ref, t_ref,
        o_ref, mine_ref, rest_ref, sums_ref, w_ref, at_ref, acc_ref, sems,
    ):
        copies = piece_copies(spot_ref, own_ref, other_ref, w_ref, sems, column, half)
        for copy in copies:
            copy.start()
        at_ref[...] = a_ref[...].T
        acc_ref[...] = jnp.zeros_like(acc_ref)
        for copy in copies:
            copy.wait()
        c = spot_ref[3]
        for owner, out_ref in ((c, mine_ref), (1 - c, rest_ref)):
            starts = block_starts(spot_ref, owner, width // 16)

            def step(n, carry):
                at = pl.ds(pl.multiple_of(owner * half + n * tile, LANES), tile)
                d = d_ref[:, at]
                put_blocks(
                    dot(at_ref[...], d), out_ref, starts, pl.multiple_of(n * tile, LANES), tile
                )
                acc_ref[...] += dot_nt(d, w_ref[:, at])
                return carry

            lax.fori_loop(0, half // tile, step, 0)
        dv, gain, shift = norm_back(h_ref[...], t_ref[GAIN1 : GAIN1 + 1, :], acc_ref[...])
        o_ref[...] = e_ref[...] + dv
        sums_ref[0:1, :] = gain
        sums_ref[1:2, :] = shift
        sums_ref[2:3, :] = column_sum(d_ref[:, :width])
        sums_ref[3:4, :] = column_sum(d_ref[:, 2 * width :])

    return pl.pallas_call(
        body,
        out_shape=[
            jax.ShapeDtypeStruct((rows, width), WIDE),
            jax.ShapeDtypeStruct((width, half), LOW),
            jax.ShapeDtypeStruct((width, half), LOW),
            jax.ShapeDtypeStruct((8, width), WIDE),
        ],
        in_specs=[pl.BlockSpec(memory_space=pltpu.SMEM)] + any_specs(2) + vmem_specs(5),
        out_specs=vmem_specs(4),
        scratch_shapes=[
            pltpu.VMEM((width, wide), LOW),
            pltpu.VMEM((width, rows), LOW),
            pltpu.VMEM((rows, width), WIDE),
            pltpu.SemaphoreType.DMA((32,)),
        ],
        compiler_params=params(),
        cost_estimate=cost(4 * rows * width * wide, 4 * width * wide + 16 * rows * width),
        name="qkv_backward",
    )(spot, own, other, dqkv, e2, h, a1, table)


def small_forward(spot, own, column, hidden):
    width = own.shape[0]

    def body(spot_ref, own_ref, t_ref, b_ref, w_ref, sems):
        rows = width // 16
        starts = block_starts(spot_ref, spot_ref[3], rows)
        copies = [
            pltpu.make_async_copy(
                own_ref.at[pl.ds(start, rows), pl.ds(column, LANES)],
                w_ref.at[pl.ds(block * rows, rows), :],
                sems.at[block],
            )
            for block, start in enumerate(starts)
        ]
        for copy in copies:
            copy.start()
        for copy in copies:
            copy.wait()
        values = w_ref[...].astype(WIDE)
        t_ref[...] = values.T[0:8, :]
        share = hidden // 32
        for device in range(32):
            at = device * (width // 32)
            b_ref[0:1, device * share : (device + 1) * share] = values[
                at : at + 1, LANES - share :
            ]

    return pl.pallas_call(
        body,
        out_shape=[
            jax.ShapeDtypeStruct((8, width), WIDE),
            jax.ShapeDtypeStruct((1, hidden), WIDE),
        ],
        in_specs=[pl.BlockSpec(memory_space=pltpu.SMEM)] + any_specs(1),
        out_specs=vmem_specs(2),
        scratch_shapes=[pltpu.VMEM((width, LANES), LOW), pltpu.SemaphoreType.DMA((16,))],
        compiler_params=params(),
        cost_estimate=cost(0, 4 * width * LANES),
        name="small_forward",
    )(spot, own)


def small_backward(spot, first, second, down_sum, up_sum):
    width = first.shape[1]
    hidden = up_sum.shape[1]

    def body(spot_ref, f_ref, s_ref, d_ref, u_ref, mine_ref, rest_ref, w_ref, p_ref):
        w_ref[...] = jnp.zeros_like(w_ref)
        for row, value in (
            (GAIN1, s_ref[0:1, :]),
            (GAIN2, f_ref[0:1, :]),
            (BQ, s_ref[2:3, :]),
            (BV, s_ref[3:4, :]),
            (BO, f_ref[2:3, :]),
            (BD, d_ref[...]),
            (SH1, s_ref[1:2, :]),
            (SH2, f_ref[1:2, :]),
        ):
            w_ref[row : row + 1, :] = value
        p_ref[...] = w_ref[...].T
        share = hidden // 32
        for device in range(32):
            at = device * (width // 32)
            p_ref[at : at + 1, LANES - share :] = u_ref[
                0:1, device * share : (device + 1) * share
            ]
        packed = p_ref[...]
        c = spot_ref[3]
        for owner, out_ref in ((c, mine_ref), (1 - c, rest_ref)):
            put_blocks(packed, out_ref, block_starts(spot_ref, owner, width // 16), 0, LANES)

    return pl.pallas_call(
        body,
        out_shape=[jax.ShapeDtypeStruct((width, LANES), LOW)] * 2,
        in_specs=[pl.BlockSpec(memory_space=pltpu.SMEM)] + vmem_specs(4),
        out_specs=vmem_specs(2),
        scratch_shapes=[pltpu.VMEM((LANES, width), WIDE), pltpu.VMEM((width, LANES), WIDE)],
        compiler_params=params(),
        cost_estimate=cost(0, 8 * width * LANES),
        name="small_backward",
    )(spot, first, second, down_sum, up_sum)


def linear(z, x, y, c):
    return ((z * 2 + x) * 2 + y) * 2 + c


def pairs_of(step):
    result = []
    for z in range(4):
        for x in range(2):
            for y in range(2):
                for c in range(2):
                    result.append((linear(z, x, y, c), linear(*step(z, x, y, c))))
    return result


TO_CORE = pairs_of(lambda z, x, y, c: (z, x, y, 1 - c))
TO_RING = pairs_of(lambda z, x, y, c: ((z + 1) % 4, x, y, c))
TO_XY = pairs_of(lambda z, x, y, c: (z, x, 1 - y, c) if c else (z, 1 - x, y, c))
TO_YX = pairs_of(lambda z, x, y, c: (z, 1 - x, y, c) if c else (z, x, 1 - y, c))


def send(value, pairs):
    return lax.ppermute(value, AXES, pairs)


def blocked():
    return lax.axis_size("dp") == 8 and lax.axis_size("fsdp") == 4


def place():
    if not blocked():
        return jnp.zeros((4,), jnp.int32)
    dp = lax.axis_index("dp")
    fsdp = lax.axis_index("fsdp")
    return jnp.stack([dp // 2, dp % 2, fsdp // 2, fsdp % 2]).astype(jnp.int32)


def halves(pieces):
    low = [piece[:, : piece.shape[1] // 2] for piece in pieces]
    high = [piece[:, piece.shape[1] // 2 :] for piece in pieces]
    return jnp.concatenate(low, axis=1), jnp.concatenate(high, axis=1)


def gather_rows(spot, pieces):
    offsets = [0]
    for piece in pieces:
        offsets.append(offsets[-1] + piece.shape[1] // 2)
    if not blocked():
        whole = [lax.all_gather(piece, AXES, axis=0, tiled=True) for piece in pieces]
        low, high = [
            part.reshape(4, 2, 2, -1, part.shape[1])[jnp.array([0, 3, 2, 1])]
            for part in halves(whole)
        ]
        width = low.shape[-1]
        own = low.transpose(2, 1, 0, 3, 4).reshape(-1, width)
        other = high.transpose(1, 2, 0, 3, 4).reshape(-1, width)
        return own, other, offsets
    c = spot[3]
    low, high = halves(pieces)
    mine = jnp.where(c == 0, low, high)
    got = send(jnp.where(c == 0, high, low), TO_CORE)
    block = jnp.where(
        c == 0, jnp.concatenate([mine, got], axis=0), jnp.concatenate([got, mine], axis=0)
    )
    ring = [block]
    for step in range(3):
        ring.append(send(ring[-1], TO_RING))
    stack = jnp.concatenate(ring, axis=0)
    stack = jnp.concatenate([stack, send(stack, TO_XY)], axis=0)
    stack = jnp.concatenate([stack, send(stack, TO_YX)], axis=0)
    return stack, send(stack, TO_CORE), offsets


def added(parts):
    total = parts[0].astype(WIDE)
    for part in parts[1:]:
        total = total + part.astype(WIDE)
    return total


def scatter_rows(spot, mines, rests):
    if not blocked():
        result = []
        for mine, rest in zip(mines, rests):
            rows, half = mine.shape[0] // 16, mine.shape[1]
            low = mine.reshape(2, 2, 4, rows, half).transpose(2, 1, 0, 3, 4)
            high = rest.reshape(2, 2, 4, rows, half).transpose(2, 0, 1, 3, 4)
            whole = jnp.concatenate([low, high], axis=-1)[jnp.array([0, 3, 2, 1])]
            whole = whole.reshape(16 * rows, 2 * half)
            result.append(
                lax.psum_scatter(whole, AXES, scatter_dimension=0, tiled=True).astype(WIDE)
            )
        return result
    c = spot[3]
    height = mines[0].shape[0]
    a = height // 2
    b = height // 4
    rows = height // 16
    gots = [send(rest, TO_CORE) for rest in rests]

    def part(start, stop):
        return jnp.concatenate(
            [added([mine[start:stop], got[start:stop]]) for mine, got in zip(mines, gots)], axis=1
        )

    got_a = send(part(a, 2 * a).astype(LOW), TO_YX)
    got_b = send(added([part(b, 2 * b), got_a[b : 2 * b]]).astype(LOW), TO_XY)

    def block_at(step):
        at = slice(step * rows, (step + 1) * rows)
        return added([part(at.start, at.stop), got_a[at], got_b[at]])

    moving = block_at(1)
    for step in (2, 3, 0):
        moving = added([block_at(step), send(moving.astype(LOW), TO_RING)])
    low, high = moving[: rows // 2], moving[rows // 2 :]
    kept = jnp.where(c == 0, low, high)
    got = send(jnp.where(c == 0, high, low).astype(LOW), TO_CORE).astype(WIDE)
    result = []
    start = 0
    for mine in mines:
        half = mine.shape[1]
        ours = kept[:, start : start + half]
        theirs = got[:, start : start + half]
        result.append(
            jnp.where(
                c == 0,
                jnp.concatenate([ours, theirs], axis=1),
                jnp.concatenate([theirs, ours], axis=1),
            )
        )
        start = start + half
    return result


def pack_small(gains, shifts, up_bias):
    rows = gains.shape[1]
    columns = jnp.concatenate([gains, shifts], axis=0).T
    share = up_bias.shape[0]
    first = jnp.pad(columns, ((0, 0), (0, LANES - share - columns.shape[1])))
    second = jnp.pad(up_bias[None, :], ((0, rows - 1), (0, 0)))
    packed = jnp.concatenate([first, second], axis=1)
    return jnp.concatenate([packed, packed], axis=1)


def unpack_small(packed, share):
    return packed[:, 0:2].T, packed[:, 2:8].T, packed[0, LANES - share : LANES]


def whole_small(gains, shifts, up_bias):
    both = jnp.concatenate([gains, shifts], axis=0)
    table = lax.all_gather(both, AXES, axis=1, tiled=True)
    return table.astype(WIDE), lax.all_gather(up_bias, AXES, axis=0, tiled=True)[None].astype(WIDE)


def spread_small(first, second, down_sum, up_sum):
    table = jnp.concatenate(
        [
            second[0:1],
            first[0:1],
            second[2:4],
            first[2:3],
            down_sum,
            second[1:2],
            first[1:2],
        ],
        axis=0,
    )
    own = lax.psum_scatter(table, AXES, scatter_dimension=1, tiled=True)
    return own[0:2], own[2:8], lax.psum_scatter(up_sum[0], AXES, scatter_dimension=0, tiled=True)


def local(
    hidden_in,
    cotangent,
    lengths,
    qkv_weight,
    out_weight,
    up_weight,
    down_weight,
    norm_gains,
    biases,
    up_bias,
):
    clips, slots, width = hidden_in.shape
    layers = qkv_weight.shape[0]
    share = up_bias.shape[1]
    hidden = down_weight.shape[1]
    assert clips == 1
    spot = place()
    down_t = jnp.swapaxes(down_weight, 1, 2).astype(LOW)
    weights = []
    for i in range(layers):
        gains, shifts, bias = (v[i].astype(LOW) for v in (norm_gains, biases, up_bias))
        pieces = [qkv_weight[i].astype(LOW)]
        if blocked():
            pieces.append(pack_small(gains, shifts, bias))
        own, other, at = gather_rows(spot, pieces)
        qkv = (own, other, at[0])
        if blocked():
            table, bias = small_forward(spot, own, at[1], hidden)
        else:
            table, bias = whole_small(gains, shifts, bias)
        own, other, at = gather_rows(spot, [out_weight[i].astype(LOW), up_weight[i].astype(LOW)])
        out, up = (own, other, at[0]), (own, other, at[1])
        own, other, at = gather_rows(spot, [down_t[i]])
        weights.append((qkv, out, up, (own, other, at[0]), table, bias))

    h = hidden_in[0]
    records = []
    for i in range(layers):
        qkv_w, out_w, up_w, down_w, table, bias = weights[i]
        qkv, a1 = qkv_forward(spot, *qkv_w, h, table)
        mixed, lse = attention_forward(lengths, qkv)
        h2, a2 = out_forward(spot, *out_w, h, mixed, table)
        z, slope, result = mlp_forward(spot, up_w, down_w, h2, a2, bias, table)
        records.append((h, a1, qkv, mixed, lse, h2, a2, z, slope))
        h = result
    output = h[None]
    e = cotangent[0]
    owned = [None] * layers
    for i in reversed(range(layers)):
        qkv_w, out_w, up_w, down_w, table, bias = weights[i]
        h, a1, qkv, mixed, lse, h2, a2, z, slope = records[i]
        du, mine, rest, down_sum, up_sum = down_backward(spot, down_w, e, z, slope)
        (own_down,) = scatter_rows(spot, [mine], [rest])
        e2, da, mine, rest, out_mine, out_rest, first = up_backward(
            spot, up_w, out_w, e, h2, a2, mixed, du, table
        )
        own_out, own_up = scatter_rows(spot, [out_mine, mine], [out_rest, rest])
        dqkv = attention_backward(lengths, qkv, da, mixed, lse)
        e, mine, rest, second = qkv_backward(spot, *qkv_w, dqkv, e2, h, a1, table)
        if blocked():
            small_mine, small_rest = small_backward(spot, first, second, down_sum, up_sum)
            own_qkv, packed = scatter_rows(spot, [mine, small_mine], [rest, small_rest])
            small = unpack_small(packed, share)
        else:
            (own_qkv,) = scatter_rows(spot, [mine], [rest])
            small = spread_small(first, second, down_sum, up_sum)
        owned[i] = (own_qkv, own_out, own_up, own_down.T, *small)

    stacked = [jnp.stack([owned[i][n] for i in range(layers)]) for n in range(7)]
    return (output, e[None], *stacked)


def solution(mesh):
    return jax.shard_map(
        local,
        mesh=mesh,
        in_specs=(
            P(("dp", "fsdp"), None, None),
            P(("dp", "fsdp"), None, None),
            P(("dp", "fsdp")),
            P(None, ("dp", "fsdp"), None),
            P(None, ("dp", "fsdp"), None),
            P(None, ("dp", "fsdp"), None),
            P(None, None, ("dp", "fsdp")),
            P(None, None, ("dp", "fsdp")),
            P(None, None, ("dp", "fsdp")),
            P(None, ("dp", "fsdp")),
        ),
        out_specs=(
            P(("dp", "fsdp"), None, None),
            P(("dp", "fsdp"), None, None),
            P(None, ("dp", "fsdp"), None),
            P(None, ("dp", "fsdp"), None),
            P(None, ("dp", "fsdp"), None),
            P(None, None, ("dp", "fsdp")),
            P(None, None, ("dp", "fsdp")),
            P(None, None, ("dp", "fsdp")),
            P(None, ("dp", "fsdp")),
        ),
        check_vma=False,
    )
```

time: 1540 us -> 589 us (0.38)
  Pallas kernels: 895 us -> 207 us
  matrix products: 169 us -> 0 us
  local copies, waits for them, and re-layouts: 115 us -> 32.1 us
  other arithmetic: 86.9 us -> 48.1 us
  waiting for transfers between devices: 208 us -> 231 us
    pallas_call x6 -> x20, Pallas kernels: 895 us -> 207 us  [the longest x2 36.9 us: up_backward(): pl.pallas_call(body, out_shape=[jax.ShapeDtypeStruct((rows, width), WIDE)...]
    dot_general x36 -> x0, matrix products: 169 us -> none  [the longest x2 38.8 us: forward_layer(): jnp.dot(normed_two, w_up, preferred_element_type=jnp.float32)]
    ppermute x84 -> x88, waiting for transfers between devices: 208 us -> 231 us  [send(): return lax.ppermute(value, AXES, pairs)]
    unnamed x276 -> x101, local copies, waits for them, and re-layouts: 35.2 us -> 15.1 us
    convert_element_type x48 -> x39, other arithmetic: 37.8 us -> 19.9 us  [the longest x18 13.3 us: scatter_rows(): moving = added([block_at(step), send(moving.astype(LOW), TO_RING)])]
    select_n x24 -> x12, other arithmetic: 18.5 us -> 2.3 us  [the longest x8 2.17 us: scatter_rows(): jnp.where(c == 0, jnp.concatenate([ours, theirs], axis=1), jnp.concatenat...]
    slice x23 -> x13, local copies, waits for them, and re-layouts: 16.8 us -> 1.24 us  [the longest x2 1.16 us: unpack_small(): return (packed[:, 0:2].T, packed[:, 2:8].T, packed[0, LANES - share:LANES])]
    ppermute x84 -> x88, starting transfers between devices: 58.9 us -> 58.8 us  [send(): return lax.ppermute(value, AXES, pairs)]
  transfers between devices with their start and end apart: 84 -> 88, of which waited for: 39 -> 45; matrix products, arithmetic and copies ran while one was open for 13% -> 12% of each run, Pallas kernels for 46% -> 22%
where the time goes in v2:
time: 589 us; the launch traced here: 580 us
  waiting for transfers between devices  231 us (39%)
  Pallas kernels  207 us (35%)
  starting transfers between devices  58.8 us (10%)
  other arithmetic  48.1 us (8%)
  local copies, waits for them, and re-layouts  32.1 us (5%)
    ppermute x88, waiting for transfers between devices, send(): return lax.ppermute(value, AXES, pairs)  231 us
    ppermute x88, starting transfers between devices, send(): return lax.ppermute(value, AXES, pairs)  58.8 us
    pallas_call x2, Pallas kernels, up_backward(): pl.pallas_call(body, out_shape=[jax.ShapeDtypeStruct((rows, width), WIDE)...  36.9 us
    pallas_call x2, Pallas kernels, mlp_forward(): pl.pallas_call(body, out_shape=[jax.ShapeDtypeStruct((rows, hidden), LOW)...  33.7 us
    pallas_call x2, Pallas kernels, down_backward(): pl.pallas_call(body, out_shape=[jax.ShapeDtypeStruct((rows, hidden), LOW)...  30.6 us
    pallas_call x2, Pallas kernels, qkv_backward(): pl.pallas_call(body, out_shape=[jax.ShapeDtypeStruct((rows, width), WIDE)...  26.9 us
    pallas_call x2, Pallas kernels, attention_backward(): pl.pallas_call(body, out_shape=jax.ShapeDtypeStruct((rows, wide), LOW), g...  25.3 us
    pallas_call x2, Pallas kernels, attention_forward(): pl.pallas_call(body, out_shape=[jax.ShapeDtypeStruct((rows, width), LOW),...  19.9 us
  transfers between devices with their start and end apart: 88, of which 45 were waited for; matrix products, arithmetic and copies ran while one was open for 12% of the time, Pallas kernels for 22%

profile of v2, /device:TPU:0, one launch (start us, length us, event | category | flops | bytes accessed | tf_op | source)
XLA Modules:
  0.0 580.1 jit_solution(15261688791517133498)
XLA Ops:
  6.9 3.0 collective-permute-start.29
  22.6 2.5 collective-permute-done.22
  25.8 3.3 collective-permute-done.1
  29.1 3.9 collective-permute-done.15
  33.7 1.9 collective-permute-done.30
  35.6 2.6 collective-permute-done.37
  38.9 2.5 collective-permute-done.9
  42.1 2.5 collective-permute-done.23
  45.3 9.8 %collective-permute-done.31 = bf16[48,1280]{1,0:T(8,128)(2,1)S(1)} collective-permute-done((bf16[48,1280]{1,0:T(8,128)(2,1)S(1)}, bf16[48,1280]{1,0:T(8,128)(2,1)S(1)}, u32[]{:S(2)}, u32[]{:S(2)}) %collective-permute-start.31) | collective-permute-done | bytes 122912 | tf_op jit(solution)/shard_map/ppermute | solution.py:670
  55.2 2.6 collective-permute-done.38
  61.4 2.1 collective-permute-done.24
  65.5 6.4 %collective-permute-done.17 = bf16[48,1920]{1,0:T(8,128)(2,1)S(1)} collective-permute-done((bf16[48,1920]{1,0:T(8,128)(2,1)S(1)}, bf16[48,1920]{1,0:T(8,128)(2,1)S(1)}, u32[]{:S(2)}, u32[]{:S(2)}) %collective-permute-start.17) | collective-permute-done | bytes 184352 | tf_op jit(solution)/shard_map/ppermute | solution.py:670
  76.3 9.8 %collective-permute-done.18 = bf16[192,1920]{1,0:T(8,128)(2,1)S(1)} collective-permute-done((bf16[192,1920]{1,0:T(8,128)(2,1)S(1)}, bf16[192,1920]{1,0:T(8,128)(2,1)S(1)}, u32[]{:S(2)}, u32[]{:S(2)}) %collective-permute-start.18) | collective-permute-done | bytes 737312 | tf_op jit(solution)/shard_map/ppermute | solution.py:670
  91.9 8.2 %collective-permute-done.4 = bf16[192,1920]{1,0:T(8,128)(2,1)S(1)} collective-permute-done((bf16[192,1920]{1,0:T(8,128)(2,1)S(1)}, bf16[192,1920]{1,0:T(8,128)(2,1)S(1)}, u32[]{:S(2)}, u32[]{:S(2)}) %collective-permute-start.4) | collective-permute-done | bytes 737312 | tf_op jit(solution)/shard_map/ppermute | solution.py:670
  100.1 2.0 collective-permute-start.26
  103.2 21.4 %collective-permute-done.33 = bf16[384,1280]{1,0:T(8,128)(2,1)S(1)} collective-permute-done((bf16[384,1280]{1,0:T(8,128)(2,1)S(1)}, bf16[384,1280]{1,0:T(8,128)(2,1)S(1)}, u32[]{:S(2)}, u32[]{:S(2)}) %collective-permute-start.33) | collective-permute-done | bytes 983072 | tf_op jit(solution)/shard_map/ppermute | solution.py:670
  126.1 2.1 collective-permute-start.34
  130.6 6.7 %collective-permute-done.26 = bf16[384,1536]{1,0:T(8,128)(2,1)S(1)} collective-permute-done((bf16[384,1536]{1,0:T(8,128)(2,1)S(1)}, bf16[384,1536]{1,0:T(8,128)(2,1)S(1)}, u32[]{:S(2)}, u32[]{:S(2)}) %collective-permute-start.26) | collective-permute-done | bytes 1179680 | tf_op jit(solution)/shard_map/ppermute | solution.py:670
  139.8 13.3 %collective-permute-done.5 = bf16[384,1920]{1,0:T(8,128)(2,1)S(1)} collective-permute-done((bf16[384,1920]{1,0:T(8,128)(2,1)S(1)}, bf16[384,1920]{1,0:T(8,128)(2,1)S(1)}, u32[]{:S(2)}, u32[]{:S(2)}) %collective-permute-start.5) | collective-permute-done | bytes 1474592 | tf_op jit(solution)/shard_map/ppermute | solution.py:670
  153.1 2.1 collective-permute-start.27
  155.4 8.3 %collective-permute-done.40 = bf16[384,1280]{1,0:T(8,128)(2,1)S(1)} collective-permute-done((bf16[384,1280]{1,0:T(8,128)(2,1)S(1)}, bf16[384,1280]{1,0:T(8,128)(2,1)S(1)}, u32[]{:S(2)}, u32[]{:S(2)}) %collective-permute-start.40) | collective-permute-done | bytes 983072 | tf_op jit(solution)/shard_map/ppermute | solution.py:670
  163.6 2.1 collective-permute-start.6
  166.7 9.6 %collective-permute-done.12 = bf16[384,1536]{1,0:T(8,128)(2,1)S(1)} collective-permute-done((bf16[384,1536]{1,0:T(8,128)(2,1)S(1)}, bf16[384,1536]{1,0:T(8,128)(2,1)S(1)}, u32[]{:S(2)}, u32[]{:S(2)}) %collective-permute-start.12) | collective-permute-done | bytes 1179680 | tf_op jit(solution)/shard_map/ppermute | solution.py:670
  176.3 1.8 collective-permute-start.41
  181.7 2.5 small_forward.3
  184.2 2.5 small_forward.2
  186.7 7.1 %qkv_forward.2 = (bf16[496,2304]{1,0:T(8,128)(2,1)}, bf16[496,768]{1,0:T(8,128)(2,1)}) custom-call(s32[4]{0:T(128)} %pad_add_fusion.spot_ref, bf16[768,1280]{1,0:T(8,128)(2,1)} %copy-done.7, bf16[768,1280]{1,0:T(8,128)(2,1)} %copy-done.36, f32[496,768]{1,0:T(8,128)} %bitcast.82, f32[8,768]{1,0:T(8,128)} %get-tuple-element.67.t_ref), custom_call_target="tpu_custom_call" | custom-call | flops 1755316224 | bytes 6967296 | tf_op jit(solution)/shard_map/qkv_forward/pallas_call | solution.py:116
  193.8 10.2 %attention_forward.2 = (bf16[496,768]{1,0:T(8,128)(2,1)}, f32[496,128]{1,0:T(8,128)}) custom-call(s32[1]{0:T(128)S(6)} %copy.88.len_ref, bf16[496,2304]{1,0:T(8,128)(2,1)} %get-tuple-element.68.q_ref.k_ref.v_ref, bf16[496,2304]{1,0:T(8,128)(2,1)} %get-tuple-element.68.q_ref.k_ref.v_ref, bf16[496,2304]{1,0:T(8,128)(2,1)} %get-tuple-element.68.q_ref.k_ref.v_ref), custom_call_target="tpu_custom_call" | custom-call | flops 3023044608 | bytes 3047424 | tf_op jit(solution)/shard_map/attention_forward/pallas_call | solution.py:158
  204.0 5.4 out_forward.2
  209.4 16.8 %mlp_forward.2 = (bf16[496,3072]{1,0:T(8,128)(2,1)}, bf16[496,3072]{1,0:T(8,128)(2,1)}, f32[496,768]{1,0:T(8,128)}) custom-call(s32[4]{0:T(128)} %pad_add_fusion.spot_ref, bf16[768,1920]{1,0:T(8,128)(2,1)} %constant_dynamic-update-slice_fusion.27.own_ref.uo_ref.oo_ref, bf16[768,1920]{1,0:T(8,128)(2,1)} %collective-permute-done.20.other_ref.up_ref.op_ref, ...), custom_call_target="tpu_custom_call" | custom-call | flops 4680843264 | bytes 15532032 | tf_op jit(solution)/shard_map/mlp_forward/pallas_call | solution.py:248
  226.3 7.1 %qkv_forward.3 = (bf16[496,2304]{1,0:T(8,128)(2,1)}, bf16[496,768]{1,0:T(8,128)(2,1)}) custom-call(s32[4]{0:T(128)} %pad_add_fusion.spot_ref, bf16[768,1280]{1,0:T(8,128)(2,1)} %constant_dynamic-update-slice_fusion.60.own_ref, bf16[768,1280]{1,0:T(8,128)(2,1)} %collective-permute-done.41.other_ref, f32[496,768]{1,0:T(8,128)} %get-tuple-element.73.h_ref, ...), custom_call_target="tpu_custom_call" | custom-call | flops 1755316224 | bytes 6967296 | tf_op jit(solution)/shard_map/qkv_forward/pallas_call | solution.py:116
  233.4 9.7 %attention_forward.3 = (bf16[496,768]{1,0:T(8,128)(2,1)}, f32[496,128]{1,0:T(8,128)}) custom-call(s32[1]{0:T(128)S(6)} %copy.88.len_ref, bf16[496,2304]{1,0:T(8,128)(2,1)} %get-tuple-element.75.q_ref.k_ref.v_ref, bf16[496,2304]{1,0:T(8,128)(2,1)} %get-tuple-element.75.q_ref.k_ref.v_ref, bf16[496,2304]{1,0:T(8,128)(2,1)} %get-tuple-element.75.q_ref.k_ref.v_ref), custom_call_target="tpu_custom_call" | custom-call | flops 3023044608 | bytes 3047424 | tf_op jit(solution)/shard_map/attention_forward/pallas_call | solution.py:158
  243.1 5.4 out_forward.3
  248.6 16.9 %mlp_forward.3 = (bf16[496,3072]{1,0:T(8,128)(2,1)}, bf16[496,3072]{1,0:T(8,128)(2,1)}, f32[496,768]{1,0:T(8,128)}) custom-call(s32[4]{0:T(128)} %pad_add_fusion.spot_ref, bf16[768,1920]{1,0:T(8,128)(2,1)} %copy-done, bf16[768,1920]{1,0:T(8,128)(2,1)} %collective-permute-done.6.other_ref.up_ref.op_ref, ...), custom_call_target="tpu_custom_call" | custom-call | flops 4680843264 | bytes 15532032 | tf_op jit(solution)/shard_map/mlp_forward/pallas_call | solution.py:248
  265.4 15.3 %down_backward.2 = (bf16[496,3072]{1,0:T(8,128)(2,1)}, bf16[768,1536]{1,0:T(8,128)(2,1)}, bf16[768,1536]{1,0:T(8,128)(2,1)}, f32[1,768]{1,0:T(1,128)}, f32[1,3072]{1,0:T(1,128)}) custom-call(s32[4]{0:T(128)} %pad_add_fusion.spot_ref, bf16[768,1536]{1,0:T(8,128)(2,1)} %constant_dynamic-update-slice_fusion.16.do_ref.own_ref, ...), custom_call_target="tpu_custom_call" | custom-call | flops 4680843264 | bytes 18579456 | tf_op jit(solution)/shard_map/down_backward/pallas_call | solution.py:332
  280.7 18.4 %up_backward.2 = (f32[496,768]{1,0:T(8,128)}, bf16[496,768]{1,0:T(8,128)(2,1)}, bf16[768,1536]{1,0:T(8,128)(2,1)}, bf16[768,1536]{1,0:T(8,128)(2,1)}, bf16[768,3...) custom-call(s32[4]{0:T(128)} %pad_add_fusion.spot_ref, bf16[768,1920]{1,0:T(8,128)(2,1)} %copy-done, ...), custom_call_target="tpu_custom_call" | custom-call | flops 5851054080 | bytes 14843904 | tf_op jit(solution)/shard_map/up_backward/pallas_call | solution.py:406
  299.1 12.6 %attention_backward.2.d_ref = bf16[496,2304]{1,0:T(8,128)(2,1)} custom-call(s32[1]{0:T(128)S(6)} %copy.88.len_ref, bf16[496,2304]{1,0:T(8,128)(2,1)} %get-tuple-element.75.q_ref.k_ref.v_ref, bf16[496,2304]{1,0:T(8,128)(2,1)} %get-tuple-element.75.q_ref.k_ref.v_ref, bf16[496,2304]{1,0:T(8,128)(2,1)} %get-tuple-element.75.q_ref.k_ref.v_ref, ...), custom_call_target="tpu_custom_call" | custom-call | flops 7557611520 | bytes 6094848 | tf_op jit(solution)/shard_map/attention_backward/pallas_call | solution.py:483
  311.7 13.3 %qkv_backward.2 = (f32[496,768]{1,0:T(8,128)}, bf16[768,1152]{1,0:T(8,128)(2,1)}, bf16[768,1152]{1,0:T(8,128)(2,1)}, f32[8,768]{1,0:T(8,128)}) custom-call(s32[4]{0:T(128)} %pad_add_fusion.spot_ref, bf16[768,1280]{1,0:T(8,128)(2,1)} %constant_dynamic-update-slice_fusion.60.own_ref, bf16[768,1280]{1,0:T(8,128)(2,1)} %collective-permute-done.41.other_ref, ...), custom_call_target="tpu_custom_call" | custom-call | flops 3510632448 | bytes 13172736 | tf_op jit(solution)/shard_map/qkv_backward/pallas_call | solution.py:544
  325.0 1.8 small_backward.3
  327.3 15.4 %down_backward.3 = (bf16[496,3072]{1,0:T(8,128)(2,1)}, bf16[768,1536]{1,0:T(8,128)(2,1)}, bf16[768,1536]{1,0:T(8,128)(2,1)}, f32[1,768]{1,0:T(1,128)}, f32[1,3072]{1,0:T(1,128)}) custom-call(s32[4]{0:T(128)} %pad_add_fusion.spot_ref, bf16[768,1536]{1,0:T(8,128)(2,1)} %constant_dynamic-update-slice_fusion.38.do_ref.own_ref, ...), custom_call_target="tpu_custom_call" | custom-call | flops 4680843264 | bytes 18579456 | tf_op jit(solution)/shard_map/down_backward/pallas_call | solution.py:332
  342.7 18.6 %up_backward.3 = (f32[496,768]{1,0:T(8,128)}, bf16[496,768]{1,0:T(8,128)(2,1)}, bf16[768,1536]{1,0:T(8,128)(2,1)}, bf16[768,1536]{1,0:T(8,128)(2,1)}, bf16[768,3...) custom-call(s32[4]{0:T(128)} %pad_add_fusion.spot_ref, ...), custom_call_target="tpu_custom_call" | custom-call | flops 5851054080 | bytes 14843904 | tf_op jit(solution)/shard_map/up_backward/pallas_call | solution.py:406
  361.3 12.6 %attention_backward.3.d_ref = bf16[496,2304]{1,0:T(8,128)(2,1)} custom-call(s32[1]{0:T(128)S(6)} %copy.88.len_ref, bf16[496,2304]{1,0:T(8,128)(2,1)} %get-tuple-element.68.q_ref.k_ref.v_ref, bf16[496,2304]{1,0:T(8,128)(2,1)} %get-tuple-element.68.q_ref.k_ref.v_ref, bf16[496,2304]{1,0:T(8,128)(2,1)} %get-tuple-element.68.q_ref.k_ref.v_ref, ...), custom_call_target="tpu_custom_call" | custom-call | flops 7557611520 | bytes 6094848 | tf_op jit(solution)/shard_map/attention_backward/pallas_call | solution.py:483
  373.9 13.7 %qkv_backward.3 = (f32[496,768]{1,0:T(8,128)}, bf16[768,1152]{1,0:T(8,128)(2,1)}, bf16[768,1152]{1,0:T(8,128)(2,1)}, f32[8,768]{1,0:T(8,128)}) custom-call(s32[4]{0:T(128)} %pad_add_fusion.spot_ref, bf16[768,1280]{1,0:T(8,128)(2,1)} %copy-done.7, bf16[768,1280]{1,0:T(8,128)(2,1)} %copy-done.36, bf16[496,2304]{1,0:T(8,128)(2,1)} %attention_backward.3.d_ref, ...), custom_call_target="tpu_custom_call" | custom-call | flops 3510632448 | bytes 13172736 | tf_op jit(solution)/shard_map/qkv_backward/pallas_call | solution.py:544
  387.6 1.8 small_backward.2
  404.4 3.5 collective-permute-done.74
  415.2 1.9 copy-done.1
  420.2 4.7 collective-permute-done.44
  425.0 3.0 collective-permute-start.45
  429.0 3.9 collective-permute-done.53
  433.2 10.1 %collective-permute-done.45 = bf16[192,1280]{1,0:T(8,128)(2,1)S(1)} collective-permute-done((bf16[192,1280]{1,0:T(8,128)(2,1)S(1)}, bf16[192,1280]{1,0:T(8,128)(2,1)S(1)}, u32[]{:S(2)}, u32[]{:S(2)}) %collective-permute-start.45) | collective-permute-done | bytes 491552 | tf_op jit(solution)/shard_map/ppermute | solution.py:670
  443.4 6.6 %collective-permute-done.54 = bf16[48,1280]{1,0:T(8,128)(2,1)S(1)} collective-permute-done((bf16[48,1280]{1,0:T(8,128)(2,1)S(1)}, bf16[48,1280]{1,0:T(8,128)(2,1)S(1)}, u32[]{:S(2)}, u32[]{:S(2)}) %collective-permute-start.54) | collective-permute-done | bytes 122912 | tf_op jit(solution)/shard_map/ppermute | solution.py:670
  450.1 6.6 %collective-permute-done.46 = bf16[48,1280]{1,0:T(8,128)(2,1)S(1)} collective-permute-done((bf16[48,1280]{1,0:T(8,128)(2,1)S(1)}, bf16[48,1280]{1,0:T(8,128)(2,1)S(1)}, u32[]{:S(2)}, u32[]{:S(2)}) %collective-permute-start.46) | collective-permute-done | bytes 122912 | tf_op jit(solution)/shard_map/ppermute | solution.py:670
  456.8 6.6 %collective-permute-done.55 = bf16[48,1280]{1,0:T(8,128)(2,1)S(1)} collective-permute-done((bf16[48,1280]{1,0:T(8,128)(2,1)S(1)}, bf16[48,1280]{1,0:T(8,128)(2,1)S(1)}, u32[]{:S(2)}, u32[]{:S(2)}) %collective-permute-start.55) | collective-permute-done | bytes 122912 | tf_op jit(solution)/shard_map/ppermute | solution.py:670
  463.5 7.6 %collective-permute-done.47 = bf16[48,1280]{1,0:T(8,128)(2,1)S(1)} collective-permute-done((bf16[48,1280]{1,0:T(8,128)(2,1)S(1)}, bf16[48,1280]{1,0:T(8,128)(2,1)S(1)}, u32[]{:S(2)}, u32[]{:S(2)}) %collective-permute-start.47) | collective-permute-done | bytes 122912 | tf_op jit(solution)/shard_map/ppermute | solution.py:670
  472.4 18.1 %collective-permute-done.82 = bf16[384,1536]{1,0:T(8,128)(2,1)S(1)} collective-permute-done((bf16[384,1536]{1,0:T(8,128)(2,1)S(1)}, bf16[384,1536]{1,0:T(8,128)(2,1)S(1)}, u32[]{:S(2)}, u32[]{:S(2)}) %collective-permute-start.82) | collective-permute-done | bytes 1179680 | tf_op jit(solution)/shard_map/ppermute | solution.py:670
  516.9 6.1 %collective-permute-done.77 = bf16[48,1536]{1,0:T(8,128)(2,1)S(1)} collective-permute-done((bf16[48,1536]{1,0:T(8,128)(2,1)S(1)}, bf16[48,1536]{1,0:T(8,128)(2,1)S(1)}, u32[]{:S(2)}, u32[]{:S(2)}) %collective-permute-start.77) | collective-permute-done | bytes 147488 | tf_op jit(solution)/shard_map/ppermute | solution.py:670
  525.8 6.0 %collective-permute-done.78 = bf16[48,1536]{1,0:T(8,128)(2,1)S(1)} collective-permute-done((bf16[48,1536]{1,0:T(8,128)(2,1)S(1)}, bf16[48,1536]{1,0:T(8,128)(2,1)S(1)}, u32[]{:S(2)}, u32[]{:S(2)}) %collective-permute-start.78) | collective-permute-done | bytes 147488 | tf_op jit(solution)/shard_map/ppermute | solution.py:670
  535.6 4.3 collective-permute-done.79
  547.1 7.0 %collective-permute-done.62 = bf16[48,1920]{1,0:T(8,128)(2,1)S(1)} collective-permute-done((bf16[48,1920]{1,0:T(8,128)(2,1)S(1)}, bf16[48,1920]{1,0:T(8,128)(2,1)S(1)}, u32[]{:S(2)}, u32[]{:S(2)}) %collective-permute-start.62) | collective-permute-done | bytes 184352 | tf_op jit(solution)/shard_map/ppermute | solution.py:670
  555.2 2.4 collective-permute-done.70
  558.8 4.1 collective-permute-done.63
  564.0 2.8 collective-permute-done.71
  567.9 3.5 collective-permute-done.64
  572.5 2.8 collective-permute-done.72
  (414 shorter events, 127.7 us)
Async XLA Ops:
  5.4 10.0 %collective-permute-start.14 = (bf16[24,1920]{1,0:T(8,128)(2,1)S(1)}, bf16[24,1920]{1,0:T(8,128)(2,1)S(1)}, u32[]{:S(2)}, u32[]{:S(2)}) collective-permute-start(bf16[24,1920]{1,0:T(8,128)(2,1)S(1)} %get-tuple-element.202), channel_id=1, source_target_pairs={{0,1},{1,0},{2,3},{3,2},{4,5},{5,4},{6,7},{7,6},{8,9},{9,8},{10,11... | collective-permute-start | bytes 276488 | tf_op jit(solution)/shard_map/ppermute | solution.py:670
  6.0 9.3 %collective-permute-start = (bf16[24,1920]{1,0:T(8,128)(2,1)S(1)}, bf16[24,1920]{1,0:T(8,128)(2,1)S(1)}, u32[]{:S(2)}, u32[]{:S(2)}) collective-permute-start(bf16[24,1920]{1,0:T(8,128)(2,1)S(1)} %get-tuple-element.210), channel_id=1, source_target_pairs={{0,1},{1,0},{2,3},{3,2},{4,5},{5,4},{6,7},{7,6},{8,9},{9,8},{10,11... | collective-permute-start | bytes 276488 | tf_op jit(solution)/shard_map/ppermute | solution.py:670
  6.9 11.0 %collective-permute-start.29 = (bf16[48,1280]{1,0:T(8,128)(2,1)S(1)}, bf16[48,1280]{1,0:T(8,128)(2,1)S(1)}, u32[]{:S(2)}, u32[]{:S(2)}) collective-permute-start(bf16[48,1280]{1,0:T(8,128)(2,1)S(1)} %get-tuple-element.137), channel_id=1, source_target_pairs={{0,8},{1,9},{2,10},{3,11},{4,12},{5,13},{6,14},{7,15},{8,16},{9,17... | collective-permute-start | bytes 368648 | tf_op jit(solution)/shard_map/ppermute | solution.py:670
  10.7 8.8 %collective-permute-start.36 = (bf16[48,1280]{1,0:T(8,128)(2,1)S(1)}, bf16[48,1280]{1,0:T(8,128)(2,1)S(1)}, u32[]{:S(2)}, u32[]{:S(2)}) collective-permute-start(bf16[48,1280]{1,0:T(8,128)(2,1)S(1)} %get-tuple-element.135), channel_id=1, source_target_pairs={{0,8},{1,9},{2,10},{3,11},{4,12},{5,13},{6,14},{7,15},{8,16},{9,17... | collective-permute-start | bytes 368648 | tf_op jit(solution)/shard_map/ppermute | solution.py:670
  13.0 9.0 %collective-permute-start.8 = (bf16[48,1536]{1,0:T(8,128)(2,1)S(1)}, bf16[48,1536]{1,0:T(8,128)(2,1)S(1)}, u32[]{:S(2)}, u32[]{:S(2)}) collective-permute-start(bf16[48,1536]{1,0:T(8,128)(2,1)S(1)} %get-tuple-element.143), channel_id=1, source_target_pairs={{0,8},{1,9},{2,10},{3,11},{4,12},{5,13},{6,14},{7,15},{8,16},{9,17... | collective-permute-start | bytes 442376 | tf_op jit(solution)/shard_map/ppermute | solution.py:670
  15.2 9.8 %collective-permute-start.22 = (bf16[48,1536]{1,0:T(8,128)(2,1)S(1)}, bf16[48,1536]{1,0:T(8,128)(2,1)S(1)}, u32[]{:S(2)}, u32[]{:S(2)}) collective-permute-start(bf16[48,1536]{1,0:T(8,128)(2,1)S(1)} %get-tuple-element.139), channel_id=1, source_target_pairs={{0,8},{1,9},{2,10},{3,11},{4,12},{5,13},{6,14},{7,15},{8,16},{9,17... | collective-permute-start | bytes 442376 | tf_op jit(solution)/shard_map/ppermute | solution.py:670
  15.4 13.6 %collective-permute-start.1 = (bf16[48,1920]{1,0:T(8,128)(2,1)S(1)}, bf16[48,1920]{1,0:T(8,128)(2,1)S(1)}, u32[]{:S(2)}, u32[]{:S(2)}) collective-permute-start(bf16[48,1920]{1,0:T(8,128)(2,1)S(1)} %get-tuple-element.145), channel_id=1, source_target_pairs={{0,8},{1,9},{2,10},{3,11},{4,12},{5,13},{6,14},{7,15},{8,16},{9,17... | collective-permute-start | bytes 552968 | tf_op jit(solution)/shard_map/ppermute | solution.py:670
  17.9 15.1 %collective-permute-start.15 = (bf16[48,1920]{1,0:T(8,128)(2,1)S(1)}, bf16[48,1920]{1,0:T(8,128)(2,1)S(1)}, u32[]{:S(2)}, u32[]{:S(2)}) collective-permute-start(bf16[48,1920]{1,0:T(8,128)(2,1)S(1)} %get-tuple-element.141), channel_id=1, source_target_pairs={{0,8},{1,9},{2,10},{3,11},{4,12},{5,13},{6,14},{7,15},{8,16},{9,17... | collective-permute-start | bytes 552968 | tf_op jit(solution)/shard_map/ppermute | solution.py:670
  19.5 16.1 %collective-permute-start.30 = (bf16[48,1280]{1,0:T(8,128)(2,1)S(1)}, bf16[48,1280]{1,0:T(8,128)(2,1)S(1)}, u32[]{:S(2)}, u32[]{:S(2)}) collective-permute-start(bf16[48,1280]{1,0:T(8,128)(2,1)S(1)} %collective-permute-done.29), channel_id=1, source_target_pairs={{0,8},{1,9},{2,10},{3,11},{4,12},{5,13},{6,14},{7,15},{8,16},{9,17... | collective-permute-start | bytes 368648 | tf_op jit(solution)/shard_map/ppermute | solution.py:670
  21.9 16.3 %collective-permute-start.37 = (bf16[48,1280]{1,0:T(8,128)(2,1)S(1)}, bf16[48,1280]{1,0:T(8,128)(2,1)S(1)}, u32[]{:S(2)}, u32[]{:S(2)}) collective-permute-start(bf16[48,1280]{1,0:T(8,128)(2,1)S(1)} %collective-permute-done.36), channel_id=1, source_target_pairs={{0,8},{1,9},{2,10},{3,11},{4,12},{5,13},{6,14},{7,15},{8,16},{9,17... | collective-permute-start | bytes 368648 | tf_op jit(solution)/shard_map/ppermute | solution.py:670
  25.1 16.3 %collective-permute-start.9 = (bf16[48,1536]{1,0:T(8,128)(2,1)S(1)}, bf16[48,1536]{1,0:T(8,128)(2,1)S(1)}, u32[]{:S(2)}, u32[]{:S(2)}) collective-permute-start(bf16[48,1536]{1,0:T(8,128)(2,1)S(1)} %collective-permute-done.8), channel_id=1, source_target_pairs={{0,8},{1,9},{2,10},{3,11},{4,12},{5,13},{6,14},{7,15},{8,16},{9,17... | collective-permute-start | bytes 442376 | tf_op jit(solution)/shard_map/ppermute | solution.py:670
  29.0 15.5 %collective-permute-start.23 = (bf16[48,1536]{1,0:T(8,128)(2,1)S(1)}, bf16[48,1536]{1,0:T(8,128)(2,1)S(1)}, u32[]{:S(2)}, u32[]{:S(2)}) collective-permute-start(bf16[48,1536]{1,0:T(8,128)(2,1)S(1)} %collective-permute-done.22), channel_id=1, source_target_pairs={{0,8},{1,9},{2,10},{3,11},{4,12},{5,13},{6,14},{7,15},{8,16},{9,17... | collective-permute-start | bytes 442376 | tf_op jit(solution)/shard_map/ppermute | solution.py:670
  33.0 27.1 %collective-permute-start.2 = (bf16[48,1920]{1,0:T(8,128)(2,1)S(1)}, bf16[48,1920]{1,0:T(8,128)(2,1)S(1)}, u32[]{:S(2)}, u32[]{:S(2)}) collective-permute-start(bf16[48,1920]{1,0:T(8,128)(2,1)S(1)} %collective-permute-done.1), channel_id=1, source_target_pairs={{0,8},{1,9},{2,10},{3,11},{4,12},{5,13},{6,14},{7,15},{8,16},{9,17... | collective-permute-start | bytes 552968 | tf_op jit(solution)/shard_map/ppermute | solution.py:670
  35.6 25.0 %collective-permute-start.16 = (bf16[48,1920]{1,0:T(8,128)(2,1)S(1)}, bf16[48,1920]{1,0:T(8,128)(2,1)S(1)}, u32[]{:S(2)}, u32[]{:S(2)}) collective-permute-start(bf16[48,1920]{1,0:T(8,128)(2,1)S(1)} %collective-permute-done.15), channel_id=1, source_target_pairs={{0,8},{1,9},{2,10},{3,11},{4,12},{5,13},{6,14},{7,15},{8,16},{9,17... | collective-permute-start | bytes 552968 | tf_op jit(solution)/shard_map/ppermute | solution.py:670
  38.3 16.9 %collective-permute-start.31 = (bf16[48,1280]{1,0:T(8,128)(2,1)S(1)}, bf16[48,1280]{1,0:T(8,128)(2,1)S(1)}, u32[]{:S(2)}, u32[]{:S(2)}) collective-permute-start(bf16[48,1280]{1,0:T(8,128)(2,1)S(1)} %collective-permute-done.30), channel_id=1, source_target_pairs={{0,8},{1,9},{2,10},{3,11},{4,12},{5,13},{6,14},{7,15},{8,16},{9,17... | collective-permute-start | bytes 368648 | tf_op jit(solution)/shard_map/ppermute | solution.py:670
  41.4 16.3 %collective-permute-start.38 = (bf16[48,1280]{1,0:T(8,128)(2,1)S(1)}, bf16[48,1280]{1,0:T(8,128)(2,1)S(1)}, u32[]{:S(2)}, u32[]{:S(2)}) collective-permute-start(bf16[48,1280]{1,0:T(8,128)(2,1)S(1)} %collective-permute-done.37), channel_id=1, source_target_pairs={{0,8},{1,9},{2,10},{3,11},{4,12},{5,13},{6,14},{7,15},{8,16},{9,17... | collective-permute-start | bytes 368648 | tf_op jit(solution)/shard_map/ppermute | solution.py:670
  44.6 19.3 %collective-permute-start.10 = (bf16[48,1536]{1,0:T(8,128)(2,1)S(1)}, bf16[48,1536]{1,0:T(8,128)(2,1)S(1)}, u32[]{:S(2)}, u32[]{:S(2)}) collective-permute-start(bf16[48,1536]{1,0:T(8,128)(2,1)S(1)} %collective-permute-done.9), channel_id=1, source_target_pairs={{0,8},{1,9},{2,10},{3,11},{4,12},{5,13},{6,14},{7,15},{8,16},{9,17... | collective-permute-start | bytes 442376 | tf_op jit(solution)/shard_map/ppermute | solution.py:670
  55.1 8.4 %collective-permute-start.24 = (bf16[48,1536]{1,0:T(8,128)(2,1)S(1)}, bf16[48,1536]{1,0:T(8,128)(2,1)S(1)}, u32[]{:S(2)}, u32[]{:S(2)}) collective-permute-start(bf16[48,1536]{1,0:T(8,128)(2,1)S(1)} %collective-permute-done.23), channel_id=1, source_target_pairs={{0,8},{1,9},{2,10},{3,11},{4,12},{5,13},{6,14},{7,15},{8,16},{9,17... | collective-permute-start | bytes 442376 | tf_op jit(solution)/shard_map/ppermute | solution.py:670
  57.7 31.0 %collective-permute-start.32 = (bf16[192,1280]{1,0:T(8,128)(2,1)S(1)}, bf16[192,1280]{1,0:T(8,128)(2,1)S(1)}, u32[]{:S(2)}, u32[]{:S(2)}) collective-permute-start(bf16[192,1280]{1,0:T(8,128)(2,1)S(1)} %pad_maximum_fusion.10), channel_id=1, source_target_pairs={{0,4},{1,3},{2,6},{3,1},{4,0},{5,7},{6,2},{7,5},{8,12},{9,11},{10,... | collective-permute-start | bytes 1474568 | tf_op jit(solution)/shard_map/ppermute | solution.py:670
  60.1 42.1 %collective-permute-start.39 = (bf16[192,1280]{1,0:T(8,128)(2,1)S(1)}, bf16[192,1280]{1,0:T(8,128)(2,1)S(1)}, u32[]{:S(2)}, u32[]{:S(2)}) collective-permute-start(bf16[192,1280]{1,0:T(8,128)(2,1)S(1)} %pad_maximum_fusion.11), channel_id=1, source_target_pairs={{0,4},{1,3},{2,6},{3,1},{4,0},{5,7},{6,2},{7,5},{8,12},{9,11},{10,... | collective-permute-start | bytes 1474568 | tf_op jit(solution)/shard_map/ppermute | solution.py:670
  60.6 14.5 %collective-permute-start.3 = (bf16[48,1920]{1,0:T(8,128)(2,1)S(1)}, bf16[48,1920]{1,0:T(8,128)(2,1)S(1)}, u32[]{:S(2)}, u32[]{:S(2)}) collective-permute-start(bf16[48,1920]{1,0:T(8,128)(2,1)S(1)} %collective-permute-done.2), channel_id=1, source_target_pairs={{0,8},{1,9},{2,10},{3,11},{4,12},{5,13},{6,14},{7,15},{8,16},{9,17... | collective-permute-start | bytes 552968 | tf_op jit(solution)/shard_map/ppermute | solution.py:670
  63.5 8.4 %collective-permute-start.17 = (bf16[48,1920]{1,0:T(8,128)(2,1)S(1)}, bf16[48,1920]{1,0:T(8,128)(2,1)S(1)}, u32[]{:S(2)}, u32[]{:S(2)}) collective-permute-start(bf16[48,1920]{1,0:T(8,128)(2,1)S(1)} %collective-permute-done.16), channel_id=1, source_target_pairs={{0,8},{1,9},{2,10},{3,11},{4,12},{5,13},{6,14},{7,15},{8,16},{9,17... | collective-permute-start | bytes 552968 | tf_op jit(solution)/shard_map/ppermute | solution.py:670
  63.9 25.3 %collective-permute-start.25 = (bf16[192,1536]{1,0:T(8,128)(2,1)S(1)}, bf16[192,1536]{1,0:T(8,128)(2,1)S(1)}, u32[]{:S(2)}, u32[]{:S(2)}) collective-permute-start(bf16[192,1536]{1,0:T(8,128)(2,1)S(1)} %pad_maximum_fusion.7), channel_id=1, source_target_pairs={{0,4},{1,3},{2,6},{3,1},{4,0},{5,7},{6,2},{7,5},{8,12},{9,11},{10,... | collective-permute-start | bytes 1769480 | tf_op jit(solution)/shard_map/ppermute | solution.py:670
  72.0 14.0 %collective-permute-start.18 = (bf16[192,1920]{1,0:T(8,128)(2,1)S(1)}, bf16[192,1920]{1,0:T(8,128)(2,1)S(1)}, u32[]{:S(2)}, u32[]{:S(2)}) collective-permute-start(bf16[192,1920]{1,0:T(8,128)(2,1)S(1)} %pad_maximum_fusion.5), channel_id=1, source_target_pairs={{0,4},{1,3},{2,6},{3,1},{4,0},{5,7},{6,2},{7,5},{8,12},{9,11},{10,... | collective-permute-start | bytes 2211848 | tf_op jit(solution)/shard_map/ppermute | solution.py:670
  75.2 24.9 %collective-permute-start.4 = (bf16[192,1920]{1,0:T(8,128)(2,1)S(1)}, bf16[192,1920]{1,0:T(8,128)(2,1)S(1)}, u32[]{:S(2)}, u32[]{:S(2)}) collective-permute-start(bf16[192,1920]{1,0:T(8,128)(2,1)S(1)} %pad_maximum_fusion.4), channel_id=1, source_target_pairs={{0,4},{1,3},{2,6},{3,1},{4,0},{5,7},{6,2},{7,5},{8,12},{9,11},{10,... | collective-permute-start | bytes 2211848 | tf_op jit(solution)/shard_map/ppermute | solution.py:670
  87.0 39.1 %collective-permute-start.19 = (bf16[384,1920]{1,0:T(8,128)(2,1)S(1)}, bf16[384,1920]{1,0:T(8,128)(2,1)S(1)}, u32[]{:S(2)}, u32[]{:S(2)}) collective-permute-start(bf16[384,1920]{1,0:T(8,128)(2,1)S(1)} %get-tuple-element.170), channel_id=1, source_target_pairs={{0,2},{1,5},{2,0},{3,7},{4,6},{5,1},{6,4},{7,3},{8,10},{9,13},{10,... | collective-permute-start | bytes 4423688 | tf_op jit(solution)/shard_map/ppermute | solution.py:670
  88.8 35.9 %collective-permute-start.33 = (bf16[384,1280]{1,0:T(8,128)(2,1)S(1)}, bf16[384,1280]{1,0:T(8,128)(2,1)S(1)}, u32[]{:S(2)}, u32[]{:S(2)}) collective-permute-start(bf16[384,1280]{1,0:T(8,128)(2,1)S(1)} %get-tuple-element.180), channel_id=1, source_target_pairs={{0,2},{1,5},{2,0},{3,7},{4,6},{5,1},{6,4},{7,3},{8,10},{9,13},{10,... | collective-permute-start | bytes 2949128 | tf_op jit(solution)/shard_map/ppermute | solution.py:670
  89.2 40.3 %collective-permute-start.11 = (bf16[192,1536]{1,0:T(8,128)(2,1)S(1)}, bf16[192,1536]{1,0:T(8,128)(2,1)S(1)}, u32[]{:S(2)}, u32[]{:S(2)}) collective-permute-start(bf16[192,1536]{1,0:T(8,128)(2,1)S(1)} %pad_maximum_fusion.6), channel_id=1, source_target_pairs={{0,4},{1,3},{2,6},{3,1},{4,0},{5,7},{6,2},{7,5},{8,12},{9,11},{10,... | collective-permute-start | bytes 1769480 | tf_op jit(solution)/shard_map/ppermute | solution.py:670
  100.1 37.2 %collective-permute-start.26 = (bf16[384,1536]{1,0:T(8,128)(2,1)S(1)}, bf16[384,1536]{1,0:T(8,128)(2,1)S(1)}, u32[]{:S(2)}, u32[]{:S(2)}) collective-permute-start(bf16[384,1536]{1,0:T(8,128)(2,1)S(1)} %get-tuple-element.174), channel_id=1, source_target_pairs={{0,2},{1,5},{2,0},{3,7},{4,6},{5,1},{6,4},{7,3},{8,10},{9,13},{10,... | collective-permute-start | bytes 3538952 | tf_op jit(solution)/shard_map/ppermute | solution.py:670
  102.3 50.8 %collective-permute-start.5 = (bf16[384,1920]{1,0:T(8,128)(2,1)S(1)}, bf16[384,1920]{1,0:T(8,128)(2,1)S(1)}, u32[]{:S(2)}, u32[]{:S(2)}) collective-permute-start(bf16[384,1920]{1,0:T(8,128)(2,1)S(1)} %get-tuple-element.172), channel_id=1, source_target_pairs={{0,2},{1,5},{2,0},{3,7},{4,6},{5,1},{6,4},{7,3},{8,10},{9,13},{10,... | collective-permute-start | bytes 4423688 | tf_op jit(solution)/shard_map/ppermute | solution.py:670
  124.7 39.0 %collective-permute-start.40 = (bf16[384,1280]{1,0:T(8,128)(2,1)S(1)}, bf16[384,1280]{1,0:T(8,128)(2,1)S(1)}, u32[]{:S(2)}, u32[]{:S(2)}) collective-permute-start(bf16[384,1280]{1,0:T(8,128)(2,1)S(1)} %get-tuple-element.178), channel_id=1, source_target_pairs={{0,2},{1,5},{2,0},{3,7},{4,6},{5,1},{6,4},{7,3},{8,10},{9,13},{10,... | collective-permute-start | bytes 2949128 | tf_op jit(solution)/shard_map/ppermute | solution.py:670
  126.1 53.1 %collective-permute-start.34 = (bf16[768,1280]{1,0:T(8,128)(2,1)S(1)}, bf16[768,1280]{1,0:T(8,128)(2,1)S(1)}, u32[]{:S(2)}, u32[]{:S(2)}) collective-permute-start(bf16[768,1280]{1,0:T(8,128)(2,1)S(1)} %constant_dynamic-update-slice_fusion.49.own_ref), channel_id=1, source_target_pairs={{0,1},{1,0},{2,3},{3,2},{4,5},{5,4},{6,7},{7,6},{8,9},{9,8},{10,11... | collective-permute-start | bytes 5898248 | tf_op jit(solution)/shard_map/ppermute | solution.py:670
  129.6 74.5 %collective-permute-start.20 = (bf16[768,1920]{1,0:T(8,128)(2,1)}, bf16[768,1920]{1,0:T(8,128)(2,1)}, u32[]{:S(2)}, u32[]{:S(2)}) collective-permute-start(bf16[768,1920]{1,0:T(8,128)(2,1)} %constant_dynamic-update-slice_fusion.27.own_ref.uo_ref.oo_ref), channel_id=1, source_target_pairs={{0,1},{1,0},{2,3},{3,2},{4,5},{5,4},{6,7},{7,6},{8,9},{9,8},{10,11... | collective-permute-start | bytes 8847368 | tf_op jit(solution)/shard_map/ppermute | solution.py:670
  137.3 39.0 %collective-permute-start.12 = (bf16[384,1536]{1,0:T(8,128)(2,1)S(1)}, bf16[384,1536]{1,0:T(8,128)(2,1)S(1)}, u32[]{:S(2)}, u32[]{:S(2)}) collective-permute-start(bf16[384,1536]{1,0:T(8,128)(2,1)S(1)} %get-tuple-element.176), channel_id=1, source_target_pairs={{0,2},{1,5},{2,0},{3,7},{4,6},{5,1},{6,4},{7,3},{8,10},{9,13},{10,... | collective-permute-start | bytes 3538952 | tf_op jit(solution)/shard_map/ppermute | solution.py:670
  153.1 56.3 %collective-permute-start.27 = (bf16[768,1536]{1,0:T(8,128)(2,1)}, bf16[768,1536]{1,0:T(8,128)(2,1)}, u32[]{:S(2)}, u32[]{:S(2)}) collective-permute-start(bf16[768,1536]{1,0:T(8,128)(2,1)} %constant_dynamic-update-slice_fusion.38.do_ref.own_ref), channel_id=1, source_target_pairs={{0,1},{1,0},{2,3},{3,2},{4,5},{5,4},{6,7},{7,6},{8,9},{9,8},{10,11... | collective-permute-start | bytes 7077896 | tf_op jit(solution)/shard_map/ppermute | solution.py:670
  163.6 79.5 %collective-permute-start.6 = (bf16[768,1920]{1,0:T(8,128)(2,1)S(1)}, bf16[768,1920]{1,0:T(8,128)(2,1)}, u32[]{:S(2)}, u32[]{:S(2)}) collective-permute-start(bf16[768,1920]{1,0:T(8,128)(2,1)S(1)} %constant_dynamic-update-slice_fusion.5.own_ref.uo_ref.oo_ref), channel_id=1, source_target_pairs={{0,1},{1,0},{2,3},{3,2},{4,5},{5,4},{6,7},{7,6},{8,9},{9,8},{10,11... | collective-permute-start | bytes 8847368 | tf_op jit(solution)/shard_map/ppermute | solution.py:670
  176.3 50.0 %collective-permute-start.41 = (bf16[768,1280]{1,0:T(8,128)(2,1)}, bf16[768,1280]{1,0:T(8,128)(2,1)}, u32[]{:S(2)}, u32[]{:S(2)}) collective-permute-start(bf16[768,1280]{1,0:T(8,128)(2,1)} %constant_dynamic-update-slice_fusion.60.own_ref), channel_id=1, source_target_pairs={{0,1},{1,0},{2,3},{3,2},{4,5},{5,4},{6,7},{7,6},{8,9},{9,8},{10,11... | collective-permute-start | bytes 5898248 | tf_op jit(solution)/shard_map/ppermute | solution.py:670
  180.4 68.1 %collective-permute-start.13 = (bf16[768,1536]{1,0:T(8,128)(2,1)}, bf16[768,1536]{1,0:T(8,128)(2,1)}, u32[]{:S(2)}, u32[]{:S(2)}) collective-permute-start(bf16[768,1536]{1,0:T(8,128)(2,1)} %constant_dynamic-update-slice_fusion.16.do_ref.own_ref), channel_id=1, source_target_pairs={{0,1},{1,0},{2,3},{3,2},{4,5},{5,4},{6,7},{7,6},{8,9},{9,8},{10,11... | collective-permute-start | bytes 7077896 | tf_op jit(solution)/shard_map/ppermute | solution.py:670
  326.8 63.6 %collective-permute-start.51 = (bf16[768,128]{1,0:T(8,128)(2,1)}, bf16[768,128]{1,0:T(8,128)(2,1)S(1)}, u32[]{:S(2)}, u32[]{:S(2)}) collective-permute-start(bf16[768,128]{1,0:T(8,128)(2,1)} %get-tuple-element.112), channel_id=1, source_target_pairs={{0,1},{1,0},{2,3},{3,2},{4,5},{5,4},{6,7},{7,6},{8,9},{9,8},{10,11... | collective-permute-start | bytes 589832 | tf_op jit(solution)/shard_map/ppermute | solution.py:670
  390.5 7.9 %collective-permute-start.42 = (bf16[768,1152]{1,0:T(8,128)(2,1)}, bf16[768,1152]{1,0:T(8,128)(2,1)S(1)}, u32[]{:S(2)}, u32[]{:S(2)}) collective-permute-start(bf16[768,1152]{1,0:T(8,128)(2,1)} %get-tuple-element.98), channel_id=1, source_target_pairs={{0,1},{1,0},{2,3},{3,2},{4,5},{5,4},{6,7},{7,6},{8,9},{9,8},{10,11... | collective-permute-start | bytes 5308424 | tf_op jit(solution)/shard_map/ppermute | solution.py:670
  391.1 10.1 %collective-permute-start.59 = (bf16[768,1536]{1,0:T(8,128)(2,1)}, bf16[768,1536]{1,0:T(8,128)(2,1)S(1)}, u32[]{:S(2)}, u32[]{:S(2)}) collective-permute-start(bf16[768,1536]{1,0:T(8,128)(2,1)} %get-tuple-element.116), channel_id=1, source_target_pairs={{0,1},{1,0},{2,3},{3,2},{4,5},{5,4},{6,7},{7,6},{8,9},{9,8},{10,11... | collective-permute-start | bytes 7077896 | tf_op jit(solution)/shard_map/ppermute | solution.py:670
  393.8 14.2 %collective-permute-start.74 = (bf16[768,1536]{1,0:T(8,128)(2,1)}, bf16[768,1536]{1,0:T(8,128)(2,1)S(1)}, u32[]{:S(2)}, u32[]{:S(2)}) collective-permute-start(bf16[768,1536]{1,0:T(8,128)(2,1)} %get-tuple-element.122), channel_id=1, source_target_pairs={{0,1},{1,0},{2,3},{3,2},{4,5},{5,4},{6,7},{7,6},{8,9},{9,8},{10,11... | collective-permute-start | bytes 7077896 | tf_op jit(solution)/shard_map/ppermute | solution.py:670
  395.7 15.6 %collective-permute-start.67 = (bf16[768,1536]{1,0:T(8,128)(2,1)}, bf16[768,1536]{1,0:T(8,128)(2,1)S(1)}, u32[]{:S(2)}, u32[]{:S(2)}) collective-permute-start(bf16[768,1536]{1,0:T(8,128)(2,1)} %get-tuple-element.120), channel_id=1, source_target_pairs={{0,1},{1,0},{2,3},{3,2},{4,5},{5,4},{6,7},{7,6},{8,9},{9,8},{10,11... | collective-permute-start | bytes 7077896 | tf_op jit(solution)/shard_map/ppermute | solution.py:670
  397.5 17.2 %collective-permute-start.81 = (bf16[768,1536]{1,0:T(8,128)(2,1)S(1)}, bf16[768,1536]{1,0:T(8,128)(2,1)S(1)}, u32[]{:S(2)}, u32[]{:S(2)}) collective-permute-start(bf16[768,1536]{1,0:T(8,128)(2,1)S(1)} %copy-done.35), channel_id=1, source_target_pairs={{0,1},{1,0},{2,3},{3,2},{4,5},{5,4},{6,7},{7,6},{8,9},{9,8},{10,11... | collective-permute-start | bytes 7077896 | tf_op jit(solution)/shard_map/ppermute | solution.py:670
  398.4 20.1 %collective-permute-start.52 = (bf16[384,1280]{1,0:T(8,128)(2,1)S(1)}, bf16[384,1280]{1,0:T(8,128)(2,1)S(1)}, u32[]{:S(2)}, u32[]{:S(2)}) collective-permute-start(bf16[384,1280]{1,0:T(8,128)(2,1)S(1)} %pad_maximum_fusion.3), channel_id=1, source_target_pairs={{0,2},{1,5},{2,0},{3,7},{4,6},{5,1},{6,4},{7,3},{8,10},{9,13},{10,... | collective-permute-start | bytes 2949128 | tf_op jit(solution)/shard_map/ppermute | solution.py:670
  401.2 23.7 %collective-permute-start.44 = (bf16[384,1280]{1,0:T(8,128)(2,1)S(1)}, bf16[384,1280]{1,0:T(8,128)(2,1)S(1)}, u32[]{:S(2)}, u32[]{:S(2)}) collective-permute-start(bf16[384,1280]{1,0:T(8,128)(2,1)S(1)} %pad_maximum_fusion.2), channel_id=1, source_target_pairs={{0,2},{1,5},{2,0},{3,7},{4,6},{5,1},{6,4},{7,3},{8,10},{9,13},{10,... | collective-permute-start | bytes 2949128 | tf_op jit(solution)/shard_map/ppermute | solution.py:670
  408.0 100.4 %collective-permute-start.60 = (bf16[384,1920]{1,0:T(8,128)(2,1)}, bf16[384,1920]{1,0:T(8,128)(2,1)}, u32[]{:S(2)}, u32[]{:S(2)}) collective-permute-start(bf16[384,1920]{1,0:T(8,128)(2,1)} %pad_maximum_fusion), channel_id=1, source_target_pairs={{0,2},{1,5},{2,0},{3,7},{4,6},{5,1},{6,4},{7,3},{8,10},{9,13},{10,... | collective-permute-start | bytes 4423688 | tf_op jit(solution)/shard_map/ppermute | solution.py:670
  411.3 59.9 %collective-permute-start.75 = (bf16[384,1536]{1,0:T(8,128)(2,1)S(1)}, bf16[384,1536]{1,0:T(8,128)(2,1)S(1)}, u32[]{:S(2)}, u32[]{:S(2)}) collective-permute-start(bf16[384,1536]{1,0:T(8,128)(2,1)S(1)} %add_convert_fusion.1), channel_id=1, source_target_pairs={{0,2},{1,5},{2,0},{3,7},{4,6},{5,1},{6,4},{7,3},{8,10},{9,13},{10,... | collective-permute-start | bytes 3538952 | tf_op jit(solution)/shard_map/ppermute | solution.py:670
  414.8 96.6 %collective-permute-start.68 = (bf16[384,1920]{1,0:T(8,128)(2,1)}, bf16[384,1920]{1,0:T(8,128)(2,1)}, u32[]{:S(2)}, u32[]{:S(2)}) collective-permute-start(bf16[384,1920]{1,0:T(8,128)(2,1)} %pad_maximum_fusion.1), channel_id=1, source_target_pairs={{0,2},{1,5},{2,0},{3,7},{4,6},{5,1},{6,4},{7,3},{8,10},{9,13},{10,... | collective-permute-start | bytes 4423688 | tf_op jit(solution)/shard_map/ppermute | solution.py:670
  418.6 14.2 %collective-permute-start.53 = (bf16[192,1280]{1,0:T(8,128)(2,1)S(1)}, bf16[192,1280]{1,0:T(8,128)(2,1)S(1)}, u32[]{:S(2)}, u32[]{:S(2)}) collective-permute-start(bf16[192,1280]{1,0:T(8,128)(2,1)S(1)} %fusion.3), channel_id=1, source_target_pairs={{0,4},{1,3},{2,6},{3,1},{4,0},{5,7},{6,2},{7,5},{8,12},{9,11},{10,... | collective-permute-start | bytes 1474568 | tf_op jit(solution)/shard_map/ppermute | solution.py:670
  425.0 18.4 %collective-permute-start.45 = (bf16[192,1280]{1,0:T(8,128)(2,1)S(1)}, bf16[192,1280]{1,0:T(8,128)(2,1)S(1)}, u32[]{:S(2)}, u32[]{:S(2)}) collective-permute-start(bf16[192,1280]{1,0:T(8,128)(2,1)S(1)} %fusion.2), channel_id=1, source_target_pairs={{0,4},{1,3},{2,6},{3,1},{4,0},{5,7},{6,2},{7,5},{8,12},{9,11},{10,... | collective-permute-start | bytes 1474568 | tf_op jit(solution)/shard_map/ppermute | solution.py:670
  432.8 57.6 %collective-permute-start.82 = (bf16[384,1536]{1,0:T(8,128)(2,1)S(1)}, bf16[384,1536]{1,0:T(8,128)(2,1)S(1)}, u32[]{:S(2)}, u32[]{:S(2)}) collective-permute-start(bf16[384,1536]{1,0:T(8,128)(2,1)S(1)} %add_convert_fusion), channel_id=1, source_target_pairs={{0,2},{1,5},{2,0},{3,7},{4,6},{5,1},{6,4},{7,3},{8,10},{9,13},{10,... | collective-permute-start | bytes 3538952 | tf_op jit(solution)/shard_map/ppermute | solution.py:670
  471.1 22.1 %collective-permute-start.56 = (bf16[48,1280]{1,0:T(8,128)(2,1)S(1)}, bf16[48,1280]{1,0:T(8,128)(2,1)S(1)}, u32[]{:S(2)}, u32[]{:S(2)}) collective-permute-start(bf16[48,1280]{1,0:T(8,128)(2,1)S(1)} %fusion.40), channel_id=1, source_target_pairs={{0,8},{1,9},{2,10},{3,11},{4,12},{5,13},{6,14},{7,15},{8,16},{9,17... | collective-permute-start | bytes 368648 | tf_op jit(solution)/shard_map/ppermute | solution.py:670
  471.2 22.5 %collective-permute-start.48 = (bf16[48,1280]{1,0:T(8,128)(2,1)S(1)}, bf16[48,1280]{1,0:T(8,128)(2,1)S(1)}, u32[]{:S(2)}, u32[]{:S(2)}) collective-permute-start(bf16[48,1280]{1,0:T(8,128)(2,1)S(1)} %fusion.30), channel_id=1, source_target_pairs={{0,8},{1,9},{2,10},{3,11},{4,12},{5,13},{6,14},{7,15},{8,16},{9,17... | collective-permute-start | bytes 368648 | tf_op jit(solution)/shard_map/ppermute | solution.py:670
  490.5 22.8 %collective-permute-start.76 = (bf16[192,1536]{1,0:T(8,128)(2,1)}, bf16[192,1536]{1,0:T(8,128)(2,1)}, u32[]{:S(2)}, u32[]{:S(2)}) collective-permute-start(bf16[192,1536]{1,0:T(8,128)(2,1)} %add_convert_fusion.7), channel_id=1, source_target_pairs={{0,4},{1,3},{2,6},{3,1},{4,0},{5,7},{6,2},{7,5},{8,12},{9,11},{10,... | collective-permute-start | bytes 1769480 | tf_op jit(solution)/shard_map/ppermute | solution.py:670
  493.2 21.2 %collective-permute-start.83 = (bf16[192,1536]{1,0:T(8,128)(2,1)}, bf16[192,1536]{1,0:T(8,128)(2,1)}, u32[]{:S(2)}, u32[]{:S(2)}) collective-permute-start(bf16[192,1536]{1,0:T(8,128)(2,1)} %add_convert_fusion.6), channel_id=1, source_target_pairs={{0,4},{1,3},{2,6},{3,1},{4,0},{5,7},{6,2},{7,5},{8,12},{9,11},{10,... | collective-permute-start | bytes 1769480 | tf_op jit(solution)/shard_map/ppermute | solution.py:670
  509.6 34.2 %collective-permute-start.61 = (bf16[192,1920]{1,0:T(8,128)(2,1)S(1)}, bf16[192,1920]{1,0:T(8,128)(2,1)S(1)}, u32[]{:S(2)}, u32[]{:S(2)}) collective-permute-start(bf16[192,1920]{1,0:T(8,128)(2,1)S(1)} %fusion), channel_id=1, source_target_pairs={{0,4},{1,3},{2,6},{3,1},{4,0},{5,7},{6,2},{7,5},{8,12},{9,11},{10,... | collective-permute-start | bytes 2211848 | tf_op jit(solution)/shard_map/ppermute | solution.py:670
  512.6 32.3 %collective-permute-start.69 = (bf16[192,1920]{1,0:T(8,128)(2,1)S(1)}, bf16[192,1920]{1,0:T(8,128)(2,1)S(1)}, u32[]{:S(2)}, u32[]{:S(2)}) collective-permute-start(bf16[192,1920]{1,0:T(8,128)(2,1)S(1)} %fusion.1), channel_id=1, source_target_pairs={{0,4},{1,3},{2,6},{3,1},{4,0},{5,7},{6,2},{7,5},{8,12},{9,11},{10,... | collective-permute-start | bytes 2211848 | tf_op jit(solution)/shard_map/ppermute | solution.py:670
  514.4 8.6 %collective-permute-start.77 = (bf16[48,1536]{1,0:T(8,128)(2,1)S(1)}, bf16[48,1536]{1,0:T(8,128)(2,1)S(1)}, u32[]{:S(2)}, u32[]{:S(2)}) collective-permute-start(bf16[48,1536]{1,0:T(8,128)(2,1)S(1)} %add_convert_fusion.15), channel_id=1, source_target_pairs={{0,8},{1,9},{2,10},{3,11},{4,12},{5,13},{6,14},{7,15},{8,16},{9,17... | collective-permute-start | bytes 442376 | tf_op jit(solution)/shard_map/ppermute | solution.py:670
  515.6 8.9 %collective-permute-start.84 = (bf16[48,1536]{1,0:T(8,128)(2,1)S(1)}, bf16[48,1536]{1,0:T(8,128)(2,1)S(1)}, u32[]{:S(2)}, u32[]{:S(2)}) collective-permute-start(bf16[48,1536]{1,0:T(8,128)(2,1)S(1)} %add_convert_fusion.12), channel_id=1, source_target_pairs={{0,8},{1,9},{2,10},{3,11},{4,12},{5,13},{6,14},{7,15},{8,16},{9,17... | collective-permute-start | bytes 442376 | tf_op jit(solution)/shard_map/ppermute | solution.py:670
  525.7 8.7 %collective-permute-start.85 = (bf16[48,1536]{1,0:T(8,128)(2,1)S(1)}, bf16[48,1536]{1,0:T(8,128)(2,1)S(1)}, u32[]{:S(2)}, u32[]{:S(2)}) collective-permute-start(bf16[48,1536]{1,0:T(8,128)(2,1)S(1)} %add_convert_fusion.11), channel_id=1, source_target_pairs={{0,8},{1,9},{2,10},{3,11},{4,12},{5,13},{6,14},{7,15},{8,16},{9,17... | collective-permute-start | bytes 442376 | tf_op jit(solution)/shard_map/ppermute | solution.py:670
  544.8 9.3 %collective-permute-start.62 = (bf16[48,1920]{1,0:T(8,128)(2,1)S(1)}, bf16[48,1920]{1,0:T(8,128)(2,1)S(1)}, u32[]{:S(2)}, u32[]{:S(2)}) collective-permute-start(bf16[48,1920]{1,0:T(8,128)(2,1)S(1)} %fusion.13), channel_id=1, source_target_pairs={{0,8},{1,9},{2,10},{3,11},{4,12},{5,13},{6,14},{7,15},{8,16},{9,17... | collective-permute-start | bytes 552968 | tf_op jit(solution)/shard_map/ppermute | solution.py:670
  546.0 11.7 %collective-permute-start.70 = (bf16[48,1920]{1,0:T(8,128)(2,1)S(1)}, bf16[48,1920]{1,0:T(8,128)(2,1)S(1)}, u32[]{:S(2)}, u32[]{:S(2)}) collective-permute-start(bf16[48,1920]{1,0:T(8,128)(2,1)S(1)} %fusion.23), channel_id=1, source_target_pairs={{0,8},{1,9},{2,10},{3,11},{4,12},{5,13},{6,14},{7,15},{8,16},{9,17... | collective-permute-start | bytes 552968 | tf_op jit(solution)/shard_map/ppermute | solution.py:670
  558.7 8.1 %collective-permute-start.71 = (bf16[48,1920]{1,0:T(8,128)(2,1)S(1)}, bf16[48,1920]{1,0:T(8,128)(2,1)S(1)}, u32[]{:S(2)}, u32[]{:S(2)}) collective-permute-start(bf16[48,1920]{1,0:T(8,128)(2,1)S(1)} %fusion.21), channel_id=1, source_target_pairs={{0,8},{1,9},{2,10},{3,11},{4,12},{5,13},{6,14},{7,15},{8,16},{9,17... | collective-permute-start | bytes 552968 | tf_op jit(solution)/shard_map/ppermute | solution.py:670
  (62 other events, 585.4 us)

commit v3 on v2

--- a/solution.py
+++ b/solution.py
@@ -128,9 +128,9 @@
     )(spot, own, other, h, table)
 
 
-def attention_forward(lengths, qkv):
+def attention_forward(lengths, qkv, begin, pairs):
     rows, wide = qkv.shape
-    width = wide // 3
+    width = pairs * LANES
 
     def body(len_ref, q_ref, k_ref, v_ref, o_ref, lse_ref):
         pair = pl.program_id(0)
@@ -163,11 +163,11 @@
         ],
         grid_spec=pltpu.PrefetchScalarGridSpec(
             num_scalar_prefetch=1,
-            grid=(PAIRS,),
+            grid=(pairs,),
             in_specs=[
-                pl.BlockSpec((rows, LANES), lambda p, n: (0, p)),
-                pl.BlockSpec((rows, LANES), lambda p, n: (0, p + PAIRS)),
-                pl.BlockSpec((rows, LANES), lambda p, n: (0, p + 2 * PAIRS)),
+                pl.BlockSpec((rows, LANES), lambda p, n: (0, p + begin)),
+                pl.BlockSpec((rows, LANES), lambda p, n: (0, p + begin + PAIRS)),
+                pl.BlockSpec((rows, LANES), lambda p, n: (0, p + begin + 2 * PAIRS)),
             ],
             out_specs=[
                 pl.BlockSpec((rows, LANES), lambda p, n: (0, p)),
@@ -175,21 +175,25 @@
             ],
         ),
         compiler_params=params(),
-        cost_estimate=cost(16 * rows * rows * width, 8 * rows * width, HEADS * rows * rows),
+        cost_estimate=cost(16 * rows * rows * width, 8 * rows * width, 2 * pairs * rows * rows),
         name="attention_forward",
     )(lengths, qkv, qkv, qkv)
 
 
 def out_forward(spot, own, other, column, h, mixed, table):
     rows, width = h.shape
-
-    def body(spot_ref, own_ref, other_ref, h_ref, m_ref, t_ref, h2_ref, a_ref, w_ref, sems):
+    part = width // 2
+
+    def body(
+        spot_ref, own_ref, other_ref, h_ref, m0_ref, m1_ref, t_ref, h2_ref, a_ref, w_ref, sems
+    ):
         copies = piece_copies(spot_ref, own_ref, other_ref, w_ref, sems, column, width // 2)
         for copy in copies:
             copy.start()
         for copy in copies:
             copy.wait()
-        h2 = h_ref[...] + (dot(m_ref[...], w_ref[...]) + t_ref[BO : BO + 1, :])
+        product = dot(m0_ref[...], w_ref[:part, :]) + dot(m1_ref[...], w_ref[part:, :])
+        h2 = h_ref[...] + (product + t_ref[BO : BO + 1, :])
         h2_ref[...] = h2
         xh, r = norm_rows(h2)
         a_ref[...] = (xh * t_ref[GAIN2 : GAIN2 + 1, :] + t_ref[SH2 : SH2 + 1, :]).astype(LOW)
@@ -200,13 +204,13 @@
             jax.ShapeDtypeStruct((rows, width), WIDE),
             jax.ShapeDtypeStruct((rows, width), LOW),
         ],
-        in_specs=[pl.BlockSpec(memory_space=pltpu.SMEM)] + any_specs(2) + vmem_specs(3),
+        in_specs=[pl.BlockSpec(memory_space=pltpu.SMEM)] + any_specs(2) + vmem_specs(4),
         out_specs=vmem_specs(2),
         scratch_shapes=[pltpu.VMEM((width, width), LOW), pltpu.SemaphoreType.DMA((32,))],
         compiler_params=params(),
         cost_estimate=cost(2 * rows * width * width, 2 * width * width + 12 * rows * width),
         name="out_forward",
-    )(spot, own, other, h, mixed, table)
+    )(spot, own, other, h, *mixed, table)
 
 
 def gelu_parts(u):
@@ -215,8 +219,8 @@
     return cdf, pdf
 
 
-def mlp_forward(spot, up, down, h2, a2, up_bias, table):
-    rows, width = h2.shape
+def mlp_forward(spot, up, down, base, a2, up_bias, table, first):
+    rows, width = base.shape
     hidden = up_bias.shape[1]
     tile = 512
     (up_own, up_other, up_col), (down_own, down_other, down_col) = up, down
@@ -229,7 +233,10 @@
         downs = piece_copies(spot_ref, do_ref, dp_ref, wd_ref, sems_d, down_col, hidden // 2)
         for copy in ups + downs:
             copy.start()
-        o_ref[...] = h_ref[...] + t_ref[BD : BD + 1, :]
+        if first:
+            o_ref[...] = h_ref[...] + t_ref[BD : BD + 1, :]
+        else:
+            o_ref[...] = h_ref[...]
         for copy in ups + downs:
             copy.wait()
 
@@ -265,7 +272,7 @@
             4 * rows * width * hidden, 4 * width * hidden + 4 * rows * hidden, 2 * rows * hidden
         ),
         name="mlp_forward",
-    )(spot, up_own, up_other, down_own, down_other, h2, a2, up_bias, table)
+    )(spot, up_own, up_other, down_own, down_other, base, a2, up_bias, table)
 
 
 def block_starts(spot, owner, rows):
@@ -297,7 +304,7 @@
     rows, width = e.shape
     hidden = z.shape[1]
     half = hidden // 2
-    tile = 512
+    tile = 384
     own, other, column = down
 
     def body(
@@ -352,41 +359,87 @@
     )(spot, own, other, e, z, slope)
 
 
-def up_backward(spot, up, out, e, h2, a2, mixed, du, table):
+def up_backward(spot, up, a2, du):
+    rows, width = a2.shape
+    hidden = du.shape[1]
+    half = hidden // 2
+    tile = 384
+    own, other, column = up
+
+    def body(
+        spot_ref, own_ref, other_ref, a_ref, du_ref, acc_ref, mine_ref, rest_ref, w_ref, at_ref, sems
+    ):
+        copies = piece_copies(spot_ref, own_ref, other_ref, w_ref, sems, column, half)
+        for copy in copies:
+            copy.start()
+        at_ref[...] = a_ref[...].T
+        acc_ref[...] = jnp.zeros_like(acc_ref)
+        for copy in copies:
+            copy.wait()
+        up_steps(spot_ref, w_ref, at_ref, du_ref, acc_ref, (mine_ref, rest_ref), half, tile)
+
+    return pl.pallas_call(
+        body,
+        out_shape=[
+            jax.ShapeDtypeStruct((rows, width), WIDE),
+            jax.ShapeDtypeStruct((width, half), LOW),
+            jax.ShapeDtypeStruct((width, half), LOW),
+        ],
+        in_specs=[pl.BlockSpec(memory_space=pltpu.SMEM)] + any_specs(2) + vmem_specs(2),
+        out_specs=vmem_specs(3),
+        scratch_shapes=[
+            pltpu.VMEM((width, hidden), LOW),
+            pltpu.VMEM((width, rows), LOW),
+            pltpu.SemaphoreType.DMA((32,)),
+        ],
+        compiler_params=params(),
+        cost_estimate=cost(4 * rows * width * hidden, 4 * width * hidden + 2 * rows * hidden),
+        name="up_backward",
+    )(spot, own, other, a2, du)
+
+
+def up_steps(spot_ref, w_ref, at_ref, d_ref, acc_ref, out_refs, half, tile):
+    c = spot_ref[3]
+    for owner, out_ref in zip((c, 1 - c), out_refs):
+        starts = block_starts(spot_ref, owner, at_ref.shape[0] // 16)
+
+        def step(n, carry):
+            at = pl.ds(pl.multiple_of(owner * half + n * tile, LANES), tile)
+            d = d_ref[:, at]
+            put_blocks(
+                dot(at_ref[...], d), out_ref, starts, pl.multiple_of(n * tile, LANES), tile
+            )
+            acc_ref[...] += dot_nt(d, w_ref[:, at])
+            return carry
+
+        lax.fori_loop(0, half // tile, step, 0)
+
+
+def middle_backward(spot, up, out, e, h2, a2, mixed, du, acc, table):
     rows, width = e.shape
     hidden = du.shape[1]
     half = hidden // 2
-    tile = 512
+    part = width // 2
+    tile = 384
     (up_own, up_other, up_col), (out_own, out_other, out_col) = up, out
 
     def body(
-        spot_ref, uo_ref, up_ref, oo_ref, op_ref, e_ref, h_ref, a_ref, m_ref, du_ref, t_ref,
+        spot_ref, uo_ref, up_ref, oo_ref, op_ref,
+        e_ref, h_ref, a_ref, m0_ref, m1_ref, du_ref, before_ref, t_ref,
         e2_ref, da_ref, mine_ref, rest_ref, omine_ref, orest_ref, sums_ref,
         wu_ref, wo_ref, at_ref, mt_ref, ey_ref, acc_ref, sems_u, sems_o,
     ):
         ups = piece_copies(spot_ref, uo_ref, up_ref, wu_ref, sems_u, up_col, half)
-        outs = piece_copies(spot_ref, oo_ref, op_ref, wo_ref, sems_o, out_col, width // 2)
+        outs = piece_copies(spot_ref, oo_ref, op_ref, wo_ref, sems_o, out_col, part)
         for copy in ups + outs:
             copy.start()
         at_ref[...] = a_ref[...].T
-        mt_ref[...] = m_ref[...].T
-        acc_ref[...] = jnp.zeros_like(acc_ref)
+        mt_ref[:part, :] = m0_ref[...].T
+        mt_ref[part:, :] = m1_ref[...].T
+        acc_ref[...] = before_ref[...]
         for copy in ups:
             copy.wait()
-        c = spot_ref[3]
-        for owner, out_ref in ((c, mine_ref), (1 - c, rest_ref)):
-            starts = block_starts(spot_ref, owner, width // 16)
-
-            def step(n, carry):
-                at = pl.ds(pl.multiple_of(owner * half + n * tile, LANES), tile)
-                d = du_ref[:, at]
-                put_blocks(
-                    dot(at_ref[...], d), out_ref, starts, pl.multiple_of(n * tile, LANES), tile
-                )
-                acc_ref[...] += dot_nt(d, wu_ref[:, at])
-                return carry
-
-            lax.fori_loop(0, half // tile, step, 0)
+        up_steps(spot_ref, wu_ref, at_ref, du_ref, acc_ref, (mine_ref, rest_ref), half, tile)
         dv, gain, shift = norm_back(h_ref[...], t_ref[GAIN2 : GAIN2 + 1, :], acc_ref[...])
         e2 = e_ref[...] + dv
         e2_ref[...] = e2
@@ -398,10 +451,11 @@
         for copy in outs:
             copy.wait()
         da_ref[...] = dot_nt(ey, wo_ref[...]).astype(LOW)
+        c = spot_ref[3]
         for owner, out_ref in ((c, omine_ref), (1 - c, orest_ref)):
             starts = block_starts(spot_ref, owner, width // 16)
-            at = pl.ds(pl.multiple_of(owner * (width // 2), LANES), width // 2)
-            put_blocks(dot(mt_ref[...], ey_ref[:, at]), out_ref, starts, 0, width // 2)
+            at = pl.ds(pl.multiple_of(owner * part, LANES), part)
+            put_blocks(dot(mt_ref[...], ey_ref[:, at]), out_ref, starts, 0, part)
 
     return pl.pallas_call(
         body,
@@ -410,11 +464,11 @@
             jax.ShapeDtypeStruct((rows, width), LOW),
             jax.ShapeDtypeStruct((width, half), LOW),
             jax.ShapeDtypeStruct((width, half), LOW),
-            jax.ShapeDtypeStruct((width, width // 2), LOW),
-            jax.ShapeDtypeStruct((width, width // 2), LOW),
+            jax.ShapeDtypeStruct((width, part), LOW),
+            jax.ShapeDtypeStruct((width, part), LOW),
             jax.ShapeDtypeStruct((8, width), WIDE),
         ],
-        in_specs=[pl.BlockSpec(memory_space=pltpu.SMEM)] + any_specs(4) + vmem_specs(6),
+        in_specs=[pl.BlockSpec(memory_space=pltpu.SMEM)] + any_specs(4) + vmem_specs(8),
         out_specs=vmem_specs(7),
         scratch_shapes=[
             pltpu.VMEM((width, hidden), LOW),
@@ -430,13 +484,13 @@
         cost_estimate=cost(
             4 * rows * width * (hidden + width), 4 * width * (hidden + width) + 2 * rows * hidden
         ),
-        name="up_backward",
-    )(spot, up_own, up_other, out_own, out_other, e, h2, a2, mixed, du, table)
-
-
-def attention_backward(lengths, qkv, da, mixed, lse):
+        name="middle_backward",
+    )(spot, up_own, up_other, out_own, out_other, e, h2, a2, *mixed, du, acc, table)
+
+
+def attention_backward(lengths, qkv, da, mixed, lse, begin, pairs):
     rows, wide = qkv.shape
-    width = wide // 3
+    width = pairs * LANES
 
     def body(len_ref, q_ref, k_ref, v_ref, d_ref, m_ref, lse_ref, out_ref, row_ref):
         pair = pl.program_id(0)
@@ -482,58 +536,50 @@
 
     return pl.pallas_call(
         body,
-        out_shape=jax.ShapeDtypeStruct((rows, wide), LOW),
+        out_shape=jax.ShapeDtypeStruct((rows, 3 * width), LOW),
         grid_spec=pltpu.PrefetchScalarGridSpec(
             num_scalar_prefetch=1,
-            grid=(PAIRS,),
+            grid=(pairs,),
             in_specs=[
-                pl.BlockSpec((rows, LANES), lambda p, n: (0, p)),
-                pl.BlockSpec((rows, LANES), lambda p, n: (0, p + PAIRS)),
-                pl.BlockSpec((rows, LANES), lambda p, n: (0, p + 2 * PAIRS)),
-                pl.BlockSpec((rows, LANES), lambda p, n: (0, p)),
+                pl.BlockSpec((rows, LANES), lambda p, n: (0, p + begin)),
+                pl.BlockSpec((rows, LANES), lambda p, n: (0, p + begin + PAIRS)),
+                pl.BlockSpec((rows, LANES), lambda p, n: (0, p + begin + 2 * PAIRS)),
+                pl.BlockSpec((rows, LANES), lambda p, n: (0, p + begin)),
                 pl.BlockSpec((rows, LANES), lambda p, n: (0, p)),
                 pl.BlockSpec((rows, LANES), lambda p, n: (0, 0)),
             ],
-            out_specs=pl.BlockSpec((rows, wide), lambda p, n: (0, 0)),
+            out_specs=pl.BlockSpec((rows, 3 * width), lambda p, n: (0, 0)),
             scratch_shapes=[pltpu.VMEM((LANES, rows), WIDE)],
         ),
         compiler_params=params(),
-        cost_estimate=cost(40 * rows * rows * width, 16 * rows * width, HEADS * rows * rows),
+        cost_estimate=cost(40 * rows * rows * width, 16 * rows * width, 2 * pairs * rows * rows),
         name="attention_backward",
     )(lengths, qkv, qkv, qkv, da, mixed, lse)
 
 
 def qkv_backward(spot, own, other, column, dqkv, e2, h, a1, table):
-    rows, wide = dqkv.shape
-    width = wide // 3
+    rows, width = e2.shape
+    wide = 3 * width
     half = wide // 2
+    part = width // 2
     tile = 384
 
     def body(
-        spot_ref, own_ref, other_ref, d_ref, e_ref, h_ref, a_ref, t_ref,
-        o_ref, mine_ref, rest_ref, sums_ref, w_ref, at_ref, acc_ref, sems,
+        spot_ref, own_ref, other_ref, d0_ref, d1_ref, e_ref, h_ref, a_ref, t_ref,
+        o_ref, mine_ref, rest_ref, sums_ref, w_ref, at_ref, d_ref, acc_ref, sems,
     ):
         copies = piece_copies(spot_ref, own_ref, other_ref, w_ref, sems, column, half)
         for copy in copies:
             copy.start()
         at_ref[...] = a_ref[...].T
         acc_ref[...] = jnp.zeros_like(acc_ref)
+        for n in range(3):
+            for side, ref in enumerate((d0_ref, d1_ref)):
+                start = n * width + side * part
+                d_ref[:, start : start + part] = ref[:, n * part : (n + 1) * part]
         for copy in copies:
             copy.wait()
-        c = spot_ref[3]
-        for owner, out_ref in ((c, mine_ref), (1 - c, rest_ref)):
-            starts = block_starts(spot_ref, owner, width // 16)
-
-            def step(n, carry):
-                at = pl.ds(pl.multiple_of(owner * half + n * tile, LANES), tile)
-                d = d_ref[:, at]
-                put_blocks(
-                    dot(at_ref[...], d), out_ref, starts, pl.multiple_of(n * tile, LANES), tile
-                )
-                acc_ref[...] += dot_nt(d, w_ref[:, at])
-                return carry
-
-            lax.fori_loop(0, half // tile, step, 0)
+        up_steps(spot_ref, w_ref, at_ref, d_ref, acc_ref, (mine_ref, rest_ref), half, tile)
         dv, gain, shift = norm_back(h_ref[...], t_ref[GAIN1 : GAIN1 + 1, :], acc_ref[...])
         o_ref[...] = e_ref[...] + dv
         sums_ref[0:1, :] = gain
@@ -549,18 +595,19 @@
             jax.ShapeDtypeStruct((width, half), LOW),
             jax.ShapeDtypeStruct((8, width), WIDE),
         ],
-        in_specs=[pl.BlockSpec(memory_space=pltpu.SMEM)] + any_specs(2) + vmem_specs(5),
+        in_specs=[pl.BlockSpec(memory_space=pltpu.SMEM)] + any_specs(2) + vmem_specs(6),
         out_specs=vmem_specs(4),
         scratch_shapes=[
             pltpu.VMEM((width, wide), LOW),
             pltpu.VMEM((width, rows), LOW),
+            pltpu.VMEM((rows, wide), LOW),
             pltpu.VMEM((rows, width), WIDE),
             pltpu.SemaphoreType.DMA((32,)),
         ],
         compiler_params=params(),
         cost_estimate=cost(4 * rows * width * wide, 4 * width * wide + 16 * rows * width),
         name="qkv_backward",
-    )(spot, own, other, dqkv, e2, h, a1, table)
+    )(spot, own, other, *dqkv, e2, h, a1, table)
 
 
 def small_forward(spot, own, column, hidden):
@@ -661,7 +708,7 @@
 
 
 TO_CORE = pairs_of(lambda z, x, y, c: (z, x, y, 1 - c))
-TO_RING = pairs_of(lambda z, x, y, c: ((z + 1) % 4, x, y, c))
+TO_Z = [pairs_of(lambda z, x, y, c, n=n: ((z + n) % 4, x, y, c)) for n in range(4)]
 TO_XY = pairs_of(lambda z, x, y, c: (z, x, 1 - y, c) if c else (z, 1 - x, y, c))
 TO_YX = pairs_of(lambda z, x, y, c: (z, 1 - x, y, c) if c else (z, x, 1 - y, c))
 
@@ -688,34 +735,78 @@
     return jnp.concatenate(low, axis=1), jnp.concatenate(high, axis=1)
 
 
-def gather_rows(spot, pieces):
+class Chain:
+    def __init__(self, steps):
+        self.steps = steps
+        self.result = None
+        self.flying = None
+        self.resume(None)
+
+    def resume(self, arrived):
+        try:
+            self.waiting = self.steps.send(arrived)
+        except StopIteration as end:
+            self.waiting = None
+            self.result = end.value
+
+    def start(self):
+        if self.waiting is not None:
+            self.flying = [send(value, pairs) for value, pairs in self.waiting]
+
+
+def stage(begin, work=None, hold=()):
+    for chain in begin:
+        chain.start()
+    landing = [chain for chain in begin if chain.flying is not None and chain not in hold]
+    outs = work() if work is not None else ()
+    arrived, outs = lax.optimization_barrier(([chain.flying for chain in landing], outs))
+    for chain, values in zip(landing, arrived):
+        chain.flying = None
+        chain.resume(values)
+    return outs
+
+
+def land(chain):
+    class Held:
+        flying = chain.flying
+
+        def start(self):
+            pass
+
+        def resume(self, values):
+            chain.flying = None
+            chain.resume(values)
+
+    return Held()
+
+
+def offsets_of(widths):
     offsets = [0]
-    for piece in pieces:
-        offsets.append(offsets[-1] + piece.shape[1] // 2)
+    for width in widths:
+        offsets.append(offsets[-1] + width // 2)
+    return offsets
+
+
+def gather_whole(pieces):
+    whole = [lax.all_gather(piece, AXES, axis=0, tiled=True) for piece in pieces]
+    low, high = [
+        part.reshape(4, 2, 2, -1, part.shape[1])[jnp.array([0, 3, 2, 1])] for part in halves(whole)
+    ]
+    width = low.shape[-1]
+    own = low.transpose(2, 1, 0, 3, 4).reshape(-1, width)
+    return own, high.transpose(1, 2, 0, 3, 4).reshape(-1, width)
+
+
+def gather_steps(pieces, block):
     if not blocked():
-        whole = [lax.all_gather(piece, AXES, axis=0, tiled=True) for piece in pieces]
-        low, high = [
-            part.reshape(4, 2, 2, -1, part.shape[1])[jnp.array([0, 3, 2, 1])]
-            for part in halves(whole)
-        ]
-        width = low.shape[-1]
-        own = low.transpose(2, 1, 0, 3, 4).reshape(-1, width)
-        other = high.transpose(1, 2, 0, 3, 4).reshape(-1, width)
-        return own, other, offsets
-    c = spot[3]
-    low, high = halves(pieces)
-    mine = jnp.where(c == 0, low, high)
-    got = send(jnp.where(c == 0, high, low), TO_CORE)
-    block = jnp.where(
-        c == 0, jnp.concatenate([mine, got], axis=0), jnp.concatenate([got, mine], axis=0)
-    )
-    ring = [block]
-    for step in range(3):
-        ring.append(send(ring[-1], TO_RING))
-    stack = jnp.concatenate(ring, axis=0)
-    stack = jnp.concatenate([stack, send(stack, TO_XY)], axis=0)
-    stack = jnp.concatenate([stack, send(stack, TO_YX)], axis=0)
-    return stack, send(stack, TO_CORE), offsets
+        return gather_whole(pieces)
+    ring = yield [(block, TO_Z[n]) for n in (1, 2, 3)]
+    stack = jnp.concatenate([block, *ring], axis=0)
+    for pairs in (TO_XY, TO_YX):
+        (got,) = yield [(stack, pairs)]
+        stack = jnp.concatenate([stack, got], axis=0)
+    (got,) = yield [(stack, TO_CORE)]
+    return stack, got
 
 
 def added(parts):
@@ -725,44 +816,52 @@
     return total
 
 
-def scatter_rows(spot, mines, rests):
+def scatter_whole(mines, rests):
+    result = []
+    for mine, rest in zip(mines, rests):
+        rows, half = mine.shape[0] // 16, mine.shape[1]
+        low = mine.reshape(2, 2, 4, rows, half).transpose(2, 1, 0, 3, 4)
+        high = rest.reshape(2, 2, 4, rows, half).transpose(2, 0, 1, 3, 4)
+        whole = jnp.concatenate([low, high], axis=-1)[jnp.array([0, 3, 2, 1])]
+        whole = whole.reshape(16 * rows, 2 * half)
+        result.append(lax.psum_scatter(whole, AXES, scatter_dimension=0, tiled=True).astype(WIDE))
+    return result
+
+
+def cross_steps(rest):
     if not blocked():
-        result = []
-        for mine, rest in zip(mines, rests):
-            rows, half = mine.shape[0] // 16, mine.shape[1]
-            low = mine.reshape(2, 2, 4, rows, half).transpose(2, 1, 0, 3, 4)
-            high = rest.reshape(2, 2, 4, rows, half).transpose(2, 0, 1, 3, 4)
-            whole = jnp.concatenate([low, high], axis=-1)[jnp.array([0, 3, 2, 1])]
-            whole = whole.reshape(16 * rows, 2 * half)
-            result.append(
-                lax.psum_scatter(whole, AXES, scatter_dimension=0, tiled=True).astype(WIDE)
-            )
-        return result
+        return rest
+    (got,) = yield [(rest, TO_CORE)]
+    return got
+
+
+def scatter_steps(spot, mines, gots):
+    if not blocked():
+        return scatter_whole(mines, gots)
     c = spot[3]
     height = mines[0].shape[0]
     a = height // 2
     b = height // 4
     rows = height // 16
-    gots = [send(rest, TO_CORE) for rest in rests]
 
     def part(start, stop):
         return jnp.concatenate(
             [added([mine[start:stop], got[start:stop]]) for mine, got in zip(mines, gots)], axis=1
         )
 
-    got_a = send(part(a, 2 * a).astype(LOW), TO_YX)
-    got_b = send(added([part(b, 2 * b), got_a[b : 2 * b]]).astype(LOW), TO_XY)
+    (got_a,) = yield [(part(a, 2 * a).astype(LOW), TO_YX)]
+    (got_b,) = yield [(added([part(b, 2 * b), got_a[b : 2 * b]]).astype(LOW), TO_XY)]
 
     def block_at(step):
         at = slice(step * rows, (step + 1) * rows)
         return added([part(at.start, at.stop), got_a[at], got_b[at]])
 
-    moving = block_at(1)
-    for step in (2, 3, 0):
-        moving = added([block_at(step), send(moving.astype(LOW), TO_RING)])
-    low, high = moving[: rows // 2], moving[rows // 2 :]
+    got_z = yield [(block_at(n).astype(LOW), TO_Z[4 - n]) for n in (1, 2, 3)]
+    total = added([block_at(0), *got_z])
+    low, high = total[: rows // 2], total[rows // 2 :]
     kept = jnp.where(c == 0, low, high)
-    got = send(jnp.where(c == 0, high, low).astype(LOW), TO_CORE).astype(WIDE)
+    (got,) = yield [(jnp.where(c == 0, high, low).astype(LOW), TO_CORE)]
+    got = got.astype(WIDE)
     result = []
     start = 0
     for mine in mines:
@@ -833,61 +932,237 @@
     layers = qkv_weight.shape[0]
     share = up_bias.shape[1]
     hidden = down_weight.shape[1]
-    assert clips == 1
+    half = hidden // 2
+    assert clips == 1 and layers == 2
     spot = place()
-    down_t = jnp.swapaxes(down_weight, 1, 2).astype(LOW)
-    weights = []
+    chunks = []
     for i in range(layers):
         gains, shifts, bias = (v[i].astype(LOW) for v in (norm_gains, biases, up_bias))
-        pieces = [qkv_weight[i].astype(LOW)]
+        up = up_weight[i].astype(LOW)
+        down = down_weight[i].T.astype(LOW)
+        first = [qkv_weight[i].astype(LOW)]
         if blocked():
-            pieces.append(pack_small(gains, shifts, bias))
-        own, other, at = gather_rows(spot, pieces)
-        qkv = (own, other, at[0])
+            first.append(pack_small(gains, shifts, bias))
+        chunks.append(first)
+        chunks.append([out_weight[i].astype(LOW), up[:, :half], down[:, :half]])
+        chunks.append([up[:, half:], down[:, half:]])
+    spots = [offsets_of([piece.shape[1] for piece in pieces]) for pieces in chunks]
+
+    def both_cores(pieces):
+        low, high = halves(pieces)
+        mine = jnp.where(spot[3] == 0, low, high)
+        got = send(jnp.where(spot[3] == 0, high, low), TO_CORE)
+        upper = jnp.concatenate([mine, got], axis=0)
+        return jnp.where(spot[3] == 0, upper, jnp.concatenate([got, mine], axis=0))
+
+    if blocked():
+        rest = both_cores([piece for pieces in chunks[1:] for piece in pieces])
+        blocks = [both_cores(chunks[0])]
+        start = 0
+        for at in spots[1:]:
+            blocks.append(rest[:, start : start + at[-1]])
+            start = start + at[-1]
+    else:
+        blocks = [None] * len(chunks)
+    q0, a0, b0, q1, a1, b1 = [Chain(gather_steps(p, block)) for p, block in zip(chunks, blocks)]
+
+    def weight(index, member):
+        chain = (q0, a0, b0, q1, a1, b1)[index]
+        return (*chain.result, spots[index][member])
+
+    def small_of(i):
         if blocked():
-            table, bias = small_forward(spot, own, at[1], hidden)
+            return small_forward(spot, weight(3 * i, 0)[0], spots[3 * i][1], hidden)
+        return whole_small(norm_gains[i].astype(LOW), biases[i].astype(LOW), up_bias[i].astype(LOW))
+
+    pairs = PAIRS // 2
+    rec = [{"h": hidden_in[0]}, {}]
+
+    def norm_and_qkv(i):
+        r = rec[i]
+        table, bias = small_of(i)
+        qkv, first = qkv_forward(spot, *weight(3 * i, 0), r["h"], table)
+        return {"table": table, "bias": bias, "qkv": qkv, "a1": first}
+
+    def attend(i, side):
+        mixed, lse = attention_forward(lengths, rec[i]["qkv"], side * pairs, pairs)
+        return {f"mixed{side}": mixed, f"lse{side}": lse}
+
+    def project(i):
+        r = rec[i]
+        h2, second = out_forward(
+            spot, *weight(3 * i + 1, 0), r["h"], (r["mixed0"], r["mixed1"]), r["table"]
+        )
+        return {"h2": h2, "a2": second}
+
+    def feed(i, side):
+        r = rec[i]
+        z, slope, total = mlp_forward(
+            spot,
+            weight(3 * i + 1 + side, 1 - side),
+            weight(3 * i + 1 + side, 2 - side),
+            r["total"] if side else r["h2"],
+            r["a2"],
+            r["bias"][:, side * half : (side + 1) * half],
+            r["table"],
+            side == 0,
+        )
+        return {f"z{side}": z, f"slope{side}": slope, "total": total}
+
+    def down_back(i, side):
+        r = rec[i]
+        du, mine, rest, down_sum, up_sum = down_backward(
+            spot, weight(3 * i + 1 + side, 2 - side), r["e"], r[f"z{side}"], r[f"slope{side}"]
+        )
+        return {
+            f"du{side}": du,
+            f"down{side}": (mine, rest),
+            "down_sum": down_sum,
+            f"up_sum{side}": up_sum,
+        }
+
+    def up_back(i):
+        r = rec[i]
+        acc, mine, rest = up_backward(spot, weight(3 * i + 1, 1), r["a2"], r["du0"])
+        return {"acc": acc, "up0": (mine, rest)}
+
+    def middle_back(i):
+        r = rec[i]
+        e2, da, mine, rest, out_mine, out_rest, sums = middle_backward(
+            spot,
+            weight(3 * i + 2, 0),
+            weight(3 * i + 1, 0),
+            r["e"],
+            r["h2"],
+            r["a2"],
+            (r["mixed0"], r["mixed1"]),
+            r["du1"],
+            r["acc"],
+            r["table"],
+        )
+        return {
+            "e2": e2,
+            "da": da,
+            "up1": (mine, rest),
+            "out": (out_mine, out_rest),
+            "sums2": sums,
+        }
+
+    def attend_back(i, side):
+        r = rec[i]
+        dqkv = attention_backward(
+            lengths, r["qkv"], r["da"], r[f"mixed{side}"], r[f"lse{side}"], side * pairs, pairs
+        )
+        return {f"dqkv{side}": dqkv}
+
+    def qkv_back(i):
+        r = rec[i]
+        e, mine, rest, sums = qkv_backward(
+            spot,
+            *weight(3 * i, 0),
+            (r["dqkv0"], r["dqkv1"]),
+            r["e2"],
+            r["h"],
+            r["a1"],
+            r["table"],
+        )
+        found = {"e_in": e, "qkv_grad": (mine, rest), "sums1": sums}
+        if blocked():
+            up_sum = jnp.concatenate([r["up_sum0"], r["up_sum1"]], axis=1)
+            found["small"] = small_backward(spot, r["sums2"], sums, r["down_sum"], up_sum)
+        return found
+
+    def run(begin, *work, hold=()):
+        def todo():
+            before = [dict(r) for r in rec]
+            found = []
+            for function, i, *rest in work:
+                new = function(i, *rest)
+                rec[i].update(new)
+                found.append(new)
+            for r, old in zip(rec, before):
+                r.clear()
+                r.update(old)
+            return found
+
+        for (function, i, *rest), new in zip(work, stage(begin, todo, hold)):
+            rec[i].update(new)
+
+    run([q0])
+    run([q0, a0], hold=[a0])
+    run([q0, land(a0)])
+    run([q0, a0, b0], hold=[b0])
+    run([a0, land(b0)], (norm_and_qkv, 0), (attend, 0, 0))
+    run([a0, b0], (attend, 0, 1))
+    run([b0, q1], (project, 0), (feed, 0, 0))
+    run([b0, q1])
+    run([q1, a1], (feed, 0, 1))
+    rec[1]["h"] = rec[0]["total"]
+    run([q1, a1, b1], hold=[b1])
+    run([a1, land(b1)], (norm_and_qkv, 1))
+    run([a1, b1], (attend, 1, 0))
+    run([b1], (attend, 1, 1), (project, 1))
+    run([b1], (feed, 1, 0))
+    run([], (feed, 1, 1))
+    output = rec[1]["total"][None]
+
+    def cross(i, *members):
+        return [Chain(cross_steps(rec[i][member][1])) for member in members]
+
+    def scatter(i, members, crossed):
+        mines = [rec[i][member][0] for member in members]
+        return Chain(scatter_steps(spot, mines, [chain.result for chain in crossed]))
+
+    small_parts = ["small"] if blocked() else []
+    rec[1]["e"] = cotangent[0]
+    run([], (down_back, 1, 0))
+    down_a = cross(1, "down0")
+    run(down_a, (down_back, 1, 1))
+    down_b = cross(1, "down1")
+    run(down_b, (up_back, 1))
+    d1 = scatter(1, ["down0", "down1"], down_a + down_b)
+    up_a = cross(1, "up0")
+    run([d1, *up_a], (middle_back, 1))
+    up_b = cross(1, "out", "up1")
+    run([d1, *up_b], (attend_back, 1, 0))
+    u1 = scatter(1, ["out", "up0", "up1"], [up_b[0], up_a[0], up_b[1]])
+    run([d1, u1], (attend_back, 1, 1), (qkv_back, 1))
+    rec[0]["e"] = rec[1]["e_in"]
+    qkv_a = cross(1, "qkv_grad", *small_parts)
+    run([d1, u1, *qkv_a], (down_back, 0, 0))
+    q1 = scatter(1, ["qkv_grad", *small_parts], qkv_a)
+    down_a = cross(0, "down0")
+    run([u1, q1, *down_a], (down_back, 0, 1))
+    down_b = cross(0, "down1")
+    run([u1, q1, *down_b], (up_back, 0))
+    d0 = scatter(0, ["down0", "down1"], down_a + down_b)
+    up_a = cross(0, "up0")
+    run([d0, q1, *up_a], (middle_back, 0))
+    up_b = cross(0, "out", "up1")
+    run([d0, q1, *up_b], (attend_back, 0, 0))
+    u0 = scatter(0, ["out", "up0", "up1"], [up_b[0], up_a[0], up_b[1]])
+    run([d0, u0], (attend_back, 0, 1), (qkv_back, 0))
+    qkv_a = cross(0, "qkv_grad", *small_parts)
+    run([d0, u0, *qkv_a])
+    q0 = scatter(0, ["qkv_grad", *small_parts], qkv_a)
+    run([u0, q0])
+    run([u0, q0])
+    run([q0])
+    run([q0])
+
+    owned = []
+    for i, (q, u, d) in enumerate(((q0, u0, d0), (q1, u1, d1))):
+        r = rec[i]
+        own_down = jnp.concatenate(d.result, axis=1).T
+        own_up = jnp.concatenate(u.result[1:], axis=1)
+        if blocked():
+            found = unpack_small(q.result[1], share)
         else:
-            table, bias = whole_small(gains, shifts, bias)
-        own, other, at = gather_rows(spot, [out_weight[i].astype(LOW), up_weight[i].astype(LOW)])
-        out, up = (own, other, at[0]), (own, other, at[1])
-        own, other, at = gather_rows(spot, [down_t[i]])
-        weights.append((qkv, out, up, (own, other, at[0]), table, bias))
-
-    h = hidden_in[0]
-    records = []
-    for i in range(layers):
-        qkv_w, out_w, up_w, down_w, table, bias = weights[i]
-        qkv, a1 = qkv_forward(spot, *qkv_w, h, table)
-        mixed, lse = attention_forward(lengths, qkv)
-        h2, a2 = out_forward(spot, *out_w, h, mixed, table)
-        z, slope, result = mlp_forward(spot, up_w, down_w, h2, a2, bias, table)
-        records.append((h, a1, qkv, mixed, lse, h2, a2, z, slope))
-        h = result
-    output = h[None]
-    e = cotangent[0]
-    owned = [None] * layers
-    for i in reversed(range(layers)):
-        qkv_w, out_w, up_w, down_w, table, bias = weights[i]
-        h, a1, qkv, mixed, lse, h2, a2, z, slope = records[i]
-        du, mine, rest, down_sum, up_sum = down_backward(spot, down_w, e, z, slope)
-        (own_down,) = scatter_rows(spot, [mine], [rest])
-        e2, da, mine, rest, out_mine, out_rest, first = up_backward(
-            spot, up_w, out_w, e, h2, a2, mixed, du, table
-        )
-        own_out, own_up = scatter_rows(spot, [out_mine, mine], [out_rest, rest])
-        dqkv = attention_backward(lengths, qkv, da, mixed, lse)
-        e, mine, rest, second = qkv_backward(spot, *qkv_w, dqkv, e2, h, a1, table)
-        if blocked():
-            small_mine, small_rest = small_backward(spot, first, second, down_sum, up_sum)
-            own_qkv, packed = scatter_rows(spot, [mine, small_mine], [rest, small_rest])
-            small = unpack_small(packed, share)
-        else:
-            (own_qkv,) = scatter_rows(spot, [mine], [rest])
-            small = spread_small(first, second, down_sum, up_sum)
-        owned[i] = (own_qkv, own_out, own_up, own_down.T, *small)
-
+            up_sum = jnp.concatenate([r["up_sum0"], r["up_sum1"]], axis=1)
+            found = spread_small(r["sums2"], r["sums1"], r["down_sum"], up_sum)
+        owned.append((q.result[0], u.result[0], own_up, own_down, *found))
     stacked = [jnp.stack([owned[i][n] for i in range(layers)]) for n in range(7)]
-    return (output, e[None], *stacked)
+    return (output, rec[0]["e_in"][None], *stacked)
 
 
 def solution(mesh):

time: 589 us -> 572 us (0.971)
  waiting for transfers between devices: 231 us -> 106 us
  Pallas kernels: 207 us -> 244 us
  other arithmetic: 48.1 us -> 79.3 us
  starting transfers between devices: 58.8 us -> 82.9 us
  local copies, waits for them, and re-layouts: 32.1 us -> 45.2 us
    ppermute x88, waiting for transfers between devices: 231 us -> 106 us  [send(): return lax.ppermute(value, AXES, pairs)]
    pallas_call x2 -> x6, Pallas kernels: 25.3 us -> 59.7 us  [the longest x2 30 us: middle_backward(): pl.pallas_call(body, out_shape=[jax.ShapeDtypeStruct((rows, width), WIDE)...]
    ppermute x88, starting transfers between devices: 58.8 us -> 82.9 us  [send(): return lax.ppermute(value, AXES, pairs)]
    add x22 -> x34, other arithmetic: 11.7 us -> 34.1 us  [added(): total = total + part.astype(WIDE)]
    pallas_call x2, Pallas kernels: 36.9 us -> 19.3 us  [up_backward(): pl.pallas_call(body, out_shape=[jax.ShapeDtypeStruct((rows, width), WIDE)...]
    unnamed x101 -> x208, local copies, waits for them, and re-layouts: 15.1 us -> 26.7 us
    pallas_call x2 -> x4, Pallas kernels: 30.6 us -> 41.5 us  [down_backward(): pl.pallas_call(body, out_shape=[jax.ShapeDtypeStruct((rows, hidden), LOW)...]
    another operation x13 -> x20, other arithmetic: 4.67 us -> 12.8 us
  transfers between devices with their start and end apart: 88 -> 88, of which waited for: 45 -> 27; matrix products, arithmetic and copies ran while one was open for 12% -> 12% of each run, Pallas kernels for 22% -> 42%
where the time goes in v3:
time: 572 us; the launch traced here: 562 us
  Pallas kernels  244 us (43%)
  waiting for transfers between devices  106 us (19%)
  starting transfers between devices  82.9 us (14%)
  other arithmetic  79.3 us (14%)
  local copies, waits for them, and re-layouts  45.2 us (8%)
    ppermute x88, waiting for transfers between devices, send(): return lax.ppermute(value, AXES, pairs)  106 us
    ppermute x88, starting transfers between devices, send(): return lax.ppermute(value, AXES, pairs)  82.9 us
    pallas_call x4, Pallas kernels, down_backward(): pl.pallas_call(body, out_shape=[jax.ShapeDtypeStruct((rows, hidden), LOW)...  41.5 us
    pallas_call x4, Pallas kernels, mlp_forward(): pl.pallas_call(body, out_shape=[jax.ShapeDtypeStruct((rows, hidden), LOW)...  40.7 us
    add x34, other arithmetic, added(): total = total + part.astype(WIDE)  34.1 us
    pallas_call x2, Pallas kernels, middle_backward(): pl.pallas_call(body, out_shape=[jax.ShapeDtypeStruct((rows, width), WIDE)...  30 us
    pallas_call x4, Pallas kernels, attention_backward(): pl.pallas_call(body, out_shape=jax.ShapeDtypeStruct((rows, 3 * width), LO...  29.7 us
    unnamed x208, local copies, waits for them, and re-layouts  26.7 us
  transfers between devices with their start and end apart: 88, of which 27 were waited for; matrix products, arithmetic and copies ran while one was open for 12% of the time, Pallas kernels for 42%

profile of v3, /device:TPU:0, one launch (start us, length us, event | category | flops | bytes accessed | tf_op | source)
XLA Modules:
  0.0 561.6 jit_solution(16871853773244281568)
XLA Ops:
  6.0 4.7 collective-permute-start.4
  11.7 2.7 collective-permute-done.4
  14.4 7.9 %collective-permute-done.3 = bf16[48,1280]{1,0:T(8,128)(2,1)S(1)} collective-permute-done((bf16[48,1280]{1,0:T(8,128)(2,1)S(1)}, bf16[48,1280]{1,0:T(8,128)(2,1)S(1)}, u32[]{:S(2)}, u32[]{:S(2)}) %collective-permute-start.3) | collective-permute-done | bytes 122912 | tf_op jit(solution)/shard_map/ppermute | solution.py:717
  24.0 7.3 %collective-permute-done.5 = bf16[192,1280]{1,0:T(8,128)(2,1)S(1)} collective-permute-done((bf16[192,1280]{1,0:T(8,128)(2,1)S(1)}, bf16[192,1280]{1,0:T(8,128)(2,1)S(1)}, u32[]{:S(2)}, u32[]{:S(2)}) %collective-permute-start.5) | collective-permute-done | bytes 491552 | tf_op jit(solution)/shard_map/ppermute | solution.py:717
  38.2 2.1 collective-permute-done.9
  40.4 10.7 %collective-permute-done.8 = bf16[48,1920]{1,0:T(8,128)(2,1)S(1)} collective-permute-done((bf16[48,1920]{1,0:T(8,128)(2,1)S(1)}, bf16[48,1920]{1,0:T(8,128)(2,1)S(1)}, u32[]{:S(2)}, u32[]{:S(2)}) %collective-permute-start.8) | collective-permute-done | bytes 184352 | tf_op jit(solution)/shard_map/ppermute | solution.py:717
  54.2 8.6 %collective-permute-done.11 = bf16[192,1920]{1,0:T(8,128)(2,1)S(1)} collective-permute-done((bf16[192,1920]{1,0:T(8,128)(2,1)S(1)}, bf16[192,1920]{1,0:T(8,128)(2,1)S(1)}, u32[]{:S(2)}, u32[]{:S(2)}) %collective-permute-start.11) | collective-permute-done | bytes 737312 | tf_op jit(solution)/shard_map/ppermute | solution.py:717
  70.4 2.0 collective-permute-start.13
  72.4 2.5 small_forward.2
  74.9 7.1 %qkv_forward.2 = (bf16[496,2304]{1,0:T(8,128)(2,1)}, bf16[496,768]{1,0:T(8,128)(2,1)}) custom-call(s32[4]{0:T(128)} %pad_add_fusion.spot_ref, bf16[768,1280]{1,0:T(8,128)(2,1)} %copy-done.3, bf16[768,1280]{1,0:T(8,128)(2,1)} %copy-done.85, f32[496,768]{1,0:T(8,128)} %bitcast.83, f32[8,768]{1,0:T(8,128)} %get-tuple-element.283.t_ref), custom_call_target="tpu_custom_call" | custom-call | flops 1755316224 | bytes 6967296 | tf_op jit(solution)/shard_map/qkv_forward/pallas_call | solution.py:116
  82.0 5.7 %attention_forward.4 = (bf16[496,384]{1,0:T(8,128)(2,1)}, f32[496,128]{1,0:T(8,128)}) custom-call(s32[1]{0:T(128)S(6)} %copy.88.len_ref, bf16[496,2304]{1,0:T(8,128)(2,1)} %get-tuple-element.276.q_ref.k_ref.v_ref, bf16[496,2304]{1,0:T(8,128)(2,1)} %get-tuple-element.276.q_ref.k_ref.v_ref, bf16[496,2304]{1,0:T(8,128)(2,1)} %get-tuple-element.276.q_ref.k_ref.v_ref), custom_call_target="tpu_custom_call" | custom-call | flops 1511522304 | bytes 1523712 | tf_op jit(solution)/shard_map/attention_forward/pallas_call | solution.py:158
  87.7 2.6 constant_dynamic-update-slice_fusion.16.own_ref.uo_ref.do_ref.oo_ref
  92.5 5.7 %attention_forward.5 = (bf16[496,384]{1,0:T(8,128)(2,1)}, f32[496,128]{1,0:T(8,128)}) custom-call(s32[1]{0:T(128)S(6)} %copy.88.len_ref, bf16[496,2304]{1,0:T(8,128)(2,1)} %get-tuple-element.276.q_ref.k_ref.v_ref, bf16[496,2304]{1,0:T(8,128)(2,1)} %get-tuple-element.276.q_ref.k_ref.v_ref, bf16[496,2304]{1,0:T(8,128)(2,1)} %get-tuple-element.276.q_ref.k_ref.v_ref), custom_call_target="tpu_custom_call" | custom-call | flops 1511522304 | bytes 1523712 | tf_op jit(solution)/shard_map/attention_forward/pallas_call | solution.py:158
  101.3 2.2 constant_dynamic-update-slice_fusion.28
  107.5 2.2 collective-permute-start.19
  110.3 5.5 out_forward.2
  115.8 10.2 %mlp_forward.4 = (bf16[496,1536]{1,0:T(8,128)(2,1)}, bf16[496,1536]{1,0:T(8,128)(2,1)}, f32[496,768]{1,0:T(8,128)}) custom-call(s32[4]{0:T(128)} %pad_add_fusion.spot_ref, bf16[768,1920]{1,0:T(8,128)(2,1)} %constant_dynamic-update-slice_fusion.16.own_ref.uo_ref.do_ref.oo_ref, bf16[768,1920]{1,0:T(8,128)(2,1)} %collective-permute-done.16.other_ref.up_ref.dp_ref.op_ref, ...), custom_call_target="tpu_custom_call" | custom-call | flops 2340421632 | bytes 7766016 | tf_op jit(solution)/shard_map/mlp_forward/pallas_call | solution.py:255
  126.0 2.4 constant_dynamic-update-slice_fusion.27.uo_ref.do_ref.own_ref
  131.2 6.1 %collective-permute-done.23 = bf16[192,1280]{1,0:T(8,128)(2,1)S(1)} collective-permute-done((bf16[192,1280]{1,0:T(8,128)(2,1)S(1)}, bf16[192,1280]{1,0:T(8,128)(2,1)S(1)}, u32[]{:S(2)}, u32[]{:S(2)}) %collective-permute-start.23) | collective-permute-done | bytes 491552 | tf_op jit(solution)/shard_map/ppermute | solution.py:717
  143.0 10.1 %mlp_forward.5 = (bf16[496,1536]{1,0:T(8,128)(2,1)}, bf16[496,1536]{1,0:T(8,128)(2,1)}, f32[496,768]{1,0:T(8,128)}) custom-call(s32[4]{0:T(128)} %pad_add_fusion.spot_ref, bf16[768,1536]{1,0:T(8,128)(2,1)} %constant_dynamic-update-slice_fusion.27.uo_ref.do_ref.own_ref, bf16[768,1536]{1,0:T(8,128)(2,1)} %collective-permute-done.22.up_ref.dp_ref.other_ref, ...), custom_call_target="tpu_custom_call" | custom-call | flops 2340421632 | bytes 7766016 | tf_op jit(solution)/shard_map/mlp_forward/pallas_call | solution.py:255
  153.1 4.4 collective-permute-done.26
  157.5 2.2 constant_dynamic-update-slice_fusion.38.own_ref
  163.5 7.9 %collective-permute-done.29 = bf16[192,1920]{1,0:T(8,128)(2,1)S(1)} collective-permute-done((bf16[192,1920]{1,0:T(8,128)(2,1)S(1)}, bf16[192,1920]{1,0:T(8,128)(2,1)S(1)}, u32[]{:S(2)}, u32[]{:S(2)}) %collective-permute-start.29) | collective-permute-done | bytes 737312 | tf_op jit(solution)/shard_map/ppermute | solution.py:717
  177.5 2.5 small_forward.3
  179.9 7.1 %qkv_forward.3 = (bf16[496,2304]{1,0:T(8,128)(2,1)}, bf16[496,768]{1,0:T(8,128)(2,1)}) custom-call(s32[4]{0:T(128)} %pad_add_fusion.spot_ref, bf16[768,1280]{1,0:T(8,128)(2,1)} %constant_dynamic-update-slice_fusion.38.own_ref, bf16[768,1280]{1,0:T(8,128)(2,1)} %copy-done.86, f32[496,768]{1,0:T(8,128)} %get-tuple-element.307.h_ref, ...), custom_call_target="tpu_custom_call" | custom-call | flops 1755316224 | bytes 6967296 | tf_op jit(solution)/shard_map/qkv_forward/pallas_call | solution.py:116
  188.3 3.9 collective-permute-done.30
  197.0 5.9 %attention_forward.6 = (bf16[496,384]{1,0:T(8,128)(2,1)}, f32[496,128]{1,0:T(8,128)}) custom-call(s32[1]{0:T(128)S(6)} %copy.88.len_ref, bf16[496,2304]{1,0:T(8,128)(2,1)} %get-tuple-element.316.q_ref.k_ref.v_ref, bf16[496,2304]{1,0:T(8,128)(2,1)} %get-tuple-element.316.q_ref.k_ref.v_ref, bf16[496,2304]{1,0:T(8,128)(2,1)} %get-tuple-element.316.q_ref.k_ref.v_ref), custom_call_target="tpu_custom_call" | custom-call | flops 1511522304 | bytes 1523712 | tf_op jit(solution)/shard_map/attention_forward/pallas_call | solution.py:158
  205.0 2.2 constant_dynamic-update-slice_fusion.55
  208.7 5.7 %attention_forward.7 = (bf16[496,384]{1,0:T(8,128)(2,1)}, f32[496,128]{1,0:T(8,128)}) custom-call(s32[1]{0:T(128)S(6)} %copy.88.len_ref, bf16[496,2304]{1,0:T(8,128)(2,1)} %get-tuple-element.316.q_ref.k_ref.v_ref, bf16[496,2304]{1,0:T(8,128)(2,1)} %get-tuple-element.316.q_ref.k_ref.v_ref, bf16[496,2304]{1,0:T(8,128)(2,1)} %get-tuple-element.316.q_ref.k_ref.v_ref), custom_call_target="tpu_custom_call" | custom-call | flops 1511522304 | bytes 1523712 | tf_op jit(solution)/shard_map/attention_forward/pallas_call | solution.py:158
  214.4 5.5 out_forward.3
  220.0 3.6 collective-permute-done.36
  225.3 10.2 %mlp_forward.6 = (bf16[496,1536]{1,0:T(8,128)(2,1)}, bf16[496,1536]{1,0:T(8,128)(2,1)}, f32[496,768]{1,0:T(8,128)}) custom-call(s32[4]{0:T(128)} %pad_add_fusion.spot_ref, bf16[768,1920]{1,0:T(8,128)(2,1)} %copy-done, bf16[768,1920]{1,0:T(8,128)(2,1)} %collective-permute-done.34.other_ref.up_ref.dp_ref.op_ref, bf16[768,1920]{1,0:T(8,128)(2,1)} %copy-done, ...), custom_call_target="tpu_custom_call" | custom-call | flops 2340421632 | bytes 7766016 | tf_op jit(solution)/shard_map/mlp_forward/pallas_call | solution.py:255
  235.6 11.0 %down_backward.4 = (bf16[496,1536]{1,0:T(8,128)(2,1)}, bf16[768,768]{1,0:T(8,128)(2,1)}, bf16[768,768]{1,0:T(8,128)(2,1)}, f32[1,768]{1,0:T(1,128)}, f32[1,1536]{1,0:T(1,128)}) custom-call(s32[4]{0:T(128)} %pad_add_fusion.spot_ref, bf16[768,1920]{1,0:T(8,128)(2,1)} %copy-done, bf16[768,1920]{1,0:T(8,128)(2,1)} %collective-permute-done.34.other_ref.up_ref.dp_ref.op_ref, ...), custom_call_target="tpu_custom_call" | custom-call | flops 2340421632 | bytes 9289728 | tf_op jit(solution)/shard_map/down_backward/pallas_call | solution.py:339
  247.2 10.2 %mlp_forward.7 = (bf16[496,1536]{1,0:T(8,128)(2,1)}, bf16[496,1536]{1,0:T(8,128)(2,1)}, f32[496,768]{1,0:T(8,128)}) custom-call(s32[4]{0:T(128)} %pad_add_fusion.spot_ref, bf16[768,1536]{1,0:T(8,128)(2,1)} %constant_dynamic-update-slice_fusion.60.uo_ref.do_ref.own_ref, bf16[768,1536]{1,0:T(8,128)(2,1)} %copy-done.1, ...), custom_call_target="tpu_custom_call" | custom-call | flops 2340421632 | bytes 7766016 | tf_op jit(solution)/shard_map/mlp_forward/pallas_call | solution.py:255
  257.4 10.1 %down_backward.5 = (bf16[496,1536]{1,0:T(8,128)(2,1)}, bf16[768,768]{1,0:T(8,128)(2,1)}, bf16[768,768]{1,0:T(8,128)(2,1)}, f32[1,768]{1,0:T(1,128)}, f32[1,1536]{1,0:T(1,128)}) custom-call(s32[4]{0:T(128)} %pad_add_fusion.spot_ref, bf16[768,1536]{1,0:T(8,128)(2,1)} %constant_dynamic-update-slice_fusion.60.uo_ref.do_ref.own_ref, bf16[768,1536]{1,0:T(8,128)(2,1)} %copy-done.1, ...), custom_call_target="tpu_custom_call" | custom-call | flops 2340421632 | bytes 9289728 | tf_op jit(solution)/shard_map/down_backward/pallas_call | solution.py:339
  267.6 9.8 %up_backward.2 = (f32[496,768]{1,0:T(8,128)}, bf16[768,768]{1,0:T(8,128)(2,1)}, bf16[768,768]{1,0:T(8,128)(2,1)}) custom-call(s32[4]{0:T(128)} %pad_add_fusion.spot_ref, bf16[768,1920]{1,0:T(8,128)(2,1)} %copy-done, bf16[768,1920]{1,0:T(8,128)(2,1)} %collective-permute-done.34.other_ref.up_ref.dp_ref.op_ref, bf16[496,768]{1,0:T(8,128)(2,1)} %get-tuple-element.329.a_ref, ...), custom_call_target="tpu_custom_call" | custom-call | flops 2340421632 | bytes 6242304 | tf_op jit(solution)/shard_map/up_backward/pallas_call | solution.py:381
  283.9 15.0 %middle_backward.2 = (f32[496,768]{1,0:T(8,128)}, bf16[496,768]{1,0:T(8,128)(2,1)}, bf16[768,768]{1,0:T(8,128)(2,1)}, bf16[768,768]{1,0:T(8,128)(2,1)}, bf16[768...) custom-call(s32[4]{0:T(128)} %pad_add_fusion.spot_ref, ...), custom_call_target="tpu_custom_call" | custom-call | flops 3510632448 | bytes 8601600 | tf_op jit(solution)/shard_map/middle_backward/pallas_call | solution.py:460
  305.1 7.4 %attention_backward.5.d1_ref = bf16[496,1152]{1,0:T(8,128)(2,1)} custom-call(s32[1]{0:T(128)S(6)} %copy.88.len_ref, bf16[496,2304]{1,0:T(8,128)(2,1)} %get-tuple-element.316.q_ref.k_ref.v_ref, bf16[496,2304]{1,0:T(8,128)(2,1)} %get-tuple-element.316.q_ref.k_ref.v_ref, bf16[496,2304]{1,0:T(8,128)(2,1)} %get-tuple-element.316.q_ref.k_ref.v_ref, ...), custom_call_target="tpu_custom_call" | custom-call | flops 3778805760 | bytes 3047424 | tf_op jit(solution)/shard_map/attention_backward/pallas_call | solution.py:537
  314.4 7.5 %attention_backward.4.d0_ref = bf16[496,1152]{1,0:T(8,128)(2,1)} custom-call(s32[1]{0:T(128)S(6)} %copy.88.len_ref, bf16[496,2304]{1,0:T(8,128)(2,1)} %get-tuple-element.316.q_ref.k_ref.v_ref, bf16[496,2304]{1,0:T(8,128)(2,1)} %get-tuple-element.316.q_ref.k_ref.v_ref, bf16[496,2304]{1,0:T(8,128)(2,1)} %get-tuple-element.316.q_ref.k_ref.v_ref, ...), custom_call_target="tpu_custom_call" | custom-call | flops 3778805760 | bytes 3047424 | tf_op jit(solution)/shard_map/attention_backward/pallas_call | solution.py:537
  329.8 3.1 collective-permute-start.45
  332.9 13.2 %qkv_backward.2 = (f32[496,768]{1,0:T(8,128)}, bf16[768,1152]{1,0:T(8,128)(2,1)}, bf16[768,1152]{1,0:T(8,128)(2,1)}, f32[8,768]{1,0:T(8,128)}) custom-call(s32[4]{0:T(128)} %pad_add_fusion.spot_ref, bf16[768,1280]{1,0:T(8,128)(2,1)} %constant_dynamic-update-slice_fusion.38.own_ref, bf16[768,1280]{1,0:T(8,128)(2,1)} %copy-done.86, ...), custom_call_target="tpu_custom_call" | custom-call | flops 3510632448 | bytes 13172736 | tf_op jit(solution)/shard_map/qkv_backward/pallas_call | solution.py:590
  357.8 10.1 %down_backward.7 = (bf16[496,1536]{1,0:T(8,128)(2,1)}, bf16[768,768]{1,0:T(8,128)(2,1)}, bf16[768,768]{1,0:T(8,128)(2,1)}, f32[1,768]{1,0:T(1,128)}, f32[1,1536]{1,0:T(1,128)}) custom-call(s32[4]{0:T(128)} %pad_add_fusion.spot_ref, bf16[768,1536]{1,0:T(8,128)(2,1)} %constant_dynamic-update-slice_fusion.27.uo_ref.do_ref.own_ref, ...), custom_call_target="tpu_custom_call" | custom-call | flops 2340421632 | bytes 9289728 | tf_op jit(solution)/shard_map/down_backward/pallas_call | solution.py:339
  368.5 10.2 %down_backward.6 = (bf16[496,1536]{1,0:T(8,128)(2,1)}, bf16[768,768]{1,0:T(8,128)(2,1)}, bf16[768,768]{1,0:T(8,128)(2,1)}, f32[1,768]{1,0:T(1,128)}, f32[1,1536]{1,0:T(1,128)}) custom-call(s32[4]{0:T(128)} %pad_add_fusion.spot_ref, bf16[768,1920]{1,0:T(8,128)(2,1)} %constant_dynamic-update-slice_fusion.16.own_ref.uo_ref.do_ref.oo_ref, ...), custom_call_target="tpu_custom_call" | custom-call | flops 2340421632 | bytes 9289728 | tf_op jit(solution)/shard_map/down_backward/pallas_call | solution.py:339
  380.6 2.1 convert_add_fusion.16
  391.0 2.8 collective-permute-start.53
  396.4 9.5 %up_backward.3 = (f32[496,768]{1,0:T(8,128)}, bf16[768,768]{1,0:T(8,128)(2,1)}, bf16[768,768]{1,0:T(8,128)(2,1)}) custom-call(s32[4]{0:T(128)} %pad_add_fusion.spot_ref, bf16[768,1920]{1,0:T(8,128)(2,1)} %constant_dynamic-update-slice_fusion.16.own_ref.uo_ref.do_ref.oo_ref, bf16[768,1920]{1,0:T(8,128)(2,1)} %collective-permute-done.16.other_ref.up_ref.dp_ref.op_ref, ...), custom_call_target="tpu_custom_call" | custom-call | flops 2340421632 | bytes 6242304 | tf_op jit(solution)/shard_map/up_backward/pallas_call | solution.py:381
  414.4 3.2 collective-permute-done.59
  421.8 2.3 collective-permute-start.63
  424.1 2.1 collective-permute-start.62
  428.5 15.0 %middle_backward.3 = (f32[496,768]{1,0:T(8,128)}, bf16[496,768]{1,0:T(8,128)(2,1)}, bf16[768,768]{1,0:T(8,128)(2,1)}, bf16[768,768]{1,0:T(8,128)(2,1)}, bf16[768...) custom-call(s32[4]{0:T(128)} %pad_add_fusion.spot_ref, ...), custom_call_target="tpu_custom_call" | custom-call | flops 3510632448 | bytes 8601600 | tf_op jit(solution)/shard_map/middle_backward/pallas_call | solution.py:460
  448.4 2.0 fusion.3
  451.8 7.4 %attention_backward.7.d1_ref = bf16[496,1152]{1,0:T(8,128)(2,1)} custom-call(s32[1]{0:T(128)S(6)} %copy.88.len_ref, bf16[496,2304]{1,0:T(8,128)(2,1)} %get-tuple-element.276.q_ref.k_ref.v_ref, bf16[496,2304]{1,0:T(8,128)(2,1)} %get-tuple-element.276.q_ref.k_ref.v_ref, bf16[496,2304]{1,0:T(8,128)(2,1)} %get-tuple-element.276.q_ref.k_ref.v_ref, ...), custom_call_target="tpu_custom_call" | custom-call | flops 3778805760 | bytes 3047424 | tf_op jit(solution)/shard_map/attention_backward/pallas_call | solution.py:537
  462.0 7.4 %attention_backward.6.d0_ref = bf16[496,1152]{1,0:T(8,128)(2,1)} custom-call(s32[1]{0:T(128)S(6)} %copy.88.len_ref, bf16[496,2304]{1,0:T(8,128)(2,1)} %get-tuple-element.276.q_ref.k_ref.v_ref, bf16[496,2304]{1,0:T(8,128)(2,1)} %get-tuple-element.276.q_ref.k_ref.v_ref, bf16[496,2304]{1,0:T(8,128)(2,1)} %get-tuple-element.276.q_ref.k_ref.v_ref, ...), custom_call_target="tpu_custom_call" | custom-call | flops 3778805760 | bytes 3047424 | tf_op jit(solution)/shard_map/attention_backward/pallas_call | solution.py:537
  477.1 2.1 fusion.41
  480.7 3.2 collective-permute-start.70
  486.0 13.2 %qkv_backward.3 = (f32[496,768]{1,0:T(8,128)}, bf16[768,1152]{1,0:T(8,128)(2,1)}, bf16[768,1152]{1,0:T(8,128)(2,1)}, f32[8,768]{1,0:T(8,128)}) custom-call(s32[4]{0:T(128)} %pad_add_fusion.spot_ref, bf16[768,1280]{1,0:T(8,128)(2,1)} %copy-done.3, bf16[768,1280]{1,0:T(8,128)(2,1)} %copy-done.85, bf16[496,1152]{1,0:T(8,128)(2,1)} %attention_backward.6.d0_ref, ...), custom_call_target="tpu_custom_call" | custom-call | flops 3510632448 | bytes 13172736 | tf_op jit(solution)/shard_map/qkv_backward/pallas_call | solution.py:590
  508.9 7.3 %collective-permute-done.75 = bf16[192,1920]{1,0:T(8,128)(2,1)S(1)} collective-permute-done((bf16[192,1920]{1,0:T(8,128)(2,1)S(1)}, bf16[192,1920]{1,0:T(8,128)(2,1)S(1)}, u32[]{:S(2)}, u32[]{:S(2)}) %collective-permute-start.75) | collective-permute-done | bytes 737312 | tf_op jit(solution)/shard_map/ppermute | solution.py:717
  519.5 2.8 collective-permute-start.78
  524.7 2.7 collective-permute-done.80
  527.4 6.6 %collective-permute-done.79 = bf16[48,1920]{1,0:T(8,128)(2,1)S(1)} collective-permute-done((bf16[48,1920]{1,0:T(8,128)(2,1)S(1)}, bf16[48,1920]{1,0:T(8,128)(2,1)S(1)}, u32[]{:S(2)}, u32[]{:S(2)}) %collective-permute-start.79) | collective-permute-done | bytes 184352 | tf_op jit(solution)/shard_map/ppermute | solution.py:717
  534.0 2.6 collective-permute-done.81
  539.5 6.3 %collective-permute-done.83 = bf16[192,1280]{1,0:T(8,128)(2,1)S(1)} collective-permute-done((bf16[192,1280]{1,0:T(8,128)(2,1)S(1)}, bf16[192,1280]{1,0:T(8,128)(2,1)S(1)}, u32[]{:S(2)}, u32[]{:S(2)}) %collective-permute-start.83) | collective-permute-done | bytes 491552 | tf_op jit(solution)/shard_map/ppermute | solution.py:717
  548.3 2.1 collective-permute-start.84
  553.0 3.7 collective-permute-done.85
  (537 shorter events, 174.2 us)
Async XLA Ops:
  5.5 27.4 %collective-permute-start = (bf16[24,8192]{1,0:T(8,128)(2,1)S(1)}, bf16[24,8192]{1,0:T(8,128)(2,1)S(1)}, u32[]{:S(2)}, u32[]{:S(2)}) collective-permute-start(bf16[24,8192]{1,0:T(8,128)(2,1)S(1)} %get-tuple-element.598), channel_id=1, source_target_pairs={{0,1},{1,0},{2,3},{3,2},{4,5},{5,4},{6,7},{7,6},{8,9},{9,8},{10,11... | collective-permute-start | bytes 1179656 | tf_op jit(solution)/shard_map/ppermute | solution.py:717
  10.7 11.6 %collective-permute-start.3 = (bf16[48,1280]{1,0:T(8,128)(2,1)S(1)}, bf16[48,1280]{1,0:T(8,128)(2,1)S(1)}, u32[]{:S(2)}, u32[]{:S(2)}) collective-permute-start(bf16[48,1280]{1,0:T(8,128)(2,1)S(1)} %get-tuple-element.515), channel_id=1, source_target_pairs={{0,16},{1,17},{2,18},{3,19},{4,20},{5,21},{6,22},{7,23},{8,24},{9,... | collective-permute-start | bytes 368648 | tf_op jit(solution)/shard_map/ppermute | solution.py:717
  10.7 11.6 %collective-permute-start.2 = (bf16[48,1280]{1,0:T(8,128)(2,1)S(1)}, bf16[48,1280]{1,0:T(8,128)(2,1)S(1)}, u32[]{:S(2)}, u32[]{:S(2)}) collective-permute-start(bf16[48,1280]{1,0:T(8,128)(2,1)S(1)} %get-tuple-element.515), channel_id=1, source_target_pairs={{0,8},{1,9},{2,10},{3,11},{4,12},{5,13},{6,14},{7,15},{8,16},{9,17... | collective-permute-start | bytes 368648 | tf_op jit(solution)/shard_map/ppermute | solution.py:717
  31.3 19.8 %collective-permute-start.6 = (bf16[384,1280]{1,0:T(8,128)(2,1)S(1)}, bf16[384,1280]{1,0:T(8,128)(2,1)S(1)}, u32[]{:S(2)}, u32[]{:S(2)}) collective-permute-start(bf16[384,1280]{1,0:T(8,128)(2,1)S(1)} %get-tuple-element.610), channel_id=1, source_target_pairs={{0,2},{1,5},{2,0},{3,7},{4,6},{5,1},{6,4},{7,3},{8,10},{9,13},{10,... | collective-permute-start | bytes 2949128 | tf_op jit(solution)/shard_map/ppermute | solution.py:717
  35.2 15.9 %collective-permute-start.8 = (bf16[48,1920]{1,0:T(8,128)(2,1)S(1)}, bf16[48,1920]{1,0:T(8,128)(2,1)S(1)}, u32[]{:S(2)}, u32[]{:S(2)}) collective-permute-start(bf16[48,1920]{1,0:T(8,128)(2,1)S(1)} %get-tuple-element.592), channel_id=1, source_target_pairs={{0,16},{1,17},{2,18},{3,19},{4,20},{5,21},{6,22},{7,23},{8,24},{9,... | collective-permute-start | bytes 552968 | tf_op jit(solution)/shard_map/ppermute | solution.py:717
  36.2 14.9 %collective-permute-start.7 = (bf16[48,1920]{1,0:T(8,128)(2,1)S(1)}, bf16[48,1920]{1,0:T(8,128)(2,1)S(1)}, u32[]{:S(2)}, u32[]{:S(2)}) collective-permute-start(bf16[48,1920]{1,0:T(8,128)(2,1)S(1)} %get-tuple-element.592), channel_id=1, source_target_pairs={{0,8},{1,9},{2,10},{3,11},{4,12},{5,13},{6,14},{7,15},{8,16},{9,17... | collective-permute-start | bytes 552968 | tf_op jit(solution)/shard_map/ppermute | solution.py:717
  51.2 11.7 %collective-permute-start.10 = (bf16[768,1280]{1,0:T(8,128)(2,1)S(1)}, bf16[768,1280]{1,0:T(8,128)(2,1)S(1)}, u32[]{:S(2)}, u32[]{:S(2)}) collective-permute-start(bf16[768,1280]{1,0:T(8,128)(2,1)S(1)} %constant_dynamic-update-slice_fusion.5.own_ref), channel_id=1, source_target_pairs={{0,1},{1,0},{2,3},{3,2},{4,5},{5,4},{6,7},{7,6},{8,9},{9,8},{10,11... | collective-permute-start | bytes 5898248 | tf_op jit(solution)/shard_map/ppermute | solution.py:717
  51.3 11.5 %collective-permute-start.11 = (bf16[192,1920]{1,0:T(8,128)(2,1)S(1)}, bf16[192,1920]{1,0:T(8,128)(2,1)S(1)}, u32[]{:S(2)}, u32[]{:S(2)}) collective-permute-start(bf16[192,1920]{1,0:T(8,128)(2,1)S(1)} %pad_maximum_fusion.6), channel_id=1, source_target_pairs={{0,4},{1,3},{2,6},{3,1},{4,0},{5,7},{6,2},{7,5},{8,12},{9,11},{10,... | collective-permute-start | bytes 2211848 | tf_op jit(solution)/shard_map/ppermute | solution.py:717
  64.6 23.0 %collective-permute-start.12 = (bf16[384,1920]{1,0:T(8,128)(2,1)}, bf16[384,1920]{1,0:T(8,128)(2,1)}, u32[]{:S(2)}, u32[]{:S(2)}) collective-permute-start(bf16[384,1920]{1,0:T(8,128)(2,1)} %get-tuple-element.602), channel_id=1, source_target_pairs={{0,2},{1,5},{2,0},{3,7},{4,6},{5,1},{6,4},{7,3},{8,10},{9,13},{10,... | collective-permute-start | bytes 4423688 | tf_op jit(solution)/shard_map/ppermute | solution.py:717
  69.3 18.4 %collective-permute-start.15 = (bf16[48,1536]{1,0:T(8,128)(2,1)S(1)}, bf16[48,1536]{1,0:T(8,128)(2,1)S(1)}, u32[]{:S(2)}, u32[]{:S(2)}) collective-permute-start(bf16[48,1536]{1,0:T(8,128)(2,1)S(1)} %get-tuple-element.586), channel_id=1, source_target_pairs={{0,24},{1,25},{2,26},{3,27},{4,28},{5,29},{6,30},{7,31},{8,0},{9,1... | collective-permute-start | bytes 442376 | tf_op jit(solution)/shard_map/ppermute | solution.py:717
  69.3 18.4 %collective-permute-start.14 = (bf16[48,1536]{1,0:T(8,128)(2,1)S(1)}, bf16[48,1536]{1,0:T(8,128)(2,1)S(1)}, u32[]{:S(2)}, u32[]{:S(2)}) collective-permute-start(bf16[48,1536]{1,0:T(8,128)(2,1)S(1)} %get-tuple-element.586), channel_id=1, source_target_pairs={{0,16},{1,17},{2,18},{3,19},{4,20},{5,21},{6,22},{7,23},{8,24},{9,... | collective-permute-start | bytes 442376 | tf_op jit(solution)/shard_map/ppermute | solution.py:717
  70.4 17.3 %collective-permute-start.13 = (bf16[48,1536]{1,0:T(8,128)(2,1)S(1)}, bf16[48,1536]{1,0:T(8,128)(2,1)S(1)}, u32[]{:S(2)}, u32[]{:S(2)}) collective-permute-start(bf16[48,1536]{1,0:T(8,128)(2,1)S(1)} %get-tuple-element.586), channel_id=1, source_target_pairs={{0,8},{1,9},{2,10},{3,11},{4,12},{5,13},{6,14},{7,15},{8,16},{9,17... | collective-permute-start | bytes 442376 | tf_op jit(solution)/shard_map/ppermute | solution.py:717
  90.3 11.1 %collective-permute-start.16 = (bf16[768,1920]{1,0:T(8,128)(2,1)}, bf16[768,1920]{1,0:T(8,128)(2,1)}, u32[]{:S(2)}, u32[]{:S(2)}) collective-permute-start(bf16[768,1920]{1,0:T(8,128)(2,1)} %constant_dynamic-update-slice_fusion.16.own_ref.uo_ref.do_ref.oo_ref), channel_id=1, source_target_pairs={{0,1},{1,0},{2,3},{3,2},{4,5},{5,4},{6,7},{7,6},{8,9},{9,8},{10,11... | collective-permute-start | bytes 8847368 | tf_op jit(solution)/shard_map/ppermute | solution.py:717
  103.5 22.5 %collective-permute-start.18 = (bf16[384,1536]{1,0:T(8,128)(2,1)}, bf16[384,1536]{1,0:T(8,128)(2,1)}, u32[]{:S(2)}, u32[]{:S(2)}) collective-permute-start(bf16[384,1536]{1,0:T(8,128)(2,1)} %get-tuple-element.606), channel_id=1, source_target_pairs={{0,2},{1,5},{2,0},{3,7},{4,6},{5,1},{6,4},{7,3},{8,10},{9,13},{10,... | collective-permute-start | bytes 3538952 | tf_op jit(solution)/shard_map/ppermute | solution.py:717
  105.7 20.3 %collective-permute-start.21 = (bf16[48,1280]{1,0:T(8,128)(2,1)S(1)}, bf16[48,1280]{1,0:T(8,128)(2,1)S(1)}, u32[]{:S(2)}, u32[]{:S(2)}) collective-permute-start(bf16[48,1280]{1,0:T(8,128)(2,1)S(1)} %get-tuple-element.596), channel_id=1, source_target_pairs={{0,24},{1,25},{2,26},{3,27},{4,28},{5,29},{6,30},{7,31},{8,0},{9,1... | collective-permute-start | bytes 368648 | tf_op jit(solution)/shard_map/ppermute | solution.py:717
  107.5 18.5 %collective-permute-start.20 = (bf16[48,1280]{1,0:T(8,128)(2,1)S(1)}, bf16[48,1280]{1,0:T(8,128)(2,1)S(1)}, u32[]{:S(2)}, u32[]{:S(2)}) collective-permute-start(bf16[48,1280]{1,0:T(8,128)(2,1)S(1)} %get-tuple-element.596), channel_id=1, source_target_pairs={{0,16},{1,17},{2,18},{3,19},{4,20},{5,21},{6,22},{7,23},{8,24},{9,... | collective-permute-start | bytes 368648 | tf_op jit(solution)/shard_map/ppermute | solution.py:717
  107.5 18.5 %collective-permute-start.19 = (bf16[48,1280]{1,0:T(8,128)(2,1)S(1)}, bf16[48,1280]{1,0:T(8,128)(2,1)S(1)}, u32[]{:S(2)}, u32[]{:S(2)}) collective-permute-start(bf16[48,1280]{1,0:T(8,128)(2,1)S(1)} %get-tuple-element.596), channel_id=1, source_target_pairs={{0,8},{1,9},{2,10},{3,11},{4,12},{5,13},{6,14},{7,15},{8,16},{9,17... | collective-permute-start | bytes 368648 | tf_op jit(solution)/shard_map/ppermute | solution.py:717
  138.4 19.2 %collective-permute-start.24 = (bf16[384,1280]{1,0:T(8,128)(2,1)}, bf16[384,1280]{1,0:T(8,128)(2,1)}, u32[]{:S(2)}, u32[]{:S(2)}) collective-permute-start(bf16[384,1280]{1,0:T(8,128)(2,1)} %get-tuple-element.608), channel_id=1, source_target_pairs={{0,2},{1,5},{2,0},{3,7},{4,6},{5,1},{6,4},{7,3},{8,10},{9,13},{10,... | collective-permute-start | bytes 2949128 | tf_op jit(solution)/shard_map/ppermute | solution.py:717
  139.9 13.2 %collective-permute-start.27 = (bf16[48,1920]{1,0:T(8,128)(2,1)S(1)}, bf16[48,1920]{1,0:T(8,128)(2,1)S(1)}, u32[]{:S(2)}, u32[]{:S(2)}) collective-permute-start(bf16[48,1920]{1,0:T(8,128)(2,1)S(1)} %get-tuple-element.593), channel_id=1, source_target_pairs={{0,24},{1,25},{2,26},{3,27},{4,28},{5,29},{6,30},{7,31},{8,0},{9,1... | collective-permute-start | bytes 552968 | tf_op jit(solution)/shard_map/ppermute | solution.py:717
  141.7 15.9 %collective-permute-start.26 = (bf16[48,1920]{1,0:T(8,128)(2,1)S(1)}, bf16[48,1920]{1,0:T(8,128)(2,1)S(1)}, u32[]{:S(2)}, u32[]{:S(2)}) collective-permute-start(bf16[48,1920]{1,0:T(8,128)(2,1)S(1)} %get-tuple-element.593), channel_id=1, source_target_pairs={{0,16},{1,17},{2,18},{3,19},{4,20},{5,21},{6,22},{7,23},{8,24},{9,... | collective-permute-start | bytes 552968 | tf_op jit(solution)/shard_map/ppermute | solution.py:717
  142.7 14.8 %collective-permute-start.25 = (bf16[48,1920]{1,0:T(8,128)(2,1)S(1)}, bf16[48,1920]{1,0:T(8,128)(2,1)S(1)}, u32[]{:S(2)}, u32[]{:S(2)}) collective-permute-start(bf16[48,1920]{1,0:T(8,128)(2,1)S(1)} %get-tuple-element.593), channel_id=1, source_target_pairs={{0,8},{1,9},{2,10},{3,11},{4,12},{5,13},{6,14},{7,15},{8,16},{9,17... | collective-permute-start | bytes 552968 | tf_op jit(solution)/shard_map/ppermute | solution.py:717
  159.8 11.6 %collective-permute-start.28 = (bf16[768,1280]{1,0:T(8,128)(2,1)}, bf16[768,1280]{1,0:T(8,128)(2,1)S(1)}, u32[]{:S(2)}, u32[]{:S(2)}) collective-permute-start(bf16[768,1280]{1,0:T(8,128)(2,1)} %constant_dynamic-update-slice_fusion.38.own_ref), channel_id=1, source_target_pairs={{0,1},{1,0},{2,3},{3,2},{4,5},{5,4},{6,7},{7,6},{8,9},{9,8},{10,11... | collective-permute-start | bytes 5898248 | tf_op jit(solution)/shard_map/ppermute | solution.py:717
  159.8 11.5 %collective-permute-start.29 = (bf16[192,1920]{1,0:T(8,128)(2,1)S(1)}, bf16[192,1920]{1,0:T(8,128)(2,1)S(1)}, u32[]{:S(2)}, u32[]{:S(2)}) collective-permute-start(bf16[192,1920]{1,0:T(8,128)(2,1)S(1)} %pad_maximum_fusion.7), channel_id=1, source_target_pairs={{0,4},{1,3},{2,6},{3,1},{4,0},{5,7},{6,2},{7,5},{8,12},{9,11},{10,... | collective-permute-start | bytes 2211848 | tf_op jit(solution)/shard_map/ppermute | solution.py:717
  172.5 19.7 %collective-permute-start.30 = (bf16[384,1920]{1,0:T(8,128)(2,1)}, bf16[384,1920]{1,0:T(8,128)(2,1)}, u32[]{:S(2)}, u32[]{:S(2)}) collective-permute-start(bf16[384,1920]{1,0:T(8,128)(2,1)} %get-tuple-element.600), channel_id=1, source_target_pairs={{0,2},{1,5},{2,0},{3,7},{4,6},{5,1},{6,4},{7,3},{8,10},{9,13},{10,... | collective-permute-start | bytes 4423688 | tf_op jit(solution)/shard_map/ppermute | solution.py:717
  174.0 13.0 %collective-permute-start.33 = (bf16[48,1536]{1,0:T(8,128)(2,1)S(1)}, bf16[48,1536]{1,0:T(8,128)(2,1)S(1)}, u32[]{:S(2)}, u32[]{:S(2)}) collective-permute-start(bf16[48,1536]{1,0:T(8,128)(2,1)S(1)} %get-tuple-element.587), channel_id=1, source_target_pairs={{0,24},{1,25},{2,26},{3,27},{4,28},{5,29},{6,30},{7,31},{8,0},{9,1... | collective-permute-start | bytes 442376 | tf_op jit(solution)/shard_map/ppermute | solution.py:717
  174.0 14.3 %collective-permute-start.32 = (bf16[48,1536]{1,0:T(8,128)(2,1)S(1)}, bf16[48,1536]{1,0:T(8,128)(2,1)S(1)}, u32[]{:S(2)}, u32[]{:S(2)}) collective-permute-start(bf16[48,1536]{1,0:T(8,128)(2,1)S(1)} %get-tuple-element.587), channel_id=1, source_target_pairs={{0,16},{1,17},{2,18},{3,19},{4,20},{5,21},{6,22},{7,23},{8,24},{9,... | collective-permute-start | bytes 442376 | tf_op jit(solution)/shard_map/ppermute | solution.py:717
  175.4 12.8 %collective-permute-start.31 = (bf16[48,1536]{1,0:T(8,128)(2,1)S(1)}, bf16[48,1536]{1,0:T(8,128)(2,1)S(1)}, u32[]{:S(2)}, u32[]{:S(2)}) collective-permute-start(bf16[48,1536]{1,0:T(8,128)(2,1)S(1)} %get-tuple-element.587), channel_id=1, source_target_pairs={{0,8},{1,9},{2,10},{3,11},{4,12},{5,13},{6,14},{7,15},{8,16},{9,17... | collective-permute-start | bytes 442376 | tf_op jit(solution)/shard_map/ppermute | solution.py:717
  193.7 11.3 %collective-permute-start.34 = (bf16[768,1920]{1,0:T(8,128)(2,1)S(1)}, bf16[768,1920]{1,0:T(8,128)(2,1)}, u32[]{:S(2)}, u32[]{:S(2)}) collective-permute-start(bf16[768,1920]{1,0:T(8,128)(2,1)S(1)} %constant_dynamic-update-slice_fusion.49.own_ref.uo_ref.do_ref.oo_ref), channel_id=1, source_target_pairs={{0,1},{1,0},{2,3},{3,2},{4,5},{5,4},{6,7},{7,6},{8,9},{9,8},{10,11... | collective-permute-start | bytes 8847368 | tf_op jit(solution)/shard_map/ppermute | solution.py:717
  207.2 16.4 %collective-permute-start.36 = (bf16[384,1536]{1,0:T(8,128)(2,1)}, bf16[384,1536]{1,0:T(8,128)(2,1)S(1)}, u32[]{:S(2)}, u32[]{:S(2)}) collective-permute-start(bf16[384,1536]{1,0:T(8,128)(2,1)} %get-tuple-element.603), channel_id=1, source_target_pairs={{0,2},{1,5},{2,0},{3,7},{4,6},{5,1},{6,4},{7,3},{8,10},{9,13},{10,... | collective-permute-start | bytes 3538952 | tf_op jit(solution)/shard_map/ppermute | solution.py:717
  246.6 20.9 %collective-permute-start.38 = (bf16[768,768]{1,0:T(8,128)(2,1)}, bf16[768,768]{1,0:T(8,128)(2,1)S(1)}, u32[]{:S(2)}, u32[]{:S(2)}) collective-permute-start(bf16[768,768]{1,0:T(8,128)(2,1)} %get-tuple-element.347), channel_id=1, source_target_pairs={{0,1},{1,0},{2,3},{3,2},{4,5},{5,4},{6,7},{7,6},{8,9},{9,8},{10,11... | collective-permute-start | bytes 3538952 | tf_op jit(solution)/shard_map/ppermute | solution.py:717
  280.0 19.0 %collective-permute-start.40 = (bf16[384,1536]{1,0:T(8,128)(2,1)}, bf16[384,1536]{1,0:T(8,128)(2,1)}, u32[]{:S(2)}, u32[]{:S(2)}) collective-permute-start(bf16[384,1536]{1,0:T(8,128)(2,1)} %pad_maximum_fusion.2), channel_id=1, source_target_pairs={{0,2},{1,5},{2,0},{3,7},{4,6},{5,1},{6,4},{7,3},{8,10},{9,13},{10,... | collective-permute-start | bytes 3538952 | tf_op jit(solution)/shard_map/ppermute | solution.py:717
  281.5 17.5 %collective-permute-start.41 = (bf16[768,768]{1,0:T(8,128)(2,1)}, bf16[768,768]{1,0:T(8,128)(2,1)}, u32[]{:S(2)}, u32[]{:S(2)}) collective-permute-start(bf16[768,768]{1,0:T(8,128)(2,1)} %get-tuple-element.363), channel_id=1, source_target_pairs={{0,1},{1,0},{2,3},{3,2},{4,5},{5,4},{6,7},{7,6},{8,9},{9,8},{10,11... | collective-permute-start | bytes 3538952 | tf_op jit(solution)/shard_map/ppermute | solution.py:717
  299.0 22.9 %collective-permute-start.43 = (bf16[768,384]{1,0:T(8,128)(2,1)}, bf16[768,384]{1,0:T(8,128)(2,1)}, u32[]{:S(2)}, u32[]{:S(2)}) collective-permute-start(bf16[768,384]{1,0:T(8,128)(2,1)} %get-tuple-element.375), channel_id=1, source_target_pairs={{0,1},{1,0},{2,3},{3,2},{4,5},{5,4},{6,7},{7,6},{8,9},{9,8},{10,11... | collective-permute-start | bytes 1769480 | tf_op jit(solution)/shard_map/ppermute | solution.py:717
  301.4 20.5 %collective-permute-start.42 = (bf16[192,1536]{1,0:T(8,128)(2,1)}, bf16[192,1536]{1,0:T(8,128)(2,1)S(1)}, u32[]{:S(2)}, u32[]{:S(2)}) collective-permute-start(bf16[192,1536]{1,0:T(8,128)(2,1)} %fusion.2), channel_id=1, source_target_pairs={{0,4},{1,3},{2,6},{3,1},{4,0},{5,7},{6,2},{7,5},{8,12},{9,11},{10,... | collective-permute-start | bytes 1769480 | tf_op jit(solution)/shard_map/ppermute | solution.py:717
  302.9 19.8 %collective-permute-start.44 = (bf16[768,768]{1,0:T(8,128)(2,1)}, bf16[768,768]{1,0:T(8,128)(2,1)}, u32[]{:S(2)}, u32[]{:S(2)}) collective-permute-start(bf16[768,768]{1,0:T(8,128)(2,1)} %get-tuple-element.376), channel_id=1, source_target_pairs={{0,1},{1,0},{2,3},{3,2},{4,5},{5,4},{6,7},{7,6},{8,9},{9,8},{10,11... | collective-permute-start | bytes 3538952 | tf_op jit(solution)/shard_map/ppermute | solution.py:717
  325.2 28.3 %collective-permute-start.48 = (bf16[384,1920]{1,0:T(8,128)(2,1)S(1)}, bf16[384,1920]{1,0:T(8,128)(2,1)S(1)}, u32[]{:S(2)}, u32[]{:S(2)}) collective-permute-start(bf16[384,1920]{1,0:T(8,128)(2,1)S(1)} %pad_maximum_fusion), channel_id=1, source_target_pairs={{0,2},{1,5},{2,0},{3,7},{4,6},{5,1},{6,4},{7,3},{8,10},{9,13},{10,... | collective-permute-start | bytes 4423688 | tf_op jit(solution)/shard_map/ppermute | solution.py:717
  328.3 25.1 %collective-permute-start.47 = (bf16[48,1536]{1,0:T(8,128)(2,1)}, bf16[48,1536]{1,0:T(8,128)(2,1)}, u32[]{:S(2)}, u32[]{:S(2)}) collective-permute-start(bf16[48,1536]{1,0:T(8,128)(2,1)} %get-tuple-element.565), channel_id=1, source_target_pairs={{0,8},{1,9},{2,10},{3,11},{4,12},{5,13},{6,14},{7,15},{8,16},{9,17... | collective-permute-start | bytes 442376 | tf_op jit(solution)/shard_map/ppermute | solution.py:717
  328.3 25.1 %collective-permute-start.46 = (bf16[48,1536]{1,0:T(8,128)(2,1)}, bf16[48,1536]{1,0:T(8,128)(2,1)}, u32[]{:S(2)}, u32[]{:S(2)}) collective-permute-start(bf16[48,1536]{1,0:T(8,128)(2,1)} %get-tuple-element.566), channel_id=1, source_target_pairs={{0,16},{1,17},{2,18},{3,19},{4,20},{5,21},{6,22},{7,23},{8,24},{9,... | collective-permute-start | bytes 442376 | tf_op jit(solution)/shard_map/ppermute | solution.py:717
  329.8 23.7 %collective-permute-start.45 = (bf16[48,1536]{1,0:T(8,128)(2,1)}, bf16[48,1536]{1,0:T(8,128)(2,1)}, u32[]{:S(2)}, u32[]{:S(2)}) collective-permute-start(bf16[48,1536]{1,0:T(8,128)(2,1)} %get-tuple-element.567), channel_id=1, source_target_pairs={{0,24},{1,25},{2,26},{3,27},{4,28},{5,29},{6,30},{7,31},{8,0},{9,1... | collective-permute-start | bytes 442376 | tf_op jit(solution)/shard_map/ppermute | solution.py:717
  354.6 24.2 %collective-permute-start.50 = (bf16[192,1920]{1,0:T(8,128)(2,1)}, bf16[192,1920]{1,0:T(8,128)(2,1)S(1)}, u32[]{:S(2)}, u32[]{:S(2)}) collective-permute-start(bf16[192,1920]{1,0:T(8,128)(2,1)} %fusion), channel_id=1, source_target_pairs={{0,4},{1,3},{2,6},{3,1},{4,0},{5,7},{6,2},{7,5},{8,12},{9,11},{10,... | collective-permute-start | bytes 2211848 | tf_op jit(solution)/shard_map/ppermute | solution.py:717
  355.2 23.6 %collective-permute-start.51 = (bf16[768,1152]{1,0:T(8,128)(2,1)}, bf16[768,1152]{1,0:T(8,128)(2,1)}, u32[]{:S(2)}, u32[]{:S(2)}) collective-permute-start(bf16[768,1152]{1,0:T(8,128)(2,1)} %get-tuple-element.404), channel_id=1, source_target_pairs={{0,1},{1,0},{2,3},{3,2},{4,5},{5,4},{6,7},{7,6},{8,9},{9,8},{10,11... | collective-permute-start | bytes 5308424 | tf_op jit(solution)/shard_map/ppermute | solution.py:717
  357.2 21.5 %collective-permute-start.49 = (bf16[24,1536]{1,0:T(8,128)(2,1)}, bf16[24,1536]{1,0:T(8,128)(2,1)S(1)}, u32[]{:S(2)}, u32[]{:S(2)}) collective-permute-start(bf16[24,1536]{1,0:T(8,128)(2,1)} %select_convert_fusion.3), channel_id=1, source_target_pairs={{0,1},{1,0},{2,3},{3,2},{4,5},{5,4},{6,7},{7,6},{8,9},{9,8},{10,11... | collective-permute-start | bytes 221192 | tf_op jit(solution)/shard_map/ppermute | solution.py:717
  357.7 21.0 %collective-permute-start.52 = (bf16[768,128]{1,0:T(8,128)(2,1)}, bf16[768,128]{1,0:T(8,128)(2,1)}, u32[]{:S(2)}, u32[]{:S(2)}) collective-permute-start(bf16[768,128]{1,0:T(8,128)(2,1)} %get-tuple-element.405), channel_id=1, source_target_pairs={{0,1},{1,0},{2,3},{3,2},{4,5},{5,4},{6,7},{7,6},{8,9},{9,8},{10,11... | collective-permute-start | bytes 589832 | tf_op jit(solution)/shard_map/ppermute | solution.py:717
  383.7 22.1 %collective-permute-start.55 = (bf16[48,1920]{1,0:T(8,128)(2,1)}, bf16[48,1920]{1,0:T(8,128)(2,1)}, u32[]{:S(2)}, u32[]{:S(2)}) collective-permute-start(bf16[48,1920]{1,0:T(8,128)(2,1)} %get-tuple-element.559), channel_id=1, source_target_pairs={{0,8},{1,9},{2,10},{3,11},{4,12},{5,13},{6,14},{7,15},{8,16},{9,17... | collective-permute-start | bytes 552968 | tf_op jit(solution)/shard_map/ppermute | solution.py:717
  385.7 20.2 %collective-permute-start.56 = (bf16[384,1280]{1,0:T(8,128)(2,1)}, bf16[384,1280]{1,0:T(8,128)(2,1)}, u32[]{:S(2)}, u32[]{:S(2)}) collective-permute-start(bf16[384,1280]{1,0:T(8,128)(2,1)} %pad_maximum_fusion.4), channel_id=1, source_target_pairs={{0,2},{1,5},{2,0},{3,7},{4,6},{5,1},{6,4},{7,3},{8,10},{9,13},{10,... | collective-permute-start | bytes 2949128 | tf_op jit(solution)/shard_map/ppermute | solution.py:717
  386.9 19.0 %collective-permute-start.57 = (bf16[768,768]{1,0:T(8,128)(2,1)}, bf16[768,768]{1,0:T(8,128)(2,1)}, u32[]{:S(2)}, u32[]{:S(2)}) collective-permute-start(bf16[768,768]{1,0:T(8,128)(2,1)} %get-tuple-element.419), channel_id=1, source_target_pairs={{0,1},{1,0},{2,3},{3,2},{4,5},{5,4},{6,7},{7,6},{8,9},{9,8},{10,11... | collective-permute-start | bytes 3538952 | tf_op jit(solution)/shard_map/ppermute | solution.py:717
  389.5 16.4 %collective-permute-start.54 = (bf16[48,1920]{1,0:T(8,128)(2,1)}, bf16[48,1920]{1,0:T(8,128)(2,1)}, u32[]{:S(2)}, u32[]{:S(2)}) collective-permute-start(bf16[48,1920]{1,0:T(8,128)(2,1)} %get-tuple-element.560), channel_id=1, source_target_pairs={{0,16},{1,17},{2,18},{3,19},{4,20},{5,21},{6,22},{7,23},{8,24},{9,... | collective-permute-start | bytes 552968 | tf_op jit(solution)/shard_map/ppermute | solution.py:717
  391.0 14.9 %collective-permute-start.53 = (bf16[48,1920]{1,0:T(8,128)(2,1)}, bf16[48,1920]{1,0:T(8,128)(2,1)}, u32[]{:S(2)}, u32[]{:S(2)}) collective-permute-start(bf16[48,1920]{1,0:T(8,128)(2,1)} %get-tuple-element.561), channel_id=1, source_target_pairs={{0,24},{1,25},{2,26},{3,27},{4,28},{5,29},{6,30},{7,31},{8,0},{9,1... | collective-permute-start | bytes 552968 | tf_op jit(solution)/shard_map/ppermute | solution.py:717
  421.7 24.9 %collective-permute-start.64 = (bf16[48,1280]{1,0:T(8,128)(2,1)}, bf16[48,1280]{1,0:T(8,128)(2,1)}, u32[]{:S(2)}, u32[]{:S(2)}) collective-permute-start(bf16[48,1280]{1,0:T(8,128)(2,1)} %get-tuple-element.571), channel_id=1, source_target_pairs={{0,8},{1,9},{2,10},{3,11},{4,12},{5,13},{6,14},{7,15},{8,16},{9,17... | collective-permute-start | bytes 368648 | tf_op jit(solution)/shard_map/ppermute | solution.py:717
  421.8 24.9 %collective-permute-start.63 = (bf16[48,1280]{1,0:T(8,128)(2,1)}, bf16[48,1280]{1,0:T(8,128)(2,1)}, u32[]{:S(2)}, u32[]{:S(2)}) collective-permute-start(bf16[48,1280]{1,0:T(8,128)(2,1)} %get-tuple-element.572), channel_id=1, source_target_pairs={{0,16},{1,17},{2,18},{3,19},{4,20},{5,21},{6,22},{7,23},{8,24},{9,... | collective-permute-start | bytes 368648 | tf_op jit(solution)/shard_map/ppermute | solution.py:717
  424.1 22.6 %collective-permute-start.62 = (bf16[48,1280]{1,0:T(8,128)(2,1)}, bf16[48,1280]{1,0:T(8,128)(2,1)}, u32[]{:S(2)}, u32[]{:S(2)}) collective-permute-start(bf16[48,1280]{1,0:T(8,128)(2,1)} %get-tuple-element.573), channel_id=1, source_target_pairs={{0,24},{1,25},{2,26},{3,27},{4,28},{5,29},{6,30},{7,31},{8,0},{9,1... | collective-permute-start | bytes 368648 | tf_op jit(solution)/shard_map/ppermute | solution.py:717
  426.2 20.5 %collective-permute-start.61 = (bf16[384,1536]{1,0:T(8,128)(2,1)S(1)}, bf16[384,1536]{1,0:T(8,128)(2,1)}, u32[]{:S(2)}, u32[]{:S(2)}) collective-permute-start(bf16[384,1536]{1,0:T(8,128)(2,1)S(1)} %pad_maximum_fusion.3), channel_id=1, source_target_pairs={{0,2},{1,5},{2,0},{3,7},{4,6},{5,1},{6,4},{7,3},{8,10},{9,13},{10,... | collective-permute-start | bytes 3538952 | tf_op jit(solution)/shard_map/ppermute | solution.py:717
  427.1 19.5 %collective-permute-start.65 = (bf16[768,768]{1,0:T(8,128)(2,1)}, bf16[768,768]{1,0:T(8,128)(2,1)S(1)}, u32[]{:S(2)}, u32[]{:S(2)}) collective-permute-start(bf16[768,768]{1,0:T(8,128)(2,1)} %get-tuple-element.440), channel_id=1, source_target_pairs={{0,1},{1,0},{2,3},{3,2},{4,5},{5,4},{6,7},{7,6},{8,9},{9,8},{10,11... | collective-permute-start | bytes 3538952 | tf_op jit(solution)/shard_map/ppermute | solution.py:717
  450.4 20.9 %collective-permute-start.66 = (bf16[192,1536]{1,0:T(8,128)(2,1)}, bf16[192,1536]{1,0:T(8,128)(2,1)}, u32[]{:S(2)}, u32[]{:S(2)}) collective-permute-start(bf16[192,1536]{1,0:T(8,128)(2,1)} %fusion.3), channel_id=1, source_target_pairs={{0,4},{1,3},{2,6},{3,1},{4,0},{5,7},{6,2},{7,5},{8,12},{9,11},{10,... | collective-permute-start | bytes 1769480 | tf_op jit(solution)/shard_map/ppermute | solution.py:717
  451.6 19.7 %collective-permute-start.69 = (bf16[768,768]{1,0:T(8,128)(2,1)}, bf16[768,768]{1,0:T(8,128)(2,1)}, u32[]{:S(2)}, u32[]{:S(2)}) collective-permute-start(bf16[768,768]{1,0:T(8,128)(2,1)} %get-tuple-element.456), channel_id=1, source_target_pairs={{0,1},{1,0},{2,3},{3,2},{4,5},{5,4},{6,7},{7,6},{8,9},{9,8},{10,11... | collective-permute-start | bytes 3538952 | tf_op jit(solution)/shard_map/ppermute | solution.py:717
  479.2 25.1 %collective-permute-start.72 = (bf16[48,1536]{1,0:T(8,128)(2,1)}, bf16[48,1536]{1,0:T(8,128)(2,1)}, u32[]{:S(2)}, u32[]{:S(2)}) collective-permute-start(bf16[48,1536]{1,0:T(8,128)(2,1)} %get-tuple-element.562), channel_id=1, source_target_pairs={{0,8},{1,9},{2,10},{3,11},{4,12},{5,13},{6,14},{7,15},{8,16},{9,17... | collective-permute-start | bytes 442376 | tf_op jit(solution)/shard_map/ppermute | solution.py:717
  479.3 25.1 %collective-permute-start.71 = (bf16[48,1536]{1,0:T(8,128)(2,1)}, bf16[48,1536]{1,0:T(8,128)(2,1)}, u32[]{:S(2)}, u32[]{:S(2)}) collective-permute-start(bf16[48,1536]{1,0:T(8,128)(2,1)} %get-tuple-element.563), channel_id=1, source_target_pairs={{0,16},{1,17},{2,18},{3,19},{4,20},{5,21},{6,22},{7,23},{8,24},{9,... | collective-permute-start | bytes 442376 | tf_op jit(solution)/shard_map/ppermute | solution.py:717
  480.7 23.6 %collective-permute-start.70 = (bf16[48,1536]{1,0:T(8,128)(2,1)}, bf16[48,1536]{1,0:T(8,128)(2,1)}, u32[]{:S(2)}, u32[]{:S(2)}) collective-permute-start(bf16[48,1536]{1,0:T(8,128)(2,1)} %get-tuple-element.564), channel_id=1, source_target_pairs={{0,24},{1,25},{2,26},{3,27},{4,28},{5,29},{6,30},{7,31},{8,0},{9,1... | collective-permute-start | bytes 442376 | tf_op jit(solution)/shard_map/ppermute | solution.py:717
  485.0 19.4 %collective-permute-start.73 = (bf16[384,1920]{1,0:T(8,128)(2,1)S(1)}, bf16[384,1920]{1,0:T(8,128)(2,1)S(1)}, u32[]{:S(2)}, u32[]{:S(2)}) collective-permute-start(bf16[384,1920]{1,0:T(8,128)(2,1)S(1)} %pad_maximum_fusion.1), channel_id=1, source_target_pairs={{0,2},{1,5},{2,0},{3,7},{4,6},{5,1},{6,4},{7,3},{8,10},{9,13},{10,... | collective-permute-start | bytes 4423688 | tf_op jit(solution)/shard_map/ppermute | solution.py:717
  504.5 11.8 %collective-permute-start.76 = (bf16[768,1152]{1,0:T(8,128)(2,1)S(1)}, bf16[768,1152]{1,0:T(8,128)(2,1)S(1)}, u32[]{:S(2)}, u32[]{:S(2)}) collective-permute-start(bf16[768,1152]{1,0:T(8,128)(2,1)S(1)} %copy-done.87), channel_id=1, source_target_pairs={{0,1},{1,0},{2,3},{3,2},{4,5},{5,4},{6,7},{7,6},{8,9},{9,8},{10,11... | collective-permute-start | bytes 5308424 | tf_op jit(solution)/shard_map/ppermute | solution.py:717
  504.7 11.5 %collective-permute-start.75 = (bf16[192,1920]{1,0:T(8,128)(2,1)S(1)}, bf16[192,1920]{1,0:T(8,128)(2,1)S(1)}, u32[]{:S(2)}, u32[]{:S(2)}) collective-permute-start(bf16[192,1920]{1,0:T(8,128)(2,1)S(1)} %fusion.1), channel_id=1, source_target_pairs={{0,4},{1,3},{2,6},{3,1},{4,0},{5,7},{6,2},{7,5},{8,12},{9,11},{10,... | collective-permute-start | bytes 2211848 | tf_op jit(solution)/shard_map/ppermute | solution.py:717
  518.0 16.0 %collective-permute-start.79 = (bf16[48,1920]{1,0:T(8,128)(2,1)S(1)}, bf16[48,1920]{1,0:T(8,128)(2,1)S(1)}, u32[]{:S(2)}, u32[]{:S(2)}) collective-permute-start(bf16[48,1920]{1,0:T(8,128)(2,1)S(1)} %get-tuple-element.557), channel_id=1, source_target_pairs={{0,16},{1,17},{2,18},{3,19},{4,20},{5,21},{6,22},{7,23},{8,24},{9,... | collective-permute-start | bytes 552968 | tf_op jit(solution)/shard_map/ppermute | solution.py:717
  519.5 14.5 %collective-permute-start.78 = (bf16[48,1920]{1,0:T(8,128)(2,1)S(1)}, bf16[48,1920]{1,0:T(8,128)(2,1)S(1)}, u32[]{:S(2)}, u32[]{:S(2)}) collective-permute-start(bf16[48,1920]{1,0:T(8,128)(2,1)S(1)} %get-tuple-element.558), channel_id=1, source_target_pairs={{0,24},{1,25},{2,26},{3,27},{4,28},{5,29},{6,30},{7,31},{8,0},{9,1... | collective-permute-start | bytes 552968 | tf_op jit(solution)/shard_map/ppermute | solution.py:717
  522.5 14.2 %collective-permute-start.81 = (bf16[384,1280]{1,0:T(8,128)(2,1)S(1)}, bf16[384,1280]{1,0:T(8,128)(2,1)S(1)}, u32[]{:S(2)}, u32[]{:S(2)}) collective-permute-start(bf16[384,1280]{1,0:T(8,128)(2,1)S(1)} %pad_maximum_fusion.5), channel_id=1, source_target_pairs={{0,2},{1,5},{2,0},{3,7},{4,6},{5,1},{6,4},{7,3},{8,10},{9,13},{10,... | collective-permute-start | bytes 2949128 | tf_op jit(solution)/shard_map/ppermute | solution.py:717
  (114 other events, 580.1 us)

commit v4 on v3

v4 whole, which is shorter than its diff:
```python
import jax
import jax.numpy as jnp
from jax import lax
from jax.experimental import pallas as pl
from jax.experimental.pallas import tpu as pltpu
from jax.sharding import PartitionSpec as P

HEADS = 12
HEAD_WIDTH = 64
LANES = 128
PAIRS = HEADS * HEAD_WIDTH // LANES
LOW = jnp.bfloat16
WIDE = jnp.float32
norm_eps = 1e-06
AXES = ("dp", "fsdp")
VMEM_LIMIT = 60 * 1024 * 1024
FORWARD_TILE = 768
BACKWARD_TILE = 768


def cost(flops, moved, hard=0):
    return pl.CostEstimate(flops=int(flops), bytes_accessed=int(moved), transcendentals=int(hard))


def params():
    return pltpu.CompilerParams(vmem_limit_bytes=VMEM_LIMIT)


def vmem_specs(count):
    return [pl.BlockSpec(memory_space=pltpu.VMEM)] * count


def any_specs(count):
    return [pl.BlockSpec(memory_space=pl.ANY)] * count


def dot(a, b):
    return jnp.dot(a, b, preferred_element_type=WIDE)


def dot_nt(a, b):
    return lax.dot_general(a, b, (((1,), (1,)), ((), ())), preferred_element_type=WIDE)


def dot_tn(a, b):
    return lax.dot_general(a, b, (((0,), (0,)), ((), ())), preferred_element_type=WIDE)


def place_of(spot, owner, block):
    z, x, y = spot[0], spot[1], spot[2]
    first, second, zr = block // 8, (block // 4) % 2, block % 4
    bz = lax.rem(z - zr + 4, 4)
    bx = lax.rem(x + jnp.where(owner == 0, second, first), 2)
    by = lax.rem(y + jnp.where(owner == 0, first, second), 2)
    return (bz * 2 + bx) * 2 + by


def piece_copies(spot, refs, target, sems, column, half, sides=(0, 1)):
    c = spot[3]
    rows = refs[0].shape[0] // 8
    copies = []
    for side in sides:
        owner = c if side == 0 else 1 - c
        to = pl.multiple_of(owner * half, LANES)
        for block in range(16):
            start = pl.multiple_of(place_of(spot, owner, block) * rows, 16)
            copies.append(
                pltpu.make_async_copy(
                    refs[2 * side + block // 8].at[
                        pl.ds((block % 8) * rows, rows), pl.ds(column, half)
                    ],
                    target.at[pl.ds(start, rows), pl.ds(to, half)],
                    sems.at[side * 16 + block],
                )
            )
    return copies


def norm_rows(v):
    center = v - jnp.mean(v, axis=-1, keepdims=True)
    r = lax.rsqrt(jnp.mean(center * center, axis=-1, keepdims=True) + norm_eps)
    return center * r, r


def norm_back(v, gain, d):
    xh, r = norm_rows(v)
    dg = d * gain
    m1 = jnp.mean(dg, axis=-1, keepdims=True)
    m2 = jnp.mean(dg * xh, axis=-1, keepdims=True)
    return (
        r * (dg - m1 - xh * m2),
        jnp.sum(d * xh, axis=0, keepdims=True),
        jnp.sum(d, axis=0, keepdims=True),
    )


GAIN1, GAIN2, BQ, BV, BO, BD, SH1, SH2 = range(8)


def qkv_forward(spot, weight, h, table):
    refs, column = weight
    rows, width = h.shape
    wide = 3 * width
    tile = width

    def body(spot_ref, r0, r1, r2, r3, h_ref, t_ref, qkv_ref, a_ref, w_ref, sems):
        copies = piece_copies(spot_ref, (r0, r1, r2, r3), w_ref, sems, column, wide // 2)
        for copy in copies:
            copy.start()
        xh, r = norm_rows(h_ref[...])
        a_ref[...] = (xh * t_ref[GAIN1 : GAIN1 + 1, :] + t_ref[SH1 : SH1 + 1, :]).astype(LOW)
        for copy in copies:
            copy.wait()
        a = a_ref[...]
        for n in range(wide // tile):
            s = n * tile
            out = dot(a, w_ref[:, s : s + tile])
            if s < width:
                out = out + t_ref[BQ : BQ + 1, s : s + tile]
            elif s >= 2 * width:
                out = out + t_ref[BV : BV + 1, s - 2 * width : s - 2 * width + tile]
            qkv_ref[:, s : s + tile] = out.astype(LOW)

    return pl.pallas_call(
        body,
        out_shape=[
            jax.ShapeDtypeStruct((rows, wide), LOW),
            jax.ShapeDtypeStruct((rows, width), LOW),
        ],
        in_specs=[pl.BlockSpec(memory_space=pltpu.SMEM)] + any_specs(4) + vmem_specs(2),
        out_specs=vmem_specs(2),
        scratch_shapes=[pltpu.VMEM((width, wide), LOW), pltpu.SemaphoreType.DMA((32,))],
        compiler_params=params(),
        cost_estimate=cost(2 * rows * width * wide, 2 * width * wide + 9 * rows * width),
        name="qkv_forward",
    )(spot, *refs, h, table)


def attention_forward(lengths, qkv, begin, pairs):
    rows, wide = qkv.shape
    width = pairs * LANES

    def body(len_ref, q_ref, k_ref, v_ref, o_ref, lse_ref):
        pair = pl.program_id(0)
        lane = lax.broadcasted_iota(jnp.int32, (1, LANES), 1)
        key = lax.broadcasted_iota(jnp.int32, (1, rows), 1)
        shut = jnp.where(key < len_ref[0], 0.0, -1e30)
        q = q_ref[...] * jnp.asarray(HEAD_WIDTH**-0.5, LOW)
        k = k_ref[...]
        v = v_ref[...]
        outs = []
        stats = jnp.where(pair == 0, jnp.zeros((rows, LANES), WIDE), lse_ref[...])
        for side in range(2):
            inside = (lane >= HEAD_WIDTH) == (side == 1)
            qs = jnp.where(inside, q, jnp.zeros_like(q))
            s = dot_nt(qs, k) + shut
            peak = jnp.max(s, axis=1, keepdims=True)
            e = jnp.exp(s - peak)
            total = jnp.sum(e, axis=1, keepdims=True)
            p = (e * (1.0 / total)).astype(LOW)
            outs.append(dot(p, v))
            stats = jnp.where(lane == pair * 2 + side, peak + jnp.log(total), stats)
        lse_ref[...] = stats
        o_ref[...] = jnp.where(lane < HEAD_WIDTH, outs[0], outs[1]).astype(LOW)

    return pl.pallas_call(
        body,
        out_shape=[
            jax.ShapeDtypeStruct((rows, width), LOW),
            jax.ShapeDtypeStruct((rows, LANES), WIDE),
        ],
        grid_spec=pltpu.PrefetchScalarGridSpec(
            num_scalar_prefetch=1,
            grid=(pairs,),
            in_specs=[
                pl.BlockSpec((rows, LANES), lambda p, n: (0, p + begin)),
                pl.BlockSpec((rows, LANES), lambda p, n: (0, p + begin + PAIRS)),
                pl.BlockSpec((rows, LANES), lambda p, n: (0, p + begin + 2 * PAIRS)),
            ],
            out_specs=[
                pl.BlockSpec((rows, LANES), lambda p, n: (0, p)),
                pl.BlockSpec((rows, LANES), lambda p, n: (0, 0)),
            ],
        ),
        compiler_params=params(),
        cost_estimate=cost(16 * rows * rows * width, 8 * rows * width, 2 * pairs * rows * rows),
        name="attention_forward",
    )(lengths, qkv, qkv, qkv)


def out_forward(spot, weight, h, mixed, table):
    refs, column = weight
    rows, width = h.shape
    part = width // 2

    def body(
        spot_ref, r0, r1, r2, r3, h_ref, m0_ref, m1_ref, t_ref, h2_ref, a_ref, w_ref, sems
    ):
        copies = piece_copies(spot_ref, (r0, r1, r2, r3), w_ref, sems, column, width // 2)
        for copy in copies:
            copy.start()
        for copy in copies:
            copy.wait()
        product = dot(m0_ref[...], w_ref[:part, :]) + dot(m1_ref[...], w_ref[part:, :])
        h2 = h_ref[...] + (product + t_ref[BO : BO + 1, :])
        h2_ref[...] = h2
        xh, r = norm_rows(h2)
        a_ref[...] = (xh * t_ref[GAIN2 : GAIN2 + 1, :] + t_ref[SH2 : SH2 + 1, :]).astype(LOW)

    return pl.pallas_call(
        body,
        out_shape=[
            jax.ShapeDtypeStruct((rows, width), WIDE),
            jax.ShapeDtypeStruct((rows, width), LOW),
        ],
        in_specs=[pl.BlockSpec(memory_space=pltpu.SMEM)] + any_specs(4) + vmem_specs(4),
        out_specs=vmem_specs(2),
        scratch_shapes=[pltpu.VMEM((width, width), LOW), pltpu.SemaphoreType.DMA((32,))],
        compiler_params=params(),
        cost_estimate=cost(2 * rows * width * width, 2 * width * width + 12 * rows * width),
        name="out_forward",
    )(spot, *refs, h, *mixed, table)


def gelu_parts(u):
    cdf = 0.5 * (1.0 + lax.erf(u * (0.5**0.5)))
    pdf = jnp.exp(-0.5 * u * u) * (0.3989422804014327)
    return cdf, pdf


def side_tiles(tiles):
    def whole(s, n, spot):
        owner = jnp.where(s == 0, spot[3], 1 - spot[3])
        return 0, owner * tiles + n

    def mine(s, n, spot):
        return 0, jnp.where(s == 0, n, tiles - 1)

    def rest(s, n, spot):
        return 0, jnp.where(s == 0, 0, n)

    def fixed(s, n, spot):
        return 0, 0

    return whole, mine, rest, fixed


def mlp_forward(spot, up, down, base, a2, up_bias, table, first):
    rows, width = base.shape
    hidden = up_bias.shape[1]
    half = hidden // 2
    tile = FORWARD_TILE
    tiles = half // tile
    whole, mine, rest, fixed = side_tiles(tiles)
    (up_refs, up_col), (down_refs, down_col) = up, down

    def body(
        spot_ref, h_ref, a_ref, b_ref, t_ref, u0, u1, u2, u3, d0, d1, d2, d3,
        z_ref, g_ref, o_ref, wu_ref, wd_ref, sems_u, sems_d,
    ):
        side, n = pl.program_id(0), pl.program_id(1)
        ups = piece_copies(spot_ref, (u0, u1, u2, u3), wu_ref, sems_u, up_col, half)
        downs = piece_copies(spot_ref, (d0, d1, d2, d3), wd_ref, sems_d, down_col, half)

        @pl.when((side == 0) & (n == 0))
        def begin():
            for copy in ups[:16] + downs[:16] + ups[16:] + downs[16:]:
                copy.start()
            if first:
                o_ref[...] = h_ref[...] + t_ref[BD : BD + 1, :]
            else:
                o_ref[...] = h_ref[...]
            for copy in ups[:16] + downs[:16]:
                copy.wait()

        @pl.when((side == 1) & (n == 0))
        def more():
            for copy in ups[16:] + downs[16:]:
                copy.wait()

        owner = jnp.where(side == 0, spot_ref[3], 1 - spot_ref[3])
        at = pl.ds(pl.multiple_of(owner * half + n * tile, LANES), tile)
        u = dot(a_ref[...], wu_ref[:, at]) + b_ref[...]
        cdf, pdf = gelu_parts(u)
        z = (u * cdf).astype(LOW)
        z_ref[...] = z
        g_ref[...] = (cdf + u * pdf).astype(LOW)
        o_ref[...] += dot_nt(z, wd_ref[:, at])

    return pl.pallas_call(
        body,
        out_shape=[
            jax.ShapeDtypeStruct((rows, hidden), LOW),
            jax.ShapeDtypeStruct((rows, hidden), LOW),
            jax.ShapeDtypeStruct((rows, width), WIDE),
        ],
        grid_spec=pltpu.PrefetchScalarGridSpec(
            num_scalar_prefetch=1,
            grid=(2, tiles),
            in_specs=[
                pl.BlockSpec((rows, width), fixed),
                pl.BlockSpec((rows, width), fixed),
                pl.BlockSpec((1, tile), whole),
                pl.BlockSpec((8, width), fixed),
            ]
            + any_specs(8),
            out_specs=[
                pl.BlockSpec((rows, tile), whole),
                pl.BlockSpec((rows, tile), whole),
                pl.BlockSpec((rows, width), fixed),
            ],
            scratch_shapes=[
                pltpu.VMEM((width, hidden), LOW),
                pltpu.VMEM((width, hidden), LOW),
                pltpu.SemaphoreType.DMA((32,)),
                pltpu.SemaphoreType.DMA((32,)),
            ],
        ),
        compiler_params=params(),
        cost_estimate=cost(
            4 * rows * width * hidden, 4 * width * hidden + 4 * rows * hidden, 2 * rows * hidden
        ),
        name="mlp_forward",
    )(spot, base, a2, up_bias, table, *up_refs, *down_refs)


def block_starts(spot, owner, rows):
    z, x, y = spot[0], spot[1], spot[2]
    result = []
    for block in range(16):
        bz, bx, by = block // 4, (block // 2) % 2, block % 2
        zr = lax.rem(z - bz + 4, 4)
        xr = lax.rem(x + bx, 2)
        yr = lax.rem(y + by, 2)
        first = jnp.where(owner == 0, yr, xr)
        second = jnp.where(owner == 0, xr, yr)
        result.append(pl.multiple_of(((first * 2 + second) * 4 + zr) * rows, 16))
    return result


def put_blocks(value, out_ref, starts, column, width):
    rows = value.shape[0] // 16
    low = value.astype(LOW)
    for block, start in enumerate(starts):
        out_ref[pl.ds(start, rows), pl.ds(column, width)] = low[block * rows : (block + 1) * rows]


def column_sum(value):
    return jnp.sum(value.astype(WIDE), axis=0, keepdims=True)


def mlp_backward(spot, up, down, e, a2, z, slope, before):
    rows, width = e.shape
    hidden = z.shape[1]
    half = hidden // 2
    tile = BACKWARD_TILE
    tiles = half // tile
    whole, mine, rest, fixed = side_tiles(tiles)
    (up_refs, up_col), (down_refs, down_col) = up, down
    extra = [] if before is None else [before]

    def body(spot_ref, e_ref, a_ref, z_ref, s_ref, *refs):
        if extra:
            before_ref, refs = refs[0], refs[1:]
        (
            u0, u1, u2, u3, d0, d1, d2, d3,
            acc_ref, um_ref, ur_ref, dm_ref, dr_ref, bd_ref, bu_ref,
            wu_ref, wd_ref, em_ref, emt_ref, at_ref, sems_u, sems_d,
        ) = refs
        side, n = pl.program_id(0), pl.program_id(1)
        ups = piece_copies(spot_ref, (u0, u1, u2, u3), wu_ref, sems_u, up_col, half)
        downs = piece_copies(spot_ref, (d0, d1, d2, d3), wd_ref, sems_d, down_col, half)

        @pl.when((side == 0) & (n == 0))
        def begin():
            for copy in downs[:16] + ups[:16] + downs[16:] + ups[16:]:
                copy.start()
            em = e_ref[...].astype(LOW)
            em_ref[...] = em
            bd_ref[...] = column_sum(em)
            emt_ref[...] = em.T
            at_ref[...] = a_ref[...].T
            acc_ref[...] = before_ref[...] if extra else jnp.zeros_like(acc_ref)
            for copy in downs[:16] + ups[:16]:
                copy.wait()

        @pl.when((side == 1) & (n == 0))
        def more():
            for copy in downs[16:] + ups[16:]:
                copy.wait()

        owner = jnp.where(side == 0, spot_ref[3], 1 - spot_ref[3])
        at = pl.ds(pl.multiple_of(owner * half + n * tile, LANES), tile)
        starts = block_starts(spot_ref, owner, width // 16)
        du = (dot(em_ref[...], wd_ref[:, at]) * s_ref[...].astype(WIDE)).astype(LOW)
        bu_ref[...] = column_sum(du)
        down_grad = dot(emt_ref[...], z_ref[...])
        up_grad = dot(at_ref[...], du)
        acc_ref[...] += dot_nt(du, wu_ref[:, at])

        @pl.when(side == 0)
        def first_half():
            put_blocks(down_grad, dm_ref, starts, 0, tile)
            put_blocks(up_grad, um_ref, starts, 0, tile)

        @pl.when(side == 1)
        def second_half():
            put_blocks(down_grad, dr_ref, starts, 0, tile)
            put_blocks(up_grad, ur_ref, starts, 0, tile)

    return pl.pallas_call(
        body,
        out_shape=[
            jax.ShapeDtypeStruct((rows, width), WIDE),
            jax.ShapeDtypeStruct((width, half), LOW),
            jax.ShapeDtypeStruct((width, half), LOW),
            jax.ShapeDtypeStruct((width, half), LOW),
            jax.ShapeDtypeStruct((width, half), LOW),
            jax.ShapeDtypeStruct((1, width), WIDE),
            jax.ShapeDtypeStruct((1, hidden), WIDE),
        ],
        grid_spec=pltpu.PrefetchScalarGridSpec(
            num_scalar_prefetch=1,
            grid=(2, tiles),
            in_specs=[
                pl.BlockSpec((rows, width), fixed),
                pl.BlockSpec((rows, width), fixed),
                pl.BlockSpec((rows, tile), whole),
                pl.BlockSpec((rows, tile), whole),
            ]
            + [pl.BlockSpec((rows, width), fixed)] * len(extra)
            + any_specs(8),
            out_specs=[
                pl.BlockSpec((rows, width), fixed),
                pl.BlockSpec((width, tile), mine),
                pl.BlockSpec((width, tile), rest),
                pl.BlockSpec((width, tile), mine),
                pl.BlockSpec((width, tile), rest),
                pl.BlockSpec((1, width), fixed),
                pl.BlockSpec((1, tile), whole),
            ],
            scratch_shapes=[
                pltpu.VMEM((width, hidden), LOW),
                pltpu.VMEM((width, hidden), LOW),
                pltpu.VMEM((rows, width), LOW),
                pltpu.VMEM((width, rows), LOW),
                pltpu.VMEM((width, rows), LOW),
                pltpu.SemaphoreType.DMA((32,)),
                pltpu.SemaphoreType.DMA((32,)),
            ],
        ),
        compiler_params=params(),
        cost_estimate=cost(8 * rows * width * hidden, 8 * width * hidden + 4 * rows * hidden),
        name="mlp_backward",
    )(spot, e, a2, z, slope, *extra, *up_refs, *down_refs)


def middle_backward(spot, out, e, h2, mixed, acc, table):
    rows, width = e.shape
    part = width // 2
    refs, column = out

    def body(
        spot_ref, r0, r1, r2, r3, e_ref, h_ref, m0_ref, m1_ref, acc_ref, t_ref,
        e2_ref, da_ref, mine_ref, rest_ref, sums_ref, w_ref, mt_ref, ey_ref, sems,
    ):
        copies = piece_copies(spot_ref, (r0, r1, r2, r3), w_ref, sems, column, part)
        for copy in copies:
            copy.start()
        mt_ref[:part, :] = m0_ref[...].T
        mt_ref[part:, :] = m1_ref[...].T
        dv, gain, shift = norm_back(h_ref[...], t_ref[GAIN2 : GAIN2 + 1, :], acc_ref[...])
        e2 = e_ref[...] + dv
        e2_ref[...] = e2
        ey = e2.astype(LOW)
        ey_ref[...] = ey
        sums_ref[0:1, :] = gain
        sums_ref[1:2, :] = shift
        sums_ref[2:3, :] = column_sum(ey)
        for copy in copies:
            copy.wait()
        da_ref[...] = dot_nt(ey, w_ref[...]).astype(LOW)
        c = spot_ref[3]
        for owner, out_ref in ((c, mine_ref), (1 - c, rest_ref)):
            starts = block_starts(spot_ref, owner, width // 16)
            at = pl.ds(pl.multiple_of(owner * part, LANES), part)
            put_blocks(dot(mt_ref[...], ey_ref[:, at]), out_ref, starts, 0, part)

    return pl.pallas_call(
        body,
        out_shape=[
            jax.ShapeDtypeStruct((rows, width), WIDE),
            jax.ShapeDtypeStruct((rows, width), LOW),
            jax.ShapeDtypeStruct((width, part), LOW),
            jax.ShapeDtypeStruct((width, part), LOW),
            jax.ShapeDtypeStruct((8, width), WIDE),
        ],
        in_specs=[pl.BlockSpec(memory_space=pltpu.SMEM)] + any_specs(4) + vmem_specs(6),
        out_specs=vmem_specs(5),
        scratch_shapes=[
            pltpu.VMEM((width, width), LOW),
            pltpu.VMEM((width, rows), LOW),
            pltpu.VMEM((rows, width), LOW),
            pltpu.SemaphoreType.DMA((32,)),
        ],
        compiler_params=params(),
        cost_estimate=cost(4 * rows * width * width, 4 * width * width + 20 * rows * width),
        name="middle_backward",
    )(spot, *refs, e, h2, *mixed, acc, table)


def attention_backward(lengths, qkv, da, mixed, lse, begin, pairs):
    rows, wide = qkv.shape
    width = pairs * LANES

    def body(len_ref, q_ref, k_ref, v_ref, d_ref, m_ref, lse_ref, out_ref, row_ref):
        pair = pl.program_id(0)

        @pl.when(pair == 0)
        def start():
            row_ref[...] = lse_ref[...].T

        lane = lax.broadcasted_iota(jnp.int32, (1, LANES), 1)
        sub = lax.broadcasted_iota(jnp.int32, (LANES, 1), 0)
        key = lax.broadcasted_iota(jnp.int32, (rows, 1), 0)
        shut = jnp.where(key < len_ref[0], 0.0, -1e30)
        scale = jnp.asarray(HEAD_WIDTH**-0.5, LOW)
        q = q_ref[...] * scale
        k = k_ref[...]
        v = v_ref[...]
        d = d_ref[...]
        kt = k.T * scale
        prod = (d.astype(WIDE) * m_ref[...].astype(WIDE)).T
        dks, dvs = [], []
        dqt = jnp.zeros((LANES, rows), WIDE)
        for side in range(2):
            inside = (lane >= HEAD_WIDTH) == (side == 1)
            down = (sub >= HEAD_WIDTH) == (side == 1)
            ks = jnp.where(inside, k, jnp.zeros_like(k))
            vs = jnp.where(inside, v, jnp.zeros_like(v))
            kts = jnp.where(down, kt, jnp.zeros_like(kt))
            first = side * HEAD_WIDTH
            delta = jnp.sum(prod[first : first + HEAD_WIDTH], axis=0, keepdims=True)
            log_total = row_ref[pl.ds(pair * 2 + side, 1), :]
            p = jnp.exp((dot_nt(ks, q) + shut) - log_total)
            dp = dot_nt(vs, d)
            dvs.append(dot(p.astype(LOW), d))
            ds = (p * (dp - delta)).astype(LOW)
            dks.append(dot(ds, q))
            dqt = dqt + dot(kts, ds)
        dq = dqt.T
        dk = jnp.where(lane < HEAD_WIDTH, dks[0], dks[1])
        dv = jnp.where(lane < HEAD_WIDTH, dvs[0], dvs[1])
        for n, value in enumerate((dq, dk, dv)):
            at = pl.ds(pl.multiple_of(n * width + pair * LANES, LANES), LANES)
            out_ref[:, at] = value.astype(LOW)

    return pl.pallas_call(
        body,
        out_shape=jax.ShapeDtypeStruct((rows, 3 * width), LOW),
        grid_spec=pltpu.PrefetchScalarGridSpec(
            num_scalar_prefetch=1,
            grid=(pairs,),
            in_specs=[
                pl.BlockSpec((rows, LANES), lambda p, n: (0, p + begin)),
                pl.BlockSpec((rows, LANES), lambda p, n: (0, p + begin + PAIRS)),
                pl.BlockSpec((rows, LANES), lambda p, n: (0, p + begin + 2 * PAIRS)),
                pl.BlockSpec((rows, LANES), lambda p, n: (0, p + begin)),
                pl.BlockSpec((rows, LANES), lambda p, n: (0, p)),
                pl.BlockSpec((rows, LANES), lambda p, n: (0, 0)),
            ],
            out_specs=pl.BlockSpec((rows, 3 * width), lambda p, n: (0, 0)),
            scratch_shapes=[pltpu.VMEM((LANES, rows), WIDE)],
        ),
        compiler_params=params(),
        cost_estimate=cost(40 * rows * rows * width, 16 * rows * width, 2 * pairs * rows * rows),
        name="attention_backward",
    )(lengths, qkv, qkv, qkv, da, mixed, lse)


def qkv_backward(spot, weight, dqkv, e2, h, a1, table, others):
    rows, width = e2.shape
    wide = 3 * width
    half = wide // 2
    part = width // 2
    refs, column = weight
    sums, down_sum, up_sums = others
    hidden = sum(value.shape[1] for value in up_sums)

    def body(
        spot_ref, r0, r1, r2, r3, d0_ref, d1_ref, e_ref, h_ref, a_ref, t_ref,
        s_ref, ds_ref, u0_ref, u1_ref, o_ref, mine_ref, rest_ref, sums_ref,
        w_ref, at_ref, d_ref, acc_ref, row_ref, pack_ref, sems,
    ):
        copies = piece_copies(spot_ref, (r0, r1, r2, r3), w_ref, sems, column, half)
        for copy in copies:
            copy.start()
        at_ref[...] = a_ref[...].T
        for n in range(3):
            for side, ref in enumerate((d0_ref, d1_ref)):
                start = n * width + side * part
                d_ref[:, start : start + part] = ref[:, n * part : (n + 1) * part]
        for copy in copies:
            copy.wait()
        c = spot_ref[3]
        order = []
        for owner, out_ref in ((c, mine_ref), (1 - c, rest_ref)):
            starts = block_starts(spot_ref, owner, width // 16)
            at = pl.ds(pl.multiple_of(owner * half, LANES), half)
            put_blocks(dot(at_ref[...], d_ref[:, at]), out_ref, starts, 0, half)
            order.append((starts, out_ref))
        acc_ref[...] = dot_nt(d_ref[...], w_ref[...])
        dv, gain, shift = norm_back(h_ref[...], t_ref[GAIN1 : GAIN1 + 1, :], acc_ref[...])
        o_ref[...] = e_ref[...] + dv
        row_ref[...] = jnp.zeros_like(row_ref)
        for row, value in (
            (GAIN1, gain),
            (GAIN2, s_ref[0:1, :]),
            (BQ, column_sum(d_ref[:, :width])),
            (BV, column_sum(d_ref[:, 2 * width :])),
            (BO, s_ref[2:3, :]),
            (BD, ds_ref[...]),
            (SH1, shift),
            (SH2, s_ref[1:2, :]),
        ):
            row_ref[row : row + 1, :] = value
        sums_ref[...] = row_ref[0:8, :]
        pack_ref[...] = row_ref[...].T
        share = hidden // 32
        per = u0_ref.shape[1] // share
        for device in range(32):
            at = device * (width // 32)
            ref, start = (u0_ref, u1_ref)[device // per], (device % per) * share
            pack_ref[at : at + 1, LANES - share :] = ref[0:1, start : start + share]
        for starts, out_ref in order:
            put_blocks(pack_ref[...], out_ref, starts, half, LANES)

    return pl.pallas_call(
        body,
        out_shape=[
            jax.ShapeDtypeStruct((rows, width), WIDE),
            jax.ShapeDtypeStruct((width, half + LANES), LOW),
            jax.ShapeDtypeStruct((width, half + LANES), LOW),
            jax.ShapeDtypeStruct((8, width), WIDE),
        ],
        in_specs=[pl.BlockSpec(memory_space=pltpu.SMEM)] + any_specs(4) + vmem_specs(10),
        out_specs=vmem_specs(4),
        scratch_shapes=[
            pltpu.VMEM((width, wide), LOW),
            pltpu.VMEM((width, rows), LOW),
            pltpu.VMEM((rows, wide), LOW),
            pltpu.VMEM((rows, width), WIDE),
            pltpu.VMEM((LANES, width), WIDE),
            pltpu.VMEM((width, LANES), WIDE),
            pltpu.SemaphoreType.DMA((32,)),
        ],
        compiler_params=params(),
        cost_estimate=cost(4 * rows * width * wide, 4 * width * wide + 16 * rows * width),
        name="qkv_backward",
    )(spot, *refs, *dqkv, e2, h, a1, table, sums, down_sum, *up_sums)


def small_forward(spot, refs, column, hidden):
    rows = refs[0].shape[0] // 8
    width = 16 * rows

    def body(spot_ref, r0, r1, t_ref, b_ref, w_ref, sems):
        copies = []
        for block in range(16):
            start = pl.multiple_of(place_of(spot_ref, spot_ref[3], block) * rows, 16)
            copies.append(
                pltpu.make_async_copy(
                    (r0, r1)[block // 8].at[pl.ds((block % 8) * rows, rows), pl.ds(column, LANES)],
                    w_ref.at[pl.ds(start, rows), :],
                    sems.at[block],
                )
            )
        for copy in copies:
            copy.start()
        for copy in copies:
            copy.wait()
        values = w_ref[...].astype(WIDE)
        t_ref[...] = values.T[0:8, :]
        share = hidden // 32
        for device in range(32):
            at = device * (width // 32)
            b_ref[0:1, device * share : (device + 1) * share] = values[
                at : at + 1, LANES - share :
            ]

    return pl.pallas_call(
        body,
        out_shape=[
            jax.ShapeDtypeStruct((8, width), WIDE),
            jax.ShapeDtypeStruct((1, hidden), WIDE),
        ],
        in_specs=[pl.BlockSpec(memory_space=pltpu.SMEM)] + any_specs(2),
        out_specs=vmem_specs(2),
        scratch_shapes=[pltpu.VMEM((width, LANES), LOW), pltpu.SemaphoreType.DMA((16,))],
        compiler_params=params(),
        cost_estimate=cost(0, 4 * width * LANES),
        name="small_forward",
    )(spot, *refs[:2])


def rows_spec(height, width, index):
    return pl.BlockSpec((height, width), lambda i: (index, 0))


def sum_call(body, ins, outs, out_specs, name, spot=None):
    specs = [rows_spec(height, value.shape[1], index) for value, height, index in ins]
    moved = sum(2 * height * value.shape[1] for value, height, index in ins)
    first = [] if spot is None else [spot]
    return pl.pallas_call(
        body,
        out_shape=outs,
        grid=(1,),
        in_specs=[pl.BlockSpec(memory_space=pltpu.SMEM)] * len(first) + specs,
        out_specs=out_specs,
        compiler_params=params(),
        cost_estimate=cost(0, 2 * moved),
        name=name,
    )(*first, *(value for value, height, index in ins))


def wide_sum(refs):
    total = refs[0][...].astype(WIDE)
    for ref in refs[1:]:
        total = total + ref[...].astype(WIDE)
    return total


def sum_pieces(mines, gots, arrived, height, index):
    count = len(mines)
    width = sum(mine.shape[1] for mine in mines)

    def body(*refs):
        out_ref = refs[-1]
        start = 0
        for n in range(count):
            half = refs[n].shape[1]
            total = wide_sum((refs[n], refs[count + n]))
            for ref in refs[2 * count : -1]:
                total = total + ref[:, start : start + half].astype(WIDE)
            out_ref[:, start : start + half] = total.astype(LOW)
            start = start + half

    ins = [(value, height, index) for value in (*mines, *gots, *arrived)]
    out = jax.ShapeDtypeStruct((height, width), LOW)
    return sum_call(body, ins, out, rows_spec(height, width, 0), "sum_pieces")


def sum_blocks(mines, gots, arrived):
    count = len(mines)
    height = mines[0].shape[0] // 4
    rows = height // 4
    width = sum(mine.shape[1] for mine in mines)

    def body(*refs):
        outs = refs[-4:]
        start = 0
        for n in range(count):
            half = refs[n].shape[1]
            total = wide_sum((refs[n], refs[count + n]))
            for ref in refs[2 * count : -4]:
                total = total + ref[:, start : start + half].astype(WIDE)
            for block, out_ref in enumerate(outs):
                out_ref[:, start : start + half] = total[
                    block * rows : (block + 1) * rows
                ].astype(out_ref.dtype)
            start = start + half

    ins = [(value, height, 0) for value in (*mines, *gots, *arrived)]
    outs = [jax.ShapeDtypeStruct((rows, width), WIDE)]
    outs += [jax.ShapeDtypeStruct((rows, width), LOW)] * 3
    return sum_call(body, ins, outs, [rows_spec(rows, width, 0)] * 4, "sum_blocks")


def sum_last(spot, own, arrived):
    rows, width = own.shape

    def body(spot_ref, *refs):
        kept_ref, sent_ref = refs[-2:]
        total = wide_sum(refs[:-2])
        low, high = total[: rows // 2], total[rows // 2 :]
        c = spot_ref[3]
        kept_ref[...] = jnp.where(c == 0, low, high)
        sent_ref[...] = jnp.where(c == 0, high, low).astype(LOW)

    ins = [(value, rows, 0) for value in (own, *arrived)]
    outs = [jax.ShapeDtypeStruct((rows // 2, width), kind) for kind in (WIDE, LOW)]
    return sum_call(body, ins, outs, [rows_spec(rows // 2, width, 0)] * 2, "sum_last", spot)


def finish_mlp(spot, parts, shapes):
    down_shape, up_shape, out_shape = shapes
    layers = len(parts)
    half = up_shape[2] // 4
    small = out_shape[2] // 2

    def body(spot_ref, *refs):
        down_ref, up_ref, out_ref = refs[-3:]
        c = spot_ref[3]
        at = 0
        for layer in range(layers):
            for part in range(2):
                for owner, ref in ((c, refs[at]), (1 - c, refs[at + 1])):
                    start = pl.multiple_of(part * 2 * half + owner * half, LANES)
                    values = ref[:, :half].astype(WIDE)
                    down_ref[layer, pl.ds(start, half), :] = values.T
                    up_ref[layer, :, pl.ds(start, half)] = ref[:, half : 2 * half].astype(WIDE)
                    if part == 0:
                        start = pl.multiple_of(owner * small, LANES)
                        out_ref[layer, :, pl.ds(start, small)] = ref[
                            :, 2 * half : 2 * half + small
                        ].astype(WIDE)
                at = at + 2

    flat = [value for layer in parts for part in layer for value in part]
    return pl.pallas_call(
        body,
        out_shape=[jax.ShapeDtypeStruct(shape, WIDE) for shape in shapes],
        in_specs=[pl.BlockSpec(memory_space=pltpu.SMEM)] + vmem_specs(len(flat)),
        out_specs=vmem_specs(3),
        compiler_params=params(),
        cost_estimate=cost(0, 16 * sum(value.size for value in flat)),
        name="finish_mlp",
    )(spot, *flat)


def finish_qkv(spot, parts, shapes):
    share = shapes[3][1]
    half = shapes[0][2] // 2

    def body(spot_ref, *refs):
        qkv_ref, gain_ref, bias_ref, up_ref = refs[-4:]
        c = spot_ref[3]
        for layer in range(len(parts)):
            kept_ref, got_ref = refs[2 * layer], refs[2 * layer + 1]
            for owner, ref in ((c, kept_ref), (1 - c, got_ref)):
                start = pl.multiple_of(owner * half, LANES)
                qkv_ref[layer, :, pl.ds(start, half)] = ref[:, :half].astype(WIDE)
            packed = kept_ref[:, half : half + LANES]
            columns = packed.T
            gain_ref[layer] = columns[0:2, :]
            bias_ref[layer] = columns[2:8, :]
            up_ref[layer : layer + 1, :] = packed[0:1, LANES - share :]

    flat = [value for part in parts for value in part]
    return pl.pallas_call(
        body,
        out_shape=[jax.ShapeDtypeStruct(shape, WIDE) for shape in shapes],
        in_specs=[pl.BlockSpec(memory_space=pltpu.SMEM)] + vmem_specs(len(flat)),
        out_specs=vmem_specs(4),
        compiler_params=params(),
        cost_estimate=cost(0, 8 * sum(value.size for value in flat)),
        name="finish_qkv",
    )(spot, *flat)


def linear(z, x, y, c):
    return ((z * 2 + x) * 2 + y) * 2 + c


def pairs_of(step):
    result = []
    for z in range(4):
        for x in range(2):
            for y in range(2):
                for c in range(2):
                    result.append((linear(z, x, y, c), linear(*step(z, x, y, c))))
    return result


TO_CORE = pairs_of(lambda z, x, y, c: (z, x, y, 1 - c))
TO_Z = [pairs_of(lambda z, x, y, c, n=n: ((z + n) % 4, x, y, c)) for n in range(4)]
TO_XY = pairs_of(lambda z, x, y, c: (z, x, 1 - y, c) if c else (z, 1 - x, y, c))
TO_YX = pairs_of(lambda z, x, y, c: (z, 1 - x, y, c) if c else (z, x, 1 - y, c))


def send(value, pairs):
    return lax.ppermute(value, AXES, pairs)


def blocked():
    return lax.axis_size("dp") == 8 and lax.axis_size("fsdp") == 4


def place():
    if not blocked():
        return jnp.zeros((4,), jnp.int32)
    dp = lax.axis_index("dp")
    fsdp = lax.axis_index("fsdp")
    return jnp.stack([dp // 2, dp % 2, fsdp // 2, fsdp % 2]).astype(jnp.int32)


def halves(pieces):
    low = [piece[:, : piece.shape[1] // 2] for piece in pieces]
    high = [piece[:, piece.shape[1] // 2 :] for piece in pieces]
    return jnp.concatenate(low, axis=1), jnp.concatenate(high, axis=1)


class Chain:
    def __init__(self, steps):
        self.steps = steps
        self.result = None
        self.flying = None
        self.resume(None)

    def resume(self, arrived):
        try:
            self.waiting = self.steps.send(arrived)
        except StopIteration as end:
            self.waiting = None
            self.result = end.value

    def start(self):
        if self.waiting is not None:
            self.flying = [send(value, pairs) for value, pairs in self.waiting]


def stage(begin, work=None, hold=()):
    for chain in begin:
        chain.start()
    landing = [chain for chain in begin if chain.flying is not None and chain not in hold]
    outs = work() if work is not None else ()
    arrived, outs = lax.optimization_barrier(([chain.flying for chain in landing], outs))
    for chain, values in zip(landing, arrived):
        chain.flying = None
        chain.resume(values)
    return outs


def land(chain):
    class Held:
        flying = chain.flying

        def start(self):
            pass

        def resume(self, values):
            chain.flying = None
            chain.resume(values)

    return Held()


def offsets_of(widths):
    offsets = [0]
    for width in widths:
        offsets.append(offsets[-1] + width // 2)
    return offsets


def gather_whole(pieces):
    whole = [lax.all_gather(piece, AXES, axis=0, tiled=True) for piece in pieces]
    low, high = [
        part.reshape(4, 2, 2, -1, part.shape[1])[jnp.array([0, 3, 2, 1])] for part in halves(whole)
    ]
    width = low.shape[-1]
    own = low.transpose(2, 1, 0, 3, 4).reshape(2, -1, width)
    other = high.transpose(1, 2, 0, 3, 4).reshape(2, -1, width)
    return own[0], own[1], other[0], other[1]


def gather_steps(pieces, block):
    if not blocked():
        return gather_whole(pieces)
    ring = yield [(block, TO_Z[n]) for n in (1, 2, 3)]
    stack = jnp.concatenate([block, *ring], axis=0)
    (got,) = yield [(stack, TO_XY)]
    near = jnp.concatenate([stack, got], axis=0)
    far, near_got = yield [(near, TO_YX), (near, TO_CORE)]
    (far_got,) = yield [(far, TO_CORE)]
    return near, far, near_got, far_got


def scatter_whole(mines, rests):
    result = []
    for mine, rest in zip(mines, rests):
        rows = mine.shape[0] // 16
        half = mine.shape[1] // (3 * LANES) * (3 * LANES)
        mine, rest = mine[:, :half], rest[:, :half]
        low = mine.reshape(2, 2, 4, rows, half).transpose(2, 1, 0, 3, 4)
        high = rest.reshape(2, 2, 4, rows, half).transpose(2, 0, 1, 3, 4)
        whole = jnp.concatenate([low, high], axis=-1)[jnp.array([0, 3, 2, 1])]
        whole = whole.reshape(16 * rows, 2 * half)
        result.append(lax.psum_scatter(whole, AXES, scatter_dimension=0, tiled=True).astype(WIDE))
    return result


def cross_steps(rest):
    if not blocked():
        return rest
    (got,) = yield [(rest, TO_CORE)]
    return got


def scatter_steps(spot, mines, gots):
    if not blocked():
        return scatter_whole(mines, gots)
    height = mines[0].shape[0]
    (got_a,) = yield [(sum_pieces(mines, gots, (), height // 2, 1), TO_YX)]
    (got_b,) = yield [(sum_pieces(mines, gots, (got_a,), height // 4, 1), TO_XY)]
    own, *blocks = sum_blocks(mines, gots, (got_a, got_b))
    arrived = yield [(block, TO_Z[3 - n]) for n, block in enumerate(blocks)]
    kept, sent = sum_last(spot, own, arrived)
    (got,) = yield [(sent, TO_CORE)]
    return kept, got


def pack_small(gains, shifts, up_bias):
    rows = gains.shape[1]
    columns = jnp.concatenate([gains, shifts], axis=0).T
    share = up_bias.shape[0]
    first = jnp.pad(columns, ((0, 0), (0, LANES - share - columns.shape[1])))
    second = jnp.pad(up_bias[None, :], ((0, rows - 1), (0, 0)))
    packed = jnp.concatenate([first, second], axis=1)
    return jnp.concatenate([packed, packed], axis=1)


def whole_small(gains, shifts, up_bias):
    both = jnp.concatenate([gains, shifts], axis=0)
    table = lax.all_gather(both, AXES, axis=1, tiled=True)
    return table.astype(WIDE), lax.all_gather(up_bias, AXES, axis=0, tiled=True)[None].astype(WIDE)


def local(
    hidden_in,
    cotangent,
    lengths,
    qkv_weight,
    out_weight,
    up_weight,
    down_weight,
    norm_gains,
    biases,
    up_bias,
):
    clips, slots, width = hidden_in.shape
    layers = qkv_weight.shape[0]
    share = up_bias.shape[1]
    hidden = down_weight.shape[1]
    half = hidden // 2
    assert clips == 1 and layers == 2
    spot = place()
    chunks = []
    for i in range(layers):
        gains, shifts, bias = (v[i].astype(LOW) for v in (norm_gains, biases, up_bias))
        up = up_weight[i].astype(LOW)
        down = down_weight[i].T.astype(LOW)
        first = [qkv_weight[i].astype(LOW)]
        if blocked():
            first.append(pack_small(gains, shifts, bias))
        chunks.append(first)
        chunks.append([out_weight[i].astype(LOW), up[:, :half], down[:, :half]])
        chunks.append([up[:, half:], down[:, half:]])
    spots = [offsets_of([piece.shape[1] for piece in pieces]) for pieces in chunks]

    def both_cores(pieces):
        low, high = halves(pieces)
        mine = jnp.where(spot[3] == 0, low, high)
        got = send(jnp.where(spot[3] == 0, high, low), TO_CORE)
        upper = jnp.concatenate([mine, got], axis=0)
        return jnp.where(spot[3] == 0, upper, jnp.concatenate([got, mine], axis=0))

    if blocked():
        rest = both_cores([piece for pieces in chunks[1:] for piece in pieces])
        blocks = [both_cores(chunks[0])]
        start = 0
        for at in spots[1:]:
            blocks.append(rest[:, start : start + at[-1]])
            start = start + at[-1]
    else:
        blocks = [None] * len(chunks)
    q0, a0, b0, q1, a1, b1 = [Chain(gather_steps(p, block)) for p, block in zip(chunks, blocks)]

    def weight(index, member):
        chain = (q0, a0, b0, q1, a1, b1)[index]
        return chain.result, spots[index][member]

    def small_of(i):
        if blocked():
            return small_forward(spot, q0.result if i == 0 else q1.result, spots[3 * i][1], hidden)
        return whole_small(norm_gains[i].astype(LOW), biases[i].astype(LOW), up_bias[i].astype(LOW))

    pairs = PAIRS // 2
    rec = [{"h": hidden_in[0]}, {}]

    def norm_and_qkv(i):
        r = rec[i]
        table, bias = small_of(i)
        qkv, first = qkv_forward(spot, weight(3 * i, 0), r["h"], table)
        return {"table": table, "bias": bias, "qkv": qkv, "a1": first}

    def attend(i, side):
        mixed, lse = attention_forward(lengths, rec[i]["qkv"], side * pairs, pairs)
        return {f"mixed{side}": mixed, f"lse{side}": lse}

    def project(i):
        r = rec[i]
        h2, second = out_forward(
            spot, weight(3 * i + 1, 0), r["h"], (r["mixed0"], r["mixed1"]), r["table"]
        )
        return {"h2": h2, "a2": second}

    def feed_weights(i, side):
        return weight(3 * i + 1 + side, 1 - side), weight(3 * i + 1 + side, 2 - side)

    def feed(i, side):
        r = rec[i]
        z, slope, total = mlp_forward(
            spot,
            *feed_weights(i, side),
            r["total"] if side else r["h2"],
            r["a2"],
            r["bias"][:, side * half : (side + 1) * half],
            r["table"],
            side == 0,
        )
        return {f"z{side}": z, f"slope{side}": slope, "total": total}

    def feed_back(i, side):
        r = rec[i]
        acc, up_mine, up_rest, down_mine, down_rest, down_sum, up_sum = mlp_backward(
            spot,
            *feed_weights(i, side),
            r["e"],
            r["a2"],
            r[f"z{side}"],
            r[f"slope{side}"],
            None if side else r["acc"],
        )
        return {
            "acc": acc,
            f"up{side}": (up_mine, up_rest),
            f"down{side}": (down_mine, down_rest),
            "down_sum": down_sum,
            f"up_sum{side}": up_sum,
        }

    def middle_back(i):
        r = rec[i]
        mixed = (r["mixed0"], r["mixed1"])
        e2, da, mine, rest, sums = middle_backward(
            spot, weight(3 * i + 1, 0), r["e"], r["h2"], mixed, r["acc"], r["table"]
        )
        return {"e2": e2, "da": da, "out": (mine, rest), "sums2": sums}

    def attend_back(i, side):
        r = rec[i]
        dqkv = attention_backward(
            lengths, r["qkv"], r["da"], r[f"mixed{side}"], r[f"lse{side}"], side * pairs, pairs
        )
        return {f"dqkv{side}": dqkv}

    def qkv_back(i):
        r = rec[i]
        e, mine, rest, table = qkv_backward(
            spot,
            weight(3 * i, 0),
            (r["dqkv0"], r["dqkv1"]),
            r["e2"],
            r["h"],
            r["a1"],
            r["table"],
            (r["sums2"], r["down_sum"], (r["up_sum0"], r["up_sum1"])),
        )
        return {"e_in": e, "qkv": (mine, rest), "small": table}

    def run(begin, *work, hold=()):
        def todo():
            before = [dict(r) for r in rec]
            found = []
            for function, i, *rest in work:
                new = function(i, *rest)
                rec[i].update(new)
                found.append(new)
            for r, old in zip(rec, before):
                r.clear()
                r.update(old)
            return found

        for (function, i, *rest), new in zip(work, stage(begin, todo, hold)):
            rec[i].update(new)

    run([q0])
    run([q0, a0], hold=[a0])
    run([q0, land(a0)])
    run([q0, a0, b0], hold=[b0])
    run([a0, land(b0)], (norm_and_qkv, 0), (attend, 0, 0))
    run([a0, b0], (attend, 0, 1))
    run([b0, q1], (project, 0), (feed, 0, 0))
    run([b0, q1])
    run([q1, a1], (feed, 0, 1))
    rec[1]["h"] = rec[0]["total"]
    run([q1, a1, b1], hold=[b1])
    run([a1, land(b1)], (norm_and_qkv, 1))
    run([a1, b1], (attend, 1, 0))
    run([b1], (attend, 1, 1), (project, 1))
    run([b1], (feed, 1, 0))
    run([], (feed, 1, 1))
    output = rec[1]["total"][None]

    def cross(i, *members):
        return [Chain(cross_steps(rec[i][member][1])) for member in members]

    def scatter(i, members, crossed):
        mines = [rec[i][member][0] for member in members]
        return Chain(scatter_steps(spot, mines, [chain.result for chain in crossed]))

    first_members, second_members = ["down1", "up1"], ["down0", "up0", "out"]
    rec[1]["e"] = cotangent[0]
    run([], (feed_back, 1, 1))
    first = cross(1, *first_members)
    run(first, (feed_back, 1, 0))
    b1 = scatter(1, first_members, first)
    second = cross(1, "down0", "up0")
    run([b1, *second], (middle_back, 1), (attend_back, 1, 0))
    second += cross(1, "out")
    run([b1, *second], (attend_back, 1, 1))
    a1 = scatter(1, second_members, second)
    run([b1, a1], (qkv_back, 1))
    rec[0]["e"] = rec[1]["e_in"]
    third = cross(1, "qkv")
    run([b1, a1, *third], (feed_back, 0, 1))
    q1 = scatter(1, ["qkv"], third)
    first = cross(0, *first_members)
    run([a1, q1, *first], (feed_back, 0, 0))
    b0 = scatter(0, first_members, first)
    second = cross(0, "down0", "up0")
    run([a1, q1, b0, *second], (middle_back, 0), (attend_back, 0, 0))
    second += cross(0, "out")
    run([q1, b0, *second], (attend_back, 0, 1))
    a0 = scatter(0, second_members, second)
    run([q1, b0, a0], (qkv_back, 0))
    third = cross(0, "qkv")
    run([b0, a0, *third])
    q0 = scatter(0, ["qkv"], third)
    run([a0, q0])
    run([a0, q0])

    input_grad = rec[0]["e_in"][None]
    mlp_shapes = [(layers, hidden, down_weight.shape[2]), up_weight.shape, out_weight.shape]
    qkv_shapes = [qkv_weight.shape, norm_gains.shape, biases.shape, up_bias.shape]
    if blocked():
        down_grad, up_grad, out_grad = finish_mlp(
            spot, [(a0.result, b0.result), (a1.result, b1.result)], mlp_shapes
        )
        run([q0])
        run([q0])
        qkv_grad, gains, shifts, up_sums = finish_qkv(spot, [q0.result, q1.result], qkv_shapes)
        return output, input_grad, qkv_grad, out_grad, up_grad, down_grad, gains, shifts, up_sums
    owned = []
    for r, q, a, b in ((rec[0], q0, a0, b0), (rec[1], q1, a1, b1)):
        down = jnp.concatenate([a.result[0], b.result[0]], axis=1).T
        up = jnp.concatenate([a.result[1], b.result[1]], axis=1)
        up_sum = jnp.concatenate([r["up_sum0"], r["up_sum1"]], axis=1)
        table = lax.psum_scatter(r["small"], AXES, scatter_dimension=1, tiled=True)
        up_sum = lax.psum_scatter(up_sum[0], AXES, scatter_dimension=0, tiled=True)
        owned.append((q.result[0], a.result[2], up, down, table[0:2], table[2:8], up_sum))
    stacked = [jnp.stack([pair[n] for pair in owned]) for n in range(7)]
    return (output, input_grad, *stacked)


def solution(mesh):
    return jax.shard_map(
        local,
        mesh=mesh,
        in_specs=(
            P(("dp", "fsdp"), None, None),
            P(("dp", "fsdp"), None, None),
            P(("dp", "fsdp")),
            P(None, ("dp", "fsdp"), None),
            P(None, ("dp", "fsdp"), None),
            P(None, ("dp", "fsdp"), None),
            P(None, None, ("dp", "fsdp")),
            P(None, None, ("dp", "fsdp")),
            P(None, None, ("dp", "fsdp")),
            P(None, ("dp", "fsdp")),
        ),
        out_specs=(
            P(("dp", "fsdp"), None, None),
            P(("dp", "fsdp"), None, None),
            P(None, ("dp", "fsdp"), None),
            P(None, ("dp", "fsdp"), None),
            P(None, ("dp", "fsdp"), None),
            P(None, None, ("dp", "fsdp")),
            P(None, None, ("dp", "fsdp")),
            P(None, None, ("dp", "fsdp")),
            P(None, ("dp", "fsdp")),
        ),
        check_vma=False,
    )
```

time: 572 us -> 544 us (0.951)
  other arithmetic: 79.3 us -> 6.25 us
  Pallas kernels: 244 us -> 285 us
  waiting for transfers between devices: 106 us -> 123 us
  local copies, waits for them, and re-layouts: 45.2 us -> 39 us
    pallas_call x8 -> x30, Pallas kernels: 64.4 us -> 123 us  [the longest x24 62 us: sum_call(): pl.pallas_call(body, out_shape=outs, grid=(1,), in_specs=[pl.BlockSpec(me...]
    add x34 -> x0, other arithmetic: 34.1 us -> none  [added(): total = total + part.astype(WIDE)]
    another operation x31 -> x6, other arithmetic: 20.3 us -> 2.54 us
    ppermute x88 -> x92, waiting for transfers between devices: 106 us -> 123 us  [send(): return lax.ppermute(value, AXES, pairs)]
    convert_element_type x22 -> x0, other arithmetic: 15.9 us -> none  [the longest x6 7.18 us: scatter_steps(): got_z = (yield [(block_at(n).astype(LOW), TO_Z[4 - n]) for n in (1, 2, 3)])]
    pallas_call x2, Pallas kernels: 30 us -> 14.8 us  [middle_backward(): pl.pallas_call(body, out_shape=[jax.ShapeDtypeStruct((rows, width), WIDE)...]
    concatenate x15 -> x6, local copies, waits for them, and re-layouts: 13.6 us -> 5.74 us  [gather_steps(): near = jnp.concatenate([stack, got], axis=0)]
    ppermute x88 -> x92, starting transfers between devices: 82.9 us -> 79 us  [send(): return lax.ppermute(value, AXES, pairs)]
  transfers between devices with their start and end apart: 88 -> 92, of which waited for: 27 -> 27; matrix products, arithmetic and copies ran while one was open for 12% -> 4% of each run, Pallas kernels for 42% -> 43%
where the time goes in v4:
time: 544 us; the launch traced here: 536 us
  Pallas kernels  285 us (52%)
  waiting for transfers between devices  123 us (23%)
  starting transfers between devices  79 us (15%)
  local copies, waits for them, and re-layouts  39 us (7%)
  other arithmetic  6.25 us (1%)
    ppermute x92, waiting for transfers between devices, send(): return lax.ppermute(value, AXES, pairs)  123 us
    ppermute x92, starting transfers between devices, send(): return lax.ppermute(value, AXES, pairs)  79 us
    pallas_call x24, Pallas kernels, sum_call(): pl.pallas_call(body, out_shape=outs, grid=(1,), in_specs=[pl.BlockSpec(me...  62 us
    pallas_call x4, Pallas kernels, mlp_backward(): pl.pallas_call(body, out_shape=[jax.ShapeDtypeStruct((rows, width), WIDE)...  55.7 us
    pallas_call x4, Pallas kernels, mlp_forward(): pl.pallas_call(body, out_shape=[jax.ShapeDtypeStruct((rows, hidden), LOW)...  39 us
    pallas_call x4, Pallas kernels, attention_backward(): pl.pallas_call(body, out_shape=jax.ShapeDtypeStruct((rows, 3 * width), LO...  29.6 us
    unnamed x157, local copies, waits for them, and re-layouts  27.9 us
    pallas_call x2, Pallas kernels, qkv_backward(): pl.pallas_call(body, out_shape=[jax.ShapeDtypeStruct((rows, width), WIDE)...  25.1 us
  transfers between devices with their start and end apart: 92, of which 27 were waited for; matrix products, arithmetic and copies ran while one was open for 4% of the time, Pallas kernels for 43%

profile of v4, /device:TPU:0, one launch (start us, length us, event | category | flops | bytes accessed | tf_op | source)
XLA Modules:
  0.0 535.7 jit_solution(16806046459196539208)
XLA Ops:
  5.7 5.0 collective-permute-start.4
  11.8 2.6 collective-permute-done.4
  14.4 7.4 %collective-permute-done.3 = bf16[48,1280]{1,0:T(8,128)(2,1)S(1)} collective-permute-done((bf16[48,1280]{1,0:T(8,128)(2,1)S(1)}, bf16[48,1280]{1,0:T(8,128)(2,1)S(1)}, u32[]{:S(2)}, u32[]{:S(2)}) %collective-permute-start.3) | collective-permute-done | bytes 122912 | tf_op jit(solution)/shard_map/ppermute | solution.py:882
  23.4 7.3 %collective-permute-done.5 = bf16[192,1280]{1,0:T(8,128)(2,1)S(1)} collective-permute-done((bf16[192,1280]{1,0:T(8,128)(2,1)S(1)}, bf16[192,1280]{1,0:T(8,128)(2,1)S(1)}, u32[]{:S(2)}, u32[]{:S(2)}) %collective-permute-start.5) | collective-permute-done | bytes 491552 | tf_op jit(solution)/shard_map/ppermute | solution.py:882
  39.4 12.5 %collective-permute-done.9 = bf16[48,1920]{1,0:T(8,128)(2,1)S(1)} collective-permute-done((bf16[48,1920]{1,0:T(8,128)(2,1)S(1)}, bf16[48,1920]{1,0:T(8,128)(2,1)S(1)}, u32[]{:S(2)}, u32[]{:S(2)}) %collective-permute-start.9) | collective-permute-done | bytes 184352 | tf_op jit(solution)/shard_map/ppermute | solution.py:882
  52.7 10.8 %collective-permute-done.12 = bf16[192,1920]{1,0:T(8,128)(2,1)S(1)} collective-permute-done((bf16[192,1920]{1,0:T(8,128)(2,1)S(1)}, bf16[192,1920]{1,0:T(8,128)(2,1)S(1)}, u32[]{:S(2)}, u32[]{:S(2)}) %collective-permute-start.12) | collective-permute-done | bytes 737312 | tf_op jit(solution)/shard_map/ppermute | solution.py:882
  72.9 2.5 small_forward.2
  75.4 7.1 %qkv_forward.2 = (bf16[496,2304]{1,0:T(8,128)(2,1)}, bf16[496,768]{1,0:T(8,128)(2,1)}) custom-call(s32[4]{0:T(128)} %pad_add_fusion.spot_ref, bf16[384,1280]{1,0:T(8,128)(2,1)} %copy-done.25, bf16[384,1280]{1,0:T(8,128)(2,1)} %copy-done.26, bf16[384,1280]{1,0:T(8,128)(2,1)} %copy-done.64, bf16[384,1280]{1,0:T(8,128)(2,1)} %copy-done.65, ...), custom_call_target="tpu_custom_call" | custom-call | flops 1755316224 | bytes 6967296 | tf_op jit(solution)/shard_map/qkv_forward/pallas_call | solution.py:124
  82.5 5.7 %attention_forward.4 = (bf16[496,384]{1,0:T(8,128)(2,1)}, f32[496,128]{1,0:T(8,128)}) custom-call(s32[1]{0:T(128)S(6)} %copy.55.len_ref, bf16[496,2304]{1,0:T(8,128)(2,1)} %get-tuple-element.312.q_ref.k_ref.v_ref, bf16[496,2304]{1,0:T(8,128)(2,1)} %get-tuple-element.312.q_ref.k_ref.v_ref, bf16[496,2304]{1,0:T(8,128)(2,1)} %get-tuple-element.312.q_ref.k_ref.v_ref), custom_call_target="tpu_custom_call" | custom-call | flops 1511522304 | bytes 1523712 | tf_op jit(solution)/shard_map/attention_forward/pallas_call | solution.py:166
  90.5 5.7 %attention_forward.5 = (bf16[496,384]{1,0:T(8,128)(2,1)}, f32[496,128]{1,0:T(8,128)}) custom-call(s32[1]{0:T(128)S(6)} %copy.55.len_ref, bf16[496,2304]{1,0:T(8,128)(2,1)} %get-tuple-element.312.q_ref.k_ref.v_ref, bf16[496,2304]{1,0:T(8,128)(2,1)} %get-tuple-element.312.q_ref.k_ref.v_ref, bf16[496,2304]{1,0:T(8,128)(2,1)} %get-tuple-element.312.q_ref.k_ref.v_ref), custom_call_target="tpu_custom_call" | custom-call | flops 1511522304 | bytes 1523712 | tf_op jit(solution)/shard_map/attention_forward/pallas_call | solution.py:166
  107.8 5.5 %out_forward.2 = (f32[496,768]{1,0:T(8,128)}, bf16[496,768]{1,0:T(8,128)(2,1)}) custom-call(s32[4]{0:T(128)} %pad_add_fusion.spot_ref, bf16[384,1920]{1,0:T(8,128)(2,1)} %copy-done.1, bf16[384,1920]{1,0:T(8,128)(2,1)} %collective-permute-done.13.r1.u1.d1.refs_2_.refs_6_, bf16[384,1920]{1,0:T(8,128)(2,1)} %collective-permute-done.14.r2.u2.d2.refs_3_.refs_7_, ...), custom_call_target="tpu_custom_call" | custom-call | flops 585105408 | bytes 5750784 | tf_op jit(solution)/shard_map/out_forward/pallas_call | solution.py:210
  113.3 9.7 %mlp_forward.4 = (bf16[496,1536]{1,0:T(8,128)(2,1)}, bf16[496,1536]{1,0:T(8,128)(2,1)}, f32[496,768]{1,0:T(8,128)}) custom-call(s32[4]{0:T(128)} %pad_add_fusion.spot_ref, f32[496,768]{1,0:T(8,128)} %get-tuple-element.486.h_ref, bf16[496,768]{1,0:T(8,128)(2,1)} %get-tuple-element.333.a_ref, f32[1,1536]{1,0:T(1,128)} %get-tuple-element.644.b_ref, ...), custom_call_target="tpu_custom_call" | custom-call | flops 2340421632 | bytes 7766016 | tf_op jit(solution)/shard_map/mlp_forward/pallas_call | solution.py:290
  125.8 6.3 %collective-permute-done.26 = bf16[192,1280]{1,0:T(8,128)(2,1)S(1)} collective-permute-done((bf16[192,1280]{1,0:T(8,128)(2,1)S(1)}, bf16[192,1280]{1,0:T(8,128)(2,1)S(1)}, u32[]{:S(2)}, u32[]{:S(2)}) %collective-permute-start.26) | collective-permute-done | bytes 491552 | tf_op jit(solution)/shard_map/ppermute | solution.py:882
  133.9 3.0 collective-permute-start.31
  138.2 9.8 %mlp_forward.5 = (bf16[496,1536]{1,0:T(8,128)(2,1)}, bf16[496,1536]{1,0:T(8,128)(2,1)}, f32[496,768]{1,0:T(8,128)}) custom-call(s32[4]{0:T(128)} %pad_add_fusion.spot_ref, f32[496,768]{1,0:T(8,128)} %get-tuple-element.332.h_ref, bf16[496,768]{1,0:T(8,128)(2,1)} %get-tuple-element.333.a_ref, f32[1,1536]{1,0:T(1,128)} %get-tuple-element.643.b_ref, ...), custom_call_target="tpu_custom_call" | custom-call | flops 2340421632 | bytes 7766016 | tf_op jit(solution)/shard_map/mlp_forward/pallas_call | solution.py:290
  148.0 5.9 %collective-permute-done.30 = bf16[48,1920]{1,0:T(8,128)(2,1)S(1)} collective-permute-done((bf16[48,1920]{1,0:T(8,128)(2,1)S(1)}, bf16[48,1920]{1,0:T(8,128)(2,1)S(1)}, u32[]{:S(2)}, u32[]{:S(2)}) %collective-permute-start.30) | collective-permute-done | bytes 184352 | tf_op jit(solution)/shard_map/ppermute | solution.py:882
  155.5 10.2 %collective-permute-done.33 = bf16[192,1920]{1,0:T(8,128)(2,1)S(1)} collective-permute-done((bf16[192,1920]{1,0:T(8,128)(2,1)S(1)}, bf16[192,1920]{1,0:T(8,128)(2,1)S(1)}, u32[]{:S(2)}, u32[]{:S(2)}) %collective-permute-start.33) | collective-permute-done | bytes 737312 | tf_op jit(solution)/shard_map/ppermute | solution.py:882
  171.5 2.5 small_forward.3
  174.0 7.1 %qkv_forward.3 = (bf16[496,2304]{1,0:T(8,128)(2,1)}, bf16[496,768]{1,0:T(8,128)(2,1)}) custom-call(s32[4]{0:T(128)} %pad_add_fusion.spot_ref, bf16[384,1280]{1,0:T(8,128)(2,1)} %constant_dynamic-update-slice_fusion.15.r0, bf16[384,1280]{1,0:T(8,128)(2,1)} %collective-permute-done.27.r1, bf16[384,1280]{1,0:T(8,128)(2,1)} %collective-permute-done.28.r2, ...), custom_call_target="tpu_custom_call" | custom-call | flops 1755316224 | bytes 6967296 | tf_op jit(solution)/shard_map/qkv_forward/pallas_call | solution.py:124
  183.1 3.2 collective-permute-done.34.r1.u1.d1.refs_2_.refs_6_
  190.9 5.9 %attention_forward.6 = (bf16[496,384]{1,0:T(8,128)(2,1)}, f32[496,128]{1,0:T(8,128)}) custom-call(s32[1]{0:T(128)S(6)} %copy.55.len_ref, bf16[496,2304]{1,0:T(8,128)(2,1)} %get-tuple-element.355.q_ref.k_ref.v_ref, bf16[496,2304]{1,0:T(8,128)(2,1)} %get-tuple-element.355.q_ref.k_ref.v_ref, bf16[496,2304]{1,0:T(8,128)(2,1)} %get-tuple-element.355.q_ref.k_ref.v_ref), custom_call_target="tpu_custom_call" | custom-call | flops 1511522304 | bytes 1523712 | tf_op jit(solution)/shard_map/attention_forward/pallas_call | solution.py:166
  202.0 5.7 %attention_forward.7 = (bf16[496,384]{1,0:T(8,128)(2,1)}, f32[496,128]{1,0:T(8,128)}) custom-call(s32[1]{0:T(128)S(6)} %copy.55.len_ref, bf16[496,2304]{1,0:T(8,128)(2,1)} %get-tuple-element.355.q_ref.k_ref.v_ref, bf16[496,2304]{1,0:T(8,128)(2,1)} %get-tuple-element.355.q_ref.k_ref.v_ref, bf16[496,2304]{1,0:T(8,128)(2,1)} %get-tuple-element.355.q_ref.k_ref.v_ref), custom_call_target="tpu_custom_call" | custom-call | flops 1511522304 | bytes 1523712 | tf_op jit(solution)/shard_map/attention_forward/pallas_call | solution.py:166
  207.7 5.6 %out_forward.3 = (f32[496,768]{1,0:T(8,128)}, bf16[496,768]{1,0:T(8,128)(2,1)}) custom-call(s32[4]{0:T(128)} %pad_add_fusion.spot_ref, bf16[384,1920]{1,0:T(8,128)(2,1)} %copy-done, bf16[384,1920]{1,0:T(8,128)(2,1)} %collective-permute-done.34.r1.u1.d1.refs_2_.refs_6_, bf16[384,1920]{1,0:T(8,128)(2,1)} %copy-done.3, bf16[384,1920]{1,0:T(8,128)(2,1)} %copy-done.4, ...), custom_call_target="tpu_custom_call" | custom-call | flops 585105408 | bytes 5750784 | tf_op jit(solution)/shard_map/out_forward/pallas_call | solution.py:210
  213.3 3.9 collective-permute-done.41.u1.d1.refs_1_.refs_5_
  217.9 9.8 %mlp_forward.6 = (bf16[496,1536]{1,0:T(8,128)(2,1)}, bf16[496,1536]{1,0:T(8,128)(2,1)}, f32[496,768]{1,0:T(8,128)}) custom-call(s32[4]{0:T(128)} %pad_add_fusion.spot_ref, f32[496,768]{1,0:T(8,128)} %get-tuple-element.368.h_ref, bf16[496,768]{1,0:T(8,128)(2,1)} %get-tuple-element.369.a_ref, f32[1,1536]{1,0:T(1,128)} %get-tuple-element.642.b_ref, ...), custom_call_target="tpu_custom_call" | custom-call | flops 2340421632 | bytes 7766016 | tf_op jit(solution)/shard_map/mlp_forward/pallas_call | solution.py:290
  228.7 9.7 %mlp_forward.7 = (bf16[496,1536]{1,0:T(8,128)(2,1)}, bf16[496,1536]{1,0:T(8,128)(2,1)}, f32[496,768]{1,0:T(8,128)}) custom-call(s32[4]{0:T(128)} %pad_add_fusion.spot_ref, f32[496,768]{1,0:T(8,128)} %get-tuple-element.374.h_ref, bf16[496,768]{1,0:T(8,128)(2,1)} %get-tuple-element.369.a_ref, f32[1,1536]{1,0:T(1,128)} %get-tuple-element.641.b_ref, ...), custom_call_target="tpu_custom_call" | custom-call | flops 2340421632 | bytes 7766016 | tf_op jit(solution)/shard_map/mlp_forward/pallas_call | solution.py:290
  238.5 13.5 %mlp_backward.4 = (f32[496,768]{1,0:T(8,128)}, bf16[768,768]{1,0:T(8,128)(2,1)}, bf16[768,768]{1,0:T(8,128)(2,1)}, bf16[768,768]{1,0:T(8,128)(2,1)}, bf16[768,76...) custom-call(s32[4]{0:T(128)} %pad_add_fusion.spot_ref, f32[496,768]{1,0:T(8,128)} %bitcast.38, ...), custom_call_target="tpu_custom_call" | custom-call | flops 4680843264 | bytes 12484608 | tf_op jit(solution)/shard_map/mlp_backward/pallas_call | solution.py:411
  252.7 14.4 %mlp_backward.5 = (f32[496,768]{1,0:T(8,128)}, bf16[768,768]{1,0:T(8,128)(2,1)}, bf16[768,768]{1,0:T(8,128)(2,1)}, bf16[768,768]{1,0:T(8,128)(2,1)}, bf16[768,76...) custom-call(s32[4]{0:T(128)} %pad_add_fusion.spot_ref, f32[496,768]{1,0:T(8,128)} %bitcast.39, ...), custom_call_target="tpu_custom_call" | custom-call | flops 4680843264 | bytes 12484608 | tf_op jit(solution)/shard_map/mlp_backward/pallas_call | solution.py:411
  268.5 3.0 sum_pieces.12
  273.2 7.4 %middle_backward.2 = (f32[496,768]{1,0:T(8,128)}, bf16[496,768]{1,0:T(8,128)(2,1)}, bf16[768,384]{1,0:T(8,128)(2,1)}, bf16[768,384]{1,0:T(8,128)(2,1)}, f32[8,768]{1,0:T(8,128)}) custom-call(s32[4]{0:T(128)} %pad_add_fusion.spot_ref, bf16[384,1920]{1,0:T(8,128)(2,1)} %copy-done, bf16[384,1920]{1,0:T(8,128)(2,1)} %collective-permute-done.34.r1.u1.d1.refs_2_.refs_6_, ...), custom_call_target="tpu_custom_call" | custom-call | flops 1170210816 | bytes 9977856 | tf_op jit(solution)/shard_map/middle_backward/pallas_call | solution.py:489
  280.6 7.4 %attention_backward.4.d0_ref = bf16[496,1152]{1,0:T(8,128)(2,1)} custom-call(s32[1]{0:T(128)S(6)} %copy.55.len_ref, bf16[496,2304]{1,0:T(8,128)(2,1)} %get-tuple-element.355.q_ref.k_ref.v_ref, bf16[496,2304]{1,0:T(8,128)(2,1)} %get-tuple-element.355.q_ref.k_ref.v_ref, bf16[496,2304]{1,0:T(8,128)(2,1)} %get-tuple-element.355.q_ref.k_ref.v_ref, ...), custom_call_target="tpu_custom_call" | custom-call | flops 3778805760 | bytes 3047424 | tf_op jit(solution)/shard_map/attention_backward/pallas_call | solution.py:558
  288.1 3.3 sum_pieces.13
  292.8 7.4 %attention_backward.5.d1_ref = bf16[496,1152]{1,0:T(8,128)(2,1)} custom-call(s32[1]{0:T(128)S(6)} %copy.55.len_ref, bf16[496,2304]{1,0:T(8,128)(2,1)} %get-tuple-element.355.q_ref.k_ref.v_ref, bf16[496,2304]{1,0:T(8,128)(2,1)} %get-tuple-element.355.q_ref.k_ref.v_ref, bf16[496,2304]{1,0:T(8,128)(2,1)} %get-tuple-element.355.q_ref.k_ref.v_ref, ...), custom_call_target="tpu_custom_call" | custom-call | flops 3778805760 | bytes 3047424 | tf_op jit(solution)/shard_map/attention_backward/pallas_call | solution.py:558
  302.3 3.2 sum_pieces.14
  306.7 2.6 sum_blocks.6
  312.9 12.5 %qkv_backward.2 = (f32[496,768]{1,0:T(8,128)}, bf16[768,1280]{1,0:T(8,128)(2,1)}, bf16[768,1280]{1,0:T(8,128)(2,1)}, f32[8,768]{1,0:T(8,128)}) custom-call(s32[4]{0:T(128)} %pad_add_fusion.spot_ref, bf16[384,1280]{1,0:T(8,128)(2,1)} %constant_dynamic-update-slice_fusion.15.r0, bf16[384,1280]{1,0:T(8,128)(2,1)} %collective-permute-done.27.r1, ...), custom_call_target="tpu_custom_call" | custom-call | flops 3510632448 | bytes 13172736 | tf_op jit(solution)/shard_map/qkv_backward/pallas_call | solution.py:638
  326.7 2.7 sum_pieces.15
  332.7 13.7 %mlp_backward.6 = (f32[496,768]{1,0:T(8,128)}, bf16[768,768]{1,0:T(8,128)(2,1)}, bf16[768,768]{1,0:T(8,128)(2,1)}, bf16[768,768]{1,0:T(8,128)(2,1)}, bf16[768,76...) custom-call(s32[4]{0:T(128)} %pad_add_fusion.spot_ref, f32[496,768]{1,0:T(8,128)} %get-tuple-element.448.e_ref, ...), custom_call_target="tpu_custom_call" | custom-call | flops 4680843264 | bytes 12484608 | tf_op jit(solution)/shard_map/mlp_backward/pallas_call | solution.py:411
  348.0 2.7 sum_pieces.16
  351.6 3.0 sum_blocks.7
  356.4 5.5 %collective-permute-done.58.refs_1_ = bf16[48,1920]{1,0:T(8,128)(2,1)S(1)} collective-permute-done((bf16[48,1920]{1,0:T(8,128)(2,1)}, bf16[48,1920]{1,0:T(8,128)(2,1)S(1)}, u32[]{:S(2)}, u32[]{:S(2)}) %collective-permute-start.58) | collective-permute-done | bytes 184352 | tf_op jit(solution)/shard_map/ppermute | solution.py:882
  363.0 14.0 %mlp_backward.7 = (f32[496,768]{1,0:T(8,128)}, bf16[768,768]{1,0:T(8,128)(2,1)}, bf16[768,768]{1,0:T(8,128)(2,1)}, bf16[768,768]{1,0:T(8,128)(2,1)}, bf16[768,76...) custom-call(s32[4]{0:T(128)} %pad_add_fusion.spot_ref, f32[496,768]{1,0:T(8,128)} %get-tuple-element.448.e_ref, ...), custom_call_target="tpu_custom_call" | custom-call | flops 4680843264 | bytes 12484608 | tf_op jit(solution)/shard_map/mlp_backward/pallas_call | solution.py:411
  378.3 2.9 sum_pieces.18
  387.7 7.4 %middle_backward.3 = (f32[496,768]{1,0:T(8,128)}, bf16[496,768]{1,0:T(8,128)(2,1)}, bf16[768,384]{1,0:T(8,128)(2,1)}, bf16[768,384]{1,0:T(8,128)(2,1)}, f32[8,768]{1,0:T(8,128)}) custom-call(s32[4]{0:T(128)} %pad_add_fusion.spot_ref, bf16[384,1920]{1,0:T(8,128)(2,1)} %copy-done.1, bf16[384,1920]{1,0:T(8,128)(2,1)} %collective-permute-done.13.r1.u1.d1.refs_2_.refs_6_, ...), custom_call_target="tpu_custom_call" | custom-call | flops 1170210816 | bytes 9977856 | tf_op jit(solution)/shard_map/middle_backward/pallas_call | solution.py:489
  395.1 7.4 %attention_backward.6.d0_ref = bf16[496,1152]{1,0:T(8,128)(2,1)} custom-call(s32[1]{0:T(128)S(6)} %copy.55.len_ref, bf16[496,2304]{1,0:T(8,128)(2,1)} %get-tuple-element.312.q_ref.k_ref.v_ref, bf16[496,2304]{1,0:T(8,128)(2,1)} %get-tuple-element.312.q_ref.k_ref.v_ref, bf16[496,2304]{1,0:T(8,128)(2,1)} %get-tuple-element.312.q_ref.k_ref.v_ref, ...), custom_call_target="tpu_custom_call" | custom-call | flops 3778805760 | bytes 3047424 | tf_op jit(solution)/shard_map/attention_backward/pallas_call | solution.py:558
  403.0 3.3 sum_pieces.19
  408.1 2.4 sum_blocks.8
  410.5 3.3 collective-permute-start.69
  415.9 7.4 %attention_backward.7.d1_ref = bf16[496,1152]{1,0:T(8,128)(2,1)} custom-call(s32[1]{0:T(128)S(6)} %copy.55.len_ref, bf16[496,2304]{1,0:T(8,128)(2,1)} %get-tuple-element.312.q_ref.k_ref.v_ref, bf16[496,2304]{1,0:T(8,128)(2,1)} %get-tuple-element.312.q_ref.k_ref.v_ref, bf16[496,2304]{1,0:T(8,128)(2,1)} %get-tuple-element.312.q_ref.k_ref.v_ref, ...), custom_call_target="tpu_custom_call" | custom-call | flops 3778805760 | bytes 3047424 | tf_op jit(solution)/shard_map/attention_backward/pallas_call | solution.py:558
  423.3 2.4 collective-permute-done.70.refs_2_
  426.6 3.3 sum_pieces.20
  430.9 2.6 sum_blocks.9
  439.7 12.6 %qkv_backward.3 = (f32[496,768]{1,0:T(8,128)}, bf16[768,1280]{1,0:T(8,128)(2,1)}, bf16[768,1280]{1,0:T(8,128)(2,1)}, f32[8,768]{1,0:T(8,128)}) custom-call(s32[4]{0:T(128)} %pad_add_fusion.spot_ref, bf16[384,1280]{1,0:T(8,128)(2,1)} %copy-done.25, bf16[384,1280]{1,0:T(8,128)(2,1)} %copy-done.26, bf16[384,1280]{1,0:T(8,128)(2,1)} %copy-done.64, ...), custom_call_target="tpu_custom_call" | custom-call | flops 3510632448 | bytes 13172736 | tf_op jit(solution)/shard_map/qkv_backward/pallas_call | solution.py:638
  453.7 2.8 sum_pieces.21
  461.2 6.9 %collective-permute-done.80.refs_7_ = bf16[192,1920]{1,0:T(8,128)(2,1)S(1)} collective-permute-done((bf16[192,1920]{1,0:T(8,128)(2,1)}, bf16[192,1920]{1,0:T(8,128)(2,1)S(1)}, u32[]{:S(2)}, u32[]{:S(2)}) %collective-permute-start.80) | collective-permute-done | bytes 737312 | tf_op jit(solution)/shard_map/ppermute | solution.py:882
  470.3 2.7 sum_pieces.22
  474.3 3.0 sum_blocks.10
  479.8 4.8 collective-permute-done.82.refs_1_
  484.6 9.7 %collective-permute-done.83.refs_2_ = bf16[48,1920]{1,0:T(8,128)(2,1)S(1)} collective-permute-done((bf16[48,1920]{1,0:T(8,128)(2,1)}, bf16[48,1920]{1,0:T(8,128)(2,1)S(1)}, u32[]{:S(2)}, u32[]{:S(2)}) %collective-permute-start.83) | collective-permute-done | bytes 184352 | tf_op jit(solution)/shard_map/ppermute | solution.py:882
  501.9 4.7 collective-permute-done.87.refs_3_
  507.4 2.4 sum_blocks.11
  515.3 6.7 %collective-permute-done.89.refs_2_ = bf16[48,1280]{1,0:T(8,128)(2,1)S(1)} collective-permute-done((bf16[48,1280]{1,0:T(8,128)(2,1)}, bf16[48,1280]{1,0:T(8,128)(2,1)S(1)}, u32[]{:S(2)}, u32[]{:S(2)}) %collective-permute-start.89) | collective-permute-done | bytes 122912 | tf_op jit(solution)/shard_map/ppermute | solution.py:882
  524.6 3.8 finish_mlp.1
  528.5 3.0 copy.27
  (379 shorter events, 140.2 us)
Async XLA Ops:
  11.8 20.7 %collective-permute-start = (bf16[24,8192]{1,0:T(8,128)(2,1)S(1)}, bf16[24,8192]{1,0:T(8,128)(2,1)S(1)}, u32[]{:S(2)}, u32[]{:S(2)}) collective-permute-start(bf16[24,8192]{1,0:T(8,128)(2,1)S(1)} %get-tuple-element.606), channel_id=1, source_target_pairs={{0,1},{1,0},{2,3},{3,2},{4,5},{5,4},{6,7},{7,6},{8,9},{9,8},{10,11... | collective-permute-start | bytes 1179656 | tf_op jit(solution)/shard_map/ppermute | solution.py:882
  30.8 21.1 %collective-permute-start.7 = (bf16[384,1280]{1,0:T(8,128)(2,1)S(1)}, bf16[384,1280]{1,0:T(8,128)(2,1)S(1)}, u32[]{:S(2)}, u32[]{:S(2)}) collective-permute-start(bf16[384,1280]{1,0:T(8,128)(2,1)S(1)} %constant_dynamic-update-slice_fusion.r0), channel_id=1, source_target_pairs={{0,1},{1,0},{2,3},{3,2},{4,5},{5,4},{6,7},{7,6},{8,9},{9,8},{10,11... | collective-permute-start | bytes 2949128 | tf_op jit(solution)/shard_map/ppermute | solution.py:882
  30.9 21.0 %collective-permute-start.6 = (bf16[384,1280]{1,0:T(8,128)(2,1)S(1)}, bf16[384,1280]{1,0:T(8,128)(2,1)S(1)}, u32[]{:S(2)}, u32[]{:S(2)}) collective-permute-start(bf16[384,1280]{1,0:T(8,128)(2,1)S(1)} %constant_dynamic-update-slice_fusion.r0), channel_id=1, source_target_pairs={{0,2},{1,5},{2,0},{3,7},{4,6},{5,1},{6,4},{7,3},{8,10},{9,13},{10,... | collective-permute-start | bytes 2949128 | tf_op jit(solution)/shard_map/ppermute | solution.py:882
  34.2 17.7 %collective-permute-start.9 = (bf16[48,1920]{1,0:T(8,128)(2,1)S(1)}, bf16[48,1920]{1,0:T(8,128)(2,1)S(1)}, u32[]{:S(2)}, u32[]{:S(2)}) collective-permute-start(bf16[48,1920]{1,0:T(8,128)(2,1)S(1)} %get-tuple-element.602), channel_id=1, source_target_pairs={{0,16},{1,17},{2,18},{3,19},{4,20},{5,21},{6,22},{7,23},{8,24},{9,... | collective-permute-start | bytes 552968 | tf_op jit(solution)/shard_map/ppermute | solution.py:882
  35.2 16.7 %collective-permute-start.8 = (bf16[48,1920]{1,0:T(8,128)(2,1)S(1)}, bf16[48,1920]{1,0:T(8,128)(2,1)S(1)}, u32[]{:S(2)}, u32[]{:S(2)}) collective-permute-start(bf16[48,1920]{1,0:T(8,128)(2,1)S(1)} %get-tuple-element.602), channel_id=1, source_target_pairs={{0,8},{1,9},{2,10},{3,11},{4,12},{5,13},{6,14},{7,15},{8,16},{9,17... | collective-permute-start | bytes 552968 | tf_op jit(solution)/shard_map/ppermute | solution.py:882
  63.7 24.5 %collective-permute-start.14 = (bf16[384,1920]{1,0:T(8,128)(2,1)S(1)}, bf16[384,1920]{1,0:T(8,128)(2,1)}, u32[]{:S(2)}, u32[]{:S(2)}) collective-permute-start(bf16[384,1920]{1,0:T(8,128)(2,1)S(1)} %constant_dynamic-update-slice_fusion.5.r0.u0.d0.refs_1_.refs_5_), channel_id=1, source_target_pairs={{0,1},{1,0},{2,3},{3,2},{4,5},{5,4},{6,7},{7,6},{8,9},{9,8},{10,11... | collective-permute-start | bytes 4423688 | tf_op jit(solution)/shard_map/ppermute | solution.py:882
  64.6 23.7 %collective-permute-start.13 = (bf16[384,1920]{1,0:T(8,128)(2,1)S(1)}, bf16[384,1920]{1,0:T(8,128)(2,1)}, u32[]{:S(2)}, u32[]{:S(2)}) collective-permute-start(bf16[384,1920]{1,0:T(8,128)(2,1)S(1)} %constant_dynamic-update-slice_fusion.5.r0.u0.d0.refs_1_.refs_5_), channel_id=1, source_target_pairs={{0,2},{1,5},{2,0},{3,7},{4,6},{5,1},{6,4},{7,3},{8,10},{9,13},{10,... | collective-permute-start | bytes 4423688 | tf_op jit(solution)/shard_map/ppermute | solution.py:882
  68.5 19.7 %collective-permute-start.17 = (bf16[48,1536]{1,0:T(8,128)(2,1)S(1)}, bf16[48,1536]{1,0:T(8,128)(2,1)S(1)}, u32[]{:S(2)}, u32[]{:S(2)}) collective-permute-start(bf16[48,1536]{1,0:T(8,128)(2,1)S(1)} %get-tuple-element.598), channel_id=1, source_target_pairs={{0,24},{1,25},{2,26},{3,27},{4,28},{5,29},{6,30},{7,31},{8,0},{9,1... | collective-permute-start | bytes 442376 | tf_op jit(solution)/shard_map/ppermute | solution.py:882
  68.5 19.7 %collective-permute-start.16 = (bf16[48,1536]{1,0:T(8,128)(2,1)S(1)}, bf16[48,1536]{1,0:T(8,128)(2,1)S(1)}, u32[]{:S(2)}, u32[]{:S(2)}) collective-permute-start(bf16[48,1536]{1,0:T(8,128)(2,1)S(1)} %get-tuple-element.598), channel_id=1, source_target_pairs={{0,16},{1,17},{2,18},{3,19},{4,20},{5,21},{6,22},{7,23},{8,24},{9,... | collective-permute-start | bytes 442376 | tf_op jit(solution)/shard_map/ppermute | solution.py:882
  70.9 17.4 %collective-permute-start.15 = (bf16[48,1536]{1,0:T(8,128)(2,1)S(1)}, bf16[48,1536]{1,0:T(8,128)(2,1)S(1)}, u32[]{:S(2)}, u32[]{:S(2)}) collective-permute-start(bf16[48,1536]{1,0:T(8,128)(2,1)S(1)} %get-tuple-element.598), channel_id=1, source_target_pairs={{0,8},{1,9},{2,10},{3,11},{4,12},{5,13},{6,14},{7,15},{8,16},{9,17... | collective-permute-start | bytes 442376 | tf_op jit(solution)/shard_map/ppermute | solution.py:882
  101.7 21.3 %collective-permute-start.21 = (bf16[384,1536]{1,0:T(8,128)(2,1)}, bf16[384,1536]{1,0:T(8,128)(2,1)}, u32[]{:S(2)}, u32[]{:S(2)}) collective-permute-start(bf16[384,1536]{1,0:T(8,128)(2,1)} %constant_dynamic-update-slice_fusion.10.u0.d0.refs_0_.refs_4_), channel_id=1, source_target_pairs={{0,1},{1,0},{2,3},{3,2},{4,5},{5,4},{6,7},{7,6},{8,9},{9,8},{10,11... | collective-permute-start | bytes 3538952 | tf_op jit(solution)/shard_map/ppermute | solution.py:882
  101.7 21.3 %collective-permute-start.20 = (bf16[384,1536]{1,0:T(8,128)(2,1)}, bf16[384,1536]{1,0:T(8,128)(2,1)}, u32[]{:S(2)}, u32[]{:S(2)}) collective-permute-start(bf16[384,1536]{1,0:T(8,128)(2,1)} %constant_dynamic-update-slice_fusion.10.u0.d0.refs_0_.refs_4_), channel_id=1, source_target_pairs={{0,2},{1,5},{2,0},{3,7},{4,6},{5,1},{6,4},{7,3},{8,10},{9,13},{10,... | collective-permute-start | bytes 3538952 | tf_op jit(solution)/shard_map/ppermute | solution.py:882
  103.9 19.1 %collective-permute-start.24 = (bf16[48,1280]{1,0:T(8,128)(2,1)S(1)}, bf16[48,1280]{1,0:T(8,128)(2,1)S(1)}, u32[]{:S(2)}, u32[]{:S(2)}) collective-permute-start(bf16[48,1280]{1,0:T(8,128)(2,1)S(1)} %get-tuple-element.603), channel_id=1, source_target_pairs={{0,24},{1,25},{2,26},{3,27},{4,28},{5,29},{6,30},{7,31},{8,0},{9,1... | collective-permute-start | bytes 368648 | tf_op jit(solution)/shard_map/ppermute | solution.py:882
  105.7 17.4 %collective-permute-start.23 = (bf16[48,1280]{1,0:T(8,128)(2,1)S(1)}, bf16[48,1280]{1,0:T(8,128)(2,1)S(1)}, u32[]{:S(2)}, u32[]{:S(2)}) collective-permute-start(bf16[48,1280]{1,0:T(8,128)(2,1)S(1)} %get-tuple-element.603), channel_id=1, source_target_pairs={{0,16},{1,17},{2,18},{3,19},{4,20},{5,21},{6,22},{7,23},{8,24},{9,... | collective-permute-start | bytes 368648 | tf_op jit(solution)/shard_map/ppermute | solution.py:882
  105.7 17.4 %collective-permute-start.22 = (bf16[48,1280]{1,0:T(8,128)(2,1)S(1)}, bf16[48,1280]{1,0:T(8,128)(2,1)S(1)}, u32[]{:S(2)}, u32[]{:S(2)}) collective-permute-start(bf16[48,1280]{1,0:T(8,128)(2,1)S(1)} %get-tuple-element.603), channel_id=1, source_target_pairs={{0,8},{1,9},{2,10},{3,11},{4,12},{5,13},{6,14},{7,15},{8,16},{9,17... | collective-permute-start | bytes 368648 | tf_op jit(solution)/shard_map/ppermute | solution.py:882
  133.0 21.0 %collective-permute-start.28 = (bf16[384,1280]{1,0:T(8,128)(2,1)}, bf16[384,1280]{1,0:T(8,128)(2,1)}, u32[]{:S(2)}, u32[]{:S(2)}) collective-permute-start(bf16[384,1280]{1,0:T(8,128)(2,1)} %constant_dynamic-update-slice_fusion.15.r0), channel_id=1, source_target_pairs={{0,1},{1,0},{2,3},{3,2},{4,5},{5,4},{6,7},{7,6},{8,9},{9,8},{10,11... | collective-permute-start | bytes 2949128 | tf_op jit(solution)/shard_map/ppermute | solution.py:882
  133.0 21.0 %collective-permute-start.27 = (bf16[384,1280]{1,0:T(8,128)(2,1)}, bf16[384,1280]{1,0:T(8,128)(2,1)}, u32[]{:S(2)}, u32[]{:S(2)}) collective-permute-start(bf16[384,1280]{1,0:T(8,128)(2,1)} %constant_dynamic-update-slice_fusion.15.r0), channel_id=1, source_target_pairs={{0,2},{1,5},{2,0},{3,7},{4,6},{5,1},{6,4},{7,3},{8,10},{9,13},{10,... | collective-permute-start | bytes 2949128 | tf_op jit(solution)/shard_map/ppermute | solution.py:882
  133.9 14.2 %collective-permute-start.31 = (bf16[48,1920]{1,0:T(8,128)(2,1)S(1)}, bf16[48,1920]{1,0:T(8,128)(2,1)S(1)}, u32[]{:S(2)}, u32[]{:S(2)}) collective-permute-start(bf16[48,1920]{1,0:T(8,128)(2,1)S(1)} %get-tuple-element.599), channel_id=1, source_target_pairs={{0,24},{1,25},{2,26},{3,27},{4,28},{5,29},{6,30},{7,31},{8,0},{9,1... | collective-permute-start | bytes 552968 | tf_op jit(solution)/shard_map/ppermute | solution.py:882
  136.9 17.1 %collective-permute-start.30 = (bf16[48,1920]{1,0:T(8,128)(2,1)S(1)}, bf16[48,1920]{1,0:T(8,128)(2,1)S(1)}, u32[]{:S(2)}, u32[]{:S(2)}) collective-permute-start(bf16[48,1920]{1,0:T(8,128)(2,1)S(1)} %get-tuple-element.599), channel_id=1, source_target_pairs={{0,16},{1,17},{2,18},{3,19},{4,20},{5,21},{6,22},{7,23},{8,24},{9,... | collective-permute-start | bytes 552968 | tf_op jit(solution)/shard_map/ppermute | solution.py:882
  138.0 16.0 %collective-permute-start.29 = (bf16[48,1920]{1,0:T(8,128)(2,1)S(1)}, bf16[48,1920]{1,0:T(8,128)(2,1)S(1)}, u32[]{:S(2)}, u32[]{:S(2)}) collective-permute-start(bf16[48,1920]{1,0:T(8,128)(2,1)S(1)} %get-tuple-element.599), channel_id=1, source_target_pairs={{0,8},{1,9},{2,10},{3,11},{4,12},{5,13},{6,14},{7,15},{8,16},{9,17... | collective-permute-start | bytes 552968 | tf_op jit(solution)/shard_map/ppermute | solution.py:882
  166.7 16.4 %collective-permute-start.35 = (bf16[384,1920]{1,0:T(8,128)(2,1)S(1)}, bf16[384,1920]{1,0:T(8,128)(2,1)S(1)}, u32[]{:S(2)}, u32[]{:S(2)}) collective-permute-start(bf16[384,1920]{1,0:T(8,128)(2,1)S(1)} %constant_dynamic-update-slice_fusion.20.r0.u0.d0.refs_1_.refs_5_), channel_id=1, source_target_pairs={{0,1},{1,0},{2,3},{3,2},{4,5},{5,4},{6,7},{7,6},{8,9},{9,8},{10,11... | collective-permute-start | bytes 4423688 | tf_op jit(solution)/shard_map/ppermute | solution.py:882
  166.8 19.5 %collective-permute-start.34 = (bf16[384,1920]{1,0:T(8,128)(2,1)S(1)}, bf16[384,1920]{1,0:T(8,128)(2,1)}, u32[]{:S(2)}, u32[]{:S(2)}) collective-permute-start(bf16[384,1920]{1,0:T(8,128)(2,1)S(1)} %constant_dynamic-update-slice_fusion.20.r0.u0.d0.refs_1_.refs_5_), channel_id=1, source_target_pairs={{0,2},{1,5},{2,0},{3,7},{4,6},{5,1},{6,4},{7,3},{8,10},{9,13},{10,... | collective-permute-start | bytes 4423688 | tf_op jit(solution)/shard_map/ppermute | solution.py:882
  168.1 13.0 %collective-permute-start.38 = (bf16[48,1536]{1,0:T(8,128)(2,1)S(1)}, bf16[48,1536]{1,0:T(8,128)(2,1)S(1)}, u32[]{:S(2)}, u32[]{:S(2)}) collective-permute-start(bf16[48,1536]{1,0:T(8,128)(2,1)S(1)} %get-tuple-element.595), channel_id=1, source_target_pairs={{0,24},{1,25},{2,26},{3,27},{4,28},{5,29},{6,30},{7,31},{8,0},{9,1... | collective-permute-start | bytes 442376 | tf_op jit(solution)/shard_map/ppermute | solution.py:882
  168.1 15.0 %collective-permute-start.37 = (bf16[48,1536]{1,0:T(8,128)(2,1)S(1)}, bf16[48,1536]{1,0:T(8,128)(2,1)S(1)}, u32[]{:S(2)}, u32[]{:S(2)}) collective-permute-start(bf16[48,1536]{1,0:T(8,128)(2,1)S(1)} %get-tuple-element.595), channel_id=1, source_target_pairs={{0,16},{1,17},{2,18},{3,19},{4,20},{5,21},{6,22},{7,23},{8,24},{9,... | collective-permute-start | bytes 442376 | tf_op jit(solution)/shard_map/ppermute | solution.py:882
  169.5 13.6 %collective-permute-start.36 = (bf16[48,1536]{1,0:T(8,128)(2,1)S(1)}, bf16[48,1536]{1,0:T(8,128)(2,1)S(1)}, u32[]{:S(2)}, u32[]{:S(2)}) collective-permute-start(bf16[48,1536]{1,0:T(8,128)(2,1)S(1)} %get-tuple-element.595), channel_id=1, source_target_pairs={{0,8},{1,9},{2,10},{3,11},{4,12},{5,13},{6,14},{7,15},{8,16},{9,17... | collective-permute-start | bytes 442376 | tf_op jit(solution)/shard_map/ppermute | solution.py:882
  186.3 12.0 %collective-permute-start.39 = (bf16[384,1920]{1,0:T(8,128)(2,1)}, bf16[384,1920]{1,0:T(8,128)(2,1)S(1)}, u32[]{:S(2)}, u32[]{:S(2)}) collective-permute-start(bf16[384,1920]{1,0:T(8,128)(2,1)} %collective-permute-done.34.r1.u1.d1.refs_2_.refs_6_), channel_id=1, source_target_pairs={{0,1},{1,0},{2,3},{3,2},{4,5},{5,4},{6,7},{7,6},{8,9},{9,8},{10,11... | collective-permute-start | bytes 4423688 | tf_op jit(solution)/shard_map/ppermute | solution.py:882
  200.6 12.6 %collective-permute-start.42 = (bf16[384,1536]{1,0:T(8,128)(2,1)}, bf16[384,1536]{1,0:T(8,128)(2,1)S(1)}, u32[]{:S(2)}, u32[]{:S(2)}) collective-permute-start(bf16[384,1536]{1,0:T(8,128)(2,1)} %constant_dynamic-update-slice_fusion.25.u0.d0.refs_0_.refs_4_), channel_id=1, source_target_pairs={{0,1},{1,0},{2,3},{3,2},{4,5},{5,4},{6,7},{7,6},{8,9},{9,8},{10,11... | collective-permute-start | bytes 3538952 | tf_op jit(solution)/shard_map/ppermute | solution.py:882
  200.8 16.4 %collective-permute-start.41 = (bf16[384,1536]{1,0:T(8,128)(2,1)}, bf16[384,1536]{1,0:T(8,128)(2,1)S(1)}, u32[]{:S(2)}, u32[]{:S(2)}) collective-permute-start(bf16[384,1536]{1,0:T(8,128)(2,1)} %constant_dynamic-update-slice_fusion.25.u0.d0.refs_0_.refs_4_), channel_id=1, source_target_pairs={{0,2},{1,5},{2,0},{3,7},{4,6},{5,1},{6,4},{7,3},{8,10},{9,13},{10,... | collective-permute-start | bytes 3538952 | tf_op jit(solution)/shard_map/ppermute | solution.py:882
  252.0 15.1 %collective-permute-start.44 = (bf16[768,768]{1,0:T(8,128)(2,1)}, bf16[768,768]{1,0:T(8,128)(2,1)S(1)}, u32[]{:S(2)}, u32[]{:S(2)}) collective-permute-start(bf16[768,768]{1,0:T(8,128)(2,1)} %get-tuple-element.391), channel_id=1, source_target_pairs={{0,1},{1,0},{2,3},{3,2},{4,5},{5,4},{6,7},{7,6},{8,9},{9,8},{10,11... | collective-permute-start | bytes 3538952 | tf_op jit(solution)/shard_map/ppermute | solution.py:882
  252.6 14.5 %collective-permute-start.45 = (bf16[768,768]{1,0:T(8,128)(2,1)}, bf16[768,768]{1,0:T(8,128)(2,1)S(1)}, u32[]{:S(2)}, u32[]{:S(2)}) collective-permute-start(bf16[768,768]{1,0:T(8,128)(2,1)} %get-tuple-element.392), channel_id=1, source_target_pairs={{0,1},{1,0},{2,3},{3,2},{4,5},{5,4},{6,7},{7,6},{8,9},{9,8},{10,11... | collective-permute-start | bytes 3538952 | tf_op jit(solution)/shard_map/ppermute | solution.py:882
  271.5 16.5 %collective-permute-start.46 = (bf16[384,1536]{1,0:T(8,128)(2,1)}, bf16[384,1536]{1,0:T(8,128)(2,1)}, u32[]{:S(2)}, u32[]{:S(2)}) collective-permute-start(bf16[384,1536]{1,0:T(8,128)(2,1)} %sum_pieces.12), channel_id=1, source_target_pairs={{0,2},{1,5},{2,0},{3,7},{4,6},{5,1},{6,4},{7,3},{8,10},{9,13},{10,... | collective-permute-start | bytes 3538952 | tf_op jit(solution)/shard_map/ppermute | solution.py:882
  272.7 15.3 %collective-permute-start.47 = (bf16[768,768]{1,0:T(8,128)(2,1)}, bf16[768,768]{1,0:T(8,128)(2,1)S(1)}, u32[]{:S(2)}, u32[]{:S(2)}) collective-permute-start(bf16[768,768]{1,0:T(8,128)(2,1)} %get-tuple-element.405), channel_id=1, source_target_pairs={{0,1},{1,0},{2,3},{3,2},{4,5},{5,4},{6,7},{7,6},{8,9},{9,8},{10,11... | collective-permute-start | bytes 3538952 | tf_op jit(solution)/shard_map/ppermute | solution.py:882
  273.1 15.0 %collective-permute-start.48 = (bf16[768,768]{1,0:T(8,128)(2,1)S(1)}, bf16[768,768]{1,0:T(8,128)(2,1)S(1)}, u32[]{:S(2)}, u32[]{:S(2)}) collective-permute-start(bf16[768,768]{1,0:T(8,128)(2,1)S(1)} %copy-done.63), channel_id=1, source_target_pairs={{0,1},{1,0},{2,3},{3,2},{4,5},{5,4},{6,7},{7,6},{8,9},{9,8},{10,11... | collective-permute-start | bytes 3538952 | tf_op jit(solution)/shard_map/ppermute | solution.py:882
  305.6 20.0 %collective-permute-start.54 = (bf16[384,1920]{1,0:T(8,128)(2,1)}, bf16[384,1920]{1,0:T(8,128)(2,1)S(1)}, u32[]{:S(2)}, u32[]{:S(2)}) collective-permute-start(bf16[384,1920]{1,0:T(8,128)(2,1)} %sum_pieces.14), channel_id=1, source_target_pairs={{0,2},{1,5},{2,0},{3,7},{4,6},{5,1},{6,4},{7,3},{8,10},{9,13},{10,... | collective-permute-start | bytes 4423688 | tf_op jit(solution)/shard_map/ppermute | solution.py:882
  309.4 16.1 %collective-permute-start.51 = (bf16[48,1536]{1,0:T(8,128)(2,1)}, bf16[48,1536]{1,0:T(8,128)(2,1)S(1)}, u32[]{:S(2)}, u32[]{:S(2)}) collective-permute-start(bf16[48,1536]{1,0:T(8,128)(2,1)} %get-tuple-element.420), channel_id=1, source_target_pairs={{0,24},{1,25},{2,26},{3,27},{4,28},{5,29},{6,30},{7,31},{8,0},{9,1... | collective-permute-start | bytes 442376 | tf_op jit(solution)/shard_map/ppermute | solution.py:882
  309.4 16.1 %collective-permute-start.52 = (bf16[48,1536]{1,0:T(8,128)(2,1)}, bf16[48,1536]{1,0:T(8,128)(2,1)S(1)}, u32[]{:S(2)}, u32[]{:S(2)}) collective-permute-start(bf16[48,1536]{1,0:T(8,128)(2,1)} %get-tuple-element.421), channel_id=1, source_target_pairs={{0,16},{1,17},{2,18},{3,19},{4,20},{5,21},{6,22},{7,23},{8,24},{9,... | collective-permute-start | bytes 442376 | tf_op jit(solution)/shard_map/ppermute | solution.py:882
  310.8 14.8 %collective-permute-start.53 = (bf16[48,1536]{1,0:T(8,128)(2,1)}, bf16[48,1536]{1,0:T(8,128)(2,1)S(1)}, u32[]{:S(2)}, u32[]{:S(2)}) collective-permute-start(bf16[48,1536]{1,0:T(8,128)(2,1)} %get-tuple-element.422), channel_id=1, source_target_pairs={{0,8},{1,9},{2,10},{3,11},{4,12},{5,13},{6,14},{7,15},{8,16},{9,17... | collective-permute-start | bytes 442376 | tf_op jit(solution)/shard_map/ppermute | solution.py:882
  325.6 20.9 %collective-permute-start.57 = (bf16[768,1280]{1,0:T(8,128)(2,1)}, bf16[768,1280]{1,0:T(8,128)(2,1)S(1)}, u32[]{:S(2)}, u32[]{:S(2)}) collective-permute-start(bf16[768,1280]{1,0:T(8,128)(2,1)} %get-tuple-element.447), channel_id=1, source_target_pairs={{0,1},{1,0},{2,3},{3,2},{4,5},{5,4},{6,7},{7,6},{8,9},{9,8},{10,11... | collective-permute-start | bytes 5898248 | tf_op jit(solution)/shard_map/ppermute | solution.py:882
  329.4 16.9 %collective-permute-start.56 = (bf16[192,1920]{1,0:T(8,128)(2,1)}, bf16[192,1920]{1,0:T(8,128)(2,1)S(1)}, u32[]{:S(2)}, u32[]{:S(2)}) collective-permute-start(bf16[192,1920]{1,0:T(8,128)(2,1)} %sum_pieces.15), channel_id=1, source_target_pairs={{0,4},{1,3},{2,6},{3,1},{4,0},{5,7},{6,2},{7,5},{8,12},{9,11},{10,... | collective-permute-start | bytes 2211848 | tf_op jit(solution)/shard_map/ppermute | solution.py:882
  332.7 13.7 %collective-permute-start.55 = (bf16[24,1536]{1,0:T(8,128)(2,1)}, bf16[24,1536]{1,0:T(8,128)(2,1)S(1)}, u32[]{:S(2)}, u32[]{:S(2)}) collective-permute-start(bf16[24,1536]{1,0:T(8,128)(2,1)} %get-tuple-element.445), channel_id=1, source_target_pairs={{0,1},{1,0},{2,3},{3,2},{4,5},{5,4},{6,7},{7,6},{8,9},{9,8},{10,11... | collective-permute-start | bytes 221192 | tf_op jit(solution)/shard_map/ppermute | solution.py:882
  346.4 30.7 %collective-permute-start.62 = (bf16[768,768]{1,0:T(8,128)(2,1)}, bf16[768,768]{1,0:T(8,128)(2,1)S(1)}, u32[]{:S(2)}, u32[]{:S(2)}) collective-permute-start(bf16[768,768]{1,0:T(8,128)(2,1)} %get-tuple-element.462), channel_id=1, source_target_pairs={{0,1},{1,0},{2,3},{3,2},{4,5},{5,4},{6,7},{7,6},{8,9},{9,8},{10,11... | collective-permute-start | bytes 3538952 | tf_op jit(solution)/shard_map/ppermute | solution.py:882
  347.0 30.2 %collective-permute-start.63 = (bf16[768,768]{1,0:T(8,128)(2,1)}, bf16[768,768]{1,0:T(8,128)(2,1)}, u32[]{:S(2)}, u32[]{:S(2)}) collective-permute-start(bf16[768,768]{1,0:T(8,128)(2,1)} %get-tuple-element.463), channel_id=1, source_target_pairs={{0,1},{1,0},{2,3},{3,2},{4,5},{5,4},{6,7},{7,6},{8,9},{9,8},{10,11... | collective-permute-start | bytes 3538952 | tf_op jit(solution)/shard_map/ppermute | solution.py:882
  350.7 26.5 %collective-permute-start.61 = (bf16[384,1280]{1,0:T(8,128)(2,1)}, bf16[384,1280]{1,0:T(8,128)(2,1)S(1)}, u32[]{:S(2)}, u32[]{:S(2)}) collective-permute-start(bf16[384,1280]{1,0:T(8,128)(2,1)} %sum_pieces.16), channel_id=1, source_target_pairs={{0,2},{1,5},{2,0},{3,7},{4,6},{5,1},{6,4},{7,3},{8,10},{9,13},{10,... | collective-permute-start | bytes 2949128 | tf_op jit(solution)/shard_map/ppermute | solution.py:882
  356.4 20.7 %collective-permute-start.59 = (bf16[48,1920]{1,0:T(8,128)(2,1)}, bf16[48,1920]{1,0:T(8,128)(2,1)S(1)}, u32[]{:S(2)}, u32[]{:S(2)}) collective-permute-start(bf16[48,1920]{1,0:T(8,128)(2,1)} %get-tuple-element.460), channel_id=1, source_target_pairs={{0,16},{1,17},{2,18},{3,19},{4,20},{5,21},{6,22},{7,23},{8,24},{9,... | collective-permute-start | bytes 552968 | tf_op jit(solution)/shard_map/ppermute | solution.py:882
  361.9 15.2 %collective-permute-start.60 = (bf16[48,1920]{1,0:T(8,128)(2,1)}, bf16[48,1920]{1,0:T(8,128)(2,1)S(1)}, u32[]{:S(2)}, u32[]{:S(2)}) collective-permute-start(bf16[48,1920]{1,0:T(8,128)(2,1)} %get-tuple-element.461), channel_id=1, source_target_pairs={{0,8},{1,9},{2,10},{3,11},{4,12},{5,13},{6,14},{7,15},{8,16},{9,17... | collective-permute-start | bytes 552968 | tf_op jit(solution)/shard_map/ppermute | solution.py:882
  381.2 21.8 %collective-permute-start.66 = (bf16[384,1536]{1,0:T(8,128)(2,1)}, bf16[384,1536]{1,0:T(8,128)(2,1)}, u32[]{:S(2)}, u32[]{:S(2)}) collective-permute-start(bf16[384,1536]{1,0:T(8,128)(2,1)} %sum_pieces.18), channel_id=1, source_target_pairs={{0,2},{1,5},{2,0},{3,7},{4,6},{5,1},{6,4},{7,3},{8,10},{9,13},{10,... | collective-permute-start | bytes 3538952 | tf_op jit(solution)/shard_map/ppermute | solution.py:882
  382.9 20.1 %collective-permute-start.67 = (bf16[768,768]{1,0:T(8,128)(2,1)}, bf16[768,768]{1,0:T(8,128)(2,1)S(1)}, u32[]{:S(2)}, u32[]{:S(2)}) collective-permute-start(bf16[768,768]{1,0:T(8,128)(2,1)} %get-tuple-element.484), channel_id=1, source_target_pairs={{0,1},{1,0},{2,3},{3,2},{4,5},{5,4},{6,7},{7,6},{8,9},{9,8},{10,11... | collective-permute-start | bytes 3538952 | tf_op jit(solution)/shard_map/ppermute | solution.py:882
  382.9 20.1 %collective-permute-start.68 = (bf16[768,768]{1,0:T(8,128)(2,1)}, bf16[768,768]{1,0:T(8,128)(2,1)S(1)}, u32[]{:S(2)}, u32[]{:S(2)}) collective-permute-start(bf16[768,768]{1,0:T(8,128)(2,1)} %get-tuple-element.485), channel_id=1, source_target_pairs={{0,1},{1,0},{2,3},{3,2},{4,5},{5,4},{6,7},{7,6},{8,9},{9,8},{10,11... | collective-permute-start | bytes 3538952 | tf_op jit(solution)/shard_map/ppermute | solution.py:882
  385.7 16.8 %collective-permute-start.65 = (bf16[192,1280]{1,0:T(8,128)(2,1)}, bf16[192,1280]{1,0:T(8,128)(2,1)S(1)}, u32[]{:S(2)}, u32[]{:S(2)}) collective-permute-start(bf16[192,1280]{1,0:T(8,128)(2,1)} %sum_pieces.17), channel_id=1, source_target_pairs={{0,4},{1,3},{2,6},{3,1},{4,0},{5,7},{6,2},{7,5},{8,12},{9,11},{10,... | collective-permute-start | bytes 1474568 | tf_op jit(solution)/shard_map/ppermute | solution.py:882
  387.7 14.8 %collective-permute-start.64 = (bf16[24,1920]{1,0:T(8,128)(2,1)}, bf16[24,1920]{1,0:T(8,128)(2,1)S(1)}, u32[]{:S(2)}, u32[]{:S(2)}) collective-permute-start(bf16[24,1920]{1,0:T(8,128)(2,1)} %get-tuple-element.479), channel_id=1, source_target_pairs={{0,1},{1,0},{2,3},{3,2},{4,5},{5,4},{6,7},{7,6},{8,9},{9,8},{10,11... | collective-permute-start | bytes 276488 | tf_op jit(solution)/shard_map/ppermute | solution.py:882
  406.3 19.4 %collective-permute-start.72 = (bf16[192,1536]{1,0:T(8,128)(2,1)}, bf16[192,1536]{1,0:T(8,128)(2,1)S(1)}, u32[]{:S(2)}, u32[]{:S(2)}) collective-permute-start(bf16[192,1536]{1,0:T(8,128)(2,1)} %sum_pieces.19), channel_id=1, source_target_pairs={{0,4},{1,3},{2,6},{3,1},{4,0},{5,7},{6,2},{7,5},{8,12},{9,11},{10,... | collective-permute-start | bytes 1769480 | tf_op jit(solution)/shard_map/ppermute | solution.py:882
  408.1 17.7 %collective-permute-start.73 = (bf16[768,384]{1,0:T(8,128)(2,1)}, bf16[768,384]{1,0:T(8,128)(2,1)S(1)}, u32[]{:S(2)}, u32[]{:S(2)}) collective-permute-start(bf16[768,384]{1,0:T(8,128)(2,1)} %get-tuple-element.500), channel_id=1, source_target_pairs={{0,1},{1,0},{2,3},{3,2},{4,5},{5,4},{6,7},{7,6},{8,9},{9,8},{10,11... | collective-permute-start | bytes 1769480 | tf_op jit(solution)/shard_map/ppermute | solution.py:882
  410.5 12.8 %collective-permute-start.69 = (bf16[48,1280]{1,0:T(8,128)(2,1)}, bf16[48,1280]{1,0:T(8,128)(2,1)S(1)}, u32[]{:S(2)}, u32[]{:S(2)}) collective-permute-start(bf16[48,1280]{1,0:T(8,128)(2,1)} %get-tuple-element.496), channel_id=1, source_target_pairs={{0,24},{1,25},{2,26},{3,27},{4,28},{5,29},{6,30},{7,31},{8,0},{9,1... | collective-permute-start | bytes 368648 | tf_op jit(solution)/shard_map/ppermute | solution.py:882
  413.7 12.0 %collective-permute-start.70 = (bf16[48,1280]{1,0:T(8,128)(2,1)}, bf16[48,1280]{1,0:T(8,128)(2,1)S(1)}, u32[]{:S(2)}, u32[]{:S(2)}) collective-permute-start(bf16[48,1280]{1,0:T(8,128)(2,1)} %get-tuple-element.497), channel_id=1, source_target_pairs={{0,16},{1,17},{2,18},{3,19},{4,20},{5,21},{6,22},{7,23},{8,24},{9,... | collective-permute-start | bytes 368648 | tf_op jit(solution)/shard_map/ppermute | solution.py:882
  413.7 12.0 %collective-permute-start.71 = (bf16[48,1280]{1,0:T(8,128)(2,1)}, bf16[48,1280]{1,0:T(8,128)(2,1)S(1)}, u32[]{:S(2)}, u32[]{:S(2)}) collective-permute-start(bf16[48,1280]{1,0:T(8,128)(2,1)} %get-tuple-element.498), channel_id=1, source_target_pairs={{0,8},{1,9},{2,10},{3,11},{4,12},{5,13},{6,14},{7,15},{8,16},{9,17... | collective-permute-start | bytes 368648 | tf_op jit(solution)/shard_map/ppermute | solution.py:882
  430.0 22.5 %collective-permute-start.78 = (bf16[384,1920]{1,0:T(8,128)(2,1)}, bf16[384,1920]{1,0:T(8,128)(2,1)S(1)}, u32[]{:S(2)}, u32[]{:S(2)}) collective-permute-start(bf16[384,1920]{1,0:T(8,128)(2,1)} %sum_pieces.20), channel_id=1, source_target_pairs={{0,2},{1,5},{2,0},{3,7},{4,6},{5,1},{6,4},{7,3},{8,10},{9,13},{10,... | collective-permute-start | bytes 4423688 | tf_op jit(solution)/shard_map/ppermute | solution.py:882
  435.4 17.0 %collective-permute-start.74 = (bf16[24,1280]{1,0:T(8,128)(2,1)}, bf16[24,1280]{1,0:T(8,128)(2,1)S(1)}, u32[]{:S(2)}, u32[]{:S(2)}) collective-permute-start(bf16[24,1280]{1,0:T(8,128)(2,1)} %get-tuple-element.506), channel_id=1, source_target_pairs={{0,1},{1,0},{2,3},{3,2},{4,5},{5,4},{6,7},{7,6},{8,9},{9,8},{10,11... | collective-permute-start | bytes 184328 | tf_op jit(solution)/shard_map/ppermute | solution.py:882
  435.4 17.0 %collective-permute-start.75 = (bf16[48,1536]{1,0:T(8,128)(2,1)}, bf16[48,1536]{1,0:T(8,128)(2,1)S(1)}, u32[]{:S(2)}, u32[]{:S(2)}) collective-permute-start(bf16[48,1536]{1,0:T(8,128)(2,1)} %get-tuple-element.508), channel_id=1, source_target_pairs={{0,24},{1,25},{2,26},{3,27},{4,28},{5,29},{6,30},{7,31},{8,0},{9,1... | collective-permute-start | bytes 442376 | tf_op jit(solution)/shard_map/ppermute | solution.py:882
  436.1 16.3 %collective-permute-start.76 = (bf16[48,1536]{1,0:T(8,128)(2,1)}, bf16[48,1536]{1,0:T(8,128)(2,1)S(1)}, u32[]{:S(2)}, u32[]{:S(2)}) collective-permute-start(bf16[48,1536]{1,0:T(8,128)(2,1)} %get-tuple-element.509), channel_id=1, source_target_pairs={{0,16},{1,17},{2,18},{3,19},{4,20},{5,21},{6,22},{7,23},{8,24},{9,... | collective-permute-start | bytes 442376 | tf_op jit(solution)/shard_map/ppermute | solution.py:882
  437.8 14.6 %collective-permute-start.77 = (bf16[48,1536]{1,0:T(8,128)(2,1)}, bf16[48,1536]{1,0:T(8,128)(2,1)S(1)}, u32[]{:S(2)}, u32[]{:S(2)}) collective-permute-start(bf16[48,1536]{1,0:T(8,128)(2,1)} %get-tuple-element.510), channel_id=1, source_target_pairs={{0,8},{1,9},{2,10},{3,11},{4,12},{5,13},{6,14},{7,15},{8,16},{9,17... | collective-permute-start | bytes 442376 | tf_op jit(solution)/shard_map/ppermute | solution.py:882
  452.4 15.7 %collective-permute-start.81 = (bf16[768,1280]{1,0:T(8,128)(2,1)}, bf16[768,1280]{1,0:T(8,128)(2,1)S(1)}, u32[]{:S(2)}, u32[]{:S(2)}) collective-permute-start(bf16[768,1280]{1,0:T(8,128)(2,1)} %get-tuple-element.536), channel_id=1, source_target_pairs={{0,1},{1,0},{2,3},{3,2},{4,5},{5,4},{6,7},{7,6},{8,9},{9,8},{10,11... | collective-permute-start | bytes 5898248 | tf_op jit(solution)/shard_map/ppermute | solution.py:882
  473.1 21.3 %collective-permute-start.85 = (bf16[384,1280]{1,0:T(8,128)(2,1)}, bf16[384,1280]{1,0:T(8,128)(2,1)S(1)}, u32[]{:S(2)}, u32[]{:S(2)}) collective-permute-start(bf16[384,1280]{1,0:T(8,128)(2,1)} %sum_pieces.22), channel_id=1, source_target_pairs={{0,2},{1,5},{2,0},{3,7},{4,6},{5,1},{6,4},{7,3},{8,10},{9,13},{10,... | collective-permute-start | bytes 2949128 | tf_op jit(solution)/shard_map/ppermute | solution.py:882
  479.2 15.2 %collective-permute-start.83 = (bf16[48,1920]{1,0:T(8,128)(2,1)}, bf16[48,1920]{1,0:T(8,128)(2,1)S(1)}, u32[]{:S(2)}, u32[]{:S(2)}) collective-permute-start(bf16[48,1920]{1,0:T(8,128)(2,1)} %get-tuple-element.540), channel_id=1, source_target_pairs={{0,16},{1,17},{2,18},{3,19},{4,20},{5,21},{6,22},{7,23},{8,24},{9,... | collective-permute-start | bytes 552968 | tf_op jit(solution)/shard_map/ppermute | solution.py:882
  479.2 15.2 %collective-permute-start.84 = (bf16[48,1920]{1,0:T(8,128)(2,1)}, bf16[48,1920]{1,0:T(8,128)(2,1)S(1)}, u32[]{:S(2)}, u32[]{:S(2)}) collective-permute-start(bf16[48,1920]{1,0:T(8,128)(2,1)} %get-tuple-element.541), channel_id=1, source_target_pairs={{0,8},{1,9},{2,10},{3,11},{4,12},{5,13},{6,14},{7,15},{8,16},{9,17... | collective-permute-start | bytes 552968 | tf_op jit(solution)/shard_map/ppermute | solution.py:882
  (96 other events, 670.9 us)

commit v5 on v4

--- a/solution.py
+++ b/solution.py
@@ -15,7 +15,6 @@
 AXES = ("dp", "fsdp")
 VMEM_LIMIT = 60 * 1024 * 1024
 FORWARD_TILE = 768
-BACKWARD_TILE = 768
 
 
 def cost(flops, moved, hard=0):
@@ -349,164 +348,181 @@
     return jnp.sum(value.astype(WIDE), axis=0, keepdims=True)
 
 
-def mlp_backward(spot, up, down, e, a2, z, slope, before):
+def mlp_backward(spot, up, down, e, a2, z, slope, before, finish):
     rows, width = e.shape
     hidden = z.shape[1]
     half = hidden // 2
-    tile = BACKWARD_TILE
-    tiles = half // tile
-    whole, mine, rest, fixed = side_tiles(tiles)
+    part = width // 2
+    wide = 2 * half + (part if finish else 0)
     (up_refs, up_col), (down_refs, down_col) = up, down
-    extra = [] if before is None else [before]
+    given = [] if before is None else [before]
+    if finish:
+        (out_refs, out_col), h2, mixed, table = finish
+        given += [h2, *mixed, table]
+        moved = [*up_refs, *down_refs, *out_refs]
+    else:
+        moved = [*up_refs, *down_refs]
+
+    def whole(s, spot):
+        return 0, jnp.where(s == 0, spot[3], 1 - spot[3])
+
+    def fixed(s, spot):
+        return 0, 0
 
     def body(spot_ref, e_ref, a_ref, z_ref, s_ref, *refs):
-        if extra:
-            before_ref, refs = refs[0], refs[1:]
-        (
-            u0, u1, u2, u3, d0, d1, d2, d3,
-            acc_ref, um_ref, ur_ref, dm_ref, dr_ref, bd_ref, bu_ref,
-            wu_ref, wd_ref, em_ref, emt_ref, at_ref, sems_u, sems_d,
-        ) = refs
-        side, n = pl.program_id(0), pl.program_id(1)
-        ups = piece_copies(spot_ref, (u0, u1, u2, u3), wu_ref, sems_u, up_col, half)
-        downs = piece_copies(spot_ref, (d0, d1, d2, d3), wd_ref, sems_d, down_col, half)
-
-        @pl.when((side == 0) & (n == 0))
+        given_refs, refs = refs[: len(given)], refs[len(given) :]
+        moved_refs, refs = refs[: len(moved)], refs[len(moved) :]
+        sides_out, refs = refs[:2], refs[2:]
+        bd_ref, bu_ref = refs[:2]
+        if finish:
+            e2_ref, da_ref, sums_ref, acc_ref, wo_ref, mt_ref, ey_ref, sems_o = refs[2:10]
+            refs = refs[10:]
+            h_ref, m0_ref, m1_ref, t_ref = given_refs[-4:]
+        else:
+            acc_ref, refs = refs[2], refs[3:]
+        wu_ref, wd_ref, em_ref, emt_ref, at_ref, grad_ref, sems_u, sems_d, sems_g = refs
+        side = pl.program_id(0)
+        c = spot_ref[3]
+        ups = piece_copies(spot_ref, moved_refs[:4], wu_ref, sems_u, up_col, half)
+        downs = piece_copies(spot_ref, moved_refs[4:8], wd_ref, sems_d, down_col, half)
+        copies = ups + downs
+        if finish:
+            outs = piece_copies(spot_ref, moved_refs[8:], wo_ref, sems_o, out_col, part)
+
+        def stored(n, start, size):
+            at = pl.ds(start, size)
+            return pltpu.make_async_copy(
+                grad_ref.at[n, :, at], sides_out[n].at[:, at], sems_g.at[n, start // (2 * half)]
+            )
+
+        @pl.when(side == 0)
         def begin():
             for copy in downs[:16] + ups[:16] + downs[16:] + ups[16:]:
                 copy.start()
+            if finish:
+                for copy in outs:
+                    copy.start()
             em = e_ref[...].astype(LOW)
             em_ref[...] = em
             bd_ref[...] = column_sum(em)
             emt_ref[...] = em.T
             at_ref[...] = a_ref[...].T
-            acc_ref[...] = before_ref[...] if extra else jnp.zeros_like(acc_ref)
+            acc_ref[...] = jnp.zeros_like(acc_ref) if before is None else given_refs[0][...]
             for copy in downs[:16] + ups[:16]:
                 copy.wait()
 
-        @pl.when((side == 1) & (n == 0))
+        @pl.when(side == 1)
         def more():
             for copy in downs[16:] + ups[16:]:
                 copy.wait()
 
-        owner = jnp.where(side == 0, spot_ref[3], 1 - spot_ref[3])
-        at = pl.ds(pl.multiple_of(owner * half + n * tile, LANES), tile)
+        owner = jnp.where(side == 0, c, 1 - c)
+        at = pl.ds(pl.multiple_of(owner * half, LANES), half)
         starts = block_starts(spot_ref, owner, width // 16)
+        grads = grad_ref.at[side]
         du = (dot(em_ref[...], wd_ref[:, at]) * s_ref[...].astype(WIDE)).astype(LOW)
         bu_ref[...] = column_sum(du)
-        down_grad = dot(emt_ref[...], z_ref[...])
-        up_grad = dot(at_ref[...], du)
+        put_blocks(dot(emt_ref[...], z_ref[...]), grads, starts, 0, half)
+        put_blocks(dot(at_ref[...], du), grads, starts, half, half)
         acc_ref[...] += dot_nt(du, wu_ref[:, at])
 
         @pl.when(side == 0)
-        def first_half():
-            put_blocks(down_grad, dm_ref, starts, 0, tile)
-            put_blocks(up_grad, um_ref, starts, 0, tile)
+        def first_out():
+            stored(0, 0, 2 * half).start()
 
         @pl.when(side == 1)
-        def second_half():
-            put_blocks(down_grad, dr_ref, starts, 0, tile)
-            put_blocks(up_grad, ur_ref, starts, 0, tile)
-
+        def end():
+            stored(1, 0, 2 * half).start()
+            if finish:
+                mt_ref[:part, :] = m0_ref[...].T
+                mt_ref[part:, :] = m1_ref[...].T
+                dv, gain, shift = norm_back(
+                    h_ref[...], t_ref[GAIN2 : GAIN2 + 1, :], acc_ref[...]
+                )
+                e2 = e_ref[...] + dv
+                e2_ref[...] = e2
+                ey = e2.astype(LOW)
+                ey_ref[...] = ey
+                sums_ref[0:1, :] = gain
+                sums_ref[1:2, :] = shift
+                sums_ref[2:3, :] = column_sum(ey)
+                for copy in outs:
+                    copy.wait()
+                da_ref[...] = dot_nt(ey, wo_ref[...]).astype(LOW)
+                for n, holder in enumerate((c, 1 - c)):
+                    to = pl.ds(pl.multiple_of(holder * part, LANES), part)
+                    put_blocks(
+                        dot(mt_ref[...], ey_ref[:, to]),
+                        grad_ref.at[n],
+                        block_starts(spot_ref, holder, width // 16),
+                        2 * half,
+                        part,
+                    )
+                    stored(n, 2 * half, part).start()
+                for n in range(2):
+                    stored(n, 2 * half, part).wait()
+            for n in range(2):
+                stored(n, 0, 2 * half).wait()
+
+    out_shape = [jax.ShapeDtypeStruct((width, wide), LOW)] * 2 + [
+        jax.ShapeDtypeStruct((1, width), WIDE),
+        jax.ShapeDtypeStruct((1, hidden), WIDE),
+    ]
+    out_specs = any_specs(2) + [
+        pl.BlockSpec((1, width), fixed),
+        pl.BlockSpec((1, half), whole),
+    ]
+    scratch = []
+    row_spec = pl.BlockSpec((rows, width), fixed)
+    if finish:
+        out_shape += [
+            jax.ShapeDtypeStruct((rows, width), WIDE),
+            jax.ShapeDtypeStruct((rows, width), LOW),
+            jax.ShapeDtypeStruct((8, width), WIDE),
+        ]
+        out_specs += [row_spec, row_spec, pl.BlockSpec((8, width), fixed)]
+        scratch += [
+            pltpu.VMEM((rows, width), WIDE),
+            pltpu.VMEM((width, width), LOW),
+            pltpu.VMEM((width, rows), LOW),
+            pltpu.VMEM((rows, width), LOW),
+            pltpu.SemaphoreType.DMA((32,)),
+        ]
+    else:
+        out_shape += [jax.ShapeDtypeStruct((rows, width), WIDE)]
+        out_specs += [row_spec]
     return pl.pallas_call(
         body,
-        out_shape=[
-            jax.ShapeDtypeStruct((rows, width), WIDE),
-            jax.ShapeDtypeStruct((width, half), LOW),
-            jax.ShapeDtypeStruct((width, half), LOW),
-            jax.ShapeDtypeStruct((width, half), LOW),
-            jax.ShapeDtypeStruct((width, half), LOW),
-            jax.ShapeDtypeStruct((1, width), WIDE),
-            jax.ShapeDtypeStruct((1, hidden), WIDE),
-        ],
+        out_shape=out_shape,
         grid_spec=pltpu.PrefetchScalarGridSpec(
             num_scalar_prefetch=1,
-            grid=(2, tiles),
+            grid=(2,),
             in_specs=[
-                pl.BlockSpec((rows, width), fixed),
-                pl.BlockSpec((rows, width), fixed),
-                pl.BlockSpec((rows, tile), whole),
-                pl.BlockSpec((rows, tile), whole),
+                row_spec,
+                row_spec,
+                pl.BlockSpec((rows, half), whole),
+                pl.BlockSpec((rows, half), whole),
             ]
-            + [pl.BlockSpec((rows, width), fixed)] * len(extra)
-            + any_specs(8),
-            out_specs=[
-                pl.BlockSpec((rows, width), fixed),
-                pl.BlockSpec((width, tile), mine),
-                pl.BlockSpec((width, tile), rest),
-                pl.BlockSpec((width, tile), mine),
-                pl.BlockSpec((width, tile), rest),
-                pl.BlockSpec((1, width), fixed),
-                pl.BlockSpec((1, tile), whole),
-            ],
-            scratch_shapes=[
+            + [pl.BlockSpec(value.shape, fixed) for value in given]
+            + any_specs(len(moved)),
+            out_specs=out_specs,
+            scratch_shapes=scratch
+            + [
                 pltpu.VMEM((width, hidden), LOW),
                 pltpu.VMEM((width, hidden), LOW),
                 pltpu.VMEM((rows, width), LOW),
                 pltpu.VMEM((width, rows), LOW),
                 pltpu.VMEM((width, rows), LOW),
+                pltpu.VMEM((2, width, wide), LOW),
                 pltpu.SemaphoreType.DMA((32,)),
                 pltpu.SemaphoreType.DMA((32,)),
+                pltpu.SemaphoreType.DMA((2, 2)),
             ],
         ),
         compiler_params=params(),
         cost_estimate=cost(8 * rows * width * hidden, 8 * width * hidden + 4 * rows * hidden),
         name="mlp_backward",
-    )(spot, e, a2, z, slope, *extra, *up_refs, *down_refs)
-
-
-def middle_backward(spot, out, e, h2, mixed, acc, table):
-    rows, width = e.shape
-    part = width // 2
-    refs, column = out
-
-    def body(
-        spot_ref, r0, r1, r2, r3, e_ref, h_ref, m0_ref, m1_ref, acc_ref, t_ref,
-        e2_ref, da_ref, mine_ref, rest_ref, sums_ref, w_ref, mt_ref, ey_ref, sems,
-    ):
-        copies = piece_copies(spot_ref, (r0, r1, r2, r3), w_ref, sems, column, part)
-        for copy in copies:
-            copy.start()
-        mt_ref[:part, :] = m0_ref[...].T
-        mt_ref[part:, :] = m1_ref[...].T
-        dv, gain, shift = norm_back(h_ref[...], t_ref[GAIN2 : GAIN2 + 1, :], acc_ref[...])
-        e2 = e_ref[...] + dv
-        e2_ref[...] = e2
-        ey = e2.astype(LOW)
-        ey_ref[...] = ey
-        sums_ref[0:1, :] = gain
-        sums_ref[1:2, :] = shift
-        sums_ref[2:3, :] = column_sum(ey)
-        for copy in copies:
-            copy.wait()
-        da_ref[...] = dot_nt(ey, w_ref[...]).astype(LOW)
-        c = spot_ref[3]
-        for owner, out_ref in ((c, mine_ref), (1 - c, rest_ref)):
-            starts = block_starts(spot_ref, owner, width // 16)
-            at = pl.ds(pl.multiple_of(owner * part, LANES), part)
-            put_blocks(dot(mt_ref[...], ey_ref[:, at]), out_ref, starts, 0, part)
-
-    return pl.pallas_call(
-        body,
-        out_shape=[
-            jax.ShapeDtypeStruct((rows, width), WIDE),
-            jax.ShapeDtypeStruct((rows, width), LOW),
-            jax.ShapeDtypeStruct((width, part), LOW),
-            jax.ShapeDtypeStruct((width, part), LOW),
-            jax.ShapeDtypeStruct((8, width), WIDE),
-        ],
-        in_specs=[pl.BlockSpec(memory_space=pltpu.SMEM)] + any_specs(4) + vmem_specs(6),
-        out_specs=vmem_specs(5),
-        scratch_shapes=[
-            pltpu.VMEM((width, width), LOW),
-            pltpu.VMEM((width, rows), LOW),
-            pltpu.VMEM((rows, width), LOW),
-            pltpu.SemaphoreType.DMA((32,)),
-        ],
-        compiler_params=params(),
-        cost_estimate=cost(4 * rows * width * width, 4 * width * width + 20 * rows * width),
-        name="middle_backward",
-    )(spot, *refs, e, h2, *mixed, acc, table)
+    )(spot, e, a2, z, slope, *given, *moved)
 
 
 def attention_backward(lengths, qkv, da, mixed, lse, begin, pairs):
@@ -703,95 +719,6 @@
     )(spot, *refs[:2])
 
 
-def rows_spec(height, width, index):
-    return pl.BlockSpec((height, width), lambda i: (index, 0))
-
-
-def sum_call(body, ins, outs, out_specs, name, spot=None):
-    specs = [rows_spec(height, value.shape[1], index) for value, height, index in ins]
-    moved = sum(2 * height * value.shape[1] for value, height, index in ins)
-    first = [] if spot is None else [spot]
-    return pl.pallas_call(
-        body,
-        out_shape=outs,
-        grid=(1,),
-        in_specs=[pl.BlockSpec(memory_space=pltpu.SMEM)] * len(first) + specs,
-        out_specs=out_specs,
-        compiler_params=params(),
-        cost_estimate=cost(0, 2 * moved),
-        name=name,
-    )(*first, *(value for value, height, index in ins))
-
-
-def wide_sum(refs):
-    total = refs[0][...].astype(WIDE)
-    for ref in refs[1:]:
-        total = total + ref[...].astype(WIDE)
-    return total
-
-
-def sum_pieces(mines, gots, arrived, height, index):
-    count = len(mines)
-    width = sum(mine.shape[1] for mine in mines)
-
-    def body(*refs):
-        out_ref = refs[-1]
-        start = 0
-        for n in range(count):
-            half = refs[n].shape[1]
-            total = wide_sum((refs[n], refs[count + n]))
-            for ref in refs[2 * count : -1]:
-                total = total + ref[:, start : start + half].astype(WIDE)
-            out_ref[:, start : start + half] = total.astype(LOW)
-            start = start + half
-
-    ins = [(value, height, index) for value in (*mines, *gots, *arrived)]
-    out = jax.ShapeDtypeStruct((height, width), LOW)
-    return sum_call(body, ins, out, rows_spec(height, width, 0), "sum_pieces")
-
-
-def sum_blocks(mines, gots, arrived):
-    count = len(mines)
-    height = mines[0].shape[0] // 4
-    rows = height // 4
-    width = sum(mine.shape[1] for mine in mines)
-
-    def body(*refs):
-        outs = refs[-4:]
-        start = 0
-        for n in range(count):
-            half = refs[n].shape[1]
-            total = wide_sum((refs[n], refs[count + n]))
-            for ref in refs[2 * count : -4]:
-                total = total + ref[:, start : start + half].astype(WIDE)
-            for block, out_ref in enumerate(outs):
-                out_ref[:, start : start + half] = total[
-                    block * rows : (block + 1) * rows
-                ].astype(out_ref.dtype)
-            start = start + half
-
-    ins = [(value, height, 0) for value in (*mines, *gots, *arrived)]
-    outs = [jax.ShapeDtypeStruct((rows, width), WIDE)]
-    outs += [jax.ShapeDtypeStruct((rows, width), LOW)] * 3
-    return sum_call(body, ins, outs, [rows_spec(rows, width, 0)] * 4, "sum_blocks")
-
-
-def sum_last(spot, own, arrived):
-    rows, width = own.shape
-
-    def body(spot_ref, *refs):
-        kept_ref, sent_ref = refs[-2:]
-        total = wide_sum(refs[:-2])
-        low, high = total[: rows // 2], total[rows // 2 :]
-        c = spot_ref[3]
-        kept_ref[...] = jnp.where(c == 0, low, high)
-        sent_ref[...] = jnp.where(c == 0, high, low).astype(LOW)
-
-    ins = [(value, rows, 0) for value in (own, *arrived)]
-    outs = [jax.ShapeDtypeStruct((rows // 2, width), kind) for kind in (WIDE, LOW)]
-    return sum_call(body, ins, outs, [rows_spec(rows // 2, width, 0)] * 2, "sum_last", spot)
-
-
 def finish_mlp(spot, parts, shapes):
     down_shape, up_shape, out_shape = shapes
     layers = len(parts)
@@ -806,8 +733,7 @@
             for part in range(2):
                 for owner, ref in ((c, refs[at]), (1 - c, refs[at + 1])):
                     start = pl.multiple_of(part * 2 * half + owner * half, LANES)
-                    values = ref[:, :half].astype(WIDE)
-                    down_ref[layer, pl.ds(start, half), :] = values.T
+                    down_ref[layer, :, pl.ds(start, half)] = ref[:, :half].astype(WIDE)
                     up_ref[layer, :, pl.ds(start, half)] = ref[:, half : 2 * half].astype(WIDE)
                     if part == 0:
                         start = pl.multiple_of(owner * small, LANES)
@@ -843,7 +769,8 @@
             packed = kept_ref[:, half : half + LANES]
             columns = packed.T
             gain_ref[layer] = columns[0:2, :]
-            bias_ref[layer] = columns[2:8, :]
+            for n in range(6):
+                bias_ref[n, layer : layer + 1, :] = columns[n + 2 : n + 3, :]
             up_ref[layer : layer + 1, :] = packed[0:1, LANES - share :]
 
     flat = [value for part in parts for value in part]
@@ -916,33 +843,20 @@
 
     def start(self):
         if self.waiting is not None:
+            assert self.flying is None
             self.flying = [send(value, pairs) for value, pairs in self.waiting]
 
 
-def stage(begin, work=None, hold=()):
+def slot(begin, end, work):
     for chain in begin:
         chain.start()
-    landing = [chain for chain in begin if chain.flying is not None and chain not in hold]
-    outs = work() if work is not None else ()
+    landing = [chain for chain in end if chain.flying is not None]
+    outs = work()
     arrived, outs = lax.optimization_barrier(([chain.flying for chain in landing], outs))
     for chain, values in zip(landing, arrived):
         chain.flying = None
         chain.resume(values)
     return outs
-
-
-def land(chain):
-    class Held:
-        flying = chain.flying
-
-        def start(self):
-            pass
-
-        def resume(self, values):
-            chain.flying = None
-            chain.resume(values)
-
-    return Held()
 
 
 def offsets_of(widths):
@@ -975,37 +889,38 @@
     return near, far, near_got, far_got
 
 
-def scatter_whole(mines, rests):
-    result = []
-    for mine, rest in zip(mines, rests):
-        rows = mine.shape[0] // 16
-        half = mine.shape[1] // (3 * LANES) * (3 * LANES)
-        mine, rest = mine[:, :half], rest[:, :half]
-        low = mine.reshape(2, 2, 4, rows, half).transpose(2, 1, 0, 3, 4)
-        high = rest.reshape(2, 2, 4, rows, half).transpose(2, 0, 1, 3, 4)
-        whole = jnp.concatenate([low, high], axis=-1)[jnp.array([0, 3, 2, 1])]
-        whole = whole.reshape(16 * rows, 2 * half)
-        result.append(lax.psum_scatter(whole, AXES, scatter_dimension=0, tiled=True).astype(WIDE))
-    return result
-
-
-def cross_steps(rest):
+def scatter_whole(mine, rest, start, half):
+    mine, rest = mine[:, start : start + half], rest[:, start : start + half]
+    rows = mine.shape[0] // 16
+    low = mine.reshape(2, 2, 4, rows, half).transpose(2, 1, 0, 3, 4)
+    high = rest.reshape(2, 2, 4, rows, half).transpose(2, 0, 1, 3, 4)
+    whole = jnp.concatenate([low, high], axis=-1)[jnp.array([0, 3, 2, 1])]
+    whole = whole.reshape(16 * rows, 2 * half)
+    return lax.psum_scatter(whole, AXES, scatter_dimension=0, tiled=True).astype(WIDE)
+
+
+def added(parts):
+    total = parts[0].astype(WIDE)
+    for part in parts[1:]:
+        total = total + part.astype(WIDE)
+    return total
+
+
+def scatter_steps(spot, mine, rest):
     if not blocked():
-        return rest
+        return mine, rest
+    rows = mine.shape[0] // 16
+    four, two, one = slice(8 * rows, 16 * rows), slice(4 * rows, 8 * rows), slice(0, 4 * rows)
     (got,) = yield [(rest, TO_CORE)]
-    return got
-
-
-def scatter_steps(spot, mines, gots):
-    if not blocked():
-        return scatter_whole(mines, gots)
-    height = mines[0].shape[0]
-    (got_a,) = yield [(sum_pieces(mines, gots, (), height // 2, 1), TO_YX)]
-    (got_b,) = yield [(sum_pieces(mines, gots, (got_a,), height // 4, 1), TO_XY)]
-    own, *blocks = sum_blocks(mines, gots, (got_a, got_b))
-    arrived = yield [(block, TO_Z[3 - n]) for n, block in enumerate(blocks)]
-    kept, sent = sum_last(spot, own, arrived)
-    (got,) = yield [(sent, TO_CORE)]
+    (got_a,) = yield [(added([mine[four], got[four]]).astype(LOW), TO_YX)]
+    (got_b,) = yield [(added([mine[two], got[two], got_a[two]]).astype(LOW), TO_XY)]
+    total = added([mine[one], got[one], got_a[one], got_b])
+    blocks = [total[n * rows : (n + 1) * rows] for n in range(4)]
+    arrived = yield [(blocks[n].astype(LOW), TO_Z[4 - n]) for n in (1, 2, 3)]
+    total = added([blocks[0], *arrived])
+    low, high = total[: rows // 2], total[rows // 2 :]
+    kept = jnp.where(spot[3] == 0, low, high)
+    (got,) = yield [(jnp.where(spot[3] == 0, high, low).astype(LOW), TO_CORE)]
     return kept, got
 
 
@@ -1122,7 +1037,10 @@
 
     def feed_back(i, side):
         r = rec[i]
-        acc, up_mine, up_rest, down_mine, down_rest, down_sum, up_sum = mlp_backward(
+        finish = None
+        if side == 0:
+            finish = (weight(3 * i + 1, 0), r["h2"], (r["mixed0"], r["mixed1"]), r["table"])
+        mine, rest, down_sum, up_sum, *others = mlp_backward(
             spot,
             *feed_weights(i, side),
             r["e"],
@@ -1130,22 +1048,10 @@
             r[f"z{side}"],
             r[f"slope{side}"],
             None if side else r["acc"],
+            finish,
         )
-        return {
-            "acc": acc,
-            f"up{side}": (up_mine, up_rest),
-            f"down{side}": (down_mine, down_rest),
-            "down_sum": down_sum,
-            f"up_sum{side}": up_sum,
-        }
-
-    def middle_back(i):
-        r = rec[i]
-        mixed = (r["mixed0"], r["mixed1"])
-        e2, da, mine, rest, sums = middle_backward(
-            spot, weight(3 * i + 1, 0), r["e"], r["h2"], mixed, r["acc"], r["table"]
-        )
-        return {"e2": e2, "da": da, "out": (mine, rest), "sums2": sums}
+        found = {f"part{side}": (mine, rest), "down_sum": down_sum, f"up_sum{side}": up_sum}
+        return {**found, **dict(zip(("e2", "da", "sums2") if finish else ("acc",), others))}
 
     def attend_back(i, side):
         r = rec[i]
@@ -1168,7 +1074,7 @@
         )
         return {"e_in": e, "qkv": (mine, rest), "small": table}
 
-    def run(begin, *work, hold=()):
+    def run(begin, end, *work):
         def todo():
             before = [dict(r) for r in rec]
             found = []
@@ -1181,84 +1087,85 @@
                 r.update(old)
             return found
 
-        for (function, i, *rest), new in zip(work, stage(begin, todo, hold)):
+        for (function, i, *rest), new in zip(work, slot(begin, end, todo)):
             rec[i].update(new)
 
-    run([q0])
-    run([q0, a0], hold=[a0])
-    run([q0, land(a0)])
-    run([q0, a0, b0], hold=[b0])
-    run([a0, land(b0)], (norm_and_qkv, 0), (attend, 0, 0))
-    run([a0, b0], (attend, 0, 1))
-    run([b0, q1], (project, 0), (feed, 0, 0))
-    run([b0, q1])
-    run([q1, a1], (feed, 0, 1))
+    run([q0], [q0])
+    run([q0, a0], [q0])
+    run([q0], [q0, a0])
+    run([q0, a0, b0], [q0])
+    run([], [a0], (norm_and_qkv, 0))
+    run([a0], [b0], (attend, 0, 0))
+    run([b0, q1], [a0], (attend, 0, 1))
+    run([a0], [a0, b0])
+    run([b0], [b0, q1], (project, 0), (feed, 0, 0))
+    run([b0, q1, a1], [b0, q1])
+    run([q1], [q1, a1], (feed, 0, 1))
     rec[1]["h"] = rec[0]["total"]
-    run([q1, a1, b1], hold=[b1])
-    run([a1, land(b1)], (norm_and_qkv, 1))
-    run([a1, b1], (attend, 1, 0))
-    run([b1], (attend, 1, 1), (project, 1))
-    run([b1], (feed, 1, 0))
-    run([], (feed, 1, 1))
+    run([q1, a1, b1], [q1])
+    run([], [a1], (norm_and_qkv, 1))
+    run([a1], [b1], (attend, 1, 0))
+    run([b1], [a1, b1], (attend, 1, 1))
+    run([a1, b1], [a1])
+    run([], [b1], (project, 1), (feed, 1, 0))
+    run([b1], [b1])
+    run([], [], (feed, 1, 1))
     output = rec[1]["total"][None]
 
-    def cross(i, *members):
-        return [Chain(cross_steps(rec[i][member][1])) for member in members]
-
-    def scatter(i, members, crossed):
-        mines = [rec[i][member][0] for member in members]
-        return Chain(scatter_steps(spot, mines, [chain.result for chain in crossed]))
-
-    first_members, second_members = ["down1", "up1"], ["down0", "up0", "out"]
+    def scatter(i, member):
+        return Chain(scatter_steps(spot, *rec[i][member]))
+
     rec[1]["e"] = cotangent[0]
-    run([], (feed_back, 1, 1))
-    first = cross(1, *first_members)
-    run(first, (feed_back, 1, 0))
-    b1 = scatter(1, first_members, first)
-    second = cross(1, "down0", "up0")
-    run([b1, *second], (middle_back, 1), (attend_back, 1, 0))
-    second += cross(1, "out")
-    run([b1, *second], (attend_back, 1, 1))
-    a1 = scatter(1, second_members, second)
-    run([b1, a1], (qkv_back, 1))
+    run([], [], (feed_back, 1, 1))
+    b1 = scatter(1, "part1")
+    run([b1], [b1], (feed_back, 1, 0))
+    a1 = scatter(1, "part0")
+    run([b1, a1], [b1, a1], (attend_back, 1, 0))
+    run([b1, a1], [b1], (attend_back, 1, 1))
+    run([b1], [b1, a1], (qkv_back, 1))
     rec[0]["e"] = rec[1]["e_in"]
-    third = cross(1, "qkv")
-    run([b1, a1, *third], (feed_back, 0, 1))
-    q1 = scatter(1, ["qkv"], third)
-    first = cross(0, *first_members)
-    run([a1, q1, *first], (feed_back, 0, 0))
-    b0 = scatter(0, first_members, first)
-    second = cross(0, "down0", "up0")
-    run([a1, q1, b0, *second], (middle_back, 0), (attend_back, 0, 0))
-    second += cross(0, "out")
-    run([q1, b0, *second], (attend_back, 0, 1))
-    a0 = scatter(0, second_members, second)
-    run([q1, b0, a0], (qkv_back, 0))
-    third = cross(0, "qkv")
-    run([b0, a0, *third])
-    q0 = scatter(0, ["qkv"], third)
-    run([a0, q0])
-    run([a0, q0])
+    q1 = scatter(1, "qkv")
+    run([b1, a1, q1], [b1, a1, q1], (feed_back, 0, 1))
+    b0 = scatter(0, "part1")
+    run([a1, q1, b0], [a1, q1, b0], (feed_back, 0, 0))
+    a0 = scatter(0, "part0")
+    run([a1, q1, b0, a0], [a1, q1, a0], (attend_back, 0, 0))
+    run([q1], [b0], (attend_back, 0, 1))
+    run([b0, a0], [q1, b0], (qkv_back, 0))
+    q0 = scatter(0, "qkv")
+    run([b0, q1, q0], [a0, q0])
+    run([a0, q0], [b0, a0])
+    run([a0, b0], [q0, q1, b0])
+    run([q0], [q0, a0])
+    run([q0, a0], [a0])
 
     input_grad = rec[0]["e_in"][None]
-    mlp_shapes = [(layers, hidden, down_weight.shape[2]), up_weight.shape, out_weight.shape]
-    qkv_shapes = [qkv_weight.shape, norm_gains.shape, biases.shape, up_bias.shape]
+    down_shape = (layers, down_weight.shape[2], hidden)
+    mlp_shapes = [down_shape, up_weight.shape, out_weight.shape]
+    bias_shape = (biases.shape[1], layers, biases.shape[2])
+    qkv_shapes = [qkv_weight.shape, norm_gains.shape, bias_shape, up_bias.shape]
     if blocked():
         down_grad, up_grad, out_grad = finish_mlp(
             spot, [(a0.result, b0.result), (a1.result, b1.result)], mlp_shapes
         )
-        run([q0])
-        run([q0])
+        run([], [q0])
+        run([q0], [q0])
         qkv_grad, gains, shifts, up_sums = finish_qkv(spot, [q0.result, q1.result], qkv_shapes)
+        shifts = jnp.swapaxes(shifts, 0, 1)
+        down_grad = jnp.swapaxes(down_grad, 1, 2)
         return output, input_grad, qkv_grad, out_grad, up_grad, down_grad, gains, shifts, up_sums
     owned = []
     for r, q, a, b in ((rec[0], q0, a0, b0), (rec[1], q1, a1, b1)):
-        down = jnp.concatenate([a.result[0], b.result[0]], axis=1).T
-        up = jnp.concatenate([a.result[1], b.result[1]], axis=1)
+        quarter = half // 2
+        down = [scatter_whole(*part.result, 0, quarter) for part in (a, b)]
+        up = [scatter_whole(*part.result, quarter, quarter) for part in (a, b)]
+        out = scatter_whole(*a.result, half, width // 2)
         up_sum = jnp.concatenate([r["up_sum0"], r["up_sum1"]], axis=1)
         table = lax.psum_scatter(r["small"], AXES, scatter_dimension=1, tiled=True)
         up_sum = lax.psum_scatter(up_sum[0], AXES, scatter_dimension=0, tiled=True)
-        owned.append((q.result[0], a.result[2], up, down, table[0:2], table[2:8], up_sum))
+        down, up = jnp.concatenate(down, axis=1).T, jnp.concatenate(up, axis=1)
+        first = scatter_whole(*q.result, 0, 3 * width // 2)
+        owned.append((first, out, up, down, table[0:2], table[2:8], up_sum))
     stacked = [jnp.stack([pair[n] for pair in owned]) for n in range(7)]
     return (output, input_grad, *stacked)
 

time: 544 us -> 511 us (0.939)
  Pallas kernels: 285 us -> 212 us
  other arithmetic: 6.25 us -> 47 us
  starting transfers between devices: 79 us -> 94.6 us
  local copies, waits for them, and re-layouts: 39 us -> 30.2 us
  waiting for transfers between devices: 123 us -> 115 us
    pallas_call x30 -> x4, Pallas kernels: 132 us -> 60.8 us  [mlp_backward(): pl.pallas_call(body, out_shape=out_shape, grid_spec=pltpu.PrefetchScalarG...]
    convert_element_type x0 -> x18, other arithmetic: none -> 21.3 us  [the longest x6 10.8 us: scatter_steps(): got_a, = (yield [(added([mine[four], got[four]]).astype(LOW), TO_YX)])]
    ppermute x92 -> x86, starting transfers between devices: 79 us -> 94.6 us  [send(): return lax.ppermute(value, AXES, pairs)]
    another operation x6 -> x12, other arithmetic: 2.54 us -> 13.7 us
    unnamed x157 -> x78, local copies, waits for them, and re-layouts: 27.9 us -> 17.5 us
    ppermute x92 -> x86, waiting for transfers between devices: 123 us -> 115 us  [send(): return lax.ppermute(value, AXES, pairs)]
  transfers between devices with their start and end apart: 92 -> 86, of which waited for: 27 -> 26; matrix products, arithmetic and copies ran while one was open for 4% -> 12% of each run, Pallas kernels for 43% -> 37%
where the time goes in v5:
time: 511 us; the launch traced here: 502 us
  Pallas kernels  212 us (41%)
  waiting for transfers between devices  115 us (23%)
  starting transfers between devices  94.6 us (19%)
  other arithmetic  47 us (9%)
  local copies, waits for them, and re-layouts  30.2 us (6%)
    ppermute x86, waiting for transfers between devices, send(): return lax.ppermute(value, AXES, pairs)  115 us
    ppermute x86, starting transfers between devices, send(): return lax.ppermute(value, AXES, pairs)  94.6 us
    pallas_call x4, Pallas kernels, mlp_backward(): pl.pallas_call(body, out_shape=out_shape, grid_spec=pltpu.PrefetchScalarG...  60.8 us
    pallas_call x4, Pallas kernels, mlp_forward(): pl.pallas_call(body, out_shape=[jax.ShapeDtypeStruct((rows, hidden), LOW)...  39.1 us
    pallas_call x4, Pallas kernels, attention_backward(): pl.pallas_call(body, out_shape=jax.ShapeDtypeStruct((rows, 3 * width), LO...  29.7 us
    pallas_call x2, Pallas kernels, qkv_backward(): pl.pallas_call(body, out_shape=[jax.ShapeDtypeStruct((rows, width), WIDE)...  25.2 us
    pallas_call x4, Pallas kernels, attention_forward(): pl.pallas_call(body, out_shape=[jax.ShapeDtypeStruct((rows, width), LOW),...  22.8 us
    unnamed x78, local copies, waits for them, and re-layouts  17.5 us
  transfers between devices with their start and end apart: 86, of which 26 were waited for; matrix products, arithmetic and copies ran while one was open for 12% of the time, Pallas kernels for 37%

profile of v5, /device:TPU:0, one launch (start us, length us, event | category | flops | bytes accessed | tf_op | source)
XLA Modules:
  0.0 501.7 jit_solution(13860378486918421390)
XLA Ops:
  6.3 4.9 collective-permute-start.10
  12.4 2.6 collective-permute-done.10
  15.0 7.4 %collective-permute-done.9 = bf16[48,1280]{1,0:T(8,128)(2,1)S(1)} collective-permute-done((bf16[48,1280]{1,0:T(8,128)(2,1)S(1)}, bf16[48,1280]{1,0:T(8,128)(2,1)S(1)}, u32[]{:S(2)}, u32[]{:S(2)}) %collective-permute-start.9) | collective-permute-done | bytes 122912 | tf_op jit(solution)/shard_map/ppermute | solution.py:809
  26.0 5.4 %collective-permute-done.11 = bf16[192,1280]{1,0:T(8,128)(2,1)S(1)} collective-permute-done((bf16[192,1280]{1,0:T(8,128)(2,1)S(1)}, bf16[192,1280]{1,0:T(8,128)(2,1)S(1)}, u32[]{:S(2)}, u32[]{:S(2)}) %collective-permute-start.11) | collective-permute-done | bytes 491552 | tf_op jit(solution)/shard_map/ppermute | solution.py:809
  39.2 2.3 collective-permute-done.16
  41.5 12.6 %collective-permute-done.15 = bf16[48,1920]{1,0:T(8,128)(2,1)} collective-permute-done((bf16[48,1920]{1,0:T(8,128)(2,1)S(1)}, bf16[48,1920]{1,0:T(8,128)(2,1)}, u32[]{:S(2)}, u32[]{:S(2)}) %collective-permute-start.15) | collective-permute-done | bytes 184352 | tf_op jit(solution)/shard_map/ppermute | solution.py:809
  58.2 2.5 small_forward.2
  61.7 7.2 %qkv_forward.2 = (bf16[496,2304]{1,0:T(8,128)(2,1)}, bf16[496,768]{1,0:T(8,128)(2,1)}) custom-call(s32[4]{0:T(128)} %pad_add_fusion.spot_ref, bf16[384,1280]{1,0:T(8,128)(2,1)} %constant_dynamic-update-slice_fusion.r0, bf16[384,1280]{1,0:T(8,128)(2,1)} %collective-permute-done.12.r1, bf16[384,1280]{1,0:T(8,128)(2,1)} %collective-permute-done.13.r2, ...), custom_call_target="tpu_custom_call" | custom-call | flops 1755316224 | bytes 6967296 | tf_op jit(solution)/shard_map/qkv_forward/pallas_call | solution.py:123
  72.5 5.7 %attention_forward.5 = (bf16[496,384]{1,0:T(8,128)(2,1)}, f32[496,128]{1,0:T(8,128)}) custom-call(s32[1]{0:T(128)S(6)} %copy.51.len_ref, bf16[496,2304]{1,0:T(8,128)(2,1)} %get-tuple-element.229.q_ref.k_ref.v_ref, bf16[496,2304]{1,0:T(8,128)(2,1)} %get-tuple-element.229.q_ref.k_ref.v_ref, bf16[496,2304]{1,0:T(8,128)(2,1)} %get-tuple-element.229.q_ref.k_ref.v_ref), custom_call_target="tpu_custom_call" | custom-call | flops 1511522304 | bytes 1523712 | tf_op jit(solution)/shard_map/attention_forward/pallas_call | solution.py:165
  78.3 11.6 %collective-permute-done.19.r1.u1.d1.refs_6_.refs_10_.refs_14_ = bf16[384,1920]{1,0:T(8,128)(2,1)} collective-permute-done((bf16[384,1920]{1,0:T(8,128)(2,1)S(1)}, bf16[384,1920]{1,0:T(8,128)(2,1)}, u32[]{:S(2)}, u32[]{:S(2)}) %collective-permute-start.19) | collective-permute-done | bytes 1474592 | tf_op jit(solution)/shard_map/ppermute | solution.py:809
  91.6 2.4 collective-permute-start.5
  96.1 5.7 %attention_forward.4 = (bf16[496,384]{1,0:T(8,128)(2,1)}, f32[496,128]{1,0:T(8,128)}) custom-call(s32[1]{0:T(128)S(6)} %copy.51.len_ref, bf16[496,2304]{1,0:T(8,128)(2,1)} %get-tuple-element.229.q_ref.k_ref.v_ref, bf16[496,2304]{1,0:T(8,128)(2,1)} %get-tuple-element.229.q_ref.k_ref.v_ref, bf16[496,2304]{1,0:T(8,128)(2,1)} %get-tuple-element.229.q_ref.k_ref.v_ref), custom_call_target="tpu_custom_call" | custom-call | flops 1511522304 | bytes 1523712 | tf_op jit(solution)/shard_map/attention_forward/pallas_call | solution.py:165
  101.8 6.3 %collective-permute-done.5 = bf16[48,1536]{1,0:T(8,128)(2,1)S(1)} collective-permute-done((bf16[48,1536]{1,0:T(8,128)(2,1)S(1)}, bf16[48,1536]{1,0:T(8,128)(2,1)S(1)}, u32[]{:S(2)}, u32[]{:S(2)}) %collective-permute-start.5) | collective-permute-done | bytes 147488 | tf_op jit(solution)/shard_map/ppermute | solution.py:809
  111.0 7.1 %collective-permute-done.22 = bf16[192,1536]{1,0:T(8,128)(2,1)S(1)} collective-permute-done((bf16[192,1536]{1,0:T(8,128)(2,1)S(1)}, bf16[192,1536]{1,0:T(8,128)(2,1)S(1)}, u32[]{:S(2)}, u32[]{:S(2)}) %collective-permute-start.22) | collective-permute-done | bytes 589856 | tf_op jit(solution)/shard_map/ppermute | solution.py:809
  125.3 5.5 %out_forward.2 = (f32[496,768]{1,0:T(8,128)}, bf16[496,768]{1,0:T(8,128)(2,1)}) custom-call(s32[4]{0:T(128)} %pad_add_fusion.spot_ref, bf16[384,1920]{1,0:T(8,128)(2,1)} %copy-done.1, bf16[384,1920]{1,0:T(8,128)(2,1)} %collective-permute-done.19.r1.u1.d1.refs_6_.refs_10_.refs_14_, ...), custom_call_target="tpu_custom_call" | custom-call | flops 585105408 | bytes 5750784 | tf_op jit(solution)/shard_map/out_forward/pallas_call | solution.py:209
  130.8 9.7 %mlp_forward.4 = (bf16[496,1536]{1,0:T(8,128)(2,1)}, bf16[496,1536]{1,0:T(8,128)(2,1)}, f32[496,768]{1,0:T(8,128)}) custom-call(s32[4]{0:T(128)} %pad_add_fusion.spot_ref, f32[496,768]{1,0:T(8,128)} %get-tuple-element.360.h_ref.refs_1_, bf16[496,768]{1,0:T(8,128)(2,1)} %get-tuple-element.257.a_ref, f32[1,1536]{1,0:T(1,128)} %get-tuple-element.506.b_ref, ...), custom_call_target="tpu_custom_call" | custom-call | flops 2340421632 | bytes 7766016 | tf_op jit(solution)/shard_map/mlp_forward/pallas_call | solution.py:289
  143.4 6.2 %collective-permute-done.29 = bf16[192,1280]{1,0:T(8,128)(2,1)S(1)} collective-permute-done((bf16[192,1280]{1,0:T(8,128)(2,1)S(1)}, bf16[192,1280]{1,0:T(8,128)(2,1)S(1)}, u32[]{:S(2)}, u32[]{:S(2)}) %collective-permute-start.29) | collective-permute-done | bytes 491552 | tf_op jit(solution)/shard_map/ppermute | solution.py:809
  155.5 9.9 %mlp_forward.5 = (bf16[496,1536]{1,0:T(8,128)(2,1)}, bf16[496,1536]{1,0:T(8,128)(2,1)}, f32[496,768]{1,0:T(8,128)}) custom-call(s32[4]{0:T(128)} %pad_add_fusion.spot_ref, f32[496,768]{1,0:T(8,128)} %get-tuple-element.256.h_ref, bf16[496,768]{1,0:T(8,128)(2,1)} %get-tuple-element.257.a_ref, f32[1,1536]{1,0:T(1,128)} %get-tuple-element.505.b_ref, ...), custom_call_target="tpu_custom_call" | custom-call | flops 2340421632 | bytes 7766016 | tf_op jit(solution)/shard_map/mlp_forward/pallas_call | solution.py:289
  165.4 4.9 collective-permute-done.33
  171.3 2.5 small_forward.3
  173.9 7.1 %qkv_forward.3 = (bf16[496,2304]{1,0:T(8,128)(2,1)}, bf16[496,768]{1,0:T(8,128)(2,1)}) custom-call(s32[4]{0:T(128)} %pad_add_fusion.spot_ref, bf16[384,1280]{1,0:T(8,128)(2,1)} %constant_dynamic-update-slice_fusion.15.r0, bf16[384,1280]{1,0:T(8,128)(2,1)} %collective-permute-done.30.r1, bf16[384,1280]{1,0:T(8,128)(2,1)} %collective-permute-done.31.r2, ...), custom_call_target="tpu_custom_call" | custom-call | flops 1755316224 | bytes 6967296 | tf_op jit(solution)/shard_map/qkv_forward/pallas_call | solution.py:123
  183.0 2.7 collective-permute-start.2
  185.7 2.2 collective-permute-start.1
  187.9 5.7 %attention_forward.6 = (bf16[496,384]{1,0:T(8,128)(2,1)}, f32[496,128]{1,0:T(8,128)}) custom-call(s32[1]{0:T(128)S(6)} %copy.51.len_ref, bf16[496,2304]{1,0:T(8,128)(2,1)} %get-tuple-element.273.q_ref.k_ref.v_ref, bf16[496,2304]{1,0:T(8,128)(2,1)} %get-tuple-element.273.q_ref.k_ref.v_ref, bf16[496,2304]{1,0:T(8,128)(2,1)} %get-tuple-element.273.q_ref.k_ref.v_ref), custom_call_target="tpu_custom_call" | custom-call | flops 1511522304 | bytes 1523712 | tf_op jit(solution)/shard_map/attention_forward/pallas_call | solution.py:165
  193.6 5.7 %collective-permute-done.2 = bf16[48,1536]{1,0:T(8,128)(2,1)S(1)} collective-permute-done((bf16[48,1536]{1,0:T(8,128)(2,1)S(1)}, bf16[48,1536]{1,0:T(8,128)(2,1)S(1)}, u32[]{:S(2)}, u32[]{:S(2)}) %collective-permute-start.2) | collective-permute-done | bytes 147488 | tf_op jit(solution)/shard_map/ppermute | solution.py:809
  200.9 5.7 %attention_forward.7 = (bf16[496,384]{1,0:T(8,128)(2,1)}, f32[496,128]{1,0:T(8,128)}) custom-call(s32[1]{0:T(128)S(6)} %copy.51.len_ref, bf16[496,2304]{1,0:T(8,128)(2,1)} %get-tuple-element.273.q_ref.k_ref.v_ref, bf16[496,2304]{1,0:T(8,128)(2,1)} %get-tuple-element.273.q_ref.k_ref.v_ref, bf16[496,2304]{1,0:T(8,128)(2,1)} %get-tuple-element.273.q_ref.k_ref.v_ref), custom_call_target="tpu_custom_call" | custom-call | flops 1511522304 | bytes 1523712 | tf_op jit(solution)/shard_map/attention_forward/pallas_call | solution.py:165
  207.3 3.1 collective-permute-done.39
  216.7 5.6 %out_forward.3 = (f32[496,768]{1,0:T(8,128)}, bf16[496,768]{1,0:T(8,128)(2,1)}) custom-call(s32[4]{0:T(128)} %pad_add_fusion.spot_ref, bf16[384,1920]{1,0:T(8,128)(2,1)} %copy-done, bf16[384,1920]{1,0:T(8,128)(2,1)} %collective-permute-done.37.r1.u1.d1.refs_6_.refs_10_.refs_14_, bf16[384,1920]{1,0:T(8,128)(2,1)} %copy-done.3, bf16[384,1920]{1,0:T(8,128)(2,1)} %copy-done.4, ...), custom_call_target="tpu_custom_call" | custom-call | flops 585105408 | bytes 5750784 | tf_op jit(solution)/shard_map/out_forward/pallas_call | solution.py:209
  222.2 9.8 %mlp_forward.6 = (bf16[496,1536]{1,0:T(8,128)(2,1)}, bf16[496,1536]{1,0:T(8,128)(2,1)}, f32[496,768]{1,0:T(8,128)}) custom-call(s32[4]{0:T(128)} %pad_add_fusion.spot_ref, f32[496,768]{1,0:T(8,128)} %get-tuple-element.313.h_ref.refs_1_, bf16[496,768]{1,0:T(8,128)(2,1)} %get-tuple-element.295.a_ref, f32[1,1536]{1,0:T(1,128)} %get-tuple-element.504.b_ref, ...), custom_call_target="tpu_custom_call" | custom-call | flops 2340421632 | bytes 7766016 | tf_op jit(solution)/shard_map/mlp_forward/pallas_call | solution.py:289
  232.1 3.0 collective-permute-done.43.u3.d3.refs_3_.refs_7_
  236.2 9.7 %mlp_forward.7 = (bf16[496,1536]{1,0:T(8,128)(2,1)}, bf16[496,1536]{1,0:T(8,128)(2,1)}, f32[496,768]{1,0:T(8,128)}) custom-call(s32[4]{0:T(128)} %pad_add_fusion.spot_ref, f32[496,768]{1,0:T(8,128)} %get-tuple-element.294.h_ref, bf16[496,768]{1,0:T(8,128)(2,1)} %get-tuple-element.295.a_ref, f32[1,1536]{1,0:T(1,128)} %get-tuple-element.503.b_ref, ...), custom_call_target="tpu_custom_call" | custom-call | flops 2340421632 | bytes 7766016 | tf_op jit(solution)/shard_map/mlp_forward/pallas_call | solution.py:289
  245.9 12.6 %mlp_backward.4 = (bf16[768,1536]{1,0:T(8,128)(2,1)}, bf16[768,1536]{1,0:T(8,128)(2,1)}, f32[1,768]{1,0:T(1,128)}, f32[1,1536]{1,0:T(1,128)}, f32[496,768]{1,0:T(8,128)}) custom-call(s32[4]{0:T(128)} %pad_add_fusion.spot_ref, f32[496,768]{1,0:T(8,128)} %bitcast.40, bf16[496,768]{1,0:T(8,128)(2,1)} %get-tuple-element.295.a_ref, ...), custom_call_target="tpu_custom_call" | custom-call | flops 4680843264 | bytes 12484608 | tf_op jit(solution)/shard_map/mlp_backward/pallas_call | solution.py:494
  258.8 18.0 %mlp_backward.5 = (bf16[768,1920]{1,0:T(8,128)(2,1)}, bf16[768,1920]{1,0:T(8,128)(2,1)}, f32[1,768]{1,0:T(1,128)}, f32[1,1536]{1,0:T(1,128)}, f32[496,768]{1,0:T...) custom-call(s32[4]{0:T(128)} %pad_add_fusion.spot_ref, f32[496,768]{1,0:T(8,128)} %bitcast.41, ...), custom_call_target="tpu_custom_call" | custom-call | flops 4680843264 | bytes 12484608 | tf_op jit(solution)/shard_map/mlp_backward/pallas_call | solution.py:494
  280.2 7.5 %attention_backward.4.d0_ref = bf16[496,1152]{1,0:T(8,128)(2,1)} custom-call(s32[1]{0:T(128)S(6)} %copy.51.len_ref, bf16[496,2304]{1,0:T(8,128)(2,1)} %get-tuple-element.273.q_ref.k_ref.v_ref, bf16[496,2304]{1,0:T(8,128)(2,1)} %get-tuple-element.273.q_ref.k_ref.v_ref, bf16[496,2304]{1,0:T(8,128)(2,1)} %get-tuple-element.273.q_ref.k_ref.v_ref, ...), custom_call_target="tpu_custom_call" | custom-call | flops 3778805760 | bytes 3047424 | tf_op jit(solution)/shard_map/attention_backward/pallas_call | solution.py:574
  287.7 7.4 %collective-permute-done.45 = bf16[384,1536]{1,0:T(8,128)(2,1)} collective-permute-done((bf16[384,1536]{1,0:T(8,128)(2,1)S(1)}, bf16[384,1536]{1,0:T(8,128)(2,1)}, u32[]{:S(2)}, u32[]{:S(2)}) %collective-permute-start.45) | collective-permute-done | bytes 1179680 | tf_op jit(solution)/shard_map/ppermute | solution.py:809
  298.3 2.8 add_convert_fusion.1
  301.7 7.4 %attention_backward.5.d1_ref = bf16[496,1152]{1,0:T(8,128)(2,1)} custom-call(s32[1]{0:T(128)S(6)} %copy.51.len_ref, bf16[496,2304]{1,0:T(8,128)(2,1)} %get-tuple-element.273.q_ref.k_ref.v_ref, bf16[496,2304]{1,0:T(8,128)(2,1)} %get-tuple-element.273.q_ref.k_ref.v_ref, bf16[496,2304]{1,0:T(8,128)(2,1)} %get-tuple-element.273.q_ref.k_ref.v_ref, ...), custom_call_target="tpu_custom_call" | custom-call | flops 3778805760 | bytes 3047424 | tf_op jit(solution)/shard_map/attention_backward/pallas_call | solution.py:574
  310.6 2.8 fusion.17
  315.0 3.0 collective-permute-start.48
  318.0 12.6 %qkv_backward.2 = (f32[496,768]{1,0:T(8,128)}, bf16[768,1280]{1,0:T(8,128)(2,1)}, bf16[768,1280]{1,0:T(8,128)(2,1)}, f32[8,768]{1,0:T(8,128)}) custom-call(s32[4]{0:T(128)} %pad_add_fusion.spot_ref, bf16[384,1280]{1,0:T(8,128)(2,1)} %constant_dynamic-update-slice_fusion.15.r0, bf16[384,1280]{1,0:T(8,128)(2,1)} %collective-permute-done.30.r1, ...), custom_call_target="tpu_custom_call" | custom-call | flops 3510632448 | bytes 13172736 | tf_op jit(solution)/shard_map/qkv_backward/pallas_call | solution.py:654
  331.4 2.5 add_convert_fusion.7
  336.6 12.6 %mlp_backward.6 = (bf16[768,1536]{1,0:T(8,128)(2,1)}, bf16[768,1536]{1,0:T(8,128)(2,1)}, f32[1,768]{1,0:T(1,128)}, f32[1,1536]{1,0:T(1,128)}, f32[496,768]{1,0:T(8,128)}) custom-call(s32[4]{0:T(128)} %pad_add_fusion.spot_ref, f32[496,768]{1,0:T(8,128)} %get-tuple-element.347.e_ref, bf16[496,768]{1,0:T(8,128)(2,1)} %get-tuple-element.257.a_ref, ...), custom_call_target="tpu_custom_call" | custom-call | flops 4680843264 | bytes 12484608 | tf_op jit(solution)/shard_map/mlp_backward/pallas_call | solution.py:494
  353.1 2.8 fusion.16
  358.4 3.1 collective-permute-start.55
  361.5 17.6 %mlp_backward.7 = (bf16[768,1920]{1,0:T(8,128)(2,1)}, bf16[768,1920]{1,0:T(8,128)(2,1)}, f32[1,768]{1,0:T(1,128)}, f32[1,1536]{1,0:T(1,128)}, f32[496,768]{1,0:T...) custom-call(s32[4]{0:T(128)} %pad_add_fusion.spot_ref, f32[496,768]{1,0:T(8,128)} %get-tuple-element.347.e_ref, ...), custom_call_target="tpu_custom_call" | custom-call | flops 4680843264 | bytes 12484608 | tf_op jit(solution)/shard_map/mlp_backward/pallas_call | solution.py:494
  384.6 2.3 add_convert_fusion.11
  386.9 7.4 %attention_backward.7.d1_ref = bf16[496,1152]{1,0:T(8,128)(2,1)} custom-call(s32[1]{0:T(128)S(6)} %copy.51.len_ref, bf16[496,2304]{1,0:T(8,128)(2,1)} %get-tuple-element.229.q_ref.k_ref.v_ref, bf16[496,2304]{1,0:T(8,128)(2,1)} %get-tuple-element.229.q_ref.k_ref.v_ref, bf16[496,2304]{1,0:T(8,128)(2,1)} %get-tuple-element.229.q_ref.k_ref.v_ref, ...), custom_call_target="tpu_custom_call" | custom-call | flops 3778805760 | bytes 3047424 | tf_op jit(solution)/shard_map/attention_backward/pallas_call | solution.py:574
  394.3 7.4 %attention_backward.6.d0_ref = bf16[496,1152]{1,0:T(8,128)(2,1)} custom-call(s32[1]{0:T(128)S(6)} %copy.51.len_ref, bf16[496,2304]{1,0:T(8,128)(2,1)} %get-tuple-element.229.q_ref.k_ref.v_ref, bf16[496,2304]{1,0:T(8,128)(2,1)} %get-tuple-element.229.q_ref.k_ref.v_ref, bf16[496,2304]{1,0:T(8,128)(2,1)} %get-tuple-element.229.q_ref.k_ref.v_ref, ...), custom_call_target="tpu_custom_call" | custom-call | flops 3778805760 | bytes 3047424 | tf_op jit(solution)/shard_map/attention_backward/pallas_call | solution.py:574
  404.2 2.3 add_convert_fusion.8
  412.4 3.2 collective-permute-start.63
  415.6 2.8 add_convert_fusion
  418.9 12.6 %qkv_backward.3 = (f32[496,768]{1,0:T(8,128)}, bf16[768,1280]{1,0:T(8,128)(2,1)}, bf16[768,1280]{1,0:T(8,128)(2,1)}, f32[8,768]{1,0:T(8,128)}) custom-call(s32[4]{0:T(128)} %pad_add_fusion.spot_ref, bf16[384,1280]{1,0:T(8,128)(2,1)} %constant_dynamic-update-slice_fusion.r0, bf16[384,1280]{1,0:T(8,128)(2,1)} %collective-permute-done.12.r1, ...), custom_call_target="tpu_custom_call" | custom-call | flops 3510632448 | bytes 13172736 | tf_op jit(solution)/shard_map/qkv_backward/pallas_call | solution.py:654
  435.3 2.8 collective-permute-done.68
  442.3 2.8 collective-permute-start.72
  445.4 3.5 collective-permute-done.74
  450.6 4.1 collective-permute-done.73
  456.7 6.4 %collective-permute-done.70 = bf16[384,1280]{1,0:T(8,128)(2,1)S(1)} collective-permute-done((bf16[384,1280]{1,0:T(8,128)(2,1)S(1)}, bf16[384,1280]{1,0:T(8,128)(2,1)S(1)}, u32[]{:S(2)}, u32[]{:S(2)}) %collective-permute-start.70) | collective-permute-done | bytes 983072 | tf_op jit(solution)/shard_map/ppermute | solution.py:809
  465.0 7.9 %collective-permute-start.80 = (bf16[48,1920]{1,0:T(8,128)(2,1)S(1)}, bf16[48,1920]{1,0:T(8,128)(2,1)S(1)}, u32[]{:S(2)}, u32[]{:S(2)}) collective-permute-start(bf16[48,1920]{1,0:T(8,128)(2,1)S(1)} %get-tuple-element.451), channel_id=1, source_target_pairs={{0,8},{1,9},{2,10},{3,11},{4,12},{5,13},{6,14},{7,15},{8,16},{9,17... | collective-permute-start | bytes 552968 | tf_op jit(solution)/shard_map/ppermute | solution.py:809
  472.9 2.5 collective-permute-start.79
  475.4 2.8 collective-permute-start.78
  481.8 3.6 collective-permute-start.83
  485.4 3.4 collective-permute-start.82
  490.1 2.4 finish_mlp.1
  492.5 4.9 collective-permute-done.82
  (303 shorter events, 118.3 us)
Async XLA Ops:
  11.3 11.1 %collective-permute-start.9 = (bf16[48,1280]{1,0:T(8,128)(2,1)S(1)}, bf16[48,1280]{1,0:T(8,128)(2,1)S(1)}, u32[]{:S(2)}, u32[]{:S(2)}) collective-permute-start(bf16[48,1280]{1,0:T(8,128)(2,1)S(1)} %get-tuple-element.438), channel_id=1, source_target_pairs={{0,16},{1,17},{2,18},{3,19},{4,20},{5,21},{6,22},{7,23},{8,24},{9,... | collective-permute-start | bytes 368648 | tf_op jit(solution)/shard_map/ppermute | solution.py:809
  11.3 11.1 %collective-permute-start.8 = (bf16[48,1280]{1,0:T(8,128)(2,1)S(1)}, bf16[48,1280]{1,0:T(8,128)(2,1)S(1)}, u32[]{:S(2)}, u32[]{:S(2)}) collective-permute-start(bf16[48,1280]{1,0:T(8,128)(2,1)S(1)} %get-tuple-element.438), channel_id=1, source_target_pairs={{0,8},{1,9},{2,10},{3,11},{4,12},{5,13},{6,14},{7,15},{8,16},{9,17... | collective-permute-start | bytes 368648 | tf_op jit(solution)/shard_map/ppermute | solution.py:809
  12.4 21.3 %collective-permute-start = (bf16[24,8192]{1,0:T(8,128)(2,1)S(1)}, bf16[24,8192]{1,0:T(8,128)(2,1)S(1)}, u32[]{:S(2)}, u32[]{:S(2)}) collective-permute-start(bf16[24,8192]{1,0:T(8,128)(2,1)S(1)} %get-tuple-element.450), channel_id=1, source_target_pairs={{0,1},{1,0},{2,3},{3,2},{4,5},{5,4},{6,7},{7,6},{8,9},{9,8},{10,11... | collective-permute-start | bytes 1179656 | tf_op jit(solution)/shard_map/ppermute | solution.py:809
  32.1 22.0 %collective-permute-start.13 = (bf16[384,1280]{1,0:T(8,128)(2,1)}, bf16[384,1280]{1,0:T(8,128)(2,1)}, u32[]{:S(2)}, u32[]{:S(2)}) collective-permute-start(bf16[384,1280]{1,0:T(8,128)(2,1)} %constant_dynamic-update-slice_fusion.r0), channel_id=1, source_target_pairs={{0,1},{1,0},{2,3},{3,2},{4,5},{5,4},{6,7},{7,6},{8,9},{9,8},{10,11... | collective-permute-start | bytes 2949128 | tf_op jit(solution)/shard_map/ppermute | solution.py:809
  32.1 22.0 %collective-permute-start.12 = (bf16[384,1280]{1,0:T(8,128)(2,1)}, bf16[384,1280]{1,0:T(8,128)(2,1)}, u32[]{:S(2)}, u32[]{:S(2)}) collective-permute-start(bf16[384,1280]{1,0:T(8,128)(2,1)} %constant_dynamic-update-slice_fusion.r0), channel_id=1, source_target_pairs={{0,2},{1,5},{2,0},{3,7},{4,6},{5,1},{6,4},{7,3},{8,10},{9,13},{10,... | collective-permute-start | bytes 2949128 | tf_op jit(solution)/shard_map/ppermute | solution.py:809
  36.3 17.9 %collective-permute-start.15 = (bf16[48,1920]{1,0:T(8,128)(2,1)S(1)}, bf16[48,1920]{1,0:T(8,128)(2,1)}, u32[]{:S(2)}, u32[]{:S(2)}) collective-permute-start(bf16[48,1920]{1,0:T(8,128)(2,1)S(1)} %get-tuple-element.441), channel_id=1, source_target_pairs={{0,16},{1,17},{2,18},{3,19},{4,20},{5,21},{6,22},{7,23},{8,24},{9,... | collective-permute-start | bytes 552968 | tf_op jit(solution)/shard_map/ppermute | solution.py:809
  37.2 16.9 %collective-permute-start.14 = (bf16[48,1920]{1,0:T(8,128)(2,1)S(1)}, bf16[48,1920]{1,0:T(8,128)(2,1)}, u32[]{:S(2)}, u32[]{:S(2)}) collective-permute-start(bf16[48,1920]{1,0:T(8,128)(2,1)S(1)} %get-tuple-element.441), channel_id=1, source_target_pairs={{0,8},{1,9},{2,10},{3,11},{4,12},{5,13},{6,14},{7,15},{8,16},{9,17... | collective-permute-start | bytes 552968 | tf_op jit(solution)/shard_map/ppermute | solution.py:809
  56.8 12.1 %collective-permute-start.17 = (bf16[192,1920]{1,0:T(8,128)(2,1)}, bf16[192,1920]{1,0:T(8,128)(2,1)}, u32[]{:S(2)}, u32[]{:S(2)}) collective-permute-start(bf16[192,1920]{1,0:T(8,128)(2,1)} %pad_maximum_fusion), channel_id=1, source_target_pairs={{0,4},{1,3},{2,6},{3,1},{4,0},{5,7},{6,2},{7,5},{8,12},{9,11},{10,... | collective-permute-start | bytes 2211848 | tf_op jit(solution)/shard_map/ppermute | solution.py:809
  70.4 19.5 %collective-permute-start.19 = (bf16[384,1920]{1,0:T(8,128)(2,1)S(1)}, bf16[384,1920]{1,0:T(8,128)(2,1)}, u32[]{:S(2)}, u32[]{:S(2)}) collective-permute-start(bf16[384,1920]{1,0:T(8,128)(2,1)S(1)} %constant_dynamic-update-slice_fusion.5.r0.u0.d0.refs_5_.refs_9_.refs_13_), channel_id=1, source_target_pairs={{0,2},{1,5},{2,0},{3,7},{4,6},{5,1},{6,4},{7,3},{8,10},{9,13},{10,... | collective-permute-start | bytes 4423688 | tf_op jit(solution)/shard_map/ppermute | solution.py:809
  89.9 28.2 %collective-permute-start.21 = (bf16[384,1920]{1,0:T(8,128)(2,1)}, bf16[384,1920]{1,0:T(8,128)(2,1)S(1)}, u32[]{:S(2)}, u32[]{:S(2)}) collective-permute-start(bf16[384,1920]{1,0:T(8,128)(2,1)} %collective-permute-done.19.r1.u1.d1.refs_6_.refs_10_.refs_14_), channel_id=1, source_target_pairs={{0,1},{1,0},{2,3},{3,2},{4,5},{5,4},{6,7},{7,6},{8,9},{9,8},{10,11... | collective-permute-start | bytes 4423688 | tf_op jit(solution)/shard_map/ppermute | solution.py:809
  91.6 16.4 %collective-permute-start.5 = (bf16[48,1536]{1,0:T(8,128)(2,1)S(1)}, bf16[48,1536]{1,0:T(8,128)(2,1)S(1)}, u32[]{:S(2)}, u32[]{:S(2)}) collective-permute-start(bf16[48,1536]{1,0:T(8,128)(2,1)S(1)} %get-tuple-element.445), channel_id=1, source_target_pairs={{0,16},{1,17},{2,18},{3,19},{4,20},{5,21},{6,22},{7,23},{8,24},{9,... | collective-permute-start | bytes 442376 | tf_op jit(solution)/shard_map/ppermute | solution.py:809
  94.1 14.0 %collective-permute-start.4 = (bf16[48,1536]{1,0:T(8,128)(2,1)S(1)}, bf16[48,1536]{1,0:T(8,128)(2,1)S(1)}, u32[]{:S(2)}, u32[]{:S(2)}) collective-permute-start(bf16[48,1536]{1,0:T(8,128)(2,1)S(1)} %get-tuple-element.445), channel_id=1, source_target_pairs={{0,8},{1,9},{2,10},{3,11},{4,12},{5,13},{6,14},{7,15},{8,16},{9,17... | collective-permute-start | bytes 442376 | tf_op jit(solution)/shard_map/ppermute | solution.py:809
  119.0 21.5 %collective-permute-start.24 = (bf16[384,1536]{1,0:T(8,128)(2,1)}, bf16[384,1536]{1,0:T(8,128)(2,1)}, u32[]{:S(2)}, u32[]{:S(2)}) collective-permute-start(bf16[384,1536]{1,0:T(8,128)(2,1)} %constant_dynamic-update-slice_fusion.10.u0.d0.refs_0_.refs_4_), channel_id=1, source_target_pairs={{0,1},{1,0},{2,3},{3,2},{4,5},{5,4},{6,7},{7,6},{8,9},{9,8},{10,11... | collective-permute-start | bytes 3538952 | tf_op jit(solution)/shard_map/ppermute | solution.py:809
  119.0 21.5 %collective-permute-start.23 = (bf16[384,1536]{1,0:T(8,128)(2,1)}, bf16[384,1536]{1,0:T(8,128)(2,1)}, u32[]{:S(2)}, u32[]{:S(2)}) collective-permute-start(bf16[384,1536]{1,0:T(8,128)(2,1)} %constant_dynamic-update-slice_fusion.10.u0.d0.refs_0_.refs_4_), channel_id=1, source_target_pairs={{0,2},{1,5},{2,0},{3,7},{4,6},{5,1},{6,4},{7,3},{8,10},{9,13},{10,... | collective-permute-start | bytes 3538952 | tf_op jit(solution)/shard_map/ppermute | solution.py:809
  121.3 19.2 %collective-permute-start.27 = (bf16[48,1280]{1,0:T(8,128)(2,1)S(1)}, bf16[48,1280]{1,0:T(8,128)(2,1)S(1)}, u32[]{:S(2)}, u32[]{:S(2)}) collective-permute-start(bf16[48,1280]{1,0:T(8,128)(2,1)S(1)} %get-tuple-element.443), channel_id=1, source_target_pairs={{0,24},{1,25},{2,26},{3,27},{4,28},{5,29},{6,30},{7,31},{8,0},{9,1... | collective-permute-start | bytes 368648 | tf_op jit(solution)/shard_map/ppermute | solution.py:809
  121.3 19.2 %collective-permute-start.26 = (bf16[48,1280]{1,0:T(8,128)(2,1)S(1)}, bf16[48,1280]{1,0:T(8,128)(2,1)S(1)}, u32[]{:S(2)}, u32[]{:S(2)}) collective-permute-start(bf16[48,1280]{1,0:T(8,128)(2,1)S(1)} %get-tuple-element.443), channel_id=1, source_target_pairs={{0,16},{1,17},{2,18},{3,19},{4,20},{5,21},{6,22},{7,23},{8,24},{9,... | collective-permute-start | bytes 368648 | tf_op jit(solution)/shard_map/ppermute | solution.py:809
  122.5 18.0 %collective-permute-start.25 = (bf16[48,1280]{1,0:T(8,128)(2,1)S(1)}, bf16[48,1280]{1,0:T(8,128)(2,1)S(1)}, u32[]{:S(2)}, u32[]{:S(2)}) collective-permute-start(bf16[48,1280]{1,0:T(8,128)(2,1)S(1)} %get-tuple-element.443), channel_id=1, source_target_pairs={{0,8},{1,9},{2,10},{3,11},{4,12},{5,13},{6,14},{7,15},{8,16},{9,17... | collective-permute-start | bytes 368648 | tf_op jit(solution)/shard_map/ppermute | solution.py:809
  150.4 19.8 %collective-permute-start.31 = (bf16[384,1280]{1,0:T(8,128)(2,1)}, bf16[384,1280]{1,0:T(8,128)(2,1)}, u32[]{:S(2)}, u32[]{:S(2)}) collective-permute-start(bf16[384,1280]{1,0:T(8,128)(2,1)} %constant_dynamic-update-slice_fusion.15.r0), channel_id=1, source_target_pairs={{0,1},{1,0},{2,3},{3,2},{4,5},{5,4},{6,7},{7,6},{8,9},{9,8},{10,11... | collective-permute-start | bytes 2949128 | tf_op jit(solution)/shard_map/ppermute | solution.py:809
  150.4 19.8 %collective-permute-start.30 = (bf16[384,1280]{1,0:T(8,128)(2,1)}, bf16[384,1280]{1,0:T(8,128)(2,1)}, u32[]{:S(2)}, u32[]{:S(2)}) collective-permute-start(bf16[384,1280]{1,0:T(8,128)(2,1)} %constant_dynamic-update-slice_fusion.15.r0), channel_id=1, source_target_pairs={{0,2},{1,5},{2,0},{3,7},{4,6},{5,1},{6,4},{7,3},{8,10},{9,13},{10,... | collective-permute-start | bytes 2949128 | tf_op jit(solution)/shard_map/ppermute | solution.py:809
  151.0 14.4 %collective-permute-start.34 = (bf16[48,1920]{1,0:T(8,128)(2,1)S(1)}, bf16[48,1920]{1,0:T(8,128)(2,1)S(1)}, u32[]{:S(2)}, u32[]{:S(2)}) collective-permute-start(bf16[48,1920]{1,0:T(8,128)(2,1)S(1)} %get-tuple-element.442), channel_id=1, source_target_pairs={{0,24},{1,25},{2,26},{3,27},{4,28},{5,29},{6,30},{7,31},{8,0},{9,1... | collective-permute-start | bytes 552968 | tf_op jit(solution)/shard_map/ppermute | solution.py:809
  152.9 17.4 %collective-permute-start.33 = (bf16[48,1920]{1,0:T(8,128)(2,1)S(1)}, bf16[48,1920]{1,0:T(8,128)(2,1)S(1)}, u32[]{:S(2)}, u32[]{:S(2)}) collective-permute-start(bf16[48,1920]{1,0:T(8,128)(2,1)S(1)} %get-tuple-element.442), channel_id=1, source_target_pairs={{0,16},{1,17},{2,18},{3,19},{4,20},{5,21},{6,22},{7,23},{8,24},{9,... | collective-permute-start | bytes 552968 | tf_op jit(solution)/shard_map/ppermute | solution.py:809
  153.4 16.8 %collective-permute-start.32 = (bf16[48,1920]{1,0:T(8,128)(2,1)S(1)}, bf16[48,1920]{1,0:T(8,128)(2,1)S(1)}, u32[]{:S(2)}, u32[]{:S(2)}) collective-permute-start(bf16[48,1920]{1,0:T(8,128)(2,1)S(1)} %get-tuple-element.442), channel_id=1, source_target_pairs={{0,8},{1,9},{2,10},{3,11},{4,12},{5,13},{6,14},{7,15},{8,16},{9,17... | collective-permute-start | bytes 552968 | tf_op jit(solution)/shard_map/ppermute | solution.py:809
  170.4 11.5 %collective-permute-start.35 = (bf16[192,1920]{1,0:T(8,128)(2,1)S(1)}, bf16[192,1920]{1,0:T(8,128)(2,1)S(1)}, u32[]{:S(2)}, u32[]{:S(2)}) collective-permute-start(bf16[192,1920]{1,0:T(8,128)(2,1)S(1)} %pad_maximum_fusion.1), channel_id=1, source_target_pairs={{0,4},{1,3},{2,6},{3,1},{4,0},{5,7},{6,2},{7,5},{8,12},{9,11},{10,... | collective-permute-start | bytes 2211848 | tf_op jit(solution)/shard_map/ppermute | solution.py:809
  182.1 28.3 %collective-permute-start.38 = (bf16[384,1920]{1,0:T(8,128)(2,1)S(1)}, bf16[384,1920]{1,0:T(8,128)(2,1)S(1)}, u32[]{:S(2)}, u32[]{:S(2)}) collective-permute-start(bf16[384,1920]{1,0:T(8,128)(2,1)S(1)} %constant_dynamic-update-slice_fusion.20.r0.u0.d0.refs_5_.refs_9_.refs_13_), channel_id=1, source_target_pairs={{0,1},{1,0},{2,3},{3,2},{4,5},{5,4},{6,7},{7,6},{8,9},{9,8},{10,11... | collective-permute-start | bytes 4423688 | tf_op jit(solution)/shard_map/ppermute | solution.py:809
  182.1 28.3 %collective-permute-start.37 = (bf16[384,1920]{1,0:T(8,128)(2,1)S(1)}, bf16[384,1920]{1,0:T(8,128)(2,1)}, u32[]{:S(2)}, u32[]{:S(2)}) collective-permute-start(bf16[384,1920]{1,0:T(8,128)(2,1)S(1)} %constant_dynamic-update-slice_fusion.20.r0.u0.d0.refs_5_.refs_9_.refs_13_), channel_id=1, source_target_pairs={{0,2},{1,5},{2,0},{3,7},{4,6},{5,1},{6,4},{7,3},{8,10},{9,13},{10,... | collective-permute-start | bytes 4423688 | tf_op jit(solution)/shard_map/ppermute | solution.py:809
  183.0 10.6 %collective-permute-start.3 = (bf16[48,1536]{1,0:T(8,128)(2,1)S(1)}, bf16[48,1536]{1,0:T(8,128)(2,1)S(1)}, u32[]{:S(2)}, u32[]{:S(2)}) collective-permute-start(bf16[48,1536]{1,0:T(8,128)(2,1)S(1)} %get-tuple-element.448), channel_id=1, source_target_pairs={{0,24},{1,25},{2,26},{3,27},{4,28},{5,29},{6,30},{7,31},{8,0},{9,1... | collective-permute-start | bytes 442376 | tf_op jit(solution)/shard_map/ppermute | solution.py:809
  183.0 16.3 %collective-permute-start.2 = (bf16[48,1536]{1,0:T(8,128)(2,1)S(1)}, bf16[48,1536]{1,0:T(8,128)(2,1)S(1)}, u32[]{:S(2)}, u32[]{:S(2)}) collective-permute-start(bf16[48,1536]{1,0:T(8,128)(2,1)S(1)} %get-tuple-element.448), channel_id=1, source_target_pairs={{0,16},{1,17},{2,18},{3,19},{4,20},{5,21},{6,22},{7,23},{8,24},{9,... | collective-permute-start | bytes 442376 | tf_op jit(solution)/shard_map/ppermute | solution.py:809
  185.7 13.6 %collective-permute-start.1 = (bf16[48,1536]{1,0:T(8,128)(2,1)S(1)}, bf16[48,1536]{1,0:T(8,128)(2,1)S(1)}, u32[]{:S(2)}, u32[]{:S(2)}) collective-permute-start(bf16[48,1536]{1,0:T(8,128)(2,1)S(1)} %get-tuple-element.448), channel_id=1, source_target_pairs={{0,8},{1,9},{2,10},{3,11},{4,12},{5,13},{6,14},{7,15},{8,16},{9,17... | collective-permute-start | bytes 442376 | tf_op jit(solution)/shard_map/ppermute | solution.py:809
  213.9 18.1 %collective-permute-start.41 = (bf16[384,1536]{1,0:T(8,128)(2,1)}, bf16[384,1536]{1,0:T(8,128)(2,1)}, u32[]{:S(2)}, u32[]{:S(2)}) collective-permute-start(bf16[384,1536]{1,0:T(8,128)(2,1)} %constant_dynamic-update-slice_fusion.25.u0.d0.refs_0_.refs_4_), channel_id=1, source_target_pairs={{0,1},{1,0},{2,3},{3,2},{4,5},{5,4},{6,7},{7,6},{8,9},{9,8},{10,11... | collective-permute-start | bytes 3538952 | tf_op jit(solution)/shard_map/ppermute | solution.py:809
  214.3 17.7 %collective-permute-start.40 = (bf16[384,1536]{1,0:T(8,128)(2,1)}, bf16[384,1536]{1,0:T(8,128)(2,1)}, u32[]{:S(2)}, u32[]{:S(2)}) collective-permute-start(bf16[384,1536]{1,0:T(8,128)(2,1)} %constant_dynamic-update-slice_fusion.25.u0.d0.refs_0_.refs_4_), channel_id=1, source_target_pairs={{0,2},{1,5},{2,0},{3,7},{4,6},{5,1},{6,4},{7,3},{8,10},{9,13},{10,... | collective-permute-start | bytes 3538952 | tf_op jit(solution)/shard_map/ppermute | solution.py:809
  258.6 18.2 %collective-permute-start.44 = (bf16[768,1536]{1,0:T(8,128)(2,1)}, bf16[768,1536]{1,0:T(8,128)(2,1)}, u32[]{:S(2)}, u32[]{:S(2)}) collective-permute-start(bf16[768,1536]{1,0:T(8,128)(2,1)} %get-tuple-element.309), channel_id=1, source_target_pairs={{0,1},{1,0},{2,3},{3,2},{4,5},{5,4},{6,7},{7,6},{8,9},{9,8},{10,11... | collective-permute-start | bytes 7077896 | tf_op jit(solution)/shard_map/ppermute | solution.py:809
  276.8 18.4 %collective-permute-start.46 = (bf16[768,1920]{1,0:T(8,128)(2,1)}, bf16[768,1920]{1,0:T(8,128)(2,1)}, u32[]{:S(2)}, u32[]{:S(2)}) collective-permute-start(bf16[768,1920]{1,0:T(8,128)(2,1)} %get-tuple-element.322), channel_id=1, source_target_pairs={{0,1},{1,0},{2,3},{3,2},{4,5},{5,4},{6,7},{7,6},{8,9},{9,8},{10,11... | collective-permute-start | bytes 8847368 | tf_op jit(solution)/shard_map/ppermute | solution.py:809
  278.8 16.4 %collective-permute-start.45 = (bf16[384,1536]{1,0:T(8,128)(2,1)S(1)}, bf16[384,1536]{1,0:T(8,128)(2,1)}, u32[]{:S(2)}, u32[]{:S(2)}) collective-permute-start(bf16[384,1536]{1,0:T(8,128)(2,1)S(1)} %add_convert_fusion.3), channel_id=1, source_target_pairs={{0,2},{1,5},{2,0},{3,7},{4,6},{5,1},{6,4},{7,3},{8,10},{9,13},{10,... | collective-permute-start | bytes 3538952 | tf_op jit(solution)/shard_map/ppermute | solution.py:809
  296.8 13.8 %collective-permute-start.47 = (bf16[192,1536]{1,0:T(8,128)(2,1)S(1)}, bf16[192,1536]{1,0:T(8,128)(2,1)S(1)}, u32[]{:S(2)}, u32[]{:S(2)}) collective-permute-start(bf16[192,1536]{1,0:T(8,128)(2,1)S(1)} %add_convert_fusion.9), channel_id=1, source_target_pairs={{0,4},{1,3},{2,6},{3,1},{4,0},{5,7},{6,2},{7,5},{8,12},{9,11},{10,... | collective-permute-start | bytes 1769480 | tf_op jit(solution)/shard_map/ppermute | solution.py:809
  301.1 29.6 %collective-permute-start.51 = (bf16[384,1920]{1,0:T(8,128)(2,1)}, bf16[384,1920]{1,0:T(8,128)(2,1)}, u32[]{:S(2)}, u32[]{:S(2)}) collective-permute-start(bf16[384,1920]{1,0:T(8,128)(2,1)} %add_convert_fusion.1), channel_id=1, source_target_pairs={{0,2},{1,5},{2,0},{3,7},{4,6},{5,1},{6,4},{7,3},{8,10},{9,13},{10,... | collective-permute-start | bytes 4423688 | tf_op jit(solution)/shard_map/ppermute | solution.py:809
  313.4 17.2 %collective-permute-start.50 = (bf16[48,1536]{1,0:T(8,128)(2,1)S(1)}, bf16[48,1536]{1,0:T(8,128)(2,1)S(1)}, u32[]{:S(2)}, u32[]{:S(2)}) collective-permute-start(bf16[48,1536]{1,0:T(8,128)(2,1)S(1)} %get-tuple-element.460), channel_id=1, source_target_pairs={{0,8},{1,9},{2,10},{3,11},{4,12},{5,13},{6,14},{7,15},{8,16},{9,17... | collective-permute-start | bytes 442376 | tf_op jit(solution)/shard_map/ppermute | solution.py:809
  313.5 17.2 %collective-permute-start.49 = (bf16[48,1536]{1,0:T(8,128)(2,1)S(1)}, bf16[48,1536]{1,0:T(8,128)(2,1)S(1)}, u32[]{:S(2)}, u32[]{:S(2)}) collective-permute-start(bf16[48,1536]{1,0:T(8,128)(2,1)S(1)} %get-tuple-element.461), channel_id=1, source_target_pairs={{0,16},{1,17},{2,18},{3,19},{4,20},{5,21},{6,22},{7,23},{8,24},{9,... | collective-permute-start | bytes 442376 | tf_op jit(solution)/shard_map/ppermute | solution.py:809
  315.0 15.7 %collective-permute-start.48 = (bf16[48,1536]{1,0:T(8,128)(2,1)S(1)}, bf16[48,1536]{1,0:T(8,128)(2,1)S(1)}, u32[]{:S(2)}, u32[]{:S(2)}) collective-permute-start(bf16[48,1536]{1,0:T(8,128)(2,1)S(1)} %get-tuple-element.462), channel_id=1, source_target_pairs={{0,24},{1,25},{2,26},{3,27},{4,28},{5,29},{6,30},{7,31},{8,0},{9,1... | collective-permute-start | bytes 442376 | tf_op jit(solution)/shard_map/ppermute | solution.py:809
  330.7 18.6 %collective-permute-start.54 = (bf16[768,1280]{1,0:T(8,128)(2,1)}, bf16[768,1280]{1,0:T(8,128)(2,1)}, u32[]{:S(2)}, u32[]{:S(2)}) collective-permute-start(bf16[768,1280]{1,0:T(8,128)(2,1)} %get-tuple-element.346), channel_id=1, source_target_pairs={{0,1},{1,0},{2,3},{3,2},{4,5},{5,4},{6,7},{7,6},{8,9},{9,8},{10,11... | collective-permute-start | bytes 5898248 | tf_op jit(solution)/shard_map/ppermute | solution.py:809
  333.8 15.5 %collective-permute-start.53 = (bf16[192,1920]{1,0:T(8,128)(2,1)}, bf16[192,1920]{1,0:T(8,128)(2,1)S(1)}, u32[]{:S(2)}, u32[]{:S(2)}) collective-permute-start(bf16[192,1920]{1,0:T(8,128)(2,1)} %add_convert_fusion.7), channel_id=1, source_target_pairs={{0,4},{1,3},{2,6},{3,1},{4,0},{5,7},{6,2},{7,5},{8,12},{9,11},{10,... | collective-permute-start | bytes 2211848 | tf_op jit(solution)/shard_map/ppermute | solution.py:809
  336.6 12.7 %collective-permute-start.52 = (bf16[24,1536]{1,0:T(8,128)(2,1)S(1)}, bf16[24,1536]{1,0:T(8,128)(2,1)S(1)}, u32[]{:S(2)}, u32[]{:S(2)}) collective-permute-start(bf16[24,1536]{1,0:T(8,128)(2,1)S(1)} %select_convert_fusion.3), channel_id=1, source_target_pairs={{0,1},{1,0},{2,3},{3,2},{4,5},{5,4},{6,7},{7,6},{8,9},{9,8},{10,11... | collective-permute-start | bytes 221192 | tf_op jit(solution)/shard_map/ppermute | solution.py:809
  349.3 29.8 %collective-permute-start.59 = (bf16[768,1536]{1,0:T(8,128)(2,1)}, bf16[768,1536]{1,0:T(8,128)(2,1)}, u32[]{:S(2)}, u32[]{:S(2)}) collective-permute-start(bf16[768,1536]{1,0:T(8,128)(2,1)} %get-tuple-element.356), channel_id=1, source_target_pairs={{0,1},{1,0},{2,3},{3,2},{4,5},{5,4},{6,7},{7,6},{8,9},{9,8},{10,11... | collective-permute-start | bytes 7077896 | tf_op jit(solution)/shard_map/ppermute | solution.py:809
  352.6 26.5 %collective-permute-start.58 = (bf16[384,1280]{1,0:T(8,128)(2,1)S(1)}, bf16[384,1280]{1,0:T(8,128)(2,1)}, u32[]{:S(2)}, u32[]{:S(2)}) collective-permute-start(bf16[384,1280]{1,0:T(8,128)(2,1)S(1)} %add_convert_fusion.5), channel_id=1, source_target_pairs={{0,2},{1,5},{2,0},{3,7},{4,6},{5,1},{6,4},{7,3},{8,10},{9,13},{10,... | collective-permute-start | bytes 2949128 | tf_op jit(solution)/shard_map/ppermute | solution.py:809
  356.6 22.4 %collective-permute-start.57 = (bf16[48,1920]{1,0:T(8,128)(2,1)}, bf16[48,1920]{1,0:T(8,128)(2,1)S(1)}, u32[]{:S(2)}, u32[]{:S(2)}) collective-permute-start(bf16[48,1920]{1,0:T(8,128)(2,1)} %get-tuple-element.454), channel_id=1, source_target_pairs={{0,8},{1,9},{2,10},{3,11},{4,12},{5,13},{6,14},{7,15},{8,16},{9,17... | collective-permute-start | bytes 552968 | tf_op jit(solution)/shard_map/ppermute | solution.py:809
  356.9 22.1 %collective-permute-start.56 = (bf16[48,1920]{1,0:T(8,128)(2,1)}, bf16[48,1920]{1,0:T(8,128)(2,1)S(1)}, u32[]{:S(2)}, u32[]{:S(2)}) collective-permute-start(bf16[48,1920]{1,0:T(8,128)(2,1)} %get-tuple-element.455), channel_id=1, source_target_pairs={{0,16},{1,17},{2,18},{3,19},{4,20},{5,21},{6,22},{7,23},{8,24},{9,... | collective-permute-start | bytes 552968 | tf_op jit(solution)/shard_map/ppermute | solution.py:809
  358.4 20.7 %collective-permute-start.55 = (bf16[48,1920]{1,0:T(8,128)(2,1)S(1)}, bf16[48,1920]{1,0:T(8,128)(2,1)S(1)}, u32[]{:S(2)}, u32[]{:S(2)}) collective-permute-start(bf16[48,1920]{1,0:T(8,128)(2,1)S(1)} %get-tuple-element.456), channel_id=1, source_target_pairs={{0,24},{1,25},{2,26},{3,27},{4,28},{5,29},{6,30},{7,31},{8,0},{9,1... | collective-permute-start | bytes 552968 | tf_op jit(solution)/shard_map/ppermute | solution.py:809
  379.1 30.0 %collective-permute-start.62 = (bf16[768,1920]{1,0:T(8,128)(2,1)}, bf16[768,1920]{1,0:T(8,128)(2,1)}, u32[]{:S(2)}, u32[]{:S(2)}) collective-permute-start(bf16[768,1920]{1,0:T(8,128)(2,1)} %get-tuple-element.372), channel_id=1, source_target_pairs={{0,1},{1,0},{2,3},{3,2},{4,5},{5,4},{6,7},{7,6},{8,9},{9,8},{10,11... | collective-permute-start | bytes 8847368 | tf_op jit(solution)/shard_map/ppermute | solution.py:809
  380.9 27.5 %collective-permute-start.60 = (bf16[24,1920]{1,0:T(8,128)(2,1)S(1)}, bf16[24,1920]{1,0:T(8,128)(2,1)S(1)}, u32[]{:S(2)}, u32[]{:S(2)}) collective-permute-start(bf16[24,1920]{1,0:T(8,128)(2,1)S(1)} %select_convert_fusion.1), channel_id=1, source_target_pairs={{0,1},{1,0},{2,3},{3,2},{4,5},{5,4},{6,7},{7,6},{8,9},{9,8},{10,11... | collective-permute-start | bytes 276488 | tf_op jit(solution)/shard_map/ppermute | solution.py:809
  382.5 21.6 %collective-permute-start.66 = (bf16[384,1536]{1,0:T(8,128)(2,1)S(1)}, bf16[384,1536]{1,0:T(8,128)(2,1)}, u32[]{:S(2)}, u32[]{:S(2)}) collective-permute-start(bf16[384,1536]{1,0:T(8,128)(2,1)S(1)} %add_convert_fusion.2), channel_id=1, source_target_pairs={{0,2},{1,5},{2,0},{3,7},{4,6},{5,1},{6,4},{7,3},{8,10},{9,13},{10,... | collective-permute-start | bytes 3538952 | tf_op jit(solution)/shard_map/ppermute | solution.py:809
  386.9 21.5 %collective-permute-start.61 = (bf16[192,1280]{1,0:T(8,128)(2,1)}, bf16[192,1280]{1,0:T(8,128)(2,1)}, u32[]{:S(2)}, u32[]{:S(2)}) collective-permute-start(bf16[192,1280]{1,0:T(8,128)(2,1)} %add_convert_fusion.11), channel_id=1, source_target_pairs={{0,4},{1,3},{2,6},{3,1},{4,0},{5,7},{6,2},{7,5},{8,12},{9,11},{10,... | collective-permute-start | bytes 1474568 | tf_op jit(solution)/shard_map/ppermute | solution.py:809
  406.5 25.1 %collective-permute-start.67 = (bf16[192,1536]{1,0:T(8,128)(2,1)}, bf16[192,1536]{1,0:T(8,128)(2,1)}, u32[]{:S(2)}, u32[]{:S(2)}) collective-permute-start(bf16[192,1536]{1,0:T(8,128)(2,1)} %add_convert_fusion.8), channel_id=1, source_target_pairs={{0,4},{1,3},{2,6},{3,1},{4,0},{5,7},{6,2},{7,5},{8,12},{9,11},{10,... | collective-permute-start | bytes 1769480 | tf_op jit(solution)/shard_map/ppermute | solution.py:809
  411.5 20.0 %collective-permute-start.65 = (bf16[48,1280]{1,0:T(8,128)(2,1)}, bf16[48,1280]{1,0:T(8,128)(2,1)S(1)}, u32[]{:S(2)}, u32[]{:S(2)}) collective-permute-start(bf16[48,1280]{1,0:T(8,128)(2,1)} %get-tuple-element.466), channel_id=1, source_target_pairs={{0,8},{1,9},{2,10},{3,11},{4,12},{5,13},{6,14},{7,15},{8,16},{9,17... | collective-permute-start | bytes 368648 | tf_op jit(solution)/shard_map/ppermute | solution.py:809
  411.5 20.0 %collective-permute-start.64 = (bf16[48,1280]{1,0:T(8,128)(2,1)}, bf16[48,1280]{1,0:T(8,128)(2,1)}, u32[]{:S(2)}, u32[]{:S(2)}) collective-permute-start(bf16[48,1280]{1,0:T(8,128)(2,1)} %get-tuple-element.467), channel_id=1, source_target_pairs={{0,16},{1,17},{2,18},{3,19},{4,20},{5,21},{6,22},{7,23},{8,24},{9,... | collective-permute-start | bytes 368648 | tf_op jit(solution)/shard_map/ppermute | solution.py:809
  412.4 19.1 %collective-permute-start.63 = (bf16[48,1280]{1,0:T(8,128)(2,1)}, bf16[48,1280]{1,0:T(8,128)(2,1)}, u32[]{:S(2)}, u32[]{:S(2)}) collective-permute-start(bf16[48,1280]{1,0:T(8,128)(2,1)} %get-tuple-element.468), channel_id=1, source_target_pairs={{0,24},{1,25},{2,26},{3,27},{4,28},{5,29},{6,30},{7,31},{8,0},{9,1... | collective-permute-start | bytes 368648 | tf_op jit(solution)/shard_map/ppermute | solution.py:809
  418.4 19.7 %collective-permute-start.68 = (bf16[384,1920]{1,0:T(8,128)(2,1)}, bf16[384,1920]{1,0:T(8,128)(2,1)}, u32[]{:S(2)}, u32[]{:S(2)}) collective-permute-start(bf16[384,1920]{1,0:T(8,128)(2,1)} %add_convert_fusion), channel_id=1, source_target_pairs={{0,2},{1,5},{2,0},{3,7},{4,6},{5,1},{6,4},{7,3},{8,10},{9,13},{10,... | collective-permute-start | bytes 4423688 | tf_op jit(solution)/shard_map/ppermute | solution.py:809
  439.7 15.0 %collective-permute-start.75 = (bf16[192,1920]{1,0:T(8,128)(2,1)S(1)}, bf16[192,1920]{1,0:T(8,128)(2,1)S(1)}, u32[]{:S(2)}, u32[]{:S(2)}) collective-permute-start(bf16[192,1920]{1,0:T(8,128)(2,1)S(1)} %add_convert_fusion.6), channel_id=1, source_target_pairs={{0,4},{1,3},{2,6},{3,1},{4,0},{5,7},{6,2},{7,5},{8,12},{9,11},{10,... | collective-permute-start | bytes 2211848 | tf_op jit(solution)/shard_map/ppermute | solution.py:809
  440.2 16.4 %collective-permute-start.71 = (bf16[24,1280]{1,0:T(8,128)(2,1)S(1)}, bf16[24,1280]{1,0:T(8,128)(2,1)S(1)}, u32[]{:S(2)}, u32[]{:S(2)}) collective-permute-start(bf16[24,1280]{1,0:T(8,128)(2,1)S(1)} %select_convert_fusion.5), channel_id=1, source_target_pairs={{0,1},{1,0},{2,3},{3,2},{4,5},{5,4},{6,7},{7,6},{8,9},{9,8},{10,11... | collective-permute-start | bytes 184328 | tf_op jit(solution)/shard_map/ppermute | solution.py:809
  440.8 13.9 %collective-permute-start.73 = (bf16[48,1536]{1,0:T(8,128)(2,1)S(1)}, bf16[48,1536]{1,0:T(8,128)(2,1)S(1)}, u32[]{:S(2)}, u32[]{:S(2)}) collective-permute-start(bf16[48,1536]{1,0:T(8,128)(2,1)S(1)} %get-tuple-element.458), channel_id=1, source_target_pairs={{0,16},{1,17},{2,18},{3,19},{4,20},{5,21},{6,22},{7,23},{8,24},{9,... | collective-permute-start | bytes 442376 | tf_op jit(solution)/shard_map/ppermute | solution.py:809
  442.3 12.4 %collective-permute-start.72 = (bf16[48,1536]{1,0:T(8,128)(2,1)S(1)}, bf16[48,1536]{1,0:T(8,128)(2,1)S(1)}, u32[]{:S(2)}, u32[]{:S(2)}) collective-permute-start(bf16[48,1536]{1,0:T(8,128)(2,1)S(1)} %get-tuple-element.459), channel_id=1, source_target_pairs={{0,24},{1,25},{2,26},{3,27},{4,28},{5,29},{6,30},{7,31},{8,0},{9,1... | collective-permute-start | bytes 442376 | tf_op jit(solution)/shard_map/ppermute | solution.py:809
  448.9 14.1 %collective-permute-start.70 = (bf16[384,1280]{1,0:T(8,128)(2,1)S(1)}, bf16[384,1280]{1,0:T(8,128)(2,1)S(1)}, u32[]{:S(2)}, u32[]{:S(2)}) collective-permute-start(bf16[384,1280]{1,0:T(8,128)(2,1)S(1)} %add_convert_fusion.4), channel_id=1, source_target_pairs={{0,2},{1,5},{2,0},{3,7},{4,6},{5,1},{6,4},{7,3},{8,10},{9,13},{10,... | collective-permute-start | bytes 2949128 | tf_op jit(solution)/shard_map/ppermute | solution.py:809
  463.2 18.1 %collective-permute-start.77 = (bf16[192,1280]{1,0:T(8,128)(2,1)S(1)}, bf16[192,1280]{1,0:T(8,128)(2,1)S(1)}, u32[]{:S(2)}, u32[]{:S(2)}) collective-permute-start(bf16[192,1280]{1,0:T(8,128)(2,1)S(1)} %add_convert_fusion.10), channel_id=1, source_target_pairs={{0,4},{1,3},{2,6},{3,1},{4,0},{5,7},{6,2},{7,5},{8,12},{9,11},{10,... | collective-permute-start | bytes 1474568 | tf_op jit(solution)/shard_map/ppermute | solution.py:809
  465.0 14.0 %collective-permute-start.80 = (bf16[48,1920]{1,0:T(8,128)(2,1)S(1)}, bf16[48,1920]{1,0:T(8,128)(2,1)S(1)}, u32[]{:S(2)}, u32[]{:S(2)}) collective-permute-start(bf16[48,1920]{1,0:T(8,128)(2,1)S(1)} %get-tuple-element.451), channel_id=1, source_target_pairs={{0,8},{1,9},{2,10},{3,11},{4,12},{5,13},{6,14},{7,15},{8,16},{9,17... | collective-permute-start | bytes 552968 | tf_op jit(solution)/shard_map/ppermute | solution.py:809
  481.8 10.7 %collective-permute-start.83 = (bf16[48,1280]{1,0:T(8,128)(2,1)S(1)}, bf16[48,1280]{1,0:T(8,128)(2,1)S(1)}, u32[]{:S(2)}, u32[]{:S(2)}) collective-permute-start(bf16[48,1280]{1,0:T(8,128)(2,1)S(1)} %get-tuple-element.463), channel_id=1, source_target_pairs={{0,8},{1,9},{2,10},{3,11},{4,12},{5,13},{6,14},{7,15},{8,16},{9,17... | collective-permute-start | bytes 368648 | tf_op jit(solution)/shard_map/ppermute | solution.py:809
  485.4 12.1 %collective-permute-start.82 = (bf16[48,1280]{1,0:T(8,128)(2,1)S(1)}, bf16[48,1280]{1,0:T(8,128)(2,1)S(1)}, u32[]{:S(2)}, u32[]{:S(2)}) collective-permute-start(bf16[48,1280]{1,0:T(8,128)(2,1)S(1)} %get-tuple-element.464), channel_id=1, source_target_pairs={{0,16},{1,17},{2,18},{3,19},{4,20},{5,21},{6,22},{7,23},{8,24},{9,... | collective-permute-start | bytes 368648 | tf_op jit(solution)/shard_map/ppermute | solution.py:809
  (51 other events, 330.3 us)

commit v6 on v0

v6 whole, which is shorter than its diff:
```python
import jax
import jax.numpy as jnp
from jax import lax
from jax.experimental import pallas as pl
from jax.experimental.pallas import tpu as pltpu
from jax.sharding import Mesh
from jax.sharding import PartitionSpec as P

HEADS = 12
HEAD_WIDTH = 64
LANES = 128
PAIRS = HEADS * HEAD_WIDTH // LANES
LOW = jnp.bfloat16
WIDE = jnp.float32
norm_eps = 1e-06
AXES = ("dp", "y", "c")
WHOLE, Z_LAST, Z_NEXT = range(3)
JOINED = (False, False)
ORDERS = (Z_LAST, Z_NEXT)
TURNS = (((1, 2, 3),),) * 6
VMEM_LIMIT = 60 * 1024 * 1024
TILE = 768


def cost(flops, moved, hard=0):
    return pl.CostEstimate(
        flops=int(flops) // 64, bytes_accessed=int(moved) // 64, transcendentals=int(hard) // 64
    )


def params():
    return pltpu.CompilerParams(vmem_limit_bytes=VMEM_LIMIT)


def vmem_specs(count):
    return [pl.BlockSpec(memory_space=pltpu.VMEM)] * count


def any_specs(count):
    return [pl.BlockSpec(memory_space=pl.ANY)] * count


def launch(body, args, after, prefetch, grid, in_specs, out_specs, out_shape, scratch, moved, name):
    count = len(args)

    def trimmed(*refs):
        body(*refs[:count], *refs[count + len(after) :])

    return pl.pallas_call(
        trimmed,
        out_shape=out_shape,
        grid_spec=pltpu.PrefetchScalarGridSpec(
            num_scalar_prefetch=prefetch,
            grid=grid,
            in_specs=in_specs + any_specs(len(after)),
            out_specs=out_specs,
            scratch_shapes=scratch,
        ),
        compiler_params=params(),
        cost_estimate=moved,
        name=name,
    )(*args, *after)


def smem_spec():
    return [pl.BlockSpec(memory_space=pltpu.SMEM)]


def dot(a, b):
    return jnp.dot(a, b, preferred_element_type=WIDE)


def dot_nt(a, b):
    return lax.dot_general(a, b, (((1,), (1,)), ((), ())), preferred_element_type=WIDE)


def dot_tn(a, b):
    return lax.dot_general(a, b, (((0,), (0,)), ((), ())), preferred_element_type=WIDE)


def place_of(spot, owner, block, z_first):
    z, x, y = spot[0], spot[1], spot[2]
    first, second, zr = block // 8, (block // 4) % 2, block % 4
    if not z_first:
        second, zr = block % 2, (block // 2) % 4
    bz = lax.rem(z - zr + 4, 4)
    bx = lax.rem(x + jnp.where(owner == 0, second, first), 2)
    by = lax.rem(y + jnp.where(owner == 0, first, second), 2)
    return (bz * 2 + bx) * 2 + by


def side_copies(spot, weight, refs, side, target, sems, width):
    arrays, column, z_first = weight
    at = pl.ds(column, width)
    if len(arrays) == 2:
        return [pltpu.make_async_copy(refs[side].at[:, at], target, sems.at[side, 0])]
    owner = spot[3] if side == 0 else 1 - spot[3]
    rows = arrays[0].shape[0] // 8
    copies = []
    for block in range(16):
        start = pl.multiple_of(place_of(spot, owner, block, z_first) * rows, 16)
        copies.append(
            pltpu.make_async_copy(
                refs[2 * side + block // 8].at[pl.ds((block % 8) * rows, rows), at],
                target.at[pl.ds(start, rows), :],
                sems.at[side, block],
            )
        )
    return copies


def start_all(*groups):
    for copies in groups:
        for copy in copies:
            copy.start()


def wait_all(*groups):
    for copies in groups:
        for copy in copies:
            copy.wait()


def norm_rows(v):
    center = v - jnp.mean(v, axis=-1, keepdims=True)
    r = lax.rsqrt(jnp.mean(center * center, axis=-1, keepdims=True) + norm_eps)
    return center * r, r


def norm_back(v, gain, d):
    xh, r = norm_rows(v)
    dg = d * gain
    m1 = jnp.mean(dg, axis=-1, keepdims=True)
    m2 = jnp.mean(dg * xh, axis=-1, keepdims=True)
    return (
        r * (dg - m1 - xh * m2),
        jnp.sum(d * xh, axis=0, keepdims=True),
        jnp.sum(d, axis=0, keepdims=True),
    )


GAIN1, GAIN2, BQ, BV, BO, BD, SH1, SH2 = range(8)


def qkv_forward(spot, weight, h, hidden, devices, after):
    rows, width = h.shape
    wide = 3 * width
    half = wide // 2
    refs = weight[0]

    def body(spot_ref, *rest):
        h_ref, qkv_ref, a_ref, t_ref, b_ref = rest[len(refs) : len(refs) + 5]
        w_ref, row_ref, sems = rest[len(refs) + 5 :]
        c = spot_ref[3]
        own, other = [
            side_copies(spot_ref, weight, rest, side, w_ref.at[side], sems, half + LANES)
            for side in range(2)
        ]
        start_all(own, other)
        xh, r = norm_rows(h_ref[...])
        wait_all(own)
        values = w_ref[0, :, half:].astype(WIDE)
        table = values.T[0:8, :]
        t_ref[...] = table
        share = hidden // devices
        for device in range(devices):
            at = device * (width // devices)
            b_ref[0:1, device * share : (device + 1) * share] = values[
                at : at + 1, LANES - share :
            ]
        row_ref[:, :width] = table[BQ : BQ + 1]
        row_ref[:, width : 2 * width] = jnp.zeros((1, width), WIDE)
        row_ref[:, 2 * width :] = table[BV : BV + 1]
        a = (xh * table[GAIN1 : GAIN1 + 1] + table[SH1 : SH1 + 1]).astype(LOW)
        a_ref[...] = a
        for side, owner in enumerate((c, 1 - c)):
            if side == 1:
                wait_all(other)
            to = pl.ds(pl.multiple_of(owner * half, LANES), half)
            qkv_ref[:, to] = (dot(a_ref[...], w_ref[side, :, :half]) + row_ref[:, to]).astype(LOW)

    return launch(
        body,
        [spot, *refs, h],
        after,
        prefetch=0,
        grid=(),
        in_specs=smem_spec() + any_specs(len(refs)) + vmem_specs(1),
        out_specs=vmem_specs(4),
        out_shape=[
            jax.ShapeDtypeStruct((rows, wide), LOW),
            jax.ShapeDtypeStruct((rows, width), LOW),
            jax.ShapeDtypeStruct((8, width), WIDE),
            jax.ShapeDtypeStruct((1, hidden), WIDE),
        ],
        scratch=[
            pltpu.VMEM((2, width, half + LANES), LOW),
            pltpu.VMEM((1, wide), WIDE),
            pltpu.SemaphoreType.DMA((2, 16)),
        ],
        moved=cost(2 * rows * width * wide, 2 * width * wide + 9 * rows * width),
        name="qkv_forward",
    )


def attention_forward(lengths, qkv, after):
    rows, wide = qkv.shape
    width = wide // 3

    def body(len_ref, q_ref, k_ref, v_ref, o_ref, lse_ref):
        pair = pl.program_id(0)
        lane = lax.broadcasted_iota(jnp.int32, (1, LANES), 1)
        key = lax.broadcasted_iota(jnp.int32, (1, rows), 1)
        shut = jnp.where(key < len_ref[0], 0.0, -1e30)
        q = q_ref[...] * jnp.asarray(HEAD_WIDTH**-0.5, LOW)
        k = k_ref[...]
        v = v_ref[...]
        outs = []
        stats = jnp.where(pair == 0, jnp.zeros((rows, LANES), WIDE), lse_ref[...])
        for side in range(2):
            inside = (lane >= HEAD_WIDTH) == (side == 1)
            qs = jnp.where(inside, q, jnp.zeros_like(q))
            s = dot_nt(qs, k) + shut
            peak = jnp.max(s, axis=1, keepdims=True)
            e = jnp.exp(s - peak)
            total = jnp.sum(e, axis=1, keepdims=True)
            p = (e * (1.0 / total)).astype(LOW)
            outs.append(dot(p, v))
            stats = jnp.where(lane == pair * 2 + side, peak + jnp.log(total), stats)
        lse_ref[...] = stats
        o_ref[...] = jnp.where(lane < HEAD_WIDTH, outs[0], outs[1]).astype(LOW)

    return launch(
        body,
        [lengths, qkv, qkv, qkv],
        after,
        out_shape=[
            jax.ShapeDtypeStruct((rows, width), LOW),
            jax.ShapeDtypeStruct((rows, LANES), WIDE),
        ],
        prefetch=1,
        grid=(PAIRS,),
        in_specs=[
            pl.BlockSpec((rows, LANES), lambda p, n: (0, p)),
            pl.BlockSpec((rows, LANES), lambda p, n: (0, p + PAIRS)),
            pl.BlockSpec((rows, LANES), lambda p, n: (0, p + 2 * PAIRS)),
        ],
        out_specs=[
            pl.BlockSpec((rows, LANES), lambda p, n: (0, p)),
            pl.BlockSpec((rows, LANES), lambda p, n: (0, 0)),
        ],
        moved=cost(16 * rows * rows * width, 8 * rows * width, HEADS * rows * rows),
        scratch=[],
        name="attention_forward",
    )


def gelu_parts(u):
    cdf = 0.5 * (1.0 + lax.erf(u * (0.5**0.5)))
    pdf = jnp.exp(-0.5 * u * u) * (0.3989422804014327)
    return cdf, pdf


def up_forward(spot, weight, out_weight, h, mixed, up_bias, table, after):
    rows, width = h.shape
    hidden = up_bias.shape[1]
    half = hidden // 2
    part = width // 2
    tile = TILE
    tiles = half // tile
    refs = weight[0]

    def body(spot_ref, *rest):
        w_refs, rest = rest[: len(refs)], rest[len(refs) :]
        (
            h_ref, m_ref, b_ref, t_ref, h2_ref, a_ref, z_out, s_out,
            w_ref, wo_ref, z_ref, s_ref, sems, sems_o, sems_t,
        ) = rest
        c = spot_ref[3]
        outs = [
            side_copies(spot_ref, out_weight, w_refs, side, wo_ref.at[side], sems_o, part)
            for side in range(2)
        ]
        sides = [
            side_copies(spot_ref, weight, w_refs, side, w_ref.at[side], sems, half)
            for side in range(2)
        ]
        start_all(*outs, *sides)
        wait_all(*outs)
        for side, owner in enumerate((c, 1 - c)):
            to = pl.ds(pl.multiple_of(owner * part, LANES), part)
            h2_ref[:, to] = h_ref[:, to] + (
                dot(m_ref[...], wo_ref[side]) + t_ref[BO : BO + 1, to]
            )
        xh, r = norm_rows(h2_ref[...])
        a_ref[...] = (xh * t_ref[GAIN2 : GAIN2 + 1, :] + t_ref[SH2 : SH2 + 1, :]).astype(LOW)

        def stored(step):
            side, n = step // tiles, lax.rem(step, tiles)
            owner = jnp.where(side == 0, c, 1 - c)
            at = pl.ds(pl.multiple_of(owner * half + n * tile, LANES), tile)
            return side, n, at, [
                pltpu.make_async_copy(ref.at[:, at], out.at[:, at], sems_t.at[which, step])
                for which, (ref, out) in enumerate(((z_ref, z_out), (s_ref, s_out)))
            ]

        def work(step, carry):
            side, n, at, copies = stored(step)

            for which in range(2):

                @pl.when(step == which * tiles)
                def ready():
                    wait_all(sides[which])

            up = pl.ds(pl.multiple_of(n * tile, LANES), tile)
            u = dot(a_ref[...], w_ref[side, :, up]) + b_ref[:, at]
            cdf, pdf = gelu_parts(u)
            z_ref[:, at] = (u * cdf).astype(LOW)
            s_ref[:, at] = (cdf + u * pdf).astype(LOW)
            start_all(copies)
            return carry

        lax.fori_loop(0, 2 * tiles, work, 0)
        for step in range(2 * tiles):
            wait_all(stored(step)[3])

    return launch(
        body,
        [spot, *refs, h, mixed, up_bias, table],
        after,
        prefetch=0,
        grid=(),
        in_specs=smem_spec() + any_specs(len(refs)) + vmem_specs(4),
        out_specs=vmem_specs(2) + any_specs(2),
        out_shape=[
            jax.ShapeDtypeStruct((rows, width), WIDE),
            jax.ShapeDtypeStruct((rows, width), LOW),
            jax.ShapeDtypeStruct((rows, hidden), LOW),
            jax.ShapeDtypeStruct((rows, hidden), LOW),
        ],
        scratch=[
            pltpu.VMEM((2, width, half), LOW),
            pltpu.VMEM((2, width, part), LOW),
            pltpu.VMEM((rows, hidden), LOW),
            pltpu.VMEM((rows, hidden), LOW),
            pltpu.SemaphoreType.DMA((2, 16)),
            pltpu.SemaphoreType.DMA((2, 16)),
            pltpu.SemaphoreType.DMA((2, 2 * tiles)),
        ],
        moved=cost(
            2 * rows * width * hidden, 2 * width * hidden + 4 * rows * hidden, 2 * rows * hidden
        ),
        name="up_forward",
    )


def down_forward(spot, weight, h2, z, table, after):
    rows, width = h2.shape
    hidden = z.shape[1]
    half = hidden // 2
    refs = weight[0]

    def body(spot_ref, *rest):
        h_ref, z_in, t_ref, o_ref, w_ref, z_ref, sems, sems_r = rest[len(refs) :]
        c = spot_ref[3]
        sides = [
            side_copies(spot_ref, weight, rest, side, w_ref.at[side], sems, half)
            for side in range(2)
        ]
        loads = []
        for side, owner in enumerate((c, 1 - c)):
            at = pl.ds(pl.multiple_of(owner * half, LANES), half)
            loads.append(
                [pltpu.make_async_copy(z_in.at[:, at], z_ref.at[side], sems_r.at[side])]
            )
        start_all(sides[0], loads[0], sides[1], loads[1])
        total = h_ref[...] + t_ref[BD : BD + 1, :]
        for side in range(2):
            wait_all(sides[side], loads[side])
            total = total + dot_nt(z_ref[side], w_ref[side])
        o_ref[...] = total

    return launch(
        body,
        [spot, *refs, h2, z, table],
        after,
        prefetch=0,
        grid=(),
        in_specs=smem_spec()
        + any_specs(len(refs))
        + vmem_specs(1)
        + any_specs(1)
        + vmem_specs(1),
        out_specs=vmem_specs(1),
        out_shape=[jax.ShapeDtypeStruct((rows, width), WIDE)],
        scratch=[
            pltpu.VMEM((2, width, half), LOW),
            pltpu.VMEM((2, rows, half), LOW),
            pltpu.SemaphoreType.DMA((2, 16)),
            pltpu.SemaphoreType.DMA((2,)),
        ],
        moved=cost(2 * rows * width * hidden, 2 * width * hidden + 2 * rows * hidden),
        name="down_forward",
    )[0]


def block_starts(spot, owner, rows, order):
    if order == WHOLE:
        return [block * rows for block in range(16)]
    z, x, y = spot[0], spot[1], spot[2]
    result = []
    for block in range(16):
        bz, bx, by = block // 4, (block // 2) % 2, block % 2
        zr = lax.rem(z - bz + 4, 4)
        xr = lax.rem(x + bx, 2)
        yr = lax.rem(y + by, 2)
        first = jnp.where(owner == 0, yr, xr)
        second = jnp.where(owner == 0, xr, yr)
        place = (first * 2 + second) * 4 + zr if order == Z_LAST else (first * 4 + zr) * 2 + second
        result.append(pl.multiple_of(place * rows, 16))
    return result


def put_blocks(value, out_ref, starts, column, width):
    rows = value.shape[0] // 16
    low = value.astype(LOW)
    for block, start in enumerate(starts):
        out_ref[pl.ds(start, rows), pl.ds(column, width)] = low[block * rows : (block + 1) * rows]


def column_sum(value):
    return jnp.sum(value.astype(WIDE), axis=0, keepdims=True)


def mlp_backward(
    spot, up, down, out_weight, e, a2, z, slope, h2, mixed, table, joined, order, after
):
    rows, width = e.shape
    hidden = z.shape[1]
    half = hidden // 2
    part = width // 2
    tile = TILE
    tiles = half // tile
    wide = hidden + part
    refs, down_refs = up[0], down[0]
    near = half + part
    widths = [wide] if joined else [near, half]

    def body(spot_ref, *rest):
        w_refs, rest = rest[: len(refs)], rest[len(refs) :]
        d_refs, rest = rest[: len(down_refs)], rest[len(down_refs) :]
        buffers = [rest[7 + 2 * n : 9 + 2 * n] for n in range(len(widths))]
        rest = rest[:7] + rest[7 + 2 * len(widths) :]
        (
            e_in, a_in, z_in, s_in, h_in, m_in, t_ref,
            bd_ref, bu_ref, e2_ref, da_ref, sums_ref,
            w_ref, wo_ref, e_ref, a_ref, z_ref, s_ref, h_ref, m_ref,
            em_ref, emt_ref, at_ref, acc_ref, grad_ref, sems, sems_d, sems_o, sems_r, sems_g,
        ) = rest
        c = spot_ref[3]
        loads = [
            pltpu.make_async_copy(source, target, sems_r.at[n])
            for n, (source, target) in enumerate(
                (
                    (e_in, e_ref), (a_in, a_ref), (z_in, z_ref), (s_in, s_ref), (h_in, h_ref),
                    (m_in, m_ref),
                )
            )
        ]
        sides = [
            side_copies(spot_ref, down, d_refs, side, w_ref.at[side, 1], sems_d, half)
            + side_copies(spot_ref, up, w_refs, side, w_ref.at[side, 0], sems, half)
            for side in range(2)
        ]
        outs = [
            side_copies(spot_ref, out_weight, w_refs, side, wo_ref.at[side], sems_o, part)
            for side in range(2)
        ]
        start_all(loads[:2], sides[0], loads[2:4], sides[1], loads[4:], *outs)
        wait_all(loads[:1])
        em = e_ref[...].astype(LOW)
        em_ref[...] = em
        bd_ref[...] = column_sum(em)
        emt_ref[...] = em.T
        wait_all(loads[1:2])
        at_ref[...] = a_ref[...].T
        acc_ref[...] = jnp.zeros_like(acc_ref)

        def stored(side, which):
            start, size = ((0, half), (half, part), (near, half))[which]
            out, to = buffers[-1][side], start
            if not joined:
                out, to = (buffers[1][side], 0) if which == 2 else (buffers[0][side], start)
            return pltpu.make_async_copy(
                grad_ref.at[side, :, pl.ds(start, size)],
                out.at[:, pl.ds(to, size)],
                sems_g.at[side, which],
            )

        def work(step, carry):
            side, n = step // tiles, lax.rem(step, tiles)
            owner = jnp.where(side == 0, c, 1 - c)

            @pl.when(step == 0)
            def first_ready():
                wait_all(sides[0], loads[2:4])

            @pl.when(step == tiles)
            def second_ready():
                stored(0, 0).start()
                stored(0, 2).start()
                wait_all(sides[1])

            at = pl.ds(pl.multiple_of(owner * half + n * tile, LANES), tile)
            column = pl.multiple_of(n * tile, LANES)
            tile_at = pl.ds(column, tile)
            starts = block_starts(spot_ref, owner, width // 16, order)
            grads = grad_ref.at[side]
            dz = dot(em_ref[...], w_ref[side, 1, :, tile_at])
            du = (dz * s_ref[:, at].astype(WIDE)).astype(LOW)
            bu_ref[:, at] = column_sum(du)
            put_blocks(dot(emt_ref[...], z_ref[:, at]), grads, starts, near + column, tile)
            put_blocks(dot(at_ref[...], du), grads, starts, column, tile)
            acc_ref[...] += dot_nt(du, w_ref[side, 0, :, tile_at])
            return carry

        lax.fori_loop(0, 2 * tiles, work, 0)
        stored(1, 0).start()
        stored(1, 2).start()
        wait_all(loads[4:])
        at_ref[...] = m_ref[...].T
        dv, gain, shift = norm_back(h_ref[...], t_ref[GAIN2 : GAIN2 + 1, :], acc_ref[...])
        e2 = e_ref[...] + dv
        e2_ref[...] = e2
        em_ref[...] = e2.astype(LOW)
        sums_ref[0:1, :] = gain
        sums_ref[1:2, :] = shift
        sums_ref[2:3, :] = column_sum(em_ref[...])
        wait_all(*outs)
        da = None
        for side, owner in enumerate((c, 1 - c)):
            to = pl.ds(pl.multiple_of(owner * part, LANES), part)
            ey = em_ref[:, to]
            product = dot_nt(ey, wo_ref[side])
            da = product if da is None else da + product
            starts = block_starts(spot_ref, owner, width // 16, order)
            put_blocks(dot(at_ref[...], ey), grad_ref.at[side], starts, half, part)
            stored(side, 1).start()
        da_ref[...] = da.astype(LOW)
        for side in range(2):
            for which in range(3):
                stored(side, which).wait()

    return launch(
        body,
        [spot, *refs, *down_refs, e, a2, z, slope, h2, mixed, table],
        after,
        prefetch=0,
        grid=(),
        in_specs=smem_spec() + any_specs(len(refs) + len(down_refs) + 6) + vmem_specs(1),
        out_specs=any_specs(2 * len(widths)) + vmem_specs(5),
        out_shape=[
            *[jax.ShapeDtypeStruct((width, size), LOW) for size in widths for side in range(2)],
            jax.ShapeDtypeStruct((1, width), WIDE),
            jax.ShapeDtypeStruct((1, hidden), WIDE),
            jax.ShapeDtypeStruct((rows, width), WIDE),
            jax.ShapeDtypeStruct((rows, width), LOW),
            jax.ShapeDtypeStruct((8, width), WIDE),
        ],
        scratch=[
            pltpu.VMEM((2, 2, width, half), LOW),
            pltpu.VMEM((2, width, part), LOW),
            pltpu.VMEM((rows, width), WIDE),
            pltpu.VMEM((rows, width), LOW),
            pltpu.VMEM((rows, hidden), LOW),
            pltpu.VMEM((rows, hidden), LOW),
            pltpu.VMEM((rows, width), WIDE),
            pltpu.VMEM((rows, width), LOW),
            pltpu.VMEM((rows, width), LOW),
            pltpu.VMEM((width, rows), LOW),
            pltpu.VMEM((width, rows), LOW),
            pltpu.VMEM((rows, width), WIDE),
            pltpu.VMEM((2, width, wide), LOW),
            pltpu.SemaphoreType.DMA((2, 16)),
            pltpu.SemaphoreType.DMA((2, 16)),
            pltpu.SemaphoreType.DMA((2, 16)),
            pltpu.SemaphoreType.DMA((6,)),
            pltpu.SemaphoreType.DMA((2, 3)),
        ],
        moved=cost(8 * rows * width * hidden, 8 * width * hidden + 4 * rows * hidden),
        name="mlp_backward",
    )


def attention_backward(lengths, qkv, da, mixed, lse, begin, pairs, after):
    rows, wide = qkv.shape
    width = pairs * LANES

    def body(len_ref, q_ref, k_ref, v_ref, d_ref, m_ref, lse_ref, out_ref, row_ref):
        pair = pl.program_id(0)

        @pl.when(pair == 0)
        def start():
            row_ref[...] = lse_ref[...].T

        lane = lax.broadcasted_iota(jnp.int32, (1, LANES), 1)
        sub = lax.broadcasted_iota(jnp.int32, (LANES, 1), 0)
        key = lax.broadcasted_iota(jnp.int32, (rows, 1), 0)
        shut = jnp.where(key < len_ref[0], 0.0, -1e30)
        scale = jnp.asarray(HEAD_WIDTH**-0.5, LOW)
        q = q_ref[...] * scale
        k = k_ref[...]
        v = v_ref[...]
        d = d_ref[...]
        kt = k.T * scale
        prod = (d.astype(WIDE) * m_ref[...].astype(WIDE)).T
        dks, dvs = [], []
        dqt = jnp.zeros((LANES, rows), WIDE)
        for side in range(2):
            inside = (lane >= HEAD_WIDTH) == (side == 1)
            down = (sub >= HEAD_WIDTH) == (side == 1)
            ks = jnp.where(inside, k, jnp.zeros_like(k))
            vs = jnp.where(inside, v, jnp.zeros_like(v))
            kts = jnp.where(down, kt, jnp.zeros_like(kt))
            first = side * HEAD_WIDTH
            delta = jnp.sum(prod[first : first + HEAD_WIDTH], axis=0, keepdims=True)
            log_total = row_ref[pl.ds((begin + pair) * 2 + side, 1), :]
            p = jnp.exp((dot_nt(ks, q) + shut) - log_total)
            dp = dot_nt(vs, d)
            dvs.append(dot(p.astype(LOW), d))
            ds = (p * (dp - delta)).astype(LOW)
            dks.append(dot(ds, q))
            dqt = dqt + dot(kts, ds)
        dq = dqt.T
        dk = jnp.where(lane < HEAD_WIDTH, dks[0], dks[1])
        dv = jnp.where(lane < HEAD_WIDTH, dvs[0], dvs[1])
        for n, value in enumerate((dq, dk, dv)):
            at = pl.ds(pl.multiple_of(n * width + pair * LANES, LANES), LANES)
            out_ref[:, at] = value.astype(LOW)

    return launch(
        body,
        [lengths, qkv, qkv, qkv, da, mixed, lse],
        after,
        out_shape=jax.ShapeDtypeStruct((rows, 3 * width), LOW),
        prefetch=1,
        grid=(pairs,),
        in_specs=[
            pl.BlockSpec((rows, LANES), lambda p, n: (0, p + begin)),
            pl.BlockSpec((rows, LANES), lambda p, n: (0, p + begin + PAIRS)),
            pl.BlockSpec((rows, LANES), lambda p, n: (0, p + begin + 2 * PAIRS)),
            pl.BlockSpec((rows, LANES), lambda p, n: (0, p + begin)),
            pl.BlockSpec((rows, LANES), lambda p, n: (0, p + begin)),
            pl.BlockSpec((rows, LANES), lambda p, n: (0, 0)),
        ],
        out_specs=pl.BlockSpec((rows, 3 * width), lambda p, n: (0, 0)),
        scratch=[pltpu.VMEM((LANES, rows), WIDE)],
        moved=cost(40 * rows * rows * width, 16 * rows * width, HEADS * rows * rows),
        name="attention_backward",
    )


def qkv_backward(spot, weight, dqkv, e2, h, a1, table, others, order, devices, after):
    rows, width = e2.shape
    wide = 3 * width
    half = wide // 2
    refs = weight[0]
    sums, down_sum, up_sum = others
    hidden = up_sum.shape[1]

    def body(spot_ref, *rest):
        w_refs, rest = rest[: len(refs)], rest[len(refs) :]
        d_ins, rest = rest[: len(dqkv)], rest[len(dqkv) :]
        (
            e_in, h_in, a_in, t_ref, s_ref, ds_ref, u_ref, o_ref, mine_out, rest_out,
            w_ref, d_ref, e_ref, h_ref, a_ref, at_ref, acc_ref, row_ref, pack_ref, grad_ref,
            sems, sems_r, sems_d, sems_g,
        ) = rest
        c = spot_ref[3]
        loads = [
            pltpu.make_async_copy(source, target, sems_r.at[n])
            for n, (source, target) in enumerate(
                ((a_in, a_ref), (h_in, h_ref), (e_in, e_ref))
            )
        ]
        part = width // len(dqkv)
        gathers = [
            pltpu.make_async_copy(
                d_in.at[:, pl.ds(third * part, part)],
                d_ref.at[:, pl.ds(third * width + n * part, part)],
                sems_d.at[n, third],
            )
            for n, d_in in enumerate(d_ins)
            for third in range(3)
        ]
        sides = [
            side_copies(spot_ref, weight, w_refs, side, w_ref.at[side], sems, half)
            for side in range(2)
        ]
        start_all(loads[:1], gathers, sides[0], sides[1], loads[1:])
        wait_all(loads[:1])
        at_ref[...] = a_ref[...].T
        wait_all(gathers)

        def stored(side, which):
            at = pl.ds((0, half)[which], (half, LANES)[which])
            out = (mine_out, rest_out)[side]
            return pltpu.make_async_copy(
                grad_ref.at[side, :, at], out.at[:, at], sems_g.at[side, which]
            )

        placed = []
        for side, owner in enumerate((c, 1 - c)):
            starts = block_starts(spot_ref, owner, width // 16, order)
            placed.append(starts)
            to = pl.ds(pl.multiple_of(owner * half, LANES), half)
            d = d_ref[:, to]
            put_blocks(dot(at_ref[...], d), grad_ref.at[side], starts, 0, half)
            stored(side, 0).start()
            wait_all(sides[side])
            product = dot_nt(d, w_ref[side])
            acc_ref[...] = product if side == 0 else acc_ref[...] + product
        wait_all(loads[1:])
        dv, gain, shift = norm_back(h_ref[...], t_ref[GAIN1 : GAIN1 + 1, :], acc_ref[...])
        o_ref[...] = e_ref[...] + dv
        row_ref[...] = jnp.zeros_like(row_ref)
        for row, value in (
            (GAIN1, gain),
            (GAIN2, s_ref[0:1, :]),
            (BQ, column_sum(d_ref[:, :width])),
            (BV, column_sum(d_ref[:, 2 * width :])),
            (BO, s_ref[2:3, :]),
            (BD, ds_ref[...]),
            (SH1, shift),
            (SH2, s_ref[1:2, :]),
        ):
            row_ref[row : row + 1, :] = value
        pack_ref[...] = row_ref[...].T
        share = hidden // devices
        for device in range(devices):
            at = device * (width // devices)
            pack_ref[at : at + 1, LANES - share :] = u_ref[
                0:1, device * share : (device + 1) * share
            ]
        for side in range(2):
            put_blocks(pack_ref[...], grad_ref.at[side], placed[side], half, LANES)
            stored(side, 1).start()
        for side in range(2):
            for which in range(2):
                stored(side, which).wait()

    return launch(
        body,
        [spot, *refs, *dqkv, e2, h, a1, table, sums, down_sum, up_sum],
        after,
        prefetch=0,
        grid=(),
        in_specs=smem_spec() + any_specs(len(refs) + len(dqkv) + 3) + vmem_specs(4),
        out_specs=vmem_specs(1) + any_specs(2),
        out_shape=[
            jax.ShapeDtypeStruct((rows, width), WIDE),
            jax.ShapeDtypeStruct((width, half + LANES), LOW),
            jax.ShapeDtypeStruct((width, half + LANES), LOW),
        ],
        scratch=[
            pltpu.VMEM((2, width, half), LOW),
            pltpu.VMEM((rows, wide), LOW),
            pltpu.VMEM((rows, width), WIDE),
            pltpu.VMEM((rows, width), WIDE),
            pltpu.VMEM((rows, width), LOW),
            pltpu.VMEM((width, rows), LOW),
            pltpu.VMEM((rows, width), WIDE),
            pltpu.VMEM((LANES, width), WIDE),
            pltpu.VMEM((width, LANES), WIDE),
            pltpu.VMEM((2, width, half + LANES), LOW),
            pltpu.SemaphoreType.DMA((2, 16)),
            pltpu.SemaphoreType.DMA((3,)),
            pltpu.SemaphoreType.DMA((len(dqkv), 3)),
            pltpu.SemaphoreType.DMA((2, 2)),
        ],
        moved=cost(4 * rows * width * wide, 4 * width * wide + 16 * rows * width),
        name="qkv_backward",
    )


def join(pieces):
    return jnp.concatenate(pieces, axis=0)


def finish_mlp(spot, parts, shapes):
    def body(spot_ref, *refs):
        outs = refs[-3:]
        c = spot_ref[3]
        for n, (layer, kept, got, columns) in enumerate(parts):
            for owner, ref in ((c, refs[2 * n]), (1 - c, refs[2 * n + 1])):
                column = 0
                for out, start, size in columns:
                    to = owner * (shapes[out][2] // 2) + start
                    outs[out][layer, :, pl.ds(pl.multiple_of(to, LANES), size)] = ref[
                        :, column : column + size
                    ].astype(WIDE)
                    column = column + size

    flat = [value for layer, kept, got, columns in parts for value in (kept, got)]
    return launch(
        body,
        [spot, *flat],
        [],
        prefetch=0,
        grid=(),
        in_specs=smem_spec() + vmem_specs(len(flat)),
        out_specs=vmem_specs(3),
        out_shape=[jax.ShapeDtypeStruct(shape, WIDE) for shape in shapes],
        scratch=[],
        moved=cost(0, 16 * sum(value.size for value in flat)),
        name="finish_mlp",
    )


def finish_qkv(spot, parts, shapes):
    share = shapes[3][1]
    half = shapes[0][2] // 2

    def body(spot_ref, *refs):
        qkv_ref, gain_ref, bias_ref, up_ref = refs[-4:]
        c = spot_ref[3]
        for layer in range(len(parts)):
            kept_ref, got_ref = refs[2 * layer], refs[2 * layer + 1]
            for owner, ref in ((c, kept_ref), (1 - c, got_ref)):
                start = pl.multiple_of(owner * half, LANES)
                qkv_ref[layer, :, pl.ds(start, half)] = ref[:, :half].astype(WIDE)
            packed = kept_ref[:, half : half + LANES]
            columns = packed.T
            gain_ref[layer] = columns[0:2, :]
            for n in range(6):
                bias_ref[n, layer : layer + 1, :] = columns[n + 2 : n + 3, :]
            up_ref[layer : layer + 1, :] = packed[0:1, LANES - share :]

    flat = [value for part in parts for value in part]
    return launch(
        body,
        [spot, *flat],
        [],
        prefetch=0,
        grid=(),
        in_specs=smem_spec() + vmem_specs(len(flat)),
        out_specs=vmem_specs(4),
        out_shape=[jax.ShapeDtypeStruct(shape, WIDE) for shape in shapes],
        scratch=[],
        moved=cost(0, 8 * sum(value.size for value in flat)),
        name="finish_qkv",
    )


def linear(z, x, y, c):
    return ((z * 2 + x) * 2 + y) * 2 + c


def pairs_of(step):
    result = []
    for z in range(4):
        for x in range(2):
            for y in range(2):
                for c in range(2):
                    result.append((linear(z, x, y, c), linear(*step(z, x, y, c))))
    return result


TO_Z = [pairs_of(lambda z, x, y, c, n=n: ((z + n) % 4, x, y, c)) for n in range(4)]
TO_XY = pairs_of(lambda z, x, y, c: (z, x, 1 - y, c) if c else (z, 1 - x, y, c))
TO_YX = pairs_of(lambda z, x, y, c: (z, 1 - x, y, c) if c else (z, x, 1 - y, c))


def send(value, pairs):
    return lax.ppermute(value, AXES, pairs)


def swap_cores(value):
    chips = lax.axis_size("dp") * lax.axis_size("y")
    return send(value, [(n, n ^ 1) for n in range(2 * chips)])


def stepped():
    return lax.axis_size("dp") == 8 and lax.axis_size("y") == 2


def place():
    dp = lax.axis_index("dp")
    return jnp.stack([dp // 2, dp % 2, lax.axis_index("y"), lax.axis_index("c")]).astype(jnp.int32)


def halves(pieces):
    low = [piece[:, : piece.shape[1] // 2] for piece in pieces]
    high = [piece[:, piece.shape[1] // 2 :] for piece in pieces]
    return jnp.concatenate(low, axis=1), jnp.concatenate(high, axis=1)


def both_cores(c, pieces):
    low, high = halves(pieces)
    mine = jnp.where(c == 0, low, high)
    got = swap_cores(jnp.where(c == 0, high, low))
    upper = jnp.concatenate([mine, got], axis=0)
    return jnp.where(c == 0, upper, jnp.concatenate([got, mine], axis=0))


class Chain:
    def __init__(self, steps):
        self.steps = steps
        self.result = None
        self.flying = None
        self.resume(None)

    def resume(self, arrived):
        try:
            self.waiting = self.steps.send(arrived)
        except StopIteration as end:
            self.waiting = None
            self.result = end.value

    def start(self):
        if self.waiting is not None:
            assert self.flying is None
            self.flying = [begin(value) for value, begin in self.waiting]


def offsets_of(widths):
    offsets = [0]
    for width in widths:
        offsets.append(offsets[-1] + width // 2)
    return offsets


def by(pairs):
    return lambda value: send(value, pairs)


def gather_steps(block, turns):
    ring = {0: block}
    for turn in turns:
        got = yield [(block, by(TO_Z[n])) for n in turn]
        ring.update(zip(turn, got))
    stack = join([ring[n] for n in range(4)])
    (got,) = yield [(stack, by(TO_XY))]
    near = join([stack, got])
    far, near_got = yield [(near, by(TO_YX)), (near, swap_cores)]
    (far_got,) = yield [(far, swap_cores)]
    return near, far, near_got, far_got


def gather_chips(block):
    return lax.all_gather(block, ("dp", "y"), axis=0, tiled=True)


def gather_at_once(block):
    (own,) = yield [(block, gather_chips)]
    (other,) = yield [(own, swap_cores)]
    return own, other


def added(parts):
    total = parts[0].astype(WIDE)
    for part in parts[1:]:
        total = total + part.astype(WIDE)
    return total


def last_step(c, total):
    rows = total.shape[0] // 2
    low, high = total[:rows], total[rows:]
    kept = jnp.where(c == 0, low, high).astype(WIDE)
    (got,) = yield [(jnp.where(c == 0, high, low).astype(LOW), swap_cores)]
    return kept, got


def scatter_steps(c, mine, rest, order):
    rows = mine.shape[0] // 16
    upper, lower = slice(8 * rows, 16 * rows), slice(0, 8 * rows)
    (got,) = yield [(rest, swap_cores)]
    (more,) = yield [(added([mine[upper], got[upper]]).astype(LOW), by(TO_YX))]
    parts = [mine[lower], got[lower], more]
    for along_z in (order == Z_NEXT, order == Z_LAST):
        size = parts[0].shape[0]
        kept = size // (4 if along_z else 2)
        if along_z:
            total = added(parts)
            sent = [
                (total[n * kept : (n + 1) * kept].astype(LOW), by(TO_Z[4 - n])) for n in (1, 2, 3)
            ]
        else:
            sent = [(added([part[kept:] for part in parts]).astype(LOW), by(TO_XY))]
        arrived = yield sent
        parts = [part[:kept] for part in parts] + arrived
    return (yield from last_step(c, added(parts)))


def scatter_chips(value):
    return lax.psum_scatter(value, ("dp", "y"), scatter_dimension=0, tiled=True)


def scatter_at_once(c, mine, rest):
    (got,) = yield [(rest, swap_cores)]
    (total,) = yield [(added([mine, got]).astype(LOW), scatter_chips)]
    return (yield from last_step(c, total))


def pack_small(gains, shifts, up_bias):
    rows = gains.shape[1]
    columns = jnp.concatenate([gains, shifts], axis=0).T
    share = up_bias.shape[0]
    first = jnp.pad(columns, ((0, 0), (0, LANES - share - columns.shape[1])))
    second = jnp.pad(up_bias[None, :], ((0, rows - 1), (0, 0)))
    packed = jnp.concatenate([first, second], axis=1)
    return jnp.concatenate([packed, packed], axis=1)


def local(
    hidden_in,
    cotangent,
    lengths,
    qkv_weight,
    out_weight,
    up_weight,
    down_weight,
    norm_gains,
    biases,
    up_bias,
):
    clips, slots, width = hidden_in.shape
    layers = qkv_weight.shape[0]
    hidden = down_weight.shape[1]
    assert clips == 1 and layers == 2
    by_steps = stepped()
    devices = lax.axis_size(AXES)
    spot = place()
    c = spot[3]
    chunks, spots = [], []
    for i in range(layers):
        gains, shifts, bias = (v[i].astype(LOW) for v in (norm_gains, biases, up_bias))
        chunks += [
            [qkv_weight[i].astype(LOW), pack_small(gains, shifts, bias)],
            [up_weight[i].astype(LOW), out_weight[i].astype(LOW)],
            [down_weight[i].T.astype(LOW)],
        ]
        spots += [offsets_of([piece.shape[1] for piece in chunk]) for chunk in chunks[-3:]]
    blocks = [both_cores(c, chunks[0])]
    rest = both_cores(c, [piece for chunk in chunks[1:] for piece in chunk])
    start = 0
    for at in spots[1:]:
        blocks.append(rest[:, start : start + at[-1]])
        start = start + at[-1]
    if by_steps:
        turns = [TURNS[n] for n in range(len(blocks))]
        gathers = [Chain(gather_steps(block, turn)) for block, turn in zip(blocks, turns)]
    else:
        gathers = [Chain(gather_at_once(block)) for block in blocks]
    q0, u0, d0, q1, u1, d1 = gathers

    def weight(i, chunk, member):
        n = 3 * i + chunk
        return gathers[n].result, spots[n][member], True

    rec = [{"h": hidden_in[0]}, {}]
    awaited = []

    def first_matmul(i):
        qkv, first, table, bias = qkv_forward(
            spot, weight(i, 0, 0), rec[i]["h"], hidden, devices, awaited
        )
        return {"qkv": qkv, "a1": first, "table": table, "bias": bias}

    def attend(i):
        mixed, lse = attention_forward(lengths, rec[i]["qkv"], awaited)
        return {"mixed": mixed, "lse": lse}

    def feed_up(i):
        r = rec[i]
        h2, second, z, slope = up_forward(
            spot,
            weight(i, 1, 0),
            weight(i, 1, 1),
            r["h"],
            r["mixed"],
            r["bias"],
            r["table"],
            awaited,
        )
        return {"h2": h2, "a2": second, "z": z, "slope": slope}

    def feed_down(i):
        r = rec[i]
        total = down_forward(spot, weight(i, 2, 0), r["h2"], r["z"], r["table"], awaited)
        return {"total": total}

    def feed_back(i):
        r = rec[i]
        *grads, down_sum, up_sum, e2, da, sums = mlp_backward(
            spot,
            weight(i, 1, 0),
            weight(i, 2, 0),
            weight(i, 1, 1),
            r["e"],
            r["a2"],
            r["z"],
            r["slope"],
            r["h2"],
            r["mixed"],
            r["table"],
            JOINED[i],
            ORDERS[i] if by_steps else WHOLE,
            awaited,
        )
        others = (sums, down_sum, up_sum)
        return {"first": grads[:2], "second": grads[2:], "e2": e2, "da": da, "others": others}

    def attend_back(i, begin):
        r = rec[i]
        dqkv = attention_backward(
            lengths, r["qkv"], r["da"], r["mixed"], r["lse"], begin, PAIRS // 2, awaited
        )
        return {f"dqkv{begin}": dqkv}

    def qkv_back(i):
        r = rec[i]
        e, mine, rest = qkv_backward(
            spot,
            weight(i, 0, 0),
            (r["dqkv0"], r[f"dqkv{PAIRS // 2}"]),
            r["e2"],
            r["h"],
            r["a1"],
            r["table"],
            r["others"],
            ORDERS[i] if by_steps else WHOLE,
            devices,
            awaited,
        )
        return {"e_in": e, "qkv_grad": (mine, rest)}

    def run(begin, end, *work):
        nonlocal awaited
        for chain in begin:
            chain.start()
        outs = []
        for function, i, *rest in work:
            outs.append(function(i, *rest))
            rec[i].update(outs[-1])
            awaited = []
        landing = [chain for chain in end if chain.flying is not None]
        flying = [chain.flying for chain in landing]
        arrived, outs = lax.optimization_barrier((flying, outs))
        for (function, i, *rest), new in zip(work, outs):
            rec[i].update(new)
        for chain, values in zip(landing, arrived):
            chain.flying = None
            chain.resume(values)
        awaited = awaited + [value for values in arrived for value in values]

    def drain(*chains):
        while any(chain.waiting is not None for chain in chains):
            for chain in chains:
                if chain.flying is not None:
                    values, chain.flying = chain.flying, None
                    chain.resume(values)
            for chain in chains:
                chain.start()

    def scatter(i, member):
        if by_steps:
            return Chain(scatter_steps(c, *rec[i][member], ORDERS[i]))
        return Chain(scatter_at_once(c, *rec[i][member]))

    run([q0], [q0])
    run([q0], [q0])
    run([q0, u0], [q0, u0])
    run([q0, u0, d0], [q0])
    run([], [u0], (first_matmul, 0))
    run([u0], [u0, d0], (attend, 0))
    run([u0, d0, q1], [u0, d0])
    run([d0], [d0, q1], (feed_up, 0))
    run([d0, q1, u1], [d0, q1])
    run([q1], [q1, u1], (feed_down, 0))
    rec[1]["h"] = rec[0]["total"]
    run([q1, u1, d1], [q1])
    run([], [u1], (first_matmul, 1))
    run([u1], [u1, d1], (attend, 1))
    run([u1, d1], [u1, d1])
    run([d1], [d1], (feed_up, 1))
    run([d1], [d1])

    left, right = 0, PAIRS // 2
    rec[1]["e"] = cotangent[0]
    run([], [], (feed_back, 1))
    u1 = scatter(1, "first")
    d1 = scatter(1, "second")
    run([d1, u1], [d1, u1], (attend_back, 1, left), (attend_back, 1, right))
    run([d1], [d1], (qkv_back, 1))
    rec[0]["e"] = rec[1]["e_in"]
    q1 = scatter(1, "qkv_grad")
    run([u1, d1, q1], [u1, d1, q1], (feed_back, 0))
    u0 = scatter(0, "first")
    d0 = scatter(0, "second")
    run([q1, d1, u1, d0, u0], [q1, d1, u1, d0, u0], (attend_back, 0, left), (attend_back, 0, right))
    run([d0, d1], [d0, d1], (qkv_back, 0))
    q0 = scatter(0, "qkv_grad")
    awaited = []
    drain(u0, d0, q0, q1, u1, d1)
    run([], [], (feed_down, 1))
    output = rec[1]["total"][None]
    input_grad = rec[0]["e_in"][None]
    down_shape = (layers, down_weight.shape[2], hidden)
    mlp_shapes = [down_shape, up_weight.shape, out_weight.shape]
    bias_shape = (biases.shape[1], layers, biases.shape[2])
    qkv_shapes = [qkv_weight.shape, norm_gains.shape, bias_shape, up_bias.shape]
    half = hidden // 2
    first, second = [(1, 0, half), (2, 0, width // 2)], [(0, 0, half)]
    parts = [
        (0, *u0.result, first),
        (0, *d0.result, second),
        (1, *u1.result, first),
        (1, *d1.result, second),
    ]
    down_grad, up_grad, out_grad = finish_mlp(spot, parts, mlp_shapes)
    qkv_grad, gains, shifts, up_sums = finish_qkv(spot, [q0.result, q1.result], qkv_shapes)
    shifts = jnp.swapaxes(shifts, 0, 1)
    down_grad = jnp.swapaxes(down_grad, 1, 2)
    return output, input_grad, qkv_grad, out_grad, up_grad, down_grad, gains, shifts, up_sums


def solution(mesh):
    size = dict(mesh.shape)
    fine = Mesh(mesh.devices.reshape(size["dp"], size["fsdp"] // 2, 2), AXES)
    return jax.shard_map(
        local,
        mesh=fine,
        in_specs=(
            P(AXES, None, None),
            P(AXES, None, None),
            P(AXES),
            P(None, AXES, None),
            P(None, AXES, None),
            P(None, AXES, None),
            P(None, None, AXES),
            P(None, None, AXES),
            P(None, None, AXES),
            P(None, AXES),
        ),
        out_specs=(
            P(AXES, None, None),
            P(AXES, None, None),
            P(None, AXES, None),
            P(None, AXES, None),
            P(None, AXES, None),
            P(None, None, AXES),
            P(None, None, AXES),
            P(None, None, AXES),
            P(None, AXES),
        ),
        check_vma=False,
    )
```

time: 1930 us -> 504 us (0.26)
  waiting for transfers between devices: 1090 us -> 116 us
  local copies, waits for them, and re-layouts: 599 us -> 36.7 us
  Pallas kernels: 0 us -> 190 us
  matrix products: 179 us -> 0 us
  starting transfers between devices: 0.29 us -> 96.2 us
    unnamed x4 -> x0, waiting for transfers between devices: 795 us -> none
    reshape x23 -> x0, local copies, waits for them, and re-layouts: 335 us -> none  [the longest x7 168 us: pack_blocks(): grad.reshape(grad.shape[0], count, -1).transpose(1, 0, 2).reshape(count, -1)]
    all_gather x2 -> x0, waiting for transfers between devices: 291 us -> none  [collect(): gathered = lax.all_gather(owned_row, ('dp', 'fsdp'), axis=0, tiled=True)]
    pallas_call x0 -> x18, Pallas kernels: none -> 190 us  [launch(): pl.pallas_call(trimmed, out_shape=out_shape, grid_spec=pltpu.PrefetchScal...]
    dot_general x36 -> x0, matrix products: 179 us -> none  [the longest x2 39 us: forward_layer(): jnp.dot(normed_two, w_up, preferred_element_type=jnp.float32)]
    ppermute x0 -> x86, waiting for transfers between devices: none -> 116 us  [send(): return lax.ppermute(value, AXES, pairs)]
    ppermute x0 -> x86, starting transfers between devices: none -> 96.2 us  [send(): return lax.ppermute(value, AXES, pairs)]
    unnamed x322 -> x153, local copies, waits for them, and re-layouts: 114 us -> 22.5 us
  transfers between devices with their start and end apart: 3 -> 86, of which waited for: 3 -> 28; matrix products, arithmetic and copies ran while one was open for 3% -> 13% of each run, Pallas kernels for 0% -> 33%
where the time goes in v6:
time: 504 us; the launch traced here: 495 us
  Pallas kernels  190 us (38%)
  waiting for transfers between devices  116 us (23%)
  starting transfers between devices  96.2 us (19%)
  other arithmetic  53.3 us (11%)
  local copies, waits for them, and re-layouts  36.7 us (7%)
    pallas_call x18, Pallas kernels, launch(): pl.pallas_call(trimmed, out_shape=out_shape, grid_spec=pltpu.PrefetchScal...  190 us
    ppermute x86, waiting for transfers between devices, send(): return lax.ppermute(value, AXES, pairs)  116 us
    ppermute x86, starting transfers between devices, send(): return lax.ppermute(value, AXES, pairs)  96.2 us
    unnamed x153, local copies, waits for them, and re-layouts  22.5 us
    convert_element_type x6, other arithmetic, scatter_steps(): more, = (yield [(added([mine[upper], got[upper]]).astype(LOW), by(TO_YX))])  15.4 us
    another operation x12, other arithmetic  11.6 us
  transfers between devices with their start and end apart: 86, of which 28 were waited for; matrix products, arithmetic and copies ran while one was open for 13% of the time, Pallas kernels for 33%

profile of v6, /device:TPU:0, one launch (start us, length us, event | category | flops | bytes accessed | tf_op | source)
XLA Modules:
  0.0 494.6 jit_solution(2571114160067053531)
XLA Ops:
  5.7 3.0 collective-permute-start.2
  8.7 2.6 collective-permute-start.3
  12.8 2.2 collective-permute-done.2.refs_6_
  14.9 4.8 collective-permute-done.3.refs_7_
  21.4 7.3 %collective-permute-done.5.refs_9_ = bf16[192,1280]{1,0:T(8,128)(2,1)S(1)} collective-permute-done((bf16[192,1280]{1,0:T(8,128)(2,1)S(1)}, bf16[192,1280]{1,0:T(8,128)(2,1)S(1)}, u32[]{:S(2)}, u32[]{:S(2)}) %collective-permute-start.5) | collective-permute-done | bytes 491552 | tf_op jit(solution)/shard_map/ppermute | solution.py:876
  32.2 4.2 collective-permute-start.10
  37.0 4.7 collective-permute-done.10.refs_14_
  41.7 4.4 collective-permute-done.8.refs_12_
  46.2 7.7 %collective-permute-done.9.refs_13_ = bf16[48,1920]{1,0:T(8,128)(2,1)S(1)} collective-permute-done((bf16[48,1920]{1,0:T(8,128)(2,1)}, bf16[48,1920]{1,0:T(8,128)(2,1)S(1)}, u32[]{:S(2)}, u32[]{:S(2)}) %collective-permute-start.9) | collective-permute-done | bytes 184352 | tf_op jit(solution)/shard_map/ppermute | solution.py:876
  54.0 2.1 pad_maximum_fusion
  61.3 7.5 %qkv_forward.2 = (bf16[496,2304]{1,0:T(8,128)(2,1)}, bf16[496,768]{1,0:T(8,128)(2,1)}, f32[8,768]{1,0:T(8,128)}, f32[1,3072]{1,0:T(1,128)}) custom-call(s32[4]{0:T(128)} %pad_add_fusion.refs_0_, bf16[384,1280]{1,0:T(8,128)(2,1)} %copy-done.20, bf16[384,1280]{1,0:T(8,128)(2,1)} %copy-done.14, bf16[384,1280]{1,0:T(8,128)(2,1)} %copy-done.15, ...), custom_call_target="tpu_custom_call" | custom-call | flops 27426816 | bytes 108864 | tf_op jit(solution)/shard_map/qkv_forward/pallas_call | solution.py:49
  68.8 2.0 constant_dynamic-update-slice_fusion.5.refs_1_
  73.1 3.2 collective-permute-start.16
  77.6 9.7 %attention_forward.2 = (bf16[496,768]{1,0:T(8,128)(2,1)}, f32[496,128]{1,0:T(8,128)}) custom-call(s32[1]{0:T(128)S(6)} %copy.51.refs_0_, bf16[496,2304]{1,0:T(8,128)(2,1)} %get-tuple-element.177.refs_1_.refs_2_.refs_3_, bf16[496,2304]{1,0:T(8,128)(2,1)} %get-tuple-element.177.refs_1_.refs_2_.refs_3_, ...), custom_call_target="tpu_custom_call" | custom-call | flops 47235072 | bytes 47616 | tf_op jit(solution)/shard_map/attention_forward/pallas_call | solution.py:49
  87.3 3.1 collective-permute-done.13.refs_2_.refs_9_
  93.3 7.1 %collective-permute-done.19.refs_15_ = bf16[192,1536]{1,0:T(8,128)(2,1)S(1)} collective-permute-done((bf16[192,1536]{1,0:T(8,128)(2,1)S(1)}, bf16[192,1536]{1,0:T(8,128)(2,1)S(1)}, u32[]{:S(2)}, u32[]{:S(2)}) %collective-permute-start.19) | collective-permute-done | bytes 589856 | tf_op jit(solution)/shard_map/ppermute | solution.py:876
  104.8 1.9 collective-permute-start.23
  107.4 13.8 %up_forward.2 = (f32[496,768]{1,0:T(8,128)}, bf16[496,768]{1,0:T(8,128)(2,1)}, bf16[496,3072]{1,0:T(8,128)(2,1)}, bf16[496,3072]{1,0:T(8,128)(2,1)}) custom-call(s32[4]{0:T(128)} %pad_add_fusion.refs_0_, bf16[384,1920]{1,0:T(8,128)(2,1)} %constant_dynamic-update-slice_fusion.5.refs_1_, bf16[384,1920]{1,0:T(8,128)(2,1)} %copy-done.2, ...), custom_call_target="tpu_custom_call" | custom-call | flops 36569088 | bytes 168960 | tf_op jit(solution)/shard_map/up_forward/pallas_call | solution.py:49
  127.6 3.3 collective-permute-done.26.refs_14_
  135.3 3.4 collective-permute-start.31
  138.7 9.1 %down_forward.2.refs_5_.refs_8_ = f32[496,768]{1,0:T(8,128)} custom-call(s32[4]{0:T(128)} %pad_add_fusion.refs_0_, bf16[384,1536]{1,0:T(8,128)(2,1)} %constant_dynamic-update-slice_fusion.10.refs_1_.refs_5_, bf16[384,1536]{1,0:T(8,128)(2,1)} %copy-done.8, bf16[384,1536]{1,0:T(8,128)(2,1)} %copy-done.9, bf16[384,1536]{1,0:T(8,128)(2,1)} %copy-done.10, ...), custom_call_target="tpu_custom_call" | custom-call | flops 36569088 | bytes 121344 | tf_op jit(solution)/shard_map/down_forward/pallas_call | solution.py:49
  147.8 2.6 collective-permute-done.30.refs_9_
  158.2 7.5 %qkv_forward.3 = (bf16[496,2304]{1,0:T(8,128)(2,1)}, bf16[496,768]{1,0:T(8,128)(2,1)}, f32[8,768]{1,0:T(8,128)}, f32[1,3072]{1,0:T(1,128)}) custom-call(s32[4]{0:T(128)} %pad_add_fusion.refs_0_, bf16[384,1280]{1,0:T(8,128)(2,1)} %constant_dynamic-update-slice_fusion.15.refs_1_, bf16[384,1280]{1,0:T(8,128)(2,1)} %collective-permute-done.27.refs_2_.refs_6_, ...), custom_call_target="tpu_custom_call" | custom-call | flops 27426816 | bytes 108864 | tf_op jit(solution)/shard_map/qkv_forward/pallas_call | solution.py:49
  167.5 4.4 collective-permute-start.36
  174.3 9.7 %attention_forward.3 = (bf16[496,768]{1,0:T(8,128)(2,1)}, f32[496,128]{1,0:T(8,128)}) custom-call(s32[1]{0:T(128)S(6)} %copy.51.refs_0_, bf16[496,2304]{1,0:T(8,128)(2,1)} %get-tuple-element.214.refs_1_.refs_2_.refs_3_, bf16[496,2304]{1,0:T(8,128)(2,1)} %get-tuple-element.214.refs_1_.refs_2_.refs_3_, ...), custom_call_target="tpu_custom_call" | custom-call | flops 47235072 | bytes 47616 | tf_op jit(solution)/shard_map/attention_forward/pallas_call | solution.py:49
  184.1 2.2 collective-permute-done.34.refs_2_.refs_9_
  191.0 6.4 %collective-permute-done.40.refs_15_ = bf16[192,1536]{1,0:T(8,128)(2,1)S(1)} collective-permute-done((bf16[192,1536]{1,0:T(8,128)(2,1)S(1)}, bf16[192,1536]{1,0:T(8,128)(2,1)S(1)}, u32[]{:S(2)}, u32[]{:S(2)}) %collective-permute-start.40) | collective-permute-done | bytes 589856 | tf_op jit(solution)/shard_map/ppermute | solution.py:876
  199.3 13.8 %up_forward.3 = (f32[496,768]{1,0:T(8,128)}, bf16[496,768]{1,0:T(8,128)(2,1)}, bf16[496,3072]{1,0:T(8,128)(2,1)}, bf16[496,3072]{1,0:T(8,128)(2,1)}) custom-call(s32[4]{0:T(128)} %pad_add_fusion.refs_0_, bf16[384,1920]{1,0:T(8,128)(2,1)} %constant_dynamic-update-slice_fusion.20.refs_1_, bf16[384,1920]{1,0:T(8,128)(2,1)} %copy-done.5, ...), custom_call_target="tpu_custom_call" | custom-call | flops 36569088 | bytes 168960 | tf_op jit(solution)/shard_map/up_forward/pallas_call | solution.py:49
  214.9 2.8 collective-permute-done.43.refs_4_.refs_8_.refs_18_
  218.8 24.5 %mlp_backward.2 = (bf16[768,1920]{1,0:T(8,128)(2,1)}, bf16[768,1920]{1,0:T(8,128)(2,1)}, bf16[768,1536]{1,0:T(8,128)(2,1)}, bf16[768,1536]{1,0:T(8,128)(2,1)}, f...) custom-call(s32[4]{0:T(128)} %pad_add_fusion.refs_0_, ...), custom_call_target="tpu_custom_call" | custom-call | flops 146276352 | bytes 390144 | tf_op jit(solution)/shard_map/mlp_backward/pallas_call | solution.py:49
  243.9 7.5 %attention_backward.5.refs_6_ = bf16[496,1152]{1,0:T(8,128)(2,1)} custom-call(s32[1]{0:T(128)S(6)} %copy.51.refs_0_, bf16[496,2304]{1,0:T(8,128)(2,1)} %get-tuple-element.214.refs_1_.refs_2_.refs_3_, bf16[496,2304]{1,0:T(8,128)(2,1)} %get-tuple-element.214.refs_1_.refs_2_.refs_3_, bf16[496,2304]{1,0:T(8,128)(2,1)} %get-tuple-element.214.refs_1_.refs_2_.refs_3_, ...), custom_call_target="tpu_custom_call" | custom-call | flops 59043840 | bytes 47616 | tf_op jit(solution)/shard_map/attention_backward/pallas_call | solution.py:49
  251.4 7.4 %attention_backward.4.refs_5_ = bf16[496,1152]{1,0:T(8,128)(2,1)} custom-call(s32[1]{0:T(128)S(6)} %copy.51.refs_0_, bf16[496,2304]{1,0:T(8,128)(2,1)} %get-tuple-element.214.refs_1_.refs_2_.refs_3_, bf16[496,2304]{1,0:T(8,128)(2,1)} %get-tuple-element.214.refs_1_.refs_2_.refs_3_, bf16[496,2304]{1,0:T(8,128)(2,1)} %get-tuple-element.214.refs_1_.refs_2_.refs_3_, ...), custom_call_target="tpu_custom_call" | custom-call | flops 59043840 | bytes 47616 | tf_op jit(solution)/shard_map/attention_backward/pallas_call | solution.py:49
  258.8 4.0 add_convert_fusion.5
  263.7 13.4 %qkv_backward.2 = (f32[496,768]{1,0:T(8,128)}, bf16[768,1280]{1,0:T(8,128)(2,1)}, bf16[768,1280]{1,0:T(8,128)(2,1)}) custom-call(s32[4]{0:T(128)} %pad_add_fusion.refs_0_, bf16[384,1280]{1,0:T(8,128)(2,1)} %constant_dynamic-update-slice_fusion.15.refs_1_, bf16[384,1280]{1,0:T(8,128)(2,1)} %collective-permute-done.27.refs_2_.refs_6_, ...), custom_call_target="tpu_custom_call" | custom-call | flops 54853632 | bytes 205824 | tf_op jit(solution)/shard_map/qkv_backward/pallas_call | solution.py:49
  277.1 2.2 collective-permute-done.47.refs_16_
  279.3 3.3 add_convert_fusion.2
  286.0 5.0 %collective-permute-start.48 = (bf16[96,1536]{1,0:T(8,128)(2,1)}, bf16[96,1536]{1,0:T(8,128)(2,1)S(1)}, u32[]{:S(2)}, u32[]{:S(2)}) collective-permute-start(bf16[96,1536]{1,0:T(8,128)(2,1)} %get-tuple-element.326), channel_id=1, source_target_pairs={{0,24},{1,25},{2,26},{3,27},{4,28},{5,29},{6,30},{7,31},{8,0},{9,1... | collective-permute-start | bytes 884744 | tf_op jit(solution)/shard_map/ppermute | solution.py:876
  291.9 24.4 %mlp_backward.3 = (bf16[768,1920]{1,0:T(8,128)(2,1)}, bf16[768,1920]{1,0:T(8,128)(2,1)}, bf16[768,1536]{1,0:T(8,128)(2,1)}, bf16[768,1536]{1,0:T(8,128)(2,1)}, f...) custom-call(s32[4]{0:T(128)} %pad_add_fusion.refs_0_, ...), custom_call_target="tpu_custom_call" | custom-call | flops 146276352 | bytes 390144 | tf_op jit(solution)/shard_map/mlp_backward/pallas_call | solution.py:49
  316.3 2.0 collective-permute-done.49.refs_9_
  318.9 2.3 add_convert_fusion.1
  322.3 1.8 collective-permute-start.54
  324.1 2.4 add_convert_fusion.8
  330.5 5.3 %collective-permute-done.53.refs_15_ = bf16[48,1536]{1,0:T(8,128)(2,1)S(1)} collective-permute-done((bf16[48,1536]{1,0:T(8,128)(2,1)S(1)}, bf16[48,1536]{1,0:T(8,128)(2,1)S(1)}, u32[]{:S(2)}, u32[]{:S(2)}) %collective-permute-start.53) | collective-permute-done | bytes 147488 | tf_op jit(solution)/shard_map/ppermute | solution.py:876
  337.2 9.1 %down_forward.3 = f32[496,768]{1,0:T(8,128)} custom-call(s32[4]{0:T(128)} %pad_add_fusion.refs_0_, bf16[384,1536]{1,0:T(8,128)(2,1)} %constant_dynamic-update-slice_fusion.25.refs_1_.refs_5_, bf16[384,1536]{1,0:T(8,128)(2,1)} %copy-done.11, bf16[384,1536]{1,0:T(8,128)(2,1)} %copy-done.12, bf16[384,1536]{1,0:T(8,128)(2,1)} %copy-done.13, ...), custom_call_target="tpu_custom_call" | custom-call | flops 36569088 | bytes 121344 | tf_op jit(solution)/shard_map/down_forward/pallas_call | solution.py:49
  346.4 7.8 %attention_backward.7.refs_6_ = bf16[496,1152]{1,0:T(8,128)(2,1)} custom-call(s32[1]{0:T(128)S(6)} %copy.51.refs_0_, bf16[496,2304]{1,0:T(8,128)(2,1)} %get-tuple-element.177.refs_1_.refs_2_.refs_3_, bf16[496,2304]{1,0:T(8,128)(2,1)} %get-tuple-element.177.refs_1_.refs_2_.refs_3_, bf16[496,2304]{1,0:T(8,128)(2,1)} %get-tuple-element.177.refs_1_.refs_2_.refs_3_, ...), custom_call_target="tpu_custom_call" | custom-call | flops 59043840 | bytes 47616 | tf_op jit(solution)/shard_map/attention_backward/pallas_call | solution.py:49
  354.1 7.4 %attention_backward.6.refs_5_ = bf16[496,1152]{1,0:T(8,128)(2,1)} custom-call(s32[1]{0:T(128)S(6)} %copy.51.refs_0_, bf16[496,2304]{1,0:T(8,128)(2,1)} %get-tuple-element.177.refs_1_.refs_2_.refs_3_, bf16[496,2304]{1,0:T(8,128)(2,1)} %get-tuple-element.177.refs_1_.refs_2_.refs_3_, bf16[496,2304]{1,0:T(8,128)(2,1)} %get-tuple-element.177.refs_1_.refs_2_.refs_3_, ...), custom_call_target="tpu_custom_call" | custom-call | flops 59043840 | bytes 47616 | tf_op jit(solution)/shard_map/attention_backward/pallas_call | solution.py:49
  364.8 2.1 add_convert_fusion.15
  368.3 2.6 add_convert_fusion.3
  373.9 2.6 collective-permute-start.68
  377.4 2.9 add_convert_fusion
  380.3 13.2 %qkv_backward.3 = (f32[496,768]{1,0:T(8,128)}, bf16[768,1280]{1,0:T(8,128)(2,1)}, bf16[768,1280]{1,0:T(8,128)(2,1)}) custom-call(s32[4]{0:T(128)} %pad_add_fusion.refs_0_, bf16[384,1280]{1,0:T(8,128)(2,1)} %copy-done.20, bf16[384,1280]{1,0:T(8,128)(2,1)} %copy-done.14, bf16[384,1280]{1,0:T(8,128)(2,1)} %copy-done.15, bf16[384,1280]{1,0:T(8,128)(2,1)} %copy-done.16, ...), custom_call_target="tpu_custom_call" | custom-call | flops 54853632 | bytes 205824 | tf_op jit(solution)/shard_map/qkv_backward/pallas_call | solution.py:49
  397.5 5.6 %collective-permute-done.70 = bf16[96,1280]{1,0:T(8,128)(2,1)S(1)} collective-permute-done((bf16[96,1280]{1,0:T(8,128)(2,1)S(1)}, bf16[96,1280]{1,0:T(8,128)(2,1)S(1)}, u32[]{:S(2)}, u32[]{:S(2)}) %collective-permute-start.70) | collective-permute-done | bytes 245792 | tf_op jit(solution)/shard_map/ppermute | solution.py:876
  405.9 4.7 collective-permute-done.71
  416.2 7.1 %collective-permute-done.79 = bf16[192,1536]{1,0:T(8,128)(2,1)S(1)} collective-permute-done((bf16[192,1536]{1,0:T(8,128)(2,1)S(1)}, bf16[192,1536]{1,0:T(8,128)(2,1)S(1)}, u32[]{:S(2)}, u32[]{:S(2)}) %collective-permute-start.79) | collective-permute-done | bytes 589856 | tf_op jit(solution)/shard_map/ppermute | solution.py:876
  424.9 1.9 collective-permute-start.80
  428.9 2.3 collective-permute-done.80
  432.6 8.1 %collective-permute-done.81 = bf16[48,1536]{1,0:T(8,128)(2,1)S(1)} collective-permute-done((bf16[48,1536]{1,0:T(8,128)(2,1)S(1)}, bf16[48,1536]{1,0:T(8,128)(2,1)S(1)}, u32[]{:S(2)}, u32[]{:S(2)}) %collective-permute-start.81) | collective-permute-done | bytes 147488 | tf_op jit(solution)/shard_map/ppermute | solution.py:876
  445.7 3.3 collective-permute-start.75
  449.0 6.9 %collective-permute-start.76 = (bf16[48,1920]{1,0:T(8,128)(2,1)S(1)}, bf16[48,1920]{1,0:T(8,128)(2,1)S(1)}, u32[]{:S(2)}, u32[]{:S(2)}) collective-permute-start(bf16[48,1920]{1,0:T(8,128)(2,1)S(1)} %get-tuple-element.344), channel_id=1, source_target_pairs={{0,16},{1,17},{2,18},{3,19},{4,20},{5,21},{6,22},{7,23},{8,24},{9,... | collective-permute-start | bytes 552968 | tf_op jit(solution)/shard_map/ppermute | solution.py:876
  457.3 3.0 collective-permute-start.77
  461.1 10.8 %collective-permute-done.76 = bf16[48,1920]{1,0:T(8,128)(2,1)S(1)} collective-permute-done((bf16[48,1920]{1,0:T(8,128)(2,1)S(1)}, bf16[48,1920]{1,0:T(8,128)(2,1)S(1)}, u32[]{:S(2)}, u32[]{:S(2)}) %collective-permute-start.76) | collective-permute-done | bytes 184352 | tf_op jit(solution)/shard_map/ppermute | solution.py:876
  474.2 6.8 %collective-permute-start.65 = (bf16[48,1280]{1,0:T(8,128)(2,1)}, bf16[48,1280]{1,0:T(8,128)(2,1)}, u32[]{:S(2)}, u32[]{:S(2)}) collective-permute-start(bf16[48,1280]{1,0:T(8,128)(2,1)} %get-tuple-element.350), channel_id=1, source_target_pairs={{0,16},{1,17},{2,18},{3,19},{4,20},{5,21},{6,22},{7,23},{8,24},{9,... | collective-permute-start | bytes 368648 | tf_op jit(solution)/shard_map/ppermute | solution.py:876
  482.3 2.4 finish_mlp.1
  485.1 4.3 collective-permute-done.65
  (369 shorter events, 114.8 us)
Async XLA Ops:
  8.7 11.0 %collective-permute-start.3 = (bf16[48,1280]{1,0:T(8,128)(2,1)S(1)}, bf16[48,1280]{1,0:T(8,128)(2,1)S(1)}, u32[]{:S(2)}, u32[]{:S(2)}) collective-permute-start(bf16[48,1280]{1,0:T(8,128)(2,1)S(1)} %get-tuple-element.320), channel_id=1, source_target_pairs={{0,16},{1,17},{2,18},{3,19},{4,20},{5,21},{6,22},{7,23},{8,24},{9,... | collective-permute-start | bytes 368648 | tf_op jit(solution)/shard_map/ppermute | solution.py:876
  12.7 17.6 %collective-permute-start = (bf16[24,8192]{1,0:T(8,128)(2,1)S(1)}, bf16[24,8192]{1,0:T(8,128)(2,1)S(1)}, u32[]{:S(2)}, u32[]{:S(2)}) collective-permute-start(bf16[24,8192]{1,0:T(8,128)(2,1)S(1)} %get-tuple-element.341), channel_id=1, source_target_pairs={{0,1},{1,0},{2,3},{3,2},{4,5},{5,4},{6,7},{7,6},{8,9},{9,8},{10,11... | collective-permute-start | bytes 1179656 | tf_op jit(solution)/shard_map/ppermute | solution.py:876
  28.7 25.1 %collective-permute-start.6 = (bf16[384,1280]{1,0:T(8,128)(2,1)S(1)}, bf16[384,1280]{1,0:T(8,128)(2,1)S(1)}, u32[]{:S(2)}, u32[]{:S(2)}) collective-permute-start(bf16[384,1280]{1,0:T(8,128)(2,1)S(1)} %constant_dynamic-update-slice_fusion.refs_1_), channel_id=1, source_target_pairs={{0,2},{1,5},{2,0},{3,7},{4,6},{5,1},{6,4},{7,3},{8,10},{9,13},{10,... | collective-permute-start | bytes 2949128 | tf_op jit(solution)/shard_map/ppermute | solution.py:876
  30.3 23.6 %collective-permute-start.7 = (bf16[384,1280]{1,0:T(8,128)(2,1)S(1)}, bf16[384,1280]{1,0:T(8,128)(2,1)S(1)}, u32[]{:S(2)}, u32[]{:S(2)}) collective-permute-start(bf16[384,1280]{1,0:T(8,128)(2,1)S(1)} %constant_dynamic-update-slice_fusion.refs_1_), channel_id=1, source_target_pairs={{0,1},{1,0},{2,3},{3,2},{4,5},{5,4},{6,7},{7,6},{8,9},{9,8},{10,11... | collective-permute-start | bytes 2949128 | tf_op jit(solution)/shard_map/ppermute | solution.py:876
  36.4 17.5 %collective-permute-start.9 = (bf16[48,1920]{1,0:T(8,128)(2,1)}, bf16[48,1920]{1,0:T(8,128)(2,1)S(1)}, u32[]{:S(2)}, u32[]{:S(2)}) collective-permute-start(bf16[48,1920]{1,0:T(8,128)(2,1)} %get-tuple-element.337), channel_id=1, source_target_pairs={{0,16},{1,17},{2,18},{3,19},{4,20},{5,21},{6,22},{7,23},{8,24},{9,... | collective-permute-start | bytes 552968 | tf_op jit(solution)/shard_map/ppermute | solution.py:876
  56.1 12.7 %collective-permute-start.11 = (bf16[192,1920]{1,0:T(8,128)(2,1)}, bf16[192,1920]{1,0:T(8,128)(2,1)}, u32[]{:S(2)}, u32[]{:S(2)}) collective-permute-start(bf16[192,1920]{1,0:T(8,128)(2,1)} %pad_maximum_fusion), channel_id=1, source_target_pairs={{0,4},{1,3},{2,6},{3,1},{4,0},{5,7},{6,2},{7,5},{8,12},{9,11},{10,... | collective-permute-start | bytes 2211848 | tf_op jit(solution)/shard_map/ppermute | solution.py:876
  70.8 19.6 %collective-permute-start.13 = (bf16[384,1920]{1,0:T(8,128)(2,1)}, bf16[384,1920]{1,0:T(8,128)(2,1)S(1)}, u32[]{:S(2)}, u32[]{:S(2)}) collective-permute-start(bf16[384,1920]{1,0:T(8,128)(2,1)} %constant_dynamic-update-slice_fusion.5.refs_1_), channel_id=1, source_target_pairs={{0,2},{1,5},{2,0},{3,7},{4,6},{5,1},{6,4},{7,3},{8,10},{9,13},{10,... | collective-permute-start | bytes 4423688 | tf_op jit(solution)/shard_map/ppermute | solution.py:876
  71.3 19.1 %collective-permute-start.14 = (bf16[384,1920]{1,0:T(8,128)(2,1)}, bf16[384,1920]{1,0:T(8,128)(2,1)S(1)}, u32[]{:S(2)}, u32[]{:S(2)}) collective-permute-start(bf16[384,1920]{1,0:T(8,128)(2,1)} %constant_dynamic-update-slice_fusion.5.refs_1_), channel_id=1, source_target_pairs={{0,1},{1,0},{2,3},{3,2},{4,5},{5,4},{6,7},{7,6},{8,9},{9,8},{10,11... | collective-permute-start | bytes 4423688 | tf_op jit(solution)/shard_map/ppermute | solution.py:876
  73.1 14.2 %collective-permute-start.15 = (bf16[48,1536]{1,0:T(8,128)(2,1)S(1)}, bf16[48,1536]{1,0:T(8,128)(2,1)S(1)}, u32[]{:S(2)}, u32[]{:S(2)}) collective-permute-start(bf16[48,1536]{1,0:T(8,128)(2,1)S(1)} %get-tuple-element.333), channel_id=1, source_target_pairs={{0,8},{1,9},{2,10},{3,11},{4,12},{5,13},{6,14},{7,15},{8,16},{9,17... | collective-permute-start | bytes 442376 | tf_op jit(solution)/shard_map/ppermute | solution.py:876
  73.1 14.2 %collective-permute-start.16 = (bf16[48,1536]{1,0:T(8,128)(2,1)S(1)}, bf16[48,1536]{1,0:T(8,128)(2,1)S(1)}, u32[]{:S(2)}, u32[]{:S(2)}) collective-permute-start(bf16[48,1536]{1,0:T(8,128)(2,1)S(1)} %get-tuple-element.333), channel_id=1, source_target_pairs={{0,16},{1,17},{2,18},{3,19},{4,20},{5,21},{6,22},{7,23},{8,24},{9,... | collective-permute-start | bytes 442376 | tf_op jit(solution)/shard_map/ppermute | solution.py:876
  76.3 11.0 %collective-permute-start.17 = (bf16[48,1536]{1,0:T(8,128)(2,1)S(1)}, bf16[48,1536]{1,0:T(8,128)(2,1)S(1)}, u32[]{:S(2)}, u32[]{:S(2)}) collective-permute-start(bf16[48,1536]{1,0:T(8,128)(2,1)S(1)} %get-tuple-element.333), channel_id=1, source_target_pairs={{0,24},{1,25},{2,26},{3,27},{4,28},{5,29},{6,30},{7,31},{8,0},{9,1... | collective-permute-start | bytes 442376 | tf_op jit(solution)/shard_map/ppermute | solution.py:876
  90.4 10.1 %collective-permute-start.18 = (bf16[384,1920]{1,0:T(8,128)(2,1)S(1)}, bf16[384,1920]{1,0:T(8,128)(2,1)S(1)}, u32[]{:S(2)}, u32[]{:S(2)}) collective-permute-start(bf16[384,1920]{1,0:T(8,128)(2,1)S(1)} %collective-permute-done.13.refs_2_.refs_9_), channel_id=1, source_target_pairs={{0,1},{1,0},{2,3},{3,2},{4,5},{5,4},{6,7},{7,6},{8,9},{9,8},{10,11... | collective-permute-start | bytes 4423688 | tf_op jit(solution)/shard_map/ppermute | solution.py:876
  101.5 19.8 %collective-permute-start.20 = (bf16[384,1536]{1,0:T(8,128)(2,1)}, bf16[384,1536]{1,0:T(8,128)(2,1)S(1)}, u32[]{:S(2)}, u32[]{:S(2)}) collective-permute-start(bf16[384,1536]{1,0:T(8,128)(2,1)} %constant_dynamic-update-slice_fusion.10.refs_1_.refs_5_), channel_id=1, source_target_pairs={{0,2},{1,5},{2,0},{3,7},{4,6},{5,1},{6,4},{7,3},{8,10},{9,13},{10,... | collective-permute-start | bytes 3538952 | tf_op jit(solution)/shard_map/ppermute | solution.py:876
  102.0 19.3 %collective-permute-start.21 = (bf16[384,1536]{1,0:T(8,128)(2,1)}, bf16[384,1536]{1,0:T(8,128)(2,1)S(1)}, u32[]{:S(2)}, u32[]{:S(2)}) collective-permute-start(bf16[384,1536]{1,0:T(8,128)(2,1)} %constant_dynamic-update-slice_fusion.10.refs_1_.refs_5_), channel_id=1, source_target_pairs={{0,1},{1,0},{2,3},{3,2},{4,5},{5,4},{6,7},{7,6},{8,9},{9,8},{10,11... | collective-permute-start | bytes 3538952 | tf_op jit(solution)/shard_map/ppermute | solution.py:876
  103.5 17.6 %collective-permute-start.22 = (bf16[48,1280]{1,0:T(8,128)(2,1)S(1)}, bf16[48,1280]{1,0:T(8,128)(2,1)S(1)}, u32[]{:S(2)}, u32[]{:S(2)}) collective-permute-start(bf16[48,1280]{1,0:T(8,128)(2,1)S(1)} %get-tuple-element.338), channel_id=1, source_target_pairs={{0,8},{1,9},{2,10},{3,11},{4,12},{5,13},{6,14},{7,15},{8,16},{9,17... | collective-permute-start | bytes 368648 | tf_op jit(solution)/shard_map/ppermute | solution.py:876
  104.8 16.4 %collective-permute-start.23 = (bf16[48,1280]{1,0:T(8,128)(2,1)S(1)}, bf16[48,1280]{1,0:T(8,128)(2,1)S(1)}, u32[]{:S(2)}, u32[]{:S(2)}) collective-permute-start(bf16[48,1280]{1,0:T(8,128)(2,1)S(1)} %get-tuple-element.338), channel_id=1, source_target_pairs={{0,16},{1,17},{2,18},{3,19},{4,20},{5,21},{6,22},{7,23},{8,24},{9,... | collective-permute-start | bytes 368648 | tf_op jit(solution)/shard_map/ppermute | solution.py:876
  106.8 14.5 %collective-permute-start.24 = (bf16[48,1280]{1,0:T(8,128)(2,1)S(1)}, bf16[48,1280]{1,0:T(8,128)(2,1)S(1)}, u32[]{:S(2)}, u32[]{:S(2)}) collective-permute-start(bf16[48,1280]{1,0:T(8,128)(2,1)S(1)} %get-tuple-element.338), channel_id=1, source_target_pairs={{0,24},{1,25},{2,26},{3,27},{4,28},{5,29},{6,30},{7,31},{8,0},{9,1... | collective-permute-start | bytes 368648 | tf_op jit(solution)/shard_map/ppermute | solution.py:876
  131.7 18.7 %collective-permute-start.27 = (bf16[384,1280]{1,0:T(8,128)(2,1)}, bf16[384,1280]{1,0:T(8,128)(2,1)}, u32[]{:S(2)}, u32[]{:S(2)}) collective-permute-start(bf16[384,1280]{1,0:T(8,128)(2,1)} %constant_dynamic-update-slice_fusion.15.refs_1_), channel_id=1, source_target_pairs={{0,2},{1,5},{2,0},{3,7},{4,6},{5,1},{6,4},{7,3},{8,10},{9,13},{10,... | collective-permute-start | bytes 2949128 | tf_op jit(solution)/shard_map/ppermute | solution.py:876
  133.3 17.2 %collective-permute-start.28 = (bf16[384,1280]{1,0:T(8,128)(2,1)}, bf16[384,1280]{1,0:T(8,128)(2,1)}, u32[]{:S(2)}, u32[]{:S(2)}) collective-permute-start(bf16[384,1280]{1,0:T(8,128)(2,1)} %constant_dynamic-update-slice_fusion.15.refs_1_), channel_id=1, source_target_pairs={{0,1},{1,0},{2,3},{3,2},{4,5},{5,4},{6,7},{7,6},{8,9},{9,8},{10,11... | collective-permute-start | bytes 2949128 | tf_op jit(solution)/shard_map/ppermute | solution.py:876
  133.3 14.6 %collective-permute-start.29 = (bf16[48,1920]{1,0:T(8,128)(2,1)}, bf16[48,1920]{1,0:T(8,128)(2,1)}, u32[]{:S(2)}, u32[]{:S(2)}) collective-permute-start(bf16[48,1920]{1,0:T(8,128)(2,1)} %get-tuple-element.334), channel_id=1, source_target_pairs={{0,8},{1,9},{2,10},{3,11},{4,12},{5,13},{6,14},{7,15},{8,16},{9,17... | collective-permute-start | bytes 552968 | tf_op jit(solution)/shard_map/ppermute | solution.py:876
  134.7 15.8 %collective-permute-start.30 = (bf16[48,1920]{1,0:T(8,128)(2,1)}, bf16[48,1920]{1,0:T(8,128)(2,1)}, u32[]{:S(2)}, u32[]{:S(2)}) collective-permute-start(bf16[48,1920]{1,0:T(8,128)(2,1)} %get-tuple-element.334), channel_id=1, source_target_pairs={{0,16},{1,17},{2,18},{3,19},{4,20},{5,21},{6,22},{7,23},{8,24},{9,... | collective-permute-start | bytes 552968 | tf_op jit(solution)/shard_map/ppermute | solution.py:876
  135.3 15.2 %collective-permute-start.31 = (bf16[48,1920]{1,0:T(8,128)(2,1)}, bf16[48,1920]{1,0:T(8,128)(2,1)}, u32[]{:S(2)}, u32[]{:S(2)}) collective-permute-start(bf16[48,1920]{1,0:T(8,128)(2,1)} %get-tuple-element.334), channel_id=1, source_target_pairs={{0,24},{1,25},{2,26},{3,27},{4,28},{5,29},{6,30},{7,31},{8,0},{9,1... | collective-permute-start | bytes 552968 | tf_op jit(solution)/shard_map/ppermute | solution.py:876
  151.8 13.9 %collective-permute-start.32 = (bf16[192,1920]{1,0:T(8,128)(2,1)S(1)}, bf16[192,1920]{1,0:T(8,128)(2,1)S(1)}, u32[]{:S(2)}, u32[]{:S(2)}) collective-permute-start(bf16[192,1920]{1,0:T(8,128)(2,1)S(1)} %pad_maximum_fusion.1), channel_id=1, source_target_pairs={{0,4},{1,3},{2,6},{3,1},{4,0},{5,7},{6,2},{7,5},{8,12},{9,11},{10,... | collective-permute-start | bytes 2211848 | tf_op jit(solution)/shard_map/ppermute | solution.py:876
  166.7 19.6 %collective-permute-start.34 = (bf16[384,1920]{1,0:T(8,128)(2,1)}, bf16[384,1920]{1,0:T(8,128)(2,1)S(1)}, u32[]{:S(2)}, u32[]{:S(2)}) collective-permute-start(bf16[384,1920]{1,0:T(8,128)(2,1)} %constant_dynamic-update-slice_fusion.20.refs_1_), channel_id=1, source_target_pairs={{0,2},{1,5},{2,0},{3,7},{4,6},{5,1},{6,4},{7,3},{8,10},{9,13},{10,... | collective-permute-start | bytes 4423688 | tf_op jit(solution)/shard_map/ppermute | solution.py:876
  167.5 18.8 %collective-permute-start.35 = (bf16[384,1920]{1,0:T(8,128)(2,1)}, bf16[384,1920]{1,0:T(8,128)(2,1)S(1)}, u32[]{:S(2)}, u32[]{:S(2)}) collective-permute-start(bf16[384,1920]{1,0:T(8,128)(2,1)} %constant_dynamic-update-slice_fusion.20.refs_1_), channel_id=1, source_target_pairs={{0,1},{1,0},{2,3},{3,2},{4,5},{5,4},{6,7},{7,6},{8,9},{9,8},{10,11... | collective-permute-start | bytes 4423688 | tf_op jit(solution)/shard_map/ppermute | solution.py:876
  167.5 16.5 %collective-permute-start.36 = (bf16[48,1536]{1,0:T(8,128)(2,1)}, bf16[48,1536]{1,0:T(8,128)(2,1)S(1)}, u32[]{:S(2)}, u32[]{:S(2)}) collective-permute-start(bf16[48,1536]{1,0:T(8,128)(2,1)} %get-tuple-element.330), channel_id=1, source_target_pairs={{0,8},{1,9},{2,10},{3,11},{4,12},{5,13},{6,14},{7,15},{8,16},{9,17... | collective-permute-start | bytes 442376 | tf_op jit(solution)/shard_map/ppermute | solution.py:876
  171.9 12.1 %collective-permute-start.37 = (bf16[48,1536]{1,0:T(8,128)(2,1)}, bf16[48,1536]{1,0:T(8,128)(2,1)S(1)}, u32[]{:S(2)}, u32[]{:S(2)}) collective-permute-start(bf16[48,1536]{1,0:T(8,128)(2,1)} %get-tuple-element.330), channel_id=1, source_target_pairs={{0,16},{1,17},{2,18},{3,19},{4,20},{5,21},{6,22},{7,23},{8,24},{9,... | collective-permute-start | bytes 442376 | tf_op jit(solution)/shard_map/ppermute | solution.py:876
  173.1 11.0 %collective-permute-start.38 = (bf16[48,1536]{1,0:T(8,128)(2,1)}, bf16[48,1536]{1,0:T(8,128)(2,1)S(1)}, u32[]{:S(2)}, u32[]{:S(2)}) collective-permute-start(bf16[48,1536]{1,0:T(8,128)(2,1)} %get-tuple-element.330), channel_id=1, source_target_pairs={{0,24},{1,25},{2,26},{3,27},{4,28},{5,29},{6,30},{7,31},{8,0},{9,1... | collective-permute-start | bytes 442376 | tf_op jit(solution)/shard_map/ppermute | solution.py:876
  186.3 11.2 %collective-permute-start.39 = (bf16[384,1920]{1,0:T(8,128)(2,1)S(1)}, bf16[384,1920]{1,0:T(8,128)(2,1)S(1)}, u32[]{:S(2)}, u32[]{:S(2)}) collective-permute-start(bf16[384,1920]{1,0:T(8,128)(2,1)S(1)} %collective-permute-done.34.refs_2_.refs_9_), channel_id=1, source_target_pairs={{0,1},{1,0},{2,3},{3,2},{4,5},{5,4},{6,7},{7,6},{8,9},{9,8},{10,11... | collective-permute-start | bytes 4423688 | tf_op jit(solution)/shard_map/ppermute | solution.py:876
  198.5 16.4 %collective-permute-start.41 = (bf16[384,1536]{1,0:T(8,128)(2,1)}, bf16[384,1536]{1,0:T(8,128)(2,1)S(1)}, u32[]{:S(2)}, u32[]{:S(2)}) collective-permute-start(bf16[384,1536]{1,0:T(8,128)(2,1)} %constant_dynamic-update-slice_fusion.25.refs_1_.refs_5_), channel_id=1, source_target_pairs={{0,2},{1,5},{2,0},{3,7},{4,6},{5,1},{6,4},{7,3},{8,10},{9,13},{10,... | collective-permute-start | bytes 3538952 | tf_op jit(solution)/shard_map/ppermute | solution.py:876
  199.3 15.6 %collective-permute-start.42 = (bf16[384,1536]{1,0:T(8,128)(2,1)}, bf16[384,1536]{1,0:T(8,128)(2,1)S(1)}, u32[]{:S(2)}, u32[]{:S(2)}) collective-permute-start(bf16[384,1536]{1,0:T(8,128)(2,1)} %constant_dynamic-update-slice_fusion.25.refs_1_.refs_5_), channel_id=1, source_target_pairs={{0,1},{1,0},{2,3},{3,2},{4,5},{5,4},{6,7},{7,6},{8,9},{9,8},{10,11... | collective-permute-start | bytes 3538952 | tf_op jit(solution)/shard_map/ppermute | solution.py:876
  243.3 15.5 %collective-permute-start.45 = (bf16[768,1920]{1,0:T(8,128)(2,1)}, bf16[768,1920]{1,0:T(8,128)(2,1)S(1)}, u32[]{:S(2)}, u32[]{:S(2)}) collective-permute-start(bf16[768,1920]{1,0:T(8,128)(2,1)} %get-tuple-element.248), channel_id=1, source_target_pairs={{0,1},{1,0},{2,3},{3,2},{4,5},{5,4},{6,7},{7,6},{8,9},{9,8},{10,11... | collective-permute-start | bytes 8847368 | tf_op jit(solution)/shard_map/ppermute | solution.py:876
  243.5 15.3 %collective-permute-start.44 = (bf16[768,1536]{1,0:T(8,128)(2,1)}, bf16[768,1536]{1,0:T(8,128)(2,1)}, u32[]{:S(2)}, u32[]{:S(2)}) collective-permute-start(bf16[768,1536]{1,0:T(8,128)(2,1)} %get-tuple-element.247), channel_id=1, source_target_pairs={{0,1},{1,0},{2,3},{3,2},{4,5},{5,4},{6,7},{7,6},{8,9},{9,8},{10,11... | collective-permute-start | bytes 7077896 | tf_op jit(solution)/shard_map/ppermute | solution.py:876
  262.9 16.4 %collective-permute-start.47 = (bf16[384,1536]{1,0:T(8,128)(2,1)}, bf16[384,1536]{1,0:T(8,128)(2,1)S(1)}, u32[]{:S(2)}, u32[]{:S(2)}) collective-permute-start(bf16[384,1536]{1,0:T(8,128)(2,1)} %add_convert_fusion.5), channel_id=1, source_target_pairs={{0,2},{1,5},{2,0},{3,7},{4,6},{5,1},{6,4},{7,3},{8,10},{9,13},{10,... | collective-permute-start | bytes 3538952 | tf_op jit(solution)/shard_map/ppermute | solution.py:876
  279.3 39.1 %collective-permute-start.51 = (bf16[768,1280]{1,0:T(8,128)(2,1)}, bf16[768,1280]{1,0:T(8,128)(2,1)}, u32[]{:S(2)}, u32[]{:S(2)}) collective-permute-start(bf16[768,1280]{1,0:T(8,128)(2,1)} %get-tuple-element.265), channel_id=1, source_target_pairs={{0,1},{1,0},{2,3},{3,2},{4,5},{5,4},{6,7},{7,6},{8,9},{9,8},{10,11... | collective-permute-start | bytes 5898248 | tf_op jit(solution)/shard_map/ppermute | solution.py:876
  282.6 35.8 %collective-permute-start.46 = (bf16[384,1920]{1,0:T(8,128)(2,1)}, bf16[384,1920]{1,0:T(8,128)(2,1)}, u32[]{:S(2)}, u32[]{:S(2)}) collective-permute-start(bf16[384,1920]{1,0:T(8,128)(2,1)} %add_convert_fusion.2), channel_id=1, source_target_pairs={{0,2},{1,5},{2,0},{3,7},{4,6},{5,1},{6,4},{7,3},{8,10},{9,13},{10,... | collective-permute-start | bytes 4423688 | tf_op jit(solution)/shard_map/ppermute | solution.py:876
  286.0 30.3 %collective-permute-start.48 = (bf16[96,1536]{1,0:T(8,128)(2,1)}, bf16[96,1536]{1,0:T(8,128)(2,1)S(1)}, u32[]{:S(2)}, u32[]{:S(2)}) collective-permute-start(bf16[96,1536]{1,0:T(8,128)(2,1)} %get-tuple-element.326), channel_id=1, source_target_pairs={{0,24},{1,25},{2,26},{3,27},{4,28},{5,29},{6,30},{7,31},{8,0},{9,1... | collective-permute-start | bytes 884744 | tf_op jit(solution)/shard_map/ppermute | solution.py:876
  291.0 27.4 %collective-permute-start.49 = (bf16[96,1536]{1,0:T(8,128)(2,1)}, bf16[96,1536]{1,0:T(8,128)(2,1)S(1)}, u32[]{:S(2)}, u32[]{:S(2)}) collective-permute-start(bf16[96,1536]{1,0:T(8,128)(2,1)} %get-tuple-element.325), channel_id=1, source_target_pairs={{0,16},{1,17},{2,18},{3,19},{4,20},{5,21},{6,22},{7,23},{8,24},{9,... | collective-permute-start | bytes 884744 | tf_op jit(solution)/shard_map/ppermute | solution.py:876
  291.9 26.5 %collective-permute-start.50 = (bf16[96,1536]{1,0:T(8,128)(2,1)S(1)}, bf16[96,1536]{1,0:T(8,128)(2,1)S(1)}, u32[]{:S(2)}, u32[]{:S(2)}) collective-permute-start(bf16[96,1536]{1,0:T(8,128)(2,1)S(1)} %get-tuple-element.324), channel_id=1, source_target_pairs={{0,8},{1,9},{2,10},{3,11},{4,12},{5,13},{6,14},{7,15},{8,16},{9,17... | collective-permute-start | bytes 884744 | tf_op jit(solution)/shard_map/ppermute | solution.py:876
  318.4 43.3 %collective-permute-start.58 = (bf16[768,1920]{1,0:T(8,128)(2,1)}, bf16[768,1920]{1,0:T(8,128)(2,1)}, u32[]{:S(2)}, u32[]{:S(2)}) collective-permute-start(bf16[768,1920]{1,0:T(8,128)(2,1)} %get-tuple-element.286), channel_id=1, source_target_pairs={{0,1},{1,0},{2,3},{3,2},{4,5},{5,4},{6,7},{7,6},{8,9},{9,8},{10,11... | collective-permute-start | bytes 8847368 | tf_op jit(solution)/shard_map/ppermute | solution.py:876
  318.4 43.2 %collective-permute-start.57 = (bf16[768,1536]{1,0:T(8,128)(2,1)}, bf16[768,1536]{1,0:T(8,128)(2,1)}, u32[]{:S(2)}, u32[]{:S(2)}) collective-permute-start(bf16[768,1536]{1,0:T(8,128)(2,1)} %get-tuple-element.285), channel_id=1, source_target_pairs={{0,1},{1,0},{2,3},{3,2},{4,5},{5,4},{6,7},{7,6},{8,9},{9,8},{10,11... | collective-permute-start | bytes 7077896 | tf_op jit(solution)/shard_map/ppermute | solution.py:876
  322.3 13.7 %collective-permute-start.54 = (bf16[96,1920]{1,0:T(8,128)(2,1)S(1)}, bf16[96,1920]{1,0:T(8,128)(2,1)}, u32[]{:S(2)}, u32[]{:S(2)}) collective-permute-start(bf16[96,1920]{1,0:T(8,128)(2,1)S(1)} %get-tuple-element.323), channel_id=1, source_target_pairs={{0,24},{1,25},{2,26},{3,27},{4,28},{5,29},{6,30},{7,31},{8,0},{9,1... | collective-permute-start | bytes 1105928 | tf_op jit(solution)/shard_map/ppermute | solution.py:876
  326.5 35.1 %collective-permute-start.52 = (bf16[384,1280]{1,0:T(8,128)(2,1)}, bf16[384,1280]{1,0:T(8,128)(2,1)S(1)}, u32[]{:S(2)}, u32[]{:S(2)}) collective-permute-start(bf16[384,1280]{1,0:T(8,128)(2,1)} %add_convert_fusion.8), channel_id=1, source_target_pairs={{0,2},{1,5},{2,0},{3,7},{4,6},{5,1},{6,4},{7,3},{8,10},{9,13},{10,... | collective-permute-start | bytes 2949128 | tf_op jit(solution)/shard_map/ppermute | solution.py:876
  335.8 25.8 %collective-permute-start.55 = (bf16[96,1920]{1,0:T(8,128)(2,1)}, bf16[96,1920]{1,0:T(8,128)(2,1)}, u32[]{:S(2)}, u32[]{:S(2)}) collective-permute-start(bf16[96,1920]{1,0:T(8,128)(2,1)} %get-tuple-element.322), channel_id=1, source_target_pairs={{0,16},{1,17},{2,18},{3,19},{4,20},{5,21},{6,22},{7,23},{8,24},{9,... | collective-permute-start | bytes 1105928 | tf_op jit(solution)/shard_map/ppermute | solution.py:876
  336.0 25.6 %collective-permute-start.56 = (bf16[96,1920]{1,0:T(8,128)(2,1)}, bf16[96,1920]{1,0:T(8,128)(2,1)}, u32[]{:S(2)}, u32[]{:S(2)}) collective-permute-start(bf16[96,1920]{1,0:T(8,128)(2,1)} %get-tuple-element.321), channel_id=1, source_target_pairs={{0,8},{1,9},{2,10},{3,11},{4,12},{5,13},{6,14},{7,15},{8,16},{9,17... | collective-permute-start | bytes 1105928 | tf_op jit(solution)/shard_map/ppermute | solution.py:876
  366.8 26.7 %collective-permute-start.84 = (bf16[48,1920]{1,0:T(8,128)(2,1)}, bf16[48,1920]{1,0:T(8,128)(2,1)S(1)}, u32[]{:S(2)}, u32[]{:S(2)}) collective-permute-start(bf16[48,1920]{1,0:T(8,128)(2,1)} %add_convert_fusion.15), channel_id=1, source_target_pairs={{0,4},{1,3},{2,6},{3,1},{4,0},{5,7},{6,2},{7,5},{8,12},{9,11},{10,... | collective-permute-start | bytes 552968 | tf_op jit(solution)/shard_map/ppermute | solution.py:876
  368.3 43.4 %collective-permute-start.60 = (bf16[24,1536]{1,0:T(8,128)(2,1)}, bf16[24,1536]{1,0:T(8,128)(2,1)}, u32[]{:S(2)}, u32[]{:S(2)}) collective-permute-start(bf16[24,1536]{1,0:T(8,128)(2,1)} %select_convert_fusion.3), channel_id=1, source_target_pairs={{0,1},{1,0},{2,3},{3,2},{4,5},{5,4},{6,7},{7,6},{8,9},{9,8},{10,11... | collective-permute-start | bytes 221192 | tf_op jit(solution)/shard_map/ppermute | solution.py:876
  370.9 40.9 %collective-permute-start.59 = (bf16[384,1536]{1,0:T(8,128)(2,1)}, bf16[384,1536]{1,0:T(8,128)(2,1)}, u32[]{:S(2)}, u32[]{:S(2)}) collective-permute-start(bf16[384,1536]{1,0:T(8,128)(2,1)} %add_convert_fusion.3), channel_id=1, source_target_pairs={{0,2},{1,5},{2,0},{3,7},{4,6},{5,1},{6,4},{7,3},{8,10},{9,13},{10,... | collective-permute-start | bytes 3538952 | tf_op jit(solution)/shard_map/ppermute | solution.py:876
  373.9 22.1 %collective-permute-start.68 = (bf16[96,1280]{1,0:T(8,128)(2,1)}, bf16[96,1280]{1,0:T(8,128)(2,1)S(1)}, u32[]{:S(2)}, u32[]{:S(2)}) collective-permute-start(bf16[96,1280]{1,0:T(8,128)(2,1)} %get-tuple-element.327), channel_id=1, source_target_pairs={{0,24},{1,25},{2,26},{3,27},{4,28},{5,29},{6,30},{7,31},{8,0},{9,1... | collective-permute-start | bytes 737288 | tf_op jit(solution)/shard_map/ppermute | solution.py:876
  376.5 21.0 %collective-permute-start.69 = (bf16[96,1280]{1,0:T(8,128)(2,1)S(1)}, bf16[96,1280]{1,0:T(8,128)(2,1)S(1)}, u32[]{:S(2)}, u32[]{:S(2)}) collective-permute-start(bf16[96,1280]{1,0:T(8,128)(2,1)S(1)} %get-tuple-element.329), channel_id=1, source_target_pairs={{0,16},{1,17},{2,18},{3,19},{4,20},{5,21},{6,22},{7,23},{8,24},{9,... | collective-permute-start | bytes 737288 | tf_op jit(solution)/shard_map/ppermute | solution.py:876
  396.0 31.0 %collective-permute-start.73 = (bf16[384,1920]{1,0:T(8,128)(2,1)S(1)}, bf16[384,1920]{1,0:T(8,128)(2,1)S(1)}, u32[]{:S(2)}, u32[]{:S(2)}) collective-permute-start(bf16[384,1920]{1,0:T(8,128)(2,1)S(1)} %copy-done.38), channel_id=1, source_target_pairs={{0,2},{1,5},{2,0},{3,7},{4,6},{5,1},{6,4},{7,3},{8,10},{9,13},{10,... | collective-permute-start | bytes 4423688 | tf_op jit(solution)/shard_map/ppermute | solution.py:876
  405.8 75.2 %collective-permute-start.85 = (bf16[24,1920]{1,0:T(8,128)(2,1)S(1)}, bf16[24,1920]{1,0:T(8,128)(2,1)S(1)}, u32[]{:S(2)}, u32[]{:S(2)}) collective-permute-start(bf16[24,1920]{1,0:T(8,128)(2,1)S(1)} %select_convert_fusion), channel_id=1, source_target_pairs={{0,1},{1,0},{2,3},{3,2},{4,5},{5,4},{6,7},{7,6},{8,9},{9,8},{10,11... | collective-permute-start | bytes 276488 | tf_op jit(solution)/shard_map/ppermute | solution.py:876
  416.2 26.7 %collective-permute-start.61 = (bf16[768,1280]{1,0:T(8,128)(2,1)S(1)}, bf16[768,1280]{1,0:T(8,128)(2,1)S(1)}, u32[]{:S(2)}, u32[]{:S(2)}) collective-permute-start(bf16[768,1280]{1,0:T(8,128)(2,1)S(1)} %copy-done.66), channel_id=1, source_target_pairs={{0,1},{1,0},{2,3},{3,2},{4,5},{5,4},{6,7},{7,6},{8,9},{9,8},{10,11... | collective-permute-start | bytes 5898248 | tf_op jit(solution)/shard_map/ppermute | solution.py:876
  426.8 13.9 %collective-permute-start.81 = (bf16[48,1536]{1,0:T(8,128)(2,1)S(1)}, bf16[48,1536]{1,0:T(8,128)(2,1)S(1)}, u32[]{:S(2)}, u32[]{:S(2)}) collective-permute-start(bf16[48,1536]{1,0:T(8,128)(2,1)S(1)} %get-tuple-element.347), channel_id=1, source_target_pairs={{0,16},{1,17},{2,18},{3,19},{4,20},{5,21},{6,22},{7,23},{8,24},{9,... | collective-permute-start | bytes 442376 | tf_op jit(solution)/shard_map/ppermute | solution.py:876
  427.0 13.7 %collective-permute-start.82 = (bf16[48,1536]{1,0:T(8,128)(2,1)S(1)}, bf16[48,1536]{1,0:T(8,128)(2,1)S(1)}, u32[]{:S(2)}, u32[]{:S(2)}) collective-permute-start(bf16[48,1536]{1,0:T(8,128)(2,1)S(1)} %get-tuple-element.346), channel_id=1, source_target_pairs={{0,8},{1,9},{2,10},{3,11},{4,12},{5,13},{6,14},{7,15},{8,16},{9,17... | collective-permute-start | bytes 442376 | tf_op jit(solution)/shard_map/ppermute | solution.py:876
  431.2 12.9 %collective-permute-start.74 = (bf16[192,1920]{1,0:T(8,128)(2,1)S(1)}, bf16[192,1920]{1,0:T(8,128)(2,1)S(1)}, u32[]{:S(2)}, u32[]{:S(2)}) collective-permute-start(bf16[192,1920]{1,0:T(8,128)(2,1)S(1)} %add_convert_fusion.10), channel_id=1, source_target_pairs={{0,4},{1,3},{2,6},{3,1},{4,0},{5,7},{6,2},{7,5},{8,12},{9,11},{10,... | collective-permute-start | bytes 2211848 | tf_op jit(solution)/shard_map/ppermute | solution.py:876
  442.5 39.2 %collective-permute-start.83 = (bf16[24,1536]{1,0:T(8,128)(2,1)S(1)}, bf16[24,1536]{1,0:T(8,128)(2,1)S(1)}, u32[]{:S(2)}, u32[]{:S(2)}) collective-permute-start(bf16[24,1536]{1,0:T(8,128)(2,1)S(1)} %select_convert_fusion.2), channel_id=1, source_target_pairs={{0,1},{1,0},{2,3},{3,2},{4,5},{5,4},{6,7},{7,6},{8,9},{9,8},{10,11... | collective-permute-start | bytes 221192 | tf_op jit(solution)/shard_map/ppermute | solution.py:876
  443.1 14.2 %collective-permute-start.62 = (bf16[384,1280]{1,0:T(8,128)(2,1)S(1)}, bf16[384,1280]{1,0:T(8,128)(2,1)S(1)}, u32[]{:S(2)}, u32[]{:S(2)}) collective-permute-start(bf16[384,1280]{1,0:T(8,128)(2,1)S(1)} %add_convert_fusion.7), channel_id=1, source_target_pairs={{0,2},{1,5},{2,0},{3,7},{4,6},{5,1},{6,4},{7,3},{8,10},{9,13},{10,... | collective-permute-start | bytes 2949128 | tf_op jit(solution)/shard_map/ppermute | solution.py:876
  445.7 14.8 %collective-permute-start.75 = (bf16[48,1920]{1,0:T(8,128)(2,1)S(1)}, bf16[48,1920]{1,0:T(8,128)(2,1)S(1)}, u32[]{:S(2)}, u32[]{:S(2)}) collective-permute-start(bf16[48,1920]{1,0:T(8,128)(2,1)S(1)} %get-tuple-element.342), channel_id=1, source_target_pairs={{0,24},{1,25},{2,26},{3,27},{4,28},{5,29},{6,30},{7,31},{8,0},{9,1... | collective-permute-start | bytes 552968 | tf_op jit(solution)/shard_map/ppermute | solution.py:876
  449.0 22.9 %collective-permute-start.76 = (bf16[48,1920]{1,0:T(8,128)(2,1)S(1)}, bf16[48,1920]{1,0:T(8,128)(2,1)S(1)}, u32[]{:S(2)}, u32[]{:S(2)}) collective-permute-start(bf16[48,1920]{1,0:T(8,128)(2,1)S(1)} %get-tuple-element.344), channel_id=1, source_target_pairs={{0,16},{1,17},{2,18},{3,19},{4,20},{5,21},{6,22},{7,23},{8,24},{9,... | collective-permute-start | bytes 552968 | tf_op jit(solution)/shard_map/ppermute | solution.py:876
  457.3 14.6 %collective-permute-start.77 = (bf16[48,1920]{1,0:T(8,128)(2,1)S(1)}, bf16[48,1920]{1,0:T(8,128)(2,1)S(1)}, u32[]{:S(2)}, u32[]{:S(2)}) collective-permute-start(bf16[48,1920]{1,0:T(8,128)(2,1)S(1)} %get-tuple-element.343), channel_id=1, source_target_pairs={{0,8},{1,9},{2,10},{3,11},{4,12},{5,13},{6,14},{7,15},{8,16},{9,17... | collective-permute-start | bytes 552968 | tf_op jit(solution)/shard_map/ppermute | solution.py:876
  460.5 12.6 %collective-permute-start.63 = (bf16[192,1280]{1,0:T(8,128)(2,1)S(1)}, bf16[192,1280]{1,0:T(8,128)(2,1)S(1)}, u32[]{:S(2)}, u32[]{:S(2)}) collective-permute-start(bf16[192,1280]{1,0:T(8,128)(2,1)S(1)} %add_convert_fusion.14), channel_id=1, source_target_pairs={{0,4},{1,3},{2,6},{3,1},{4,0},{5,7},{6,2},{7,5},{8,12},{9,11},{10,... | collective-permute-start | bytes 1474568 | tf_op jit(solution)/shard_map/ppermute | solution.py:876
  474.2 11.0 %collective-permute-start.64 = (bf16[48,1280]{1,0:T(8,128)(2,1)}, bf16[48,1280]{1,0:T(8,128)(2,1)S(1)}, u32[]{:S(2)}, u32[]{:S(2)}) collective-permute-start(bf16[48,1280]{1,0:T(8,128)(2,1)} %get-tuple-element.348), channel_id=1, source_target_pairs={{0,24},{1,25},{2,26},{3,27},{4,28},{5,29},{6,30},{7,31},{8,0},{9,1... | collective-permute-start | bytes 368648 | tf_op jit(solution)/shard_map/ppermute | solution.py:876
  474.2 15.3 %collective-permute-start.65 = (bf16[48,1280]{1,0:T(8,128)(2,1)}, bf16[48,1280]{1,0:T(8,128)(2,1)}, u32[]{:S(2)}, u32[]{:S(2)}) collective-permute-start(bf16[48,1280]{1,0:T(8,128)(2,1)} %get-tuple-element.350), channel_id=1, source_target_pairs={{0,16},{1,17},{2,18},{3,19},{4,20},{5,21},{6,22},{7,23},{8,24},{9,... | collective-permute-start | bytes 368648 | tf_op jit(solution)/shard_map/ppermute | solution.py:876
  (89 other events, 670.2 us)
